TPU v7x, 128 devices: a whole 4x4x4 slice. The times are simulated.
128 devices in a mesh: seq: 8 (over y, core), vocab: 16 (over x, z).
Axes of the slice: x: 4, y: 4, z: 4, core: 2. Of those that a mesh axis runs over, the one named last changes fastest.
Arguments:
- hidden: bfloat16 [2, 4096, 2048], P(None, 'seq'), may hold values from -6 to 6
- w_inner: bfloat16 [2, 2048, 2, 4096], P(None, None, None, 'vocab'), may hold values from -0.125 to 0.125
- w_state: bfloat16 [2, 2048, 2, 128], replicated, may hold values from -0.125 to 0.125
- w_step: bfloat16 [2, 2048, 64], P(None, None, 'vocab'), may hold values from -0.125 to 0.125
- step_bias: float32 [2, 64], P(None, 'vocab'), may hold values from -5 to -2
- rate: float32 [2, 64], P(None, 'vocab'), may hold values from 0.01 to 1.5
- skip_gain: float32 [2, 64], P(None, 'vocab'), may hold values from 0.5 to 1.5
- norm_gain: float32 [2, 4096], P(None, 'vocab'), may hold values from 0.1 to 1.9
- w_out: bfloat16 [2, 4096, 2048], P(None, 'vocab'), may hold values from -0.09375 to 0.09375
- final_gain: float32 [2, 2048], replicated, may hold values from 0.1 to 1.9
- head: bfloat16 [2, 2048, 26624], P(None, None, 'vocab'), as said below
- pool: bfloat16 [2, 16, 64, 64, 128], P(None, None, 'vocab'), may hold values from -3 to 3
- targets: int32 [4096], P('seq'), may hold values from 0 to 26623
- segment_ids: int32 [4096], P('seq'), may hold values from 0 to 3, never falling along the last dimension, each value on 1 to 2048 neighbouring positions
- flags: int32 [4], replicated, may hold values from 0 to 1, as said below
- pages: int32 [4], replicated, may hold values from 0 to 15
- live: int32 [16], P('seq'), may hold values 0 or 1
- owners: int32 [4], replicated, may hold values from 0 to 7
Outputs:
- token_diff: float32 [4096], P('seq')
- owned: float32 [8, 4], P('seq')
Inputs may be any that keep to these rules, and one draw needn't show every extreme that they name: `segment_ids`: ids never fall along the positions, and every id from 0 to 3 occurs. `flags`: exactly one sequence has flag 0. `head`: each vocabulary column's entries are normal with a scale between 3 and 30 over the square root of 2048.
All inputs are finite; a program needn't handle non-finite values. No bound on the sum of `live` on one device may be relied on, other than what follows from the above.
Results may differ from a plain program's by a relative error of at most 0.029.
Values may be sent and summed in bfloat16 or wider, within the bound.
No kernel may reach another device: no remote copies, remote signals or barrier semaphores. Data moves between devices by JAX's collectives and lax.ppermute only.
A program may use at most 128 MiB of HBM per device.

v0:
```python
import jax
import jax.numpy as jnp
from jax import lax
from jax.sharding import PartitionSpec as P

SPAN = 256


NORM_EPS = 1e-05
HIGH = lax.Precision.HIGHEST


def passed_along(value, axis, by):
    devices = lax.axis_size(axis)
    pairs = [(i, i + by) for i in range(devices) if 0 <= i + by < devices]
    return lax.ppermute(value, axis, pairs)


def merged_2(value, axis, combine):
    everything = jax.tree.map(lambda part: lax.all_gather(part, axis), value)
    first = jax.tree.map(lambda part: part[0], everything)

    def lap(k, so_far):
        return combine(so_far, jax.tree.map(lambda part: part[k], everything))

    return lax.fori_loop(1, lax.axis_size(axis), lap, first)


def block_step(carried, pieces):
    values_in, input_map, output_map, log_decay, step_size, onehot, segment = pieces
    length = values_in.shape[0]
    running = jnp.cumsum(log_decay, axis=0)
    seg_decay = jnp.dot(onehot.T, log_decay, precision=HIGH)
    upto_end = jnp.cumsum(seg_decay, axis=0)
    before = upto_end - seg_decay
    end_rows = jnp.dot(onehot, upto_end, precision=HIGH)
    start_rows = jnp.dot(onehot, before, precision=HIGH)
    places = jnp.arange(length, dtype=jnp.int32)
    allowed = (places[:, None] >= places[None, :]) & (segment[:, None] == segment[None, :])
    log_gap = running.T[:, :, None] - running.T[:, None, :]
    decay_kernel = jnp.exp(jnp.where(allowed[None], log_gap, -jnp.inf))
    scores = jnp.dot(output_map, input_map.T, precision=HIGH)
    weights = decay_kernel * scores[None] * step_size.T[:, None, :]
    mixer_out = jnp.einsum("hts,shp->thp", weights, values_in, precision=HIGH)
    from_state = jnp.einsum("tn,jhpn->tjhp", output_map, carried, precision=HIGH)
    picked = jnp.sum(onehot[:, :, None, None] * from_state, axis=1)
    mixer_out = mixer_out + picked * jnp.exp(running - start_rows)[:, :, None]
    retain = jnp.exp(end_rows - running) * step_size
    spread = onehot[:, :, None, None] * (retain[:, None, :, None] * values_in[:, None, :, :])
    added_state = jnp.einsum("tjhp,tn->jhpn", spread, input_map, precision=HIGH)
    carried = jnp.exp(seg_decay)[:, :, None, None] * carried + added_state
    return (carried, mixer_out)


def scan_blocks(
    values_in, input_map, output_map, log_decay, step_size, onehot, segment, init_state, length
):
    turns = values_in.shape[0] // length

    def to_blocks(array):
        return array.reshape((turns, length) + array.shape[1:])

    pieces = tuple(
        (
            to_blocks(array)
            for array in (values_in, input_map, output_map, log_decay, step_size, onehot, segment)
        )
    )
    end_state, outputs = lax.scan(block_step, init_state, pieces)
    return (outputs.reshape(values_in.shape), end_state)


def combine_states(earlier, later):
    return (earlier[0] * later[0], later[0][:, :, None, None] * earlier[1] + later[1])


def merge_rows(left_side, right_side):
    merged = []
    for offset_index in range(0, 6, 3):
        left_top, left_total, left_pick = left_side[offset_index : offset_index + 3]
        right_top, right_total, right_pick = right_side[offset_index : offset_index + 3]
        row_top = jnp.maximum(left_top, right_top)
        merged.append(row_top)
        merged.append(
            left_total * jnp.exp(left_top - row_top) + right_total * jnp.exp(right_top - row_top)
        )
        merged.append(left_pick + right_pick)
    return tuple(merged)


def per_device(
    hidden,
    w_inner,
    w_state,
    w_step,
    step_bias,
    rate,
    skip_gain,
    norm_gain,
    w_out,
    final_gain,
    head,
    pool,
    targets,
    segment_ids,
    flags,
    pages,
    live,
    owners,
):
    row_count = targets.shape[0]
    seq_count = flags.shape[0]
    head_count = rate.shape[1]
    head_width = pool.shape[3]
    state_width = pool.shape[4]
    page_count = pool.shape[1]
    model_width = hidden.shape[2]
    inner_local = w_inner.shape[3]
    inner_total = inner_local * lax.axis_size("vocab")
    vocab_local = head.shape[2]
    seg_onehot = (segment_ids[:, None] == jnp.arange(seq_count, dtype=jnp.int32)[None, :]).astype(
        jnp.float32
    )
    page_onehot = (pages[:, None] == jnp.arange(page_count, dtype=jnp.int32)[None, :]).astype(
        jnp.bfloat16
    )
    start_weight = flags.astype(jnp.float32)[:, None, None, None]
    live_rows = jnp.repeat(live.astype(jnp.float32), SPAN)
    target_local = targets - lax.axis_index("vocab") * vocab_local
    hits = target_local[:, None] == jnp.arange(vocab_local, dtype=jnp.int32)[None, :]
    is_first = lax.axis_index("seq") == 0
    row_stats = []
    for which_model in range(2):
        tokens_in = hidden[which_model]
        inner_proj = jnp.dot(
            tokens_in,
            w_inner[which_model].reshape(model_width, 2 * inner_local),
            preferred_element_type=jnp.float32,
        )
        gate_in = inner_proj[:, :inner_local]
        values_bf = jax.nn.silu(inner_proj[:, inner_local:]).astype(jnp.bfloat16)
        values_in = (
            lax.optimization_barrier(values_bf)
            .astype(jnp.float32)
            .reshape(row_count, head_count, head_width)
        )
        state_bf = jax.nn.silu(
            jnp.dot(
                tokens_in,
                w_state[which_model].reshape(model_width, 2 * state_width),
                preferred_element_type=jnp.float32,
            )
        ).astype(jnp.bfloat16)
        state_proj = lax.optimization_barrier(state_bf).astype(jnp.float32)
        input_map = state_proj[:, :state_width]
        output_map = state_proj[:, state_width:]
        step_size = jax.nn.softplus(
            jnp.dot(tokens_in, w_step[which_model], preferred_element_type=jnp.float32)
            + step_bias[which_model][None, :]
        )
        log_decay = -step_size * rate[which_model][None, :]
        zero_state = jnp.zeros((seq_count, head_count, head_width, state_width), jnp.float32)
        mixer_out, block_state = scan_blocks(
            values_in,
            input_map,
            output_map,
            log_decay,
            step_size,
            seg_onehot,
            segment_ids,
            zero_state,
            SPAN,
        )
        seg_decay = jnp.dot(seg_onehot.T, log_decay, precision=HIGH)
        before = jnp.cumsum(seg_decay, axis=0) - seg_decay
        running = jnp.cumsum(log_decay, axis=0)
        block_decay = jnp.exp(seg_decay)
        identity = (jnp.ones_like(block_decay), jnp.zeros_like(block_state))

        def relay_step(turn_index, current):
            joined = combine_states(current, (block_decay, block_state))
            moved = passed_along((joined[0], joined[1]), "seq", 1)
            return (
                jnp.where(is_first, identity[0], moved[0]),
                jnp.where(is_first, identity[1], moved[1]),
            )

        prior = lax.fori_loop(0, lax.axis_size("seq") - 1, relay_step, identity)
        pool_rows = pool[which_model].reshape(page_count, head_count * head_width * state_width)
        init_state = (
            jnp.dot(page_onehot, pool_rows, preferred_element_type=jnp.float32).reshape(
                zero_state.shape
            )
            * start_weight
        )
        carried = prior[1] + prior[0][:, :, None, None] * init_state
        from_state = jnp.einsum("tn,jhpn->tjhp", output_map, carried, precision=HIGH)
        picked = jnp.sum(seg_onehot[:, :, None, None] * from_state, axis=1)
        start_rows = jnp.dot(seg_onehot, before, precision=HIGH)
        mixer_out = mixer_out + picked * jnp.exp(running - start_rows)[:, :, None]
        mixer_out = mixer_out + skip_gain[which_model][None, :, None] * values_in
        gated_rows = mixer_out.reshape(row_count, inner_local) * jax.nn.silu(gate_in)
        square_sum = lax.psum(jnp.sum(gated_rows * gated_rows, axis=1), "vocab")
        mixed_rows = (
            gated_rows
            * lax.rsqrt(square_sum / inner_total + NORM_EPS)[:, None]
            * norm_gain[which_model][None, :]
        ).astype(jnp.bfloat16)
        out_part = jnp.dot(mixed_rows, w_out[which_model], preferred_element_type=jnp.float32)
        out_sum = lax.psum(out_part.astype(jnp.bfloat16), "vocab").astype(jnp.float32)
        residual = tokens_in.astype(jnp.float32) + out_sum
        normed = (
            residual
            * lax.rsqrt(jnp.mean(residual * residual, axis=1, keepdims=True) + NORM_EPS)
            * final_gain[which_model][None, :]
        ).astype(jnp.bfloat16)
        head_model = head[which_model]
        logits = jnp.dot(normed, head_model, preferred_element_type=jnp.float32)
        row_top = jnp.max(logits, axis=1)
        row_stats.append(row_top)
        row_stats.append(jnp.sum(jnp.exp(logits - row_top[:, None]), axis=1))
        row_stats.append(jnp.sum(jnp.where(hits, logits, 0.0), axis=1))
    merged = merged_2(
        (row_stats[0], row_stats[1], row_stats[2], row_stats[3], row_stats[4], row_stats[5]),
        "vocab",
        merge_rows,
    )
    policy_score = merged[2] - merged[0] - jnp.log(merged[1])
    frozen_score = merged[5] - merged[3] - jnp.log(merged[4])
    token_diff = live_rows * (policy_score - frozen_score)
    per_sequence = jnp.dot(seg_onehot.T, token_diff, precision=HIGH)
    owner_onehot = (
        owners[None, :] == jnp.arange(lax.axis_size("seq"), dtype=jnp.int32)[:, None]
    ).astype(jnp.float32)
    owned = lax.psum_scatter(
        owner_onehot * per_sequence[None, :], "seq", scatter_dimension=0, tiled=True
    )
    return (token_diff, owned)


def solution(mesh):
    placed = (
        P(None, "seq", None),
        P(None, None, None, "vocab"),
        P(),
        P(None, None, "vocab"),
        P(None, "vocab"),
        P(None, "vocab"),
        P(None, "vocab"),
        P(None, "vocab"),
        P(None, "vocab", None),
        P(),
        P(None, None, "vocab"),
        P(None, None, "vocab", None, None),
        P("seq"),
        P("seq"),
        P(),
        P(),
        P("seq"),
        P(),
    )
    return jax.shard_map(
        per_device,
        mesh=mesh,
        in_specs=placed,
        out_specs=(P("seq"), P("seq", None)),
        check_vma=False,
    )
```

profile of v0, /device:TPU:1, one launch (start us, length us, event | category | flops | bytes accessed | tf_op | source)
XLA Modules:
  0.0 602.6 jit_solution(8975860454961522274)
XLA Ops:
  10.1 5.7 fusion.199
  21.6 3.6 fusion.201
  27.0 2.3 compare_select_fusion.1
  30.4 28.6 %while.80 = (s32[]{:T(128)}, f32[4,4,64,128]{3,2,1,0:T(8,128)S(1)}, f32[2,256,4,64]{1,0,3,2:T(2,128)}, f32[2,256,4]{1,2,0:T(4,128)S(1)}, f32[2,256,4]{1,2,0:T(4,...) while((s32[]{:T(128)}, f32[4,4,64,128]{3,2,1,0:T(8,128)S(1)}, ...), condition=%wide.region_24.25_spmd.clone, body=%wide.region_19.24_spmd.clone.sunk | while | flops 1110264832 | bytes 6286312 | solution.py:69
  36.9 6.3 %dynamic_update_slice.12 = f32[2,256,4,64]{1,0,3,2:T(2,128)} dynamic-update-slice(f32[2,256,4,64]{1,0,3,2:T(2,128)} %get-tuple-element.1228, f32[1,256,4,64]{1,0,3,2:T(1,128)S(1)} %copy.265, s32[]{:T(128)} %get-tuple-element.1226, s32[]{:T(128)} %constant.137.clone.1..sunk.3, s32[]{:T(128)} %constant.137.clone.1..sunk.3, s32[]{:T(128)} %constant.137.clone.1..sunk.3) | dynamic-update-slice | bytes 524292 | tf_op jit(solution)/shard_map/while/body/jit(dynamic_update_index_in_dim)/dynamic_update_slice | solution.py:69
  51.2 6.3 %dynamic_update_slice.12 = f32[2,256,4,64]{1,0,3,2:T(2,128)} dynamic-update-slice(f32[2,256,4,64]{1,0,3,2:T(2,128)} %get-tuple-element.1228, f32[1,256,4,64]{1,0,3,2:T(1,128)S(1)} %copy.265, s32[]{:T(128)} %get-tuple-element.1226, s32[]{:T(128)} %constant.137.clone.1..sunk.3, s32[]{:T(128)} %constant.137.clone.1..sunk.3, s32[]{:T(128)} %constant.137.clone.1..sunk.3) | dynamic-update-slice | bytes 524292 | tf_op jit(solution)/shard_map/while/body/jit(dynamic_update_index_in_dim)/dynamic_update_slice | solution.py:69
  59.0 75.2 %while.81 = (s32[]{:T(128)}, f32[4,4]{1,0:T(4,128)S(1)}, f32[4,4,64,128]{3,2,1,0:T(8,128)S(1)}, pred[]{:T(512)}, f32[4,4]{1,0:T(4,128)S(1)}, /*index=5*/f32[4,4,64,128]{3,2,1,0:T(8,128)S(1)}, s32[]{:T(128)}, s32[]{:T(128)}) while((s32[]{:T(128)}, f32[4,4]{1,0:T(4,128)S(1)}, f32[4,4,64,128]{3,2,1,0:T(8,128)S(1)}, pred[]{:T(512)}, ...), condition=%wide.region_26.27_spmd.clone, body=%wide.region_25.26_spmd.clone.sunk | while | flops 524339 | bytes 4719410 | solution.py:188
  59.2 4.6 collective-permute-start.3
  63.8 1.9 collective-permute-start.2
  65.7 4.2 collective-permute-done.2
  70.1 4.4 collective-permute-start.3
  74.5 1.9 collective-permute-start.2
  76.4 4.2 collective-permute-done.2
  80.8 4.4 collective-permute-start.3
  87.1 4.2 collective-permute-done.2
  91.5 4.4 collective-permute-start.3
  97.9 4.2 collective-permute-done.2
  102.2 4.4 collective-permute-start.3
  108.6 4.2 collective-permute-done.2
  112.9 4.4 collective-permute-start.3
  117.4 1.9 collective-permute-start.2
  119.3 4.2 collective-permute-done.2
  123.7 4.4 collective-permute-start.3
  128.1 1.9 collective-permute-start.2
  130.0 4.2 collective-permute-done.2
  134.3 3.2 fusion.200
  140.6 2.3 compare_select_fusion.3
  145.6 2.2 copy.168
  151.2 2.7 multiply_convert_fusion.8
  155.8 26.6 %while.78 = (s32[]{:T(128)}, f32[4,4,64,128]{3,2,1,0:T(8,128)S(1)}, f32[2,256,4,64]{1,0,3,2:T(2,128)}, f32[2,256,4]{1,2,0:T(4,128)S(1)}, f32[2,256,4]{1,2,0:T(4,...) while((s32[]{:T(128)}, f32[4,4,64,128]{3,2,1,0:T(8,128)S(1)}, ...), condition=%wide.region_5.6_spmd.clone, body=%wide.region_0.5_spmd.clone.sunk | while | flops 1110264832 | bytes 6286312 | solution.py:69
  161.3 6.3 %dynamic_update_slice.11 = f32[2,256,4,64]{1,0,3,2:T(2,128)} dynamic-update-slice(f32[2,256,4,64]{1,0,3,2:T(2,128)} %get-tuple-element.1165, f32[1,256,4,64]{1,0,3,2:T(1,128)S(1)} %copy.257, s32[]{:T(128)} %get-tuple-element.1163, s32[]{:T(128)} %constant.137.clone.1..sunk.1, s32[]{:T(128)} %constant.137.clone.1..sunk.1, s32[]{:T(128)} %constant.137.clone.1..sunk.1) | dynamic-update-slice | bytes 524292 | tf_op jit(solution)/shard_map/while/body/jit(dynamic_update_index_in_dim)/dynamic_update_slice | solution.py:69
  174.6 6.3 %dynamic_update_slice.11 = f32[2,256,4,64]{1,0,3,2:T(2,128)} dynamic-update-slice(f32[2,256,4,64]{1,0,3,2:T(2,128)} %get-tuple-element.1165, f32[1,256,4,64]{1,0,3,2:T(1,128)S(1)} %copy.257, s32[]{:T(128)} %get-tuple-element.1163, s32[]{:T(128)} %constant.137.clone.1..sunk.1, s32[]{:T(128)} %constant.137.clone.1..sunk.1, s32[]{:T(128)} %constant.137.clone.1..sunk.1) | dynamic-update-slice | bytes 524292 | tf_op jit(solution)/shard_map/while/body/jit(dynamic_update_index_in_dim)/dynamic_update_slice | solution.py:69
  182.4 75.0 %while.79 = (s32[]{:T(128)}, f32[4,4]{1,0:T(4,128)S(1)}, f32[4,4,64,128]{3,2,1,0:T(8,128)S(1)}, pred[]{:T(512)}, f32[4,4]{1,0:T(4,128)S(1)}, /*index=5*/f32[4,4,64,128]{3,2,1,0:T(8,128)S(1)}, s32[]{:T(128)}, s32[]{:T(128)}) while((s32[]{:T(128)}, f32[4,4]{1,0:T(4,128)S(1)}, f32[4,4,64,128]{3,2,1,0:T(8,128)S(1)}, pred[]{:T(512)}, ...), condition=%wide.region_7.8_spmd.clone, body=%wide.region_6.7_spmd.clone.sunk | while | flops 524339 | bytes 4719410 | solution.py:188
  182.5 4.4 collective-permute-start.1
  186.9 1.9 collective-permute-start
  188.9 4.2 collective-permute-done
  193.3 4.4 collective-permute-start.1
  199.6 4.2 collective-permute-done
  204.0 4.4 collective-permute-start.1
  210.3 4.2 collective-permute-done
  214.7 4.4 collective-permute-start.1
  221.0 4.2 collective-permute-done
  225.4 4.4 collective-permute-start.1
  231.7 4.2 collective-permute-done
  236.1 4.4 collective-permute-start.1
  242.4 4.2 collective-permute-done
  246.8 4.4 collective-permute-start.1
  253.2 4.2 collective-permute-done
  269.4 43.3 %all-reduce.1 = (f32[512]{0:T(512)S(1)}, f32[512]{0:T(512)S(1)}) all-reduce(f32[512]{0:T(512)S(1)} %get-tuple-element.797, f32[512]{0:T(512)S(1)} %get-tuple-element.795), channel_id=1, replica_groups=mesh['seq'=8,'vocab'=16] {'vocab'}, use_global_device_ids=true, to_apply=%region_13.14 | all-reduce | flops 1024 | bytes 8192 | tf_op jit(solution)/shard_map/psum | solution.py:203
  312.7 3.4 convolution_convert_fusion
  316.1 3.4 convolution_convert_fusion.1
  320.3 107.4 %all-reduce.5.cloned.1.call-done = (bf16[512,2048]{1,0:T(8,128)(2,1)}, bf16[512,2048]{1,0:T(8,128)(2,1)}) async-done(((bf16[512,2048]{1,0:T(8,128)(2,1)}, bf16[512,2048]{1,0:T(8,128)(2,1)}), (bf16[512,2048]{1,0:T(8,128)(2,1)}, bf16[512,2048]{1,0:T(8,128)(2,1)})) %all-reduce.5.cloned.1.call-update) | async-done | bytes 4194320 | tf_op jit(solution)/shard_map/psum | solution.py:210
  427.7 5.0 multiply_reduce_fusion
  433.0 7.5 %fusion.209 = (f32[512]{0:T(512)S(1)}, f32[512,1664]{1,0:T(8,128)S(1)}) fusion(bf16[2,2048,1664]{2,1,0:T(8,128)(2,1)} %param.38, bf16[512,2048]{1,0:T(8,128)(2,1)S(1)} %copy-done.10, f32[2048]{0:T(1024)S(1)} %bitcast.559, f32[512]{0:T(512)S(1)} %add_rsqrt_fusion, bf16[2,512,2048]{2,1,0:T(8,128)(2,1)S(1)} %copy-done.4), kind=kOutput, calls=%fused_computation.312 | convolution fusion | flops 3496803840 | bytes 14430208 | tf_op jit(solution)/shard_map/dot_general | solution.py:218
  440.5 4.4 fusion.208
  444.9 2.6 select_reduce_fusion
  447.5 17.7 %all-gather.7 = f32[16,1,512]{2,1,0:T(1,128)S(1)} all-gather(f32[1,1,512]{2,1,0:T(1,128)S(1)} %bitcast.555), channel_id=3, replica_groups=mesh['seq'=8,'vocab'=16] {'vocab'}, dimensions={0}, use_global_device_ids=true | all-gather | bytes 34816 | tf_op jit(solution)/shard_map/all_gather | solution.py:20
  465.2 15.8 %all-gather.8 = f32[16,1,512]{2,1,0:T(1,128)S(1)} all-gather(f32[1,1,512]{2,1,0:T(1,128)S(1)} %bitcast.554), channel_id=4, replica_groups=mesh['seq'=8,'vocab'=16] {'vocab'}, dimensions={0}, use_global_device_ids=true | all-gather | bytes 34816 | tf_op jit(solution)/shard_map/all_gather | solution.py:20
  481.0 17.0 %all-gather.10 = f32[16,1,512]{2,1,0:T(1,128)S(1)} all-gather(f32[1,1,512]{2,1,0:T(1,128)S(1)} %bitcast.553), channel_id=6, replica_groups=mesh['seq'=8,'vocab'=16] {'vocab'}, dimensions={0}, use_global_device_ids=true | all-gather | bytes 34816 | tf_op jit(solution)/shard_map/all_gather | solution.py:20
  498.0 15.7 %all-gather.11 = f32[16,1,512]{2,1,0:T(1,128)S(1)} all-gather(f32[1,1,512]{2,1,0:T(1,128)S(1)} %bitcast.552), channel_id=7, replica_groups=mesh['seq'=8,'vocab'=16] {'vocab'}, dimensions={0}, use_global_device_ids=true | all-gather | bytes 34816 | tf_op jit(solution)/shard_map/all_gather | solution.py:20
  513.7 17.0 %all-gather.9 = f32[16,1,512]{2,1,0:T(1,128)S(1)} all-gather(f32[1,1,512]{2,1,0:T(1,128)S(1)} %bitcast.550), channel_id=5, replica_groups=mesh['seq'=8,'vocab'=16] {'vocab'}, dimensions={0}, use_global_device_ids=true | all-gather | bytes 34816 | tf_op jit(solution)/shard_map/all_gather | solution.py:20
  530.8 15.8 %all-gather.6 = f32[16,1,512]{2,1,0:T(1,128)S(1)} all-gather(f32[1,1,512]{2,1,0:T(1,128)S(1)} %bitcast.551), channel_id=2, replica_groups=mesh['seq'=8,'vocab'=16] {'vocab'}, dimensions={0}, use_global_device_ids=true | all-gather | bytes 34816 | tf_op jit(solution)/shard_map/all_gather | solution.py:20
  546.6 2.6 while.77
  549.4 45.1 %all-reduce = f32[8,4]{1,0:T(8,128)S(1)} all-reduce(f32[8,4]{1,0:T(8,128)S(1)} %fusion.187), channel_id=8, replica_groups=mesh['seq'=8,'vocab'=16] {'seq'}, use_global_device_ids=true, to_apply=%region_40.41.clone | all-reduce | flops 32 | bytes 256
  (457 shorter events, 87.3 us)
Async XLA Ops:
  7.2 420.5 %all-reduce.5.cloned.1.call-start = ((), (), s32[]{:S(2)}) async-start(), calls=%async_computation | async-start | bytes 8388608 | tf_op jit(solution)/shard_map/psum | solution.py:210
  15.8 2.2 copy-start.1
  19.3 1.0 copy-start.11
  21.6 3.6 copy-start.2
  25.2 1.8 copy-start.25
  26.0 0.7 copy-start.13
  26.0 3.3 copy-start.17
  59.2 10.7 %collective-permute-start.3 = (f32[4,4,64,128]{3,2,1,0:T(8,128)S(1)}, f32[4,4,64,128]{3,2,1,0:T(8,128)S(1)}, u32[]{:S(2)}, u32[]{:S(2)}) collective-permute-start(f32[4,4,64,128]{3,2,1,0:T(8,128)S(1)} %fusion.306), channel_id=1, source_target_pairs={{0,16},{16,32},{32,48},{48,64},{64,80},{80,96},{96,112},{1,17},{17... | collective-permute-start | bytes 1572872 | tf_op jit(solution)/shard_map/while/body/eval_jaxpr/ppermute | solution.py:16
  63.8 6.1 %collective-permute-start.2 = (f32[4,4]{1,0:T(4,128)S(1)}, f32[4,4]{1,0:T(4,128)S(1)}, u32[]{:S(2)}, u32[]{:S(2)}) collective-permute-start(f32[4,4]{1,0:T(4,128)S(1)} %select_multiply_fusion.7), channel_id=1, source_target_pairs={{0,16},{16,32},{32,48},{48,64},{64,80},{80,96},{96,112},{1,17},{17... | collective-permute-start | bytes 200 | tf_op jit(solution)/shard_map/while/body/eval_jaxpr/ppermute | solution.py:16
  70.1 10.5 %collective-permute-start.3 = (f32[4,4,64,128]{3,2,1,0:T(8,128)S(1)}, f32[4,4,64,128]{3,2,1,0:T(8,128)S(1)}, u32[]{:S(2)}, u32[]{:S(2)}) collective-permute-start(f32[4,4,64,128]{3,2,1,0:T(8,128)S(1)} %fusion.306), channel_id=1, source_target_pairs={{0,16},{16,32},{32,48},{48,64},{64,80},{80,96},{96,112},{1,17},{17... | collective-permute-start | bytes 1572872 | tf_op jit(solution)/shard_map/while/body/eval_jaxpr/ppermute | solution.py:16
  74.5 6.1 %collective-permute-start.2 = (f32[4,4]{1,0:T(4,128)S(1)}, f32[4,4]{1,0:T(4,128)S(1)}, u32[]{:S(2)}, u32[]{:S(2)}) collective-permute-start(f32[4,4]{1,0:T(4,128)S(1)} %select_multiply_fusion.7), channel_id=1, source_target_pairs={{0,16},{16,32},{32,48},{48,64},{64,80},{80,96},{96,112},{1,17},{17... | collective-permute-start | bytes 200 | tf_op jit(solution)/shard_map/while/body/eval_jaxpr/ppermute | solution.py:16
  80.8 10.5 %collective-permute-start.3 = (f32[4,4,64,128]{3,2,1,0:T(8,128)S(1)}, f32[4,4,64,128]{3,2,1,0:T(8,128)S(1)}, u32[]{:S(2)}, u32[]{:S(2)}) collective-permute-start(f32[4,4,64,128]{3,2,1,0:T(8,128)S(1)} %fusion.306), channel_id=1, source_target_pairs={{0,16},{16,32},{32,48},{48,64},{64,80},{80,96},{96,112},{1,17},{17... | collective-permute-start | bytes 1572872 | tf_op jit(solution)/shard_map/while/body/eval_jaxpr/ppermute | solution.py:16
  85.2 6.1 %collective-permute-start.2 = (f32[4,4]{1,0:T(4,128)S(1)}, f32[4,4]{1,0:T(4,128)S(1)}, u32[]{:S(2)}, u32[]{:S(2)}) collective-permute-start(f32[4,4]{1,0:T(4,128)S(1)} %select_multiply_fusion.7), channel_id=1, source_target_pairs={{0,16},{16,32},{32,48},{48,64},{64,80},{80,96},{96,112},{1,17},{17... | collective-permute-start | bytes 200 | tf_op jit(solution)/shard_map/while/body/eval_jaxpr/ppermute | solution.py:16
  91.5 10.5 %collective-permute-start.3 = (f32[4,4,64,128]{3,2,1,0:T(8,128)S(1)}, f32[4,4,64,128]{3,2,1,0:T(8,128)S(1)}, u32[]{:S(2)}, u32[]{:S(2)}) collective-permute-start(f32[4,4,64,128]{3,2,1,0:T(8,128)S(1)} %fusion.306), channel_id=1, source_target_pairs={{0,16},{16,32},{32,48},{48,64},{64,80},{80,96},{96,112},{1,17},{17... | collective-permute-start | bytes 1572872 | tf_op jit(solution)/shard_map/while/body/eval_jaxpr/ppermute | solution.py:16
  95.9 6.1 %collective-permute-start.2 = (f32[4,4]{1,0:T(4,128)S(1)}, f32[4,4]{1,0:T(4,128)S(1)}, u32[]{:S(2)}, u32[]{:S(2)}) collective-permute-start(f32[4,4]{1,0:T(4,128)S(1)} %select_multiply_fusion.7), channel_id=1, source_target_pairs={{0,16},{16,32},{32,48},{48,64},{64,80},{80,96},{96,112},{1,17},{17... | collective-permute-start | bytes 200 | tf_op jit(solution)/shard_map/while/body/eval_jaxpr/ppermute | solution.py:16
  102.2 10.5 %collective-permute-start.3 = (f32[4,4,64,128]{3,2,1,0:T(8,128)S(1)}, f32[4,4,64,128]{3,2,1,0:T(8,128)S(1)}, u32[]{:S(2)}, u32[]{:S(2)}) collective-permute-start(f32[4,4,64,128]{3,2,1,0:T(8,128)S(1)} %fusion.306), channel_id=1, source_target_pairs={{0,16},{16,32},{32,48},{48,64},{64,80},{80,96},{96,112},{1,17},{17... | collective-permute-start | bytes 1572872 | tf_op jit(solution)/shard_map/while/body/eval_jaxpr/ppermute | solution.py:16
  106.6 6.1 %collective-permute-start.2 = (f32[4,4]{1,0:T(4,128)S(1)}, f32[4,4]{1,0:T(4,128)S(1)}, u32[]{:S(2)}, u32[]{:S(2)}) collective-permute-start(f32[4,4]{1,0:T(4,128)S(1)} %select_multiply_fusion.7), channel_id=1, source_target_pairs={{0,16},{16,32},{32,48},{48,64},{64,80},{80,96},{96,112},{1,17},{17... | collective-permute-start | bytes 200 | tf_op jit(solution)/shard_map/while/body/eval_jaxpr/ppermute | solution.py:16
  112.9 10.5 %collective-permute-start.3 = (f32[4,4,64,128]{3,2,1,0:T(8,128)S(1)}, f32[4,4,64,128]{3,2,1,0:T(8,128)S(1)}, u32[]{:S(2)}, u32[]{:S(2)}) collective-permute-start(f32[4,4,64,128]{3,2,1,0:T(8,128)S(1)} %fusion.306), channel_id=1, source_target_pairs={{0,16},{16,32},{32,48},{48,64},{64,80},{80,96},{96,112},{1,17},{17... | collective-permute-start | bytes 1572872 | tf_op jit(solution)/shard_map/while/body/eval_jaxpr/ppermute | solution.py:16
  117.4 6.1 %collective-permute-start.2 = (f32[4,4]{1,0:T(4,128)S(1)}, f32[4,4]{1,0:T(4,128)S(1)}, u32[]{:S(2)}, u32[]{:S(2)}) collective-permute-start(f32[4,4]{1,0:T(4,128)S(1)} %select_multiply_fusion.7), channel_id=1, source_target_pairs={{0,16},{16,32},{32,48},{48,64},{64,80},{80,96},{96,112},{1,17},{17... | collective-permute-start | bytes 200 | tf_op jit(solution)/shard_map/while/body/eval_jaxpr/ppermute | solution.py:16
  123.7 10.5 %collective-permute-start.3 = (f32[4,4,64,128]{3,2,1,0:T(8,128)S(1)}, f32[4,4,64,128]{3,2,1,0:T(8,128)S(1)}, u32[]{:S(2)}, u32[]{:S(2)}) collective-permute-start(f32[4,4,64,128]{3,2,1,0:T(8,128)S(1)} %fusion.306), channel_id=1, source_target_pairs={{0,16},{16,32},{32,48},{48,64},{64,80},{80,96},{96,112},{1,17},{17... | collective-permute-start | bytes 1572872 | tf_op jit(solution)/shard_map/while/body/eval_jaxpr/ppermute | solution.py:16
  128.1 6.1 %collective-permute-start.2 = (f32[4,4]{1,0:T(4,128)S(1)}, f32[4,4]{1,0:T(4,128)S(1)}, u32[]{:S(2)}, u32[]{:S(2)}) collective-permute-start(f32[4,4]{1,0:T(4,128)S(1)} %select_multiply_fusion.7), channel_id=1, source_target_pairs={{0,16},{16,32},{32,48},{48,64},{64,80},{80,96},{96,112},{1,17},{17... | collective-permute-start | bytes 200 | tf_op jit(solution)/shard_map/while/body/eval_jaxpr/ppermute | solution.py:16
  134.3 6.2 %copy-start.26 = (s32[4]{0:T(128)S(1)}, s32[4]{0:T(128)}, u32[]{:S(2)}) copy-start(s32[4]{0:T(128)} %param.42) | copy-start | bytes 52
  137.5 7.1 %copy-start.8 = (f32[2,256,4,64]{1,0,3,2:T(2,128)S(1)}, f32[2,256,4,64]{1,0,3,2:T(2,128)}, u32[]{:S(2)}) copy-start(f32[2,256,4,64]{1,0,3,2:T(2,128)} %get-tuple-element.491) | copy-start | bytes 1572868
  139.4 6.1 %copy-start.23 = (f32[2,4]{1,0:T(2,128)S(1)}, f32[2,4]{1,0:T(2,128)}, u32[]{:S(2)}) copy-start(f32[2,4]{1,0:T(2,128)} %param.34) | copy-start | bytes 100
  145.6 2.8 copy-start.3
  149.7 1.0 copy-start.12
  150.8 3.0 copy-start.5
  153.9 0.7 copy-start.15
  182.5 10.5 %collective-permute-start.1 = (f32[4,4,64,128]{3,2,1,0:T(8,128)S(1)}, f32[4,4,64,128]{3,2,1,0:T(8,128)S(1)}, u32[]{:S(2)}, u32[]{:S(2)}) collective-permute-start(f32[4,4,64,128]{3,2,1,0:T(8,128)S(1)} %fusion.285), channel_id=1, source_target_pairs={{0,16},{16,32},{32,48},{48,64},{64,80},{80,96},{96,112},{1,17},{17... | collective-permute-start | bytes 1572872 | tf_op jit(solution)/shard_map/while/body/eval_jaxpr/ppermute | solution.py:16
  186.9 6.1 %collective-permute-start = (f32[4,4]{1,0:T(4,128)S(1)}, f32[4,4]{1,0:T(4,128)S(1)}, u32[]{:S(2)}, u32[]{:S(2)}) collective-permute-start(f32[4,4]{1,0:T(4,128)S(1)} %select_multiply_fusion.6), channel_id=1, source_target_pairs={{0,16},{16,32},{32,48},{48,64},{64,80},{80,96},{96,112},{1,17},{17... | collective-permute-start | bytes 200 | tf_op jit(solution)/shard_map/while/body/eval_jaxpr/ppermute | solution.py:16
  193.3 10.5 %collective-permute-start.1 = (f32[4,4,64,128]{3,2,1,0:T(8,128)S(1)}, f32[4,4,64,128]{3,2,1,0:T(8,128)S(1)}, u32[]{:S(2)}, u32[]{:S(2)}) collective-permute-start(f32[4,4,64,128]{3,2,1,0:T(8,128)S(1)} %fusion.285), channel_id=1, source_target_pairs={{0,16},{16,32},{32,48},{48,64},{64,80},{80,96},{96,112},{1,17},{17... | collective-permute-start | bytes 1572872 | tf_op jit(solution)/shard_map/while/body/eval_jaxpr/ppermute | solution.py:16
  197.7 6.1 %collective-permute-start = (f32[4,4]{1,0:T(4,128)S(1)}, f32[4,4]{1,0:T(4,128)S(1)}, u32[]{:S(2)}, u32[]{:S(2)}) collective-permute-start(f32[4,4]{1,0:T(4,128)S(1)} %select_multiply_fusion.6), channel_id=1, source_target_pairs={{0,16},{16,32},{32,48},{48,64},{64,80},{80,96},{96,112},{1,17},{17... | collective-permute-start | bytes 200 | tf_op jit(solution)/shard_map/while/body/eval_jaxpr/ppermute | solution.py:16
  204.0 10.5 %collective-permute-start.1 = (f32[4,4,64,128]{3,2,1,0:T(8,128)S(1)}, f32[4,4,64,128]{3,2,1,0:T(8,128)S(1)}, u32[]{:S(2)}, u32[]{:S(2)}) collective-permute-start(f32[4,4,64,128]{3,2,1,0:T(8,128)S(1)} %fusion.285), channel_id=1, source_target_pairs={{0,16},{16,32},{32,48},{48,64},{64,80},{80,96},{96,112},{1,17},{17... | collective-permute-start | bytes 1572872 | tf_op jit(solution)/shard_map/while/body/eval_jaxpr/ppermute | solution.py:16
  208.4 6.1 %collective-permute-start = (f32[4,4]{1,0:T(4,128)S(1)}, f32[4,4]{1,0:T(4,128)S(1)}, u32[]{:S(2)}, u32[]{:S(2)}) collective-permute-start(f32[4,4]{1,0:T(4,128)S(1)} %select_multiply_fusion.6), channel_id=1, source_target_pairs={{0,16},{16,32},{32,48},{48,64},{64,80},{80,96},{96,112},{1,17},{17... | collective-permute-start | bytes 200 | tf_op jit(solution)/shard_map/while/body/eval_jaxpr/ppermute | solution.py:16
  214.7 10.5 %collective-permute-start.1 = (f32[4,4,64,128]{3,2,1,0:T(8,128)S(1)}, f32[4,4,64,128]{3,2,1,0:T(8,128)S(1)}, u32[]{:S(2)}, u32[]{:S(2)}) collective-permute-start(f32[4,4,64,128]{3,2,1,0:T(8,128)S(1)} %fusion.285), channel_id=1, source_target_pairs={{0,16},{16,32},{32,48},{48,64},{64,80},{80,96},{96,112},{1,17},{17... | collective-permute-start | bytes 1572872 | tf_op jit(solution)/shard_map/while/body/eval_jaxpr/ppermute | solution.py:16
  219.1 6.1 %collective-permute-start = (f32[4,4]{1,0:T(4,128)S(1)}, f32[4,4]{1,0:T(4,128)S(1)}, u32[]{:S(2)}, u32[]{:S(2)}) collective-permute-start(f32[4,4]{1,0:T(4,128)S(1)} %select_multiply_fusion.6), channel_id=1, source_target_pairs={{0,16},{16,32},{32,48},{48,64},{64,80},{80,96},{96,112},{1,17},{17... | collective-permute-start | bytes 200 | tf_op jit(solution)/shard_map/while/body/eval_jaxpr/ppermute | solution.py:16
  225.4 10.5 %collective-permute-start.1 = (f32[4,4,64,128]{3,2,1,0:T(8,128)S(1)}, f32[4,4,64,128]{3,2,1,0:T(8,128)S(1)}, u32[]{:S(2)}, u32[]{:S(2)}) collective-permute-start(f32[4,4,64,128]{3,2,1,0:T(8,128)S(1)} %fusion.285), channel_id=1, source_target_pairs={{0,16},{16,32},{32,48},{48,64},{64,80},{80,96},{96,112},{1,17},{17... | collective-permute-start | bytes 1572872 | tf_op jit(solution)/shard_map/while/body/eval_jaxpr/ppermute | solution.py:16
  229.8 6.1 %collective-permute-start = (f32[4,4]{1,0:T(4,128)S(1)}, f32[4,4]{1,0:T(4,128)S(1)}, u32[]{:S(2)}, u32[]{:S(2)}) collective-permute-start(f32[4,4]{1,0:T(4,128)S(1)} %select_multiply_fusion.6), channel_id=1, source_target_pairs={{0,16},{16,32},{32,48},{48,64},{64,80},{80,96},{96,112},{1,17},{17... | collective-permute-start | bytes 200 | tf_op jit(solution)/shard_map/while/body/eval_jaxpr/ppermute | solution.py:16
  236.1 10.5 %collective-permute-start.1 = (f32[4,4,64,128]{3,2,1,0:T(8,128)S(1)}, f32[4,4,64,128]{3,2,1,0:T(8,128)S(1)}, u32[]{:S(2)}, u32[]{:S(2)}) collective-permute-start(f32[4,4,64,128]{3,2,1,0:T(8,128)S(1)} %fusion.285), channel_id=1, source_target_pairs={{0,16},{16,32},{32,48},{48,64},{64,80},{80,96},{96,112},{1,17},{17... | collective-permute-start | bytes 1572872 | tf_op jit(solution)/shard_map/while/body/eval_jaxpr/ppermute | solution.py:16
  240.5 6.1 %collective-permute-start = (f32[4,4]{1,0:T(4,128)S(1)}, f32[4,4]{1,0:T(4,128)S(1)}, u32[]{:S(2)}, u32[]{:S(2)}) collective-permute-start(f32[4,4]{1,0:T(4,128)S(1)} %select_multiply_fusion.6), channel_id=1, source_target_pairs={{0,16},{16,32},{32,48},{48,64},{64,80},{80,96},{96,112},{1,17},{17... | collective-permute-start | bytes 200 | tf_op jit(solution)/shard_map/while/body/eval_jaxpr/ppermute | solution.py:16
  246.8 10.5 %collective-permute-start.1 = (f32[4,4,64,128]{3,2,1,0:T(8,128)S(1)}, f32[4,4,64,128]{3,2,1,0:T(8,128)S(1)}, u32[]{:S(2)}, u32[]{:S(2)}) collective-permute-start(f32[4,4,64,128]{3,2,1,0:T(8,128)S(1)} %fusion.285), channel_id=1, source_target_pairs={{0,16},{16,32},{32,48},{48,64},{64,80},{80,96},{96,112},{1,17},{17... | collective-permute-start | bytes 1572872 | tf_op jit(solution)/shard_map/while/body/eval_jaxpr/ppermute | solution.py:16
  251.2 6.1 %collective-permute-start = (f32[4,4]{1,0:T(4,128)S(1)}, f32[4,4]{1,0:T(4,128)S(1)}, u32[]{:S(2)}, u32[]{:S(2)}) collective-permute-start(f32[4,4]{1,0:T(4,128)S(1)} %select_multiply_fusion.6), channel_id=1, source_target_pairs={{0,16},{16,32},{32,48},{48,64},{64,80},{80,96},{96,112},{1,17},{17... | collective-permute-start | bytes 200 | tf_op jit(solution)/shard_map/while/body/eval_jaxpr/ppermute | solution.py:16
  257.4 1.9 copy-start
  257.4 1.9 copy-start.19
  259.1 1.1 copy-start.14
  259.1 3.1 copy-start.16
  261.3 5.5 copy-start.7
  262.2 5.9 copy-start.6
  266.4 46.3 %copy-start.20 = (f32[2,256]{1,0:T(2,128)S(1)}, f32[2,256]{1,0:T(2,128)}, u32[]{:S(2)}) copy-start(f32[2,256]{1,0:T(2,128)} %param.35) | copy-start | bytes 6148
  316.1 3.5 copy-start.27
  316.1 3.6 copy-start.28
  316.1 4.1 copy-start.21
  316.1 4.1 copy-start.18
  427.6 5.1 copy-start.4
  427.6 5.3 copy-start.10
  427.7 12.8 %slice-start = ((s8[13631488]{0:T(1024)(128)(4,1)}), s8[4194304]{0:T(1024)(128)(4,1)S(1)}, s32[]{:S(2)}) async-start(s8[13631488]{0:T(1024)(128)(4,1)} %bitcast.564), calls=%async_computation.1 | async-start | bytes 8388608
  433.0 7.5 %copy-start.9 = (bf16[512,2048]{1,0:T(8,128)(2,1)S(1)}, bf16[512,2048]{1,0:T(8,128)(2,1)}, u32[]{:S(2)}) copy-start(bf16[512,2048]{1,0:T(8,128)(2,1)} %get-tuple-element.789) | copy-start | bytes 6291460
  433.0 7.5 %slice-start.1 = ((s8[13631488]{0:T(1024)(128)(4,1)}), s8[4194304]{0:T(1024)(128)(4,1)S(1)}, s32[]{:S(2)}) async-start(s8[13631488]{0:T(1024)(128)(4,1)} %bitcast.564), calls=%async_computation.2 | async-start | bytes 8388608
  433.0 7.5 %slice-start.2 = ((s8[13631488]{0:T(1024)(128)(4,1)}), s8[4194304]{0:T(1024)(128)(4,1)S(1)}, s32[]{:S(2)}) async-start(s8[13631488]{0:T(1024)(128)(4,1)} %bitcast.564), calls=%async_computation.3 | async-start | bytes 8388608
  433.0 7.5 %slice-start.3 = ((s8[13631488]{0:T(1024)(128)(4,1)}), s8[1048576]{0:T(1024)(128)(4,1)S(1)}, s32[]{:S(2)}) async-start(s8[13631488]{0:T(1024)(128)(4,1)} %bitcast.564), calls=%async_computation.4 | async-start | bytes 2097152
  444.9 104.5 %copy-start.24 = (s32[4]{0:T(128)S(1)}, s32[4]{0:T(128)}, u32[]{:S(2)}) copy-start(s32[4]{0:T(128)} %param.45) | copy-start | bytes 52
  549.2 46.3 %copy-start.22 = (f32[512]{0:T(512)}, f32[512]{0:T(512)S(1)}, u32[]{:S(2)}) copy-start(f32[512]{0:T(512)S(1)} %subtract_multiply_fusion) | copy-start | bytes 6148
Sparse Core Ops, SparseCore 0:
  319.7 107.8 all-reduce.4
where the time goes:
time: 615 us; the launch traced here: 603 us
  blocking collectives  187 us (30%)
  waiting for transfers between devices  166 us (27%)
  starting transfers between devices  88.6 us (14%)
  local copies, waits for them, and re-layouts  68.3 us (11%)
  matrix products  51.8 us (8%)
  other arithmetic  23.4 us (4%)
  between operations  14.9 us (2%)
    psum x1, waiting for transfers between devices, per_device(): lax.psum(out_part.astype(jnp.bfloat16), 'vocab').astype(jnp.float32)  107 us
    all_gather x6, blocking collectives, merged_2(): everything = jax.tree.map(lambda part: lax.all_gather(part, axis), value)  99 us
    ppermute x28, starting transfers between devices, passed_along(): return lax.ppermute(value, axis, pairs)  88.5 us
    ppermute x28, waiting for transfers between devices, passed_along(): return lax.ppermute(value, axis, pairs)  58.6 us
    unnamed x1, blocking collectives  45.1 us
    psum x1, blocking collectives, per_device(): square_sum = lax.psum(jnp.sum(gated_rows * gated_rows, axis=1), 'vocab')  43.3 us
    dynamic_update_slice x8, local copies, waits for them, and re-layouts, scan_blocks(): end_state, outputs = lax.scan(block_step, init_state, pieces)  26.5 us
    unnamed x86, local copies, waits for them, and re-layouts  14 us
  transfers between devices with their start and end apart: 29, of which 15 were waited for; matrix products, arithmetic and copies ran while one was open for 0% of the time, Pallas kernels for 0%

commit v1 on v0

v1 whole, which is shorter than its diff:
```python
import functools

import jax
import jax.numpy as jnp
from jax import lax
from jax.experimental import pallas as pl
from jax.experimental.pallas import tpu as pltpu
from jax.sharding import Mesh
from jax.sharding import PartitionSpec as P

NORM_EPS = 1e-05
SPAN = 256
REACH = 4
SEQ = ("y", "core")
VOC = ("x", "z")
F32 = jnp.float32
BF16 = jnp.bfloat16
LOW = -1e30


def silu(v):
    return v / (1.0 + jnp.exp(-v))


def contract(a, b, dims):
    return lax.dot_general(a, b, (dims, ((), ())), preferred_element_type=F32)


def mix_kernel(val_ref, st_ref, stp_ref, bias_ref, rate_ref, skip_ref, seg_ref, y_ref, c_ref, e_ref, pay_ref):
    rows, inner = y_ref.shape
    heads = stp_ref.shape[0]
    wide = inner // heads
    state = c_ref.shape[1]
    seg = seg_ref[...]
    raw = stp_ref[...] + bias_ref[...]
    dt = jnp.maximum(raw, 0.0) + jnp.log1p(jnp.exp(-jnp.abs(raw)))
    la = -dt * rate_ref[...]
    lane = lax.broadcasted_iota(jnp.int32, la.shape, 1)
    run = la
    step = 1
    while step < rows:
        run = run + jnp.where(lane >= step, pltpu.roll(run, step, 1), 0.0)
        step *= 2
    last = jnp.max(seg, axis=1, keepdims=True)
    base = jnp.zeros_like(la)
    for j in range(4):
        base_j = jnp.sum(jnp.where(seg < j, la, 0.0), axis=1, keepdims=True)
        base = jnp.where(seg == j, base_j, base)
    total = jnp.sum(la, axis=1, keepdims=True)
    grow = jnp.exp(run - base)
    keep = jnp.where(seg == last, jnp.exp(jnp.minimum(total - run, 0.0)) * dt, 0.0)
    tail = jnp.exp(jnp.sum(jnp.where(seg == last, la, 0.0), axis=1, keepdims=True))
    cols = jnp.transpose(jnp.concatenate([run, keep], axis=0))
    segf = jnp.broadcast_to(seg.astype(F32), (heads, rows))
    ecol = jnp.transpose(jnp.concatenate([grow, segf], axis=0))
    e_ref[...] = ecol
    values = silu(val_ref[...]).astype(BF16)
    in_map = silu(st_ref[0]).astype(BF16)
    out_map = silu(st_ref[1]).astype(BF16)
    c_ref[...] = out_map
    vf = values.astype(F32)
    kept = jnp.concatenate(
        [vf[:, h * wide : (h + 1) * wide] * cols[:, heads + h : heads + h + 1] for h in range(heads)], axis=1
    ).astype(BF16)
    added = contract(kept, in_map, ((0,), (0,)))
    pay_ref[0:inner, :] = added.astype(BF16)
    high = tail.astype(BF16).astype(F32)
    low = tail - high
    meta = jnp.concatenate(
        [
            jnp.broadcast_to(high, (heads, state)),
            jnp.broadcast_to(low, (heads, state)),
            jnp.broadcast_to(last.astype(F32) + 1.0, (8, state)),
        ],
        axis=0,
    )
    pay_ref[inner : inner + 16, :] = meta.astype(BF16)
    blocks = rows // SPAN
    for i in range(blocks):
        t0 = i * SPAN
        acc = [vf[t0 : t0 + SPAN, h * wide : (h + 1) * wide] * skip_ref[h : h + 1, :] for h in range(heads)]
        for j in range(i + 1):
            s0 = j * SPAN
            scores = contract(out_map[t0 : t0 + SPAN], in_map[s0 : s0 + SPAN], ((1,), (1,)))
            same = ecol[t0 : t0 + SPAN, heads : heads + 1] == segf[0:1, s0 : s0 + SPAN]
            if i == j:
                same = same & (
                    lax.broadcasted_iota(jnp.int32, (SPAN, SPAN), 0)
                    >= lax.broadcasted_iota(jnp.int32, (SPAN, SPAN), 1)
                )
            for h in range(heads):
                gap = cols[t0 : t0 + SPAN, h : h + 1] - run[h : h + 1, s0 : s0 + SPAN]
                weight = jnp.exp(jnp.where(same, gap, LOW)) * (scores * dt[h : h + 1, s0 : s0 + SPAN])
                acc[h] = acc[h] + contract(
                    weight.astype(BF16), values[s0 : s0 + SPAN, h * wide : (h + 1) * wide], ((1,), (0,))
                )
        y_ref[t0 : t0 + SPAN, :] = jnp.concatenate(acc, axis=1)


def mix_local(val, st, stp, bias, rate, skip, seg):
    rows, inner = val.shape
    state = st.shape[2]
    return pl.pallas_call(
        mix_kernel,
        out_shape=(
            jax.ShapeDtypeStruct((rows, inner), F32),
            jax.ShapeDtypeStruct((rows, state), BF16),
            jax.ShapeDtypeStruct((rows, 8), F32),
            jax.ShapeDtypeStruct((inner + 16, state), BF16),
        ),
        cost_estimate=pl.CostEstimate(flops=3 * 10**9, bytes_accessed=3 * 10**6, transcendentals=10**6),
        name="mix_local",
    )(val, st, stp, bias, rate, skip, seg)


def gate_kernel(
    pages_ref, flags_ref, y_ref, gate_ref, c_ref, e_ref, r1_ref, r2_ref, r3_ref, r4_ref,
    p0_ref, p1_ref, p2_ref, p3_ref, gain_ref, w_ref, out_ref,
):
    rows, inner = y_ref.shape
    heads = p0_ref.shape[0]
    wide = inner // heads
    state = c_ref.shape[1]
    width = w_ref.shape[1]
    e_col = e_ref[...]
    seg_col = e_col[:, heads : heads + 1]
    seg_first = e_col[0:1, heads : heads + 1]
    init = [
        p.reshape(inner, state)[...].astype(F32) * flags_ref[j].astype(F32)
        for j, p in enumerate((p0_ref, p1_ref, p2_ref, p3_ref))
    ]
    through = jnp.ones((heads, state), F32)
    parts = [jnp.zeros((wide, state), F32) for _ in range(heads)]
    for r in (r1_ref, r2_ref, r3_ref, r4_ref):
        meta = r[inner : inner + 16, :].astype(F32)
        hit = meta[8:9, :] == seg_first + 1.0
        piece = r[0:inner, :].astype(F32)
        weight = jnp.where(hit, through, 0.0)
        for h in range(heads):
            parts[h] = parts[h] + weight[h : h + 1, :] * piece[h * wide : (h + 1) * wide, :]
        through = jnp.where(hit, through * (meta[0:heads] + meta[heads : 2 * heads]), through)
    prior = jnp.concatenate(parts, axis=0)
    through = jnp.concatenate([jnp.broadcast_to(through[h : h + 1, :], (wide, state)) for h in range(heads)], axis=0)
    out_map = c_ref[...]
    picked = jnp.zeros((rows, inner), F32)
    for j in range(4):
        start = jnp.where(seg_first == float(j), prior + through * init[j], init[j])
        high = start.astype(BF16)
        low = (start - high.astype(F32)).astype(BF16)
        from_state = contract(out_map, high, ((1,), (1,))) + contract(out_map, low, ((1,), (1,)))
        picked = jnp.where(seg_col == float(j), from_state, picked)
    spread = jnp.concatenate([jnp.broadcast_to(e_col[:, h : h + 1], (rows, wide)) for h in range(heads)], axis=1)
    gated = (y_ref[...] + picked * spread) * silu(gate_ref[...])
    square = jnp.sum(gated * gated, axis=1, keepdims=True)
    mixed = (gated * gain_ref[...]).astype(BF16)
    out_ref[:, 0:width] = contract(mixed, w_ref[...], ((1,), (0,))).astype(BF16)
    high = square.astype(BF16).astype(F32)
    mid = (square - high).astype(BF16).astype(F32)
    low = square - high - mid
    lane = lax.broadcasted_iota(jnp.int32, (rows, 128), 1)
    extra = jnp.where(lane == 0, high, jnp.where(lane == 1, mid, jnp.where(lane == 2, low, 0.0)))
    out_ref[:, width : width + 128] = extra.astype(BF16)


def gate_out(m, pages, flags, y, gate, c, e, recv, pool, gain, w_out):
    rows, inner = y.shape
    heads = pool.shape[2]
    state = c.shape[1]
    width = w_out.shape[2]
    whole = lambda a: pl.BlockSpec(a.shape, lambda g, pg, fl: (0,) * a.ndim)
    page = lambda j: pl.BlockSpec(
        (None, None, heads, pool.shape[3], state), lambda g, pg, fl: (m, pg[j], 0, 0, 0)
    )
    return pl.pallas_call(
        gate_kernel,
        grid_spec=pltpu.PrefetchScalarGridSpec(
            num_scalar_prefetch=2,
            grid=(1,),
            in_specs=[whole(y), whole(gate), whole(c), whole(e)]
            + [whole(r) for r in recv]
            + [page(j) for j in range(4)]
            + [
                pl.BlockSpec((1, inner), lambda g, pg, fl: (0, 0)),
                pl.BlockSpec((None, inner, width), lambda g, pg, fl: (m, 0, 0)),
            ],
            out_specs=pl.BlockSpec((rows, width + 128), lambda g, pg, fl: (0, 0)),
        ),
        out_shape=jax.ShapeDtypeStruct((rows, width + 128), BF16),
        cost_estimate=pl.CostEstimate(flops=3 * 10**9, bytes_accessed=6 * 10**6, transcendentals=10**5),
        name="gate_out",
    )(pages, flags, y, gate, c, e, *recv, pool, pool, pool, pool, gain, w_out)


def norm_kernel(units, part_ref, hid_ref, gain_ref, out_ref):
    width = hid_ref.shape[1]
    total = jnp.sum(part_ref[...].astype(F32), axis=0)
    square = total[:, width : width + 1] + total[:, width + 1 : width + 2] + total[:, width + 2 : width + 3]
    res = hid_ref[...].astype(F32) + total[:, 0:width] * lax.rsqrt(square / units + NORM_EPS)
    mean = jnp.sum(res * res, axis=1, keepdims=True) / width
    normed = (res * lax.rsqrt(mean + NORM_EPS) * gain_ref[...]).astype(BF16)
    out_ref[...] = jnp.broadcast_to(normed[None], out_ref.shape)


def final_norm(part, hid, gain, units):
    return pl.pallas_call(
        functools.partial(norm_kernel, float(units)),
        out_shape=jax.ShapeDtypeStruct((part.shape[0],) + hid.shape, BF16),
        cost_estimate=pl.CostEstimate(flops=10**7, bytes_accessed=4 * 10**6, transcendentals=100),
        name="final_norm",
    )(part, hid, gain)


def head_kernel(x_ref, w_ref, tgt_ref, out_ref):
    logits = contract(x_ref[...], w_ref[...], ((1,), (0,)))
    top = jnp.max(logits, axis=1, keepdims=True)
    total = jnp.sum(jnp.exp(logits - top), axis=1, keepdims=True)
    lse = top + jnp.log(total)
    at = lax.broadcasted_iota(jnp.int32, logits.shape, 1)
    chosen = jnp.sum(jnp.where(at == tgt_ref[...], logits, 0.0), axis=1, keepdims=True)
    lane = lax.broadcasted_iota(jnp.int32, (logits.shape[0], 8), 1)
    out_ref[...] = jnp.transpose(jnp.where(lane == 0, lse, jnp.where(lane == 1, chosen, 0.0)))


def head_stats(m, x, head, tgt, tile=256):
    rows, depth = x.shape
    vocab = head.shape[2]
    return pl.pallas_call(
        head_kernel,
        grid=(rows // tile,),
        in_specs=[
            pl.BlockSpec((tile, depth), lambda i: (i, 0)),
            pl.BlockSpec((None, depth, vocab), lambda i: (m, 0, 0)),
            pl.BlockSpec((tile, 1), lambda i: (i, 0)),
        ],
        out_specs=pl.BlockSpec((8, tile), lambda i: (0, i)),
        out_shape=jax.ShapeDtypeStruct((8, rows), F32),
        cost_estimate=pl.CostEstimate(
            flops=2 * rows * depth * vocab, bytes_accessed=2 * depth * vocab, transcendentals=rows * vocab
        ),
        name="head_stats",
    )(x, head, tgt)


def diff_kernel(s0_ref, s1_ref, live_ref, seg_ref, diff_ref, sums_ref):
    scores = []
    for ref in (s0_ref, s1_ref):
        part = ref[...]
        lse = part[:, 0, :]
        top = jnp.max(lse, axis=0, keepdims=True)
        total = top + jnp.log(jnp.sum(jnp.exp(lse - top), axis=0, keepdims=True))
        scores.append(jnp.sum(part[:, 1, :], axis=0, keepdims=True) - total)
    rows = seg_ref.shape[1]
    alive = jnp.where(
        lax.broadcasted_iota(jnp.int32, (1, rows), 1) < SPAN, live_ref[0].astype(F32), live_ref[1].astype(F32)
    )
    diff = alive * (scores[0] - scores[1])
    diff_ref[...] = diff
    which = lax.broadcasted_iota(jnp.int32, (8, rows), 0)
    sums = jnp.sum(jnp.where(which == seg_ref[...], diff, 0.0), axis=1, keepdims=True)
    sums_ref[...] = jnp.broadcast_to(sums, sums_ref.shape)


def token_diffs(s0, s1, live, seg):
    rows = seg.shape[1]
    vm = pl.BlockSpec(memory_space=pltpu.VMEM)
    return pl.pallas_call(
        diff_kernel,
        in_specs=[vm, vm, pl.BlockSpec(memory_space=pltpu.SMEM), vm],
        out_shape=(jax.ShapeDtypeStruct((1, rows), F32), jax.ShapeDtypeStruct((8, 128), F32)),
        name="token_diffs",
    )(s0, s1, live, seg)


def to_all(value, axes):
    count = lax.axis_size(axes)
    return lax.all_to_all(jnp.broadcast_to(value[None], (count,) + value.shape), axes, 0, 0)


def per_device(
    hidden, w_inner, w_state, w_step, step_bias, rate, skip_gain, norm_gain, w_out, final_gain, head, pool,
    targets, segment_ids, flags, pages, live, owners,
):
    rows = targets.shape[0]
    depth = hidden.shape[2]
    inner = w_inner.shape[3]
    group = lax.axis_size(VOC)
    devices = lax.axis_size(SEQ)
    place = lax.axis_index(VOC)
    share = rows // group
    seg = segment_ids.reshape(1, rows)
    tgt = (targets - place * head.shape[2]).reshape(rows, 1)
    stats = []
    for m in range(2):
        tokens = hidden[m]
        proj = jnp.einsum("td,dgi->gti", tokens, w_inner[m], preferred_element_type=F32)
        st = jnp.einsum("td,dgn->gtn", tokens, w_state[m], preferred_element_type=F32)
        stp = jnp.einsum("td,dh->ht", tokens, w_step[m], preferred_element_type=F32)
        wide = inner // rate.shape[1]
        y, c, e, pay = mix_local(
            proj[1], st, stp, step_bias[m][:, None], rate[m][:, None],
            jnp.broadcast_to(skip_gain[m][:, None], (rate.shape[1], wide)), seg,
        )
        recv = [lax.ppermute(pay, SEQ, [(i, i + k) for i in range(devices - k)]) for k in range(1, REACH + 1)]
        part = gate_out(m, pages, flags, y, proj[0], c, e, recv, pool, norm_gain[m][None], w_out)
        part = lax.all_to_all(part.reshape(group, share, depth + 128), VOC, 0, 0)
        mine = lax.dynamic_slice_in_dim(tokens, place * share, share, 0)
        normed = final_norm(part, mine, final_gain[m][None], inner * group)
        normed = lax.all_to_all(normed, VOC, 0, 0).reshape(rows, depth)
        stats.append(to_all(head_stats(m, normed, head, tgt), VOC))
    diff, sums = token_diffs(stats[0], stats[1], live, seg)
    sums = jnp.sum(to_all(sums, SEQ)[:, 0:4, 0], axis=0)
    owned = jnp.where(owners == lax.axis_index(SEQ), sums, 0.0)
    return diff.reshape(rows), owned[None]


def solution(mesh):
    seq, vocab = mesh.devices.shape
    fine = Mesh(mesh.devices.reshape(seq // 2, 2, 4, vocab // 4), ("y", "core", "x", "z"))
    placed = (
        P(None, SEQ, None),
        P(None, None, None, VOC),
        P(),
        P(None, None, VOC),
        P(None, VOC),
        P(None, VOC),
        P(None, VOC),
        P(None, VOC),
        P(None, VOC, None),
        P(),
        P(None, None, VOC),
        P(None, None, VOC, None, None),
        P(SEQ),
        P(SEQ),
        P(),
        P(),
        P(SEQ),
        P(),
    )
    return jax.shard_map(
        per_device, mesh=fine, in_specs=placed, out_specs=(P(SEQ), P(SEQ, None)), check_vma=False
    )
```

time: 615 us -> 256 us (0.42); the launches traced: 603 us -> 254 us
  blocking collectives: 187 us -> 13.9 us
  waiting for transfers between devices: 166 us -> 69.5 us
  Pallas kernels: 0 us -> 47 us
  matrix products: 51.8 us -> 16.1 us
  starting transfers between devices: 88.6 us -> 61.8 us
  local copies, waits for them, and re-layouts: 68.3 us -> 44.4 us
  other arithmetic: 23.4 us -> 0.64 us
  between operations: 14.9 us -> 0.97 us
    psum x1 -> x0, waiting for transfers between devices: 107 us -> none  [per_device(): lax.psum(out_part.astype(jnp.bfloat16), 'vocab').astype(jnp.float32)]
    all_gather x6 -> x0, blocking collectives: 99 us -> none  [merged_2(): everything = jax.tree.map(lambda part: lax.all_gather(part, axis), value)]
    ppermute x28 -> x8, starting transfers between devices: 88.5 us -> 21.6 us  [per_device(): lax.ppermute(pay, SEQ, [(i, i + k) for i in range(devices - k)])]
    all_to_all x0 -> x6, waiting for transfers between devices: none -> 66.9 us  [the longest x2 39.4 us: per_device(): normed = lax.all_to_all(normed, VOC, 0, 0).reshape(rows, depth)]
    ppermute x28 -> x8, waiting for transfers between devices: 58.6 us -> 2.66 us  [per_device(): lax.ppermute(pay, SEQ, [(i, i + k) for i in range(devices - k)])]
    pallas_call x0 -> x9, Pallas kernels: none -> 47 us  [the longest x2 17.8 us: head_stats(): pl.pallas_call(head_kernel, grid=(rows // tile,), in_specs=[pl.BlockSpec(...]
    unnamed x1 -> x0, blocking collectives: 45.1 us -> none
    psum x1 -> x0, blocking collectives: 43.3 us -> none  [per_device(): square_sum = lax.psum(jnp.sum(gated_rows * gated_rows, axis=1), 'vocab')]
  transfers between devices with their start and end apart: 29 -> 14, of which waited for: 15 -> 6; matrix products, arithmetic and copies ran while one was open for 0% -> 10% of each run, Pallas kernels for 0% -> 14%
where the time goes in v1:
time: 256 us; the launch traced here: 254 us
  waiting for transfers between devices  69.5 us (27%)
  starting transfers between devices  61.8 us (24%)
  Pallas kernels  47 us (18%)
  local copies, waits for them, and re-layouts  44.4 us (17%)
  matrix products  16.1 us (6%)
  blocking collectives  13.9 us (5%)
    all_to_all x2, waiting for transfers between devices, per_device(): normed = lax.all_to_all(normed, VOC, 0, 0).reshape(rows, depth)  39.4 us
    all_to_all x2, waiting for transfers between devices, per_device(): part = lax.all_to_all(part.reshape(group, share, depth + 128), VOC, 0, 0)  22.7 us
    ppermute x8, starting transfers between devices, per_device(): lax.ppermute(pay, SEQ, [(i, i + k) for i in range(devices - k)])  21.6 us
    unnamed x42, local copies, waits for them, and re-layouts  17.8 us
    pallas_call x2, Pallas kernels, head_stats(): pl.pallas_call(head_kernel, grid=(rows // tile,), in_specs=[pl.BlockSpec(...  17.8 us
    all_to_all x2, starting transfers between devices, per_device(): part = lax.all_to_all(part.reshape(group, share, depth + 128), VOC, 0, 0)  14.6 us
    all_to_all x1, blocking collectives, to_all(): lax.all_to_all(jnp.broadcast_to(value[None], (count,) + value.shape), axe...  13.9 us
    all_to_all x2, starting transfers between devices, to_all(): lax.all_to_all(jnp.broadcast_to(value[None], (count,) + value.shape), axe...  13.9 us
  transfers between devices with their start and end apart: 14, of which 6 were waited for; matrix products, arithmetic and copies ran while one was open for 10% of the time, Pallas kernels for 14%

profile of v1, /device:TPU:1, one launch (start us, length us, event | category | flops | bytes accessed | tf_op | source)
XLA Modules:
  0.0 254.3 jit_solution(756102517446514610)
XLA Ops:
  0.6 0.8 slice_bitcast_fusion.6
  1.4 0.8 slice_bitcast_fusion.5
  2.1 0.8 slice_bitcast_fusion.4
  2.9 0.7 copy.66.rate_ref
  3.6 0.7 copy.65.bias_ref
  4.2 2.7 %fusion.45 = (bf16[1,2048,2,128]{3,2,1,0:T(2,128)(2,1)S(1)}, bf16[1,2048,2,128]{3,2,1,0:T(2,128)(2,1)S(1)}) fusion(bf16[2,2048,2,128]{3,2,1,0:T(2,128)(2,1)} %param.20), kind=kLoop, calls=%fused_computation.48 | loop fusion | bytes 4194304 | tf_op jit(solution)/shard_map/slice | solution.py:296
  6.9 0.8 copy.82
  7.7 2.8 %fusion.11.stp_ref = f32[4,512]{1,0:T(4,128)} fusion(bf16[2,2048,4]{1,2,0:T(4,128)(2,1)S(1)} %copy-done.14, bf16[2,512,2048]{2,1,0:T(8,128)(2,1)} %param.18), kind=kOutput, calls=%fused_computation.11 | convolution fusion | flops 8388608 | bytes 2121728 | tf_op jit(solution)/shard_map/td,dh->ht/dot_general | solution.py:297
  10.6 3.3 %fusion.24.st_ref = f32[2,512,128]{2,1,0:T(8,128)} fusion(bf16[1,2048,2,128]{1,3,2,0:T(8,128)(2,1)S(1)} %copy.82, bf16[2,512,2048]{2,1,0:T(8,128)(2,1)} %param.18), kind=kOutput, calls=%fused_computation.16 | convolution fusion | flops 536870912 | bytes 3670016 | tf_op jit(solution)/shard_map/td,dgn->gtn/dot_general | solution.py:296
  13.9 3.8 %fusion.44 = (bf16[1,2048,2,256]{3,2,1,0:T(2,128)(2,1)}, bf16[1,2048,2,256]{3,2,1,0:T(2,128)(2,1)S(1)}) fusion(bf16[2,2048,2,256]{3,2,1,0:T(2,128)(2,1)S(1)} %copy-done.3), kind=kLoop, calls=%fused_computation.47 | loop fusion | bytes 8388608 | tf_op jit(solution)/shard_map/slice | solution.py:295
  17.7 4.7 %copy.81 = bf16[1,2048,2,256]{1,3,2,0:T(8,128)(2,1)} copy(bf16[1,2048,2,256]{3,2,1,0:T(2,128)(2,1)S(1)} %get-tuple-element.25) | data formatting | bytes 4194304
  22.4 3.5 %fusion.14 = f32[2,512,256]{2,1,0:T(8,128)S(1)} fusion(bf16[1,2048,2,256]{1,3,2,0:T(8,128)(2,1)} %copy.81, bf16[2,512,2048]{2,1,0:T(8,128)(2,1)} %param.18), kind=kOutput, calls=%fused_computation.14 | convolution fusion | flops 1073741824 | bytes 5242880 | tf_op jit(solution)/shard_map/td,dgi->gti/dot_general | solution.py:295
  25.9 1.1 slice_bitcast_fusion.2
  27.0 0.6 broadcast_in_dim.40.skip_ref
  27.6 4.6 %mix_local.2 = (f32[512,256]{1,0:T(8,128)}, bf16[512,128]{1,0:T(8,128)(2,1)}, f32[512,8]{1,0:T(8,128)}, bf16[272,128]{1,0:T(8,128)(2,1)}) custom-call(f32[512,256]{1,0:T(8,128)} %get-tuple-element.31.val_ref, f32[2,512,128]{2,1,0:T(8,128)} %fusion.24.st_ref, f32[4,512]{1,0:T(4,128)} %fusion.11.stp_ref, f32[4,1]{1,0:T(4,128)} %copy.65.bias_ref, ...), custom_call_target="tpu_custom_call" | custom-call | flops 3000000000 | bytes 3000000 | tf_op jit(solution)/shard_map/mix_local/pallas_call | solution.py:103
  32.2 5.6 %collective-permute-start.3 = (bf16[272,128]{1,0:T(8,128)(2,1)}, bf16[272,128]{1,0:T(8,128)(2,1)S(1)}, u32[]{:S(2)}, u32[]{:S(2)}) collective-permute-start(bf16[272,128]{1,0:T(8,128)(2,1)} %get-tuple-element.15), channel_id=1, source_target_pairs={{0,64},{16,80},{32,96},{48,112},{1,65},{17,81},{33,97},{49,113},{2... | collective-permute-start | bytes 208904 | tf_op jit(solution)/shard_map/ppermute | solution.py:303
  37.9 1.9 collective-permute-start.2
  39.7 2.4 collective-permute-start.1
  42.1 2.1 collective-permute-start
  44.9 1.0 collective-permute-done.r1_ref
  45.9 0.6 copy-done.12
  46.5 5.4 %gate_out.2 = bf16[512,2176]{1,0:T(8,128)(2,1)} custom-call(s32[4]{0:T(128)} %pages_ref.3, s32[4]{0:T(128)} %flags_ref.3, f32[512,256]{1,0:T(8,128)} %get-tuple-element.12.y_ref, f32[512,256]{1,0:T(8,128)} %get-tuple-element.30.gate_ref, bf16[512,128]{1,0:T(8,128)(2,1)} %get-tuple-element.13.c_ref, f32[512,8]{1,0:T(8,128)} %get-tuple-element.14.e_ref, ...), custom_call_target="tpu_custom_call" | custom-call | flops 3000000000 | bytes 6000000 | tf_op jit(solution)/shard_map/gate_out/pallas_call | solution.py:174
  51.9 7.6 %all-to-all-start = ((bf16[16,32,2176]{2,1,0:T(8,128)(2,1)}), bf16[16,32,2176]{2,1,0:T(8,128)(2,1)S(1)}, u32[]{:S(2)}, u32[]{:S(2)}) async-start(bf16[16,32,2176]{2,1,0:T(8,128)(2,1)} %bitcast.87), calls=%async_computation | async-start | bytes 4456448 | tf_op jit(solution)/shard_map/all_to_all | solution.py:305
  59.5 0.7 copy.73.rate_ref
  60.2 0.7 copy.72.bias_ref
  60.9 2.1 copy.84
  62.9 6.2 %copy.83 = bf16[1,2048,2,256]{1,3,2,0:T(8,128)(2,1)} copy(bf16[1,2048,2,256]{3,2,1,0:T(2,128)(2,1)} %get-tuple-element.24) | data formatting | bytes 4194304
  69.1 3.6 %fusion.19 = f32[2,512,256]{2,1,0:T(8,128)S(1)} fusion(bf16[1,2048,2,256]{1,3,2,0:T(8,128)(2,1)} %copy.83, bf16[2,512,2048]{2,1,0:T(8,128)(2,1)} %param.18), kind=kOutput, calls=%fused_computation.15 | convolution fusion | flops 1073741824 | bytes 5242880 | tf_op jit(solution)/shard_map/td,dgi->gti/dot_general | solution.py:295
  72.8 1.1 slice_bitcast_fusion
  73.9 1.3 fusion.4.stp_ref
  75.1 1.5 fusion.27.st_ref
  76.7 0.7 broadcast_in_dim.43.skip_ref
  77.3 4.6 %mix_local.3 = (f32[512,256]{1,0:T(8,128)}, bf16[512,128]{1,0:T(8,128)(2,1)}, f32[512,8]{1,0:T(8,128)}, bf16[272,128]{1,0:T(8,128)(2,1)}) custom-call(f32[512,256]{1,0:T(8,128)} %get-tuple-element.29.val_ref, f32[2,512,128]{2,1,0:T(8,128)} %fusion.27.st_ref, f32[4,512]{1,0:T(4,128)} %fusion.4.stp_ref, f32[4,1]{1,0:T(4,128)} %copy.72.bias_ref, ...), custom_call_target="tpu_custom_call" | custom-call | flops 3000000000 | bytes 3000000 | tf_op jit(solution)/shard_map/mix_local/pallas_call | solution.py:103
  82.0 2.9 %collective-permute-start.7 = (bf16[272,128]{1,0:T(8,128)(2,1)}, bf16[272,128]{1,0:T(8,128)(2,1)S(1)}, u32[]{:S(2)}, u32[]{:S(2)}) collective-permute-start(bf16[272,128]{1,0:T(8,128)(2,1)} %get-tuple-element.19), channel_id=1, source_target_pairs={{0,64},{16,80},{32,96},{48,112},{1,65},{17,81},{33,97},{49,113},{2... | collective-permute-start | bytes 208904 | tf_op jit(solution)/shard_map/ppermute | solution.py:303
  84.9 2.9 %collective-permute-start.6 = (bf16[272,128]{1,0:T(8,128)(2,1)}, bf16[272,128]{1,0:T(8,128)(2,1)S(1)}, u32[]{:S(2)}, u32[]{:S(2)}) collective-permute-start(bf16[272,128]{1,0:T(8,128)(2,1)} %get-tuple-element.19), channel_id=1, source_target_pairs={{0,48},{16,64},{32,80},{48,96},{64,112},{1,49},{17,65},{33,81},{49... | collective-permute-start | bytes 208904 | tf_op jit(solution)/shard_map/ppermute | solution.py:303
  87.8 1.3 collective-permute-start.5
  89.1 2.5 collective-permute-start.4
  91.7 1.6 collective-permute-done.4.r1_ref
  93.9 5.4 %gate_out.3 = bf16[512,2176]{1,0:T(8,128)(2,1)} custom-call(s32[4]{0:T(128)} %pages_ref.3, s32[4]{0:T(128)} %flags_ref.3, f32[512,256]{1,0:T(8,128)} %get-tuple-element.16.y_ref, f32[512,256]{1,0:T(8,128)} %get-tuple-element.28.gate_ref, bf16[512,128]{1,0:T(8,128)(2,1)} %get-tuple-element.17.c_ref, f32[512,8]{1,0:T(8,128)} %get-tuple-element.18.e_ref, ...), custom_call_target="tpu_custom_call" | custom-call | flops 3000000000 | bytes 6000000 | tf_op jit(solution)/shard_map/gate_out/pallas_call | solution.py:174
  99.3 1.4 copy-done.1
  100.7 7.0 %all-to-all-start.3 = ((bf16[16,32,2176]{2,1,0:T(8,128)(2,1)}), bf16[16,32,2176]{2,1,0:T(8,128)(2,1)}, u32[]{:S(2)}, u32[]{:S(2)}) async-start(bf16[16,32,2176]{2,1,0:T(8,128)(2,1)} %bitcast.88), calls=%async_computation.3 | async-start | bytes 4456448 | tf_op jit(solution)/shard_map/all_to_all | solution.py:305
  107.7 4.1 %fusion.43 = (bf16[1,512,2048]{2,1,0:T(8,128)(2,1)}, bf16[1,512,2048]{2,1,0:T(8,128)(2,1)S(1)}) fusion(bf16[2,512,2048]{2,1,0:T(8,128)(2,1)} %param.18), kind=kLoop, calls=%fused_computation.46 | loop fusion | bytes 8388608 | tf_op jit(solution)/shard_map/slice | solution.py:294
  111.8 0.7 dynamic-slice_bitcast_fusion.1.hid_ref
  112.5 0.6 fusion.46
  113.1 3.7 %final_norm.2 = bf16[16,32,2048]{2,1,0:T(8,128)(2,1)} custom-call(bf16[16,32,2176]{2,1,0:T(8,128)(2,1)} %copy-done.1, bf16[32,2048]{1,0:T(8,128)(2,1)} %dynamic-slice_bitcast_fusion.1.hid_ref, f32[1,2048]{1,0:T(1,128)} %get-tuple-element.33.gain_ref), custom_call_target="tpu_custom_call" | custom-call | flops 10000000 | bytes 4000000 | tf_op jit(solution)/shard_map/final_norm/pallas_call | solution.py:205
  116.8 22.7 %all-to-all-done.3.part_ref = bf16[16,32,2176]{2,1,0:T(8,128)(2,1)} async-done(((bf16[16,32,2176]{2,1,0:T(8,128)(2,1)}), bf16[16,32,2176]{2,1,0:T(8,128)(2,1)}, u32[]{:S(2)}, u32[]{:S(2)}) %all-to-all-start.3) | async-done | bytes 2228256 | tf_op jit(solution)/shard_map/all_to_all | solution.py:305
  139.5 7.3 %all-to-all-start.1 = ((bf16[16,32,2048]{2,1,0:T(8,128)(2,1)}), bf16[16,32,2048]{2,1,0:T(8,128)(2,1)S(1)}, u32[]{:S(2)}, u32[]{:S(2)}) async-start(bf16[16,32,2048]{2,1,0:T(8,128)(2,1)} %final_norm.2), calls=%async_computation.1 | async-start | bytes 4194304 | tf_op jit(solution)/shard_map/all_to_all | solution.py:308
  146.7 1.6 dynamic-slice_bitcast_fusion.hid_ref
  148.3 3.7 %final_norm.3 = bf16[16,32,2048]{2,1,0:T(8,128)(2,1)} custom-call(bf16[16,32,2176]{2,1,0:T(8,128)(2,1)} %all-to-all-done.3.part_ref, bf16[32,2048]{1,0:T(8,128)(2,1)} %dynamic-slice_bitcast_fusion.hid_ref, f32[1,2048]{1,0:T(1,128)} %get-tuple-element.32.gain_ref), custom_call_target="tpu_custom_call" | custom-call | flops 10000000 | bytes 4000000 | tf_op jit(solution)/shard_map/final_norm/pallas_call | solution.py:205
  152.0 23.7 %all-to-all-done.1 = bf16[16,32,2048]{2,1,0:T(8,128)(2,1)S(1)} async-done(((bf16[16,32,2048]{2,1,0:T(8,128)(2,1)}), bf16[16,32,2048]{2,1,0:T(8,128)(2,1)S(1)}, u32[]{:S(2)}, u32[]{:S(2)}) %all-to-all-start.1) | async-done | bytes 2097184 | tf_op jit(solution)/shard_map/all_to_all | solution.py:308
  175.7 1.4 copy-done.2
  177.0 4.4 %all-to-all-start.4 = ((bf16[16,32,2048]{2,1,0:T(8,128)(2,1)}), bf16[16,32,2048]{2,1,0:T(8,128)(2,1)}, u32[]{:S(2)}, u32[]{:S(2)}) async-start(bf16[16,32,2048]{2,1,0:T(8,128)(2,1)} %final_norm.3), calls=%async_computation.4 | async-start | bytes 4194304 | tf_op jit(solution)/shard_map/all_to_all | solution.py:308
  181.5 0.9 copy.67.tgt_ref
  182.4 8.9 %head_stats.2 = f32[8,512]{1,0:T(8,128)} custom-call(bf16[512,2048]{1,0:T(8,128)(2,1)} %bitcast.89, bf16[2,2048,1664]{2,1,0:T(8,128)(2,1)} %w_ref.7, s32[512,1]{1,0:T(8,128)} %copy.67.tgt_ref), custom_call_target="tpu_custom_call" | custom-call | flops 3489660928 | bytes 6815744 | tf_op jit(solution)/shard_map/head_stats/pallas_call | solution.py:227
  191.3 15.7 %all-to-all-done.4 = bf16[16,32,2048]{2,1,0:T(8,128)(2,1)} async-done(((bf16[16,32,2048]{2,1,0:T(8,128)(2,1)}), bf16[16,32,2048]{2,1,0:T(8,128)(2,1)}, u32[]{:S(2)}, u32[]{:S(2)}) %all-to-all-start.4) | async-done | bytes 2097184 | tf_op jit(solution)/shard_map/all_to_all | solution.py:308
  207.0 1.5 broadcast_in_dim.41
  208.4 5.8 %all-to-all-start.2 = ((f32[16,8,512]{2,1,0:T(8,128)}), f32[16,8,512]{2,1,0:T(8,128)S(1)}, u32[]{:S(2)}, u32[]{:S(2)}) async-start(f32[16,8,512]{2,1,0:T(8,128)} %broadcast_in_dim.41), calls=%async_computation.2 | async-start | bytes 524288 | tf_op jit(solution)/shard_map/all_to_all | solution.py:276
  214.2 8.9 %head_stats.3 = f32[8,512]{1,0:T(8,128)} custom-call(bf16[512,2048]{1,0:T(8,128)(2,1)} %bitcast.31.x_ref, bf16[2,2048,1664]{2,1,0:T(8,128)(2,1)} %w_ref.7, s32[512,1]{1,0:T(8,128)} %copy.67.tgt_ref), custom_call_target="tpu_custom_call" | custom-call | flops 3489660928 | bytes 6815744 | tf_op jit(solution)/shard_map/head_stats/pallas_call | solution.py:227
  223.1 0.7 broadcast_in_dim.44
  223.9 13.9 %all_to_all.35.s1_ref = f32[16,8,512]{2,1,0:T(8,128)} all-to-all(f32[16,8,512]{2,1,0:T(8,128)S(1)} %broadcast_in_dim.44), channel_id=1, replica_groups=mesh['y'=4,'core'=2,'x'=4,'z'=4] {'x','z'}, dimensions={0} | all-to-all | bytes 524288 | tf_op jit(solution)/shard_map/all_to_all | solution.py:276
  237.8 1.8 token_diffs.1
  239.6 1.3 broadcast_in_dim.45
  240.9 8.1 %all-to-all-start.6 = ((f32[8,8,128]{2,1,0:T(8,128)}), f32[8,8,128]{2,1,0:T(8,128)S(1)}, u32[]{:S(2)}, u32[]{:S(2)}) async-start(f32[8,8,128]{2,1,0:T(8,128)} %broadcast_in_dim.45), calls=%async_computation.6 | async-start | bytes 65536 | tf_op jit(solution)/shard_map/all_to_all | solution.py:276
  248.9 4.7 %all-to-all-done.6 = f32[8,8,128]{2,1,0:T(8,128)S(1)} async-done(((f32[8,8,128]{2,1,0:T(8,128)}), f32[8,8,128]{2,1,0:T(8,128)S(1)}, u32[]{:S(2)}, u32[]{:S(2)}) %all-to-all-start.6) | async-done | bytes 32800 | tf_op jit(solution)/shard_map/all_to_all | solution.py:276
  (47 shorter events, 1.9 us)
Async XLA Ops:
  6.9 0.8 copy-start.14
  10.6 3.3 %copy-start.3 = (bf16[2,2048,2,256]{3,2,1,0:T(2,128)(2,1)S(1)}, bf16[2,2048,2,256]{3,2,1,0:T(2,128)(2,1)}, u32[]{:S(2)}) copy-start(bf16[2,2048,2,256]{3,2,1,0:T(2,128)(2,1)} %param.19) | copy-start | bytes 12582916
  27.6 16.7 %copy-start.16 = (f32[2,256]{1,0:T(2,128)S(1)}, f32[2,256]{1,0:T(2,128)}, u32[]{:S(2)}) copy-start(f32[2,256]{1,0:T(2,128)} %param.25) | copy-start | bytes 6148
  32.2 12.6 %collective-permute-start.3 = (bf16[272,128]{1,0:T(8,128)(2,1)}, bf16[272,128]{1,0:T(8,128)(2,1)S(1)}, u32[]{:S(2)}, u32[]{:S(2)}) collective-permute-start(bf16[272,128]{1,0:T(8,128)(2,1)} %get-tuple-element.15), channel_id=1, source_target_pairs={{0,64},{16,80},{32,96},{48,112},{1,65},{17,81},{33,97},{49,113},{2... | collective-permute-start | bytes 208904 | tf_op jit(solution)/shard_map/ppermute | solution.py:303
  37.9 7.0 %collective-permute-start.2 = (bf16[272,128]{1,0:T(8,128)(2,1)}, bf16[272,128]{1,0:T(8,128)(2,1)S(1)}, u32[]{:S(2)}, u32[]{:S(2)}) collective-permute-start(bf16[272,128]{1,0:T(8,128)(2,1)} %get-tuple-element.15), channel_id=1, source_target_pairs={{0,48},{16,64},{32,80},{48,96},{64,112},{1,49},{17,65},{33,81},{49... | collective-permute-start | bytes 208904 | tf_op jit(solution)/shard_map/ppermute | solution.py:303
  39.7 5.1 %collective-permute-start.1 = (bf16[272,128]{1,0:T(8,128)(2,1)}, bf16[272,128]{1,0:T(8,128)(2,1)S(1)}, u32[]{:S(2)}, u32[]{:S(2)}) collective-permute-start(bf16[272,128]{1,0:T(8,128)(2,1)} %get-tuple-element.15), channel_id=1, source_target_pairs={{0,32},{16,48},{32,64},{48,80},{64,96},{80,112},{1,33},{17,49},{33... | collective-permute-start | bytes 208904 | tf_op jit(solution)/shard_map/ppermute | solution.py:303
  42.1 3.8 %collective-permute-start = (bf16[272,128]{1,0:T(8,128)(2,1)}, bf16[272,128]{1,0:T(8,128)(2,1)S(1)}, u32[]{:S(2)}, u32[]{:S(2)}) collective-permute-start(bf16[272,128]{1,0:T(8,128)(2,1)} %get-tuple-element.15), channel_id=1, source_target_pairs={{0,16},{16,32},{32,48},{48,64},{64,80},{80,96},{96,112},{1,17},{17... | collective-permute-start | bytes 208904 | tf_op jit(solution)/shard_map/ppermute | solution.py:303
  44.8 1.1 copy-start.6
  44.8 1.1 copy-start.8
  44.9 1.1 copy-start.10
  45.9 0.6 copy-start.12
  51.9 47.4 %all-to-all-start = ((bf16[16,32,2176]{2,1,0:T(8,128)(2,1)}), bf16[16,32,2176]{2,1,0:T(8,128)(2,1)S(1)}, u32[]{:S(2)}, u32[]{:S(2)}) async-start(bf16[16,32,2176]{2,1,0:T(8,128)(2,1)} %bitcast.87), calls=%async_computation | async-start | bytes 4456448 | tf_op jit(solution)/shard_map/all_to_all | solution.py:305
  69.1 4.8 %copy-start = (bf16[2,512,2048]{2,1,0:T(8,128)(2,1)S(1)}, bf16[2,512,2048]{2,1,0:T(8,128)(2,1)}, u32[]{:S(2)}) copy-start(bf16[2,512,2048]{2,1,0:T(8,128)(2,1)} %param.18) | copy-start | bytes 12582916
  72.8 2.4 copy-start.5
  82.0 9.7 %collective-permute-start.7 = (bf16[272,128]{1,0:T(8,128)(2,1)}, bf16[272,128]{1,0:T(8,128)(2,1)S(1)}, u32[]{:S(2)}, u32[]{:S(2)}) collective-permute-start(bf16[272,128]{1,0:T(8,128)(2,1)} %get-tuple-element.19), channel_id=1, source_target_pairs={{0,64},{16,80},{32,96},{48,112},{1,65},{17,81},{33,97},{49,113},{2... | collective-permute-start | bytes 208904 | tf_op jit(solution)/shard_map/ppermute | solution.py:303
  84.9 6.8 %collective-permute-start.6 = (bf16[272,128]{1,0:T(8,128)(2,1)}, bf16[272,128]{1,0:T(8,128)(2,1)S(1)}, u32[]{:S(2)}, u32[]{:S(2)}) collective-permute-start(bf16[272,128]{1,0:T(8,128)(2,1)} %get-tuple-element.19), channel_id=1, source_target_pairs={{0,48},{16,64},{32,80},{48,96},{64,112},{1,49},{17,65},{33,81},{49... | collective-permute-start | bytes 208904 | tf_op jit(solution)/shard_map/ppermute | solution.py:303
  87.8 3.8 %collective-permute-start.5 = (bf16[272,128]{1,0:T(8,128)(2,1)}, bf16[272,128]{1,0:T(8,128)(2,1)S(1)}, u32[]{:S(2)}, u32[]{:S(2)}) collective-permute-start(bf16[272,128]{1,0:T(8,128)(2,1)} %get-tuple-element.19), channel_id=1, source_target_pairs={{0,32},{16,48},{32,64},{48,80},{64,96},{80,112},{1,33},{17,49},{33... | collective-permute-start | bytes 208904 | tf_op jit(solution)/shard_map/ppermute | solution.py:303
  89.1 4.2 %collective-permute-start.4 = (bf16[272,128]{1,0:T(8,128)(2,1)}, bf16[272,128]{1,0:T(8,128)(2,1)S(1)}, u32[]{:S(2)}, u32[]{:S(2)}) collective-permute-start(bf16[272,128]{1,0:T(8,128)(2,1)} %get-tuple-element.19), channel_id=1, source_target_pairs={{0,16},{16,32},{32,48},{48,64},{64,80},{80,96},{96,112},{1,17},{17... | collective-permute-start | bytes 208904 | tf_op jit(solution)/shard_map/ppermute | solution.py:303
  91.6 1.7 copy-start.7
  91.7 1.6 copy-start.9
  91.7 1.6 copy-start.11
  93.3 0.6 copy-start.13
  99.3 1.4 copy-start.1
  100.7 38.7 %all-to-all-start.3 = ((bf16[16,32,2176]{2,1,0:T(8,128)(2,1)}), bf16[16,32,2176]{2,1,0:T(8,128)(2,1)}, u32[]{:S(2)}, u32[]{:S(2)}) async-start(bf16[16,32,2176]{2,1,0:T(8,128)(2,1)} %bitcast.88), calls=%async_computation.3 | async-start | bytes 4456448 | tf_op jit(solution)/shard_map/all_to_all | solution.py:305
  107.7 4.7 %copy-start.15 = (f32[2,2048]{1,0:T(2,128)S(1)}, f32[2,2048]{1,0:T(2,128)}, u32[]{:S(2)}) copy-start(f32[2,2048]{1,0:T(2,128)} %param.27) | copy-start | bytes 49156
  139.5 36.2 %all-to-all-start.1 = ((bf16[16,32,2048]{2,1,0:T(8,128)(2,1)}), bf16[16,32,2048]{2,1,0:T(8,128)(2,1)S(1)}, u32[]{:S(2)}, u32[]{:S(2)}) async-start(bf16[16,32,2048]{2,1,0:T(8,128)(2,1)} %final_norm.2), calls=%async_computation.1 | async-start | bytes 4194304 | tf_op jit(solution)/shard_map/all_to_all | solution.py:308
  151.9 29.5 %copy-start.17 = (s32[512]{0:T(512)S(1)}, s32[512]{0:T(512)}, u32[]{:S(2)}) copy-start(s32[512]{0:T(512)} %param.30) | copy-start | bytes 6148
  175.7 1.4 copy-start.2
  177.0 29.9 %all-to-all-start.4 = ((bf16[16,32,2048]{2,1,0:T(8,128)(2,1)}), bf16[16,32,2048]{2,1,0:T(8,128)(2,1)}, u32[]{:S(2)}, u32[]{:S(2)}) async-start(bf16[16,32,2048]{2,1,0:T(8,128)(2,1)} %final_norm.3), calls=%async_computation.4 | async-start | bytes 4194304 | tf_op jit(solution)/shard_map/all_to_all | solution.py:308
  208.4 14.7 %all-to-all-start.2 = ((f32[16,8,512]{2,1,0:T(8,128)}), f32[16,8,512]{2,1,0:T(8,128)S(1)}, u32[]{:S(2)}, u32[]{:S(2)}) async-start(f32[16,8,512]{2,1,0:T(8,128)} %broadcast_in_dim.41), calls=%async_computation.2 | async-start | bytes 524288 | tf_op jit(solution)/shard_map/all_to_all | solution.py:276
  214.2 39.6 %copy-start.18 = (s32[4]{0:T(128)S(1)}, s32[4]{0:T(128)}, u32[]{:S(2)}) copy-start(s32[4]{0:T(128)} %param.35) | copy-start | bytes 52
  223.1 14.6 %copy-start.4 = (f32[16,8,512]{2,1,0:T(8,128)}, f32[16,8,512]{2,1,0:T(8,128)S(1)}, u32[]{:S(2)}) copy-start(f32[16,8,512]{2,1,0:T(8,128)S(1)} %all-to-all-done.2.s0_ref) | copy-start | bytes 786436
  240.9 12.8 %all-to-all-start.6 = ((f32[8,8,128]{2,1,0:T(8,128)}), f32[8,8,128]{2,1,0:T(8,128)S(1)}, u32[]{:S(2)}, u32[]{:S(2)}) async-start(f32[8,8,128]{2,1,0:T(8,128)} %broadcast_in_dim.45), calls=%async_computation.6 | async-start | bytes 65536 | tf_op jit(solution)/shard_map/all_to_all | solution.py:276

commit v2 on v1

--- a/solution.py
+++ b/solution.py
@@ -26,15 +26,50 @@
     return lax.dot_general(a, b, (dims, ((), ())), preferred_element_type=F32)
 
 
-def mix_kernel(val_ref, st_ref, stp_ref, bias_ref, rate_ref, skip_ref, seg_ref, y_ref, c_ref, e_ref, pay_ref):
+def as_column(row):
+    count = row.shape[1]
+    spread = jnp.broadcast_to(row, (count, count))
+    eye = lax.broadcasted_iota(jnp.int32, spread.shape, 0) == lax.broadcasted_iota(jnp.int32, spread.shape, 1)
+    return jnp.sum(jnp.where(eye, spread, 0.0), axis=1, keepdims=True)
+
+
+def mix_kernel(
+    m, tok_ref, wi_ref, ws_ref, wp_ref, bias_ref, rate_ref, skip_ref, seg_ref,
+    y_ref, gate_ref, c_ref, e_ref, pay_ref, val_ref, st_ref, stp_ref,
+):
+    k = pl.program_id(0)
+    inner = y_ref.shape[1]
+
+    @pl.when(k == 0)
+    def _():
+        gate_ref[...] = jnp.zeros_like(gate_ref)
+        val_ref[...] = jnp.zeros_like(val_ref)
+        st_ref[...] = jnp.zeros_like(st_ref)
+        stp_ref[...] = jnp.zeros_like(stp_ref)
+
+    tokens = tok_ref[...]
+    gate_ref[...] += contract(tokens, wi_ref[:, 0:inner], ((1,), (0,)))
+    val_ref[...] += contract(tokens, wi_ref[:, inner:], ((1,), (0,)))
+    st_ref[...] += contract(tokens, ws_ref[...], ((1,), (0,)))
+    stp_ref[...] += contract(tokens, wp_ref[...], ((1,), (1,)))
+
+    @pl.when(k == pl.num_programs(0) - 1)
+    def _():
+        scan_rows(
+            m, bias_ref, rate_ref, skip_ref, seg_ref, y_ref, c_ref, e_ref, pay_ref, val_ref, st_ref, stp_ref
+        )
+
+
+def scan_rows(m, bias_ref, rate_ref, skip_ref, seg_ref, y_ref, c_ref, e_ref, pay_ref, val_ref, st_ref, stp_ref):
     rows, inner = y_ref.shape
-    heads = stp_ref.shape[0]
+    heads = bias_ref.shape[1]
     wide = inner // heads
     state = c_ref.shape[1]
     seg = seg_ref[...]
-    raw = stp_ref[...] + bias_ref[...]
+    raw = jnp.transpose(stp_ref[...])[0:heads, :] + as_column(bias_ref[m : m + 1, :])
     dt = jnp.maximum(raw, 0.0) + jnp.log1p(jnp.exp(-jnp.abs(raw)))
-    la = -dt * rate_ref[...]
+    la = -dt * as_column(rate_ref[m : m + 1, :])
+    skip = as_column(skip_ref[m : m + 1, :])
     lane = lax.broadcasted_iota(jnp.int32, la.shape, 1)
     run = la
     step = 1
@@ -55,8 +90,8 @@
     ecol = jnp.transpose(jnp.concatenate([grow, segf], axis=0))
     e_ref[...] = ecol
     values = silu(val_ref[...]).astype(BF16)
-    in_map = silu(st_ref[0]).astype(BF16)
-    out_map = silu(st_ref[1]).astype(BF16)
+    in_map = silu(st_ref[:, 0:state]).astype(BF16)
+    out_map = silu(st_ref[:, state:]).astype(BF16)
     c_ref[...] = out_map
     vf = values.astype(F32)
     kept = jnp.concatenate(
@@ -78,7 +113,7 @@
     blocks = rows // SPAN
     for i in range(blocks):
         t0 = i * SPAN
-        acc = [vf[t0 : t0 + SPAN, h * wide : (h + 1) * wide] * skip_ref[h : h + 1, :] for h in range(heads)]
+        acc = [vf[t0 : t0 + SPAN, h * wide : (h + 1) * wide] * skip[h : h + 1, :] for h in range(heads)]
         for j in range(i + 1):
             s0 = j * SPAN
             scores = contract(out_map[t0 : t0 + SPAN], in_map[s0 : s0 + SPAN], ((1,), (1,)))
@@ -97,24 +132,38 @@
         y_ref[t0 : t0 + SPAN, :] = jnp.concatenate(acc, axis=1)
 
 
-def mix_local(val, st, stp, bias, rate, skip, seg):
-    rows, inner = val.shape
-    state = st.shape[2]
+def mix_local(m, hidden, w_inner, w_state, w_step, bias, rate, skip, seg, chunks=4):
+    rows, depth = hidden.shape[1:]
+    inner = w_inner.shape[2] // 2
+    state = w_state.shape[2] // 2
+    heads = bias.shape[1]
+    deep = depth // chunks
+    whole = lambda a: pl.BlockSpec(a.shape, lambda k: (0,) * a.ndim)
+    const = lambda shape: pl.BlockSpec(shape, lambda k: (0, 0))
+    shapes = ((rows, inner), F32), ((rows, inner), F32), ((rows, state), BF16), ((rows, 2 * heads), F32), (
+        (inner + 16, state), BF16)
     return pl.pallas_call(
-        mix_kernel,
-        out_shape=(
-            jax.ShapeDtypeStruct((rows, inner), F32),
-            jax.ShapeDtypeStruct((rows, state), BF16),
-            jax.ShapeDtypeStruct((rows, 8), F32),
-            jax.ShapeDtypeStruct((inner + 16, state), BF16),
-        ),
-        cost_estimate=pl.CostEstimate(flops=3 * 10**9, bytes_accessed=3 * 10**6, transcendentals=10**6),
+        functools.partial(mix_kernel, m),
+        grid=(chunks,),
+        in_specs=[
+            pl.BlockSpec((None, rows, deep), lambda k: (m, 0, k)),
+            pl.BlockSpec((None, deep, 2 * inner), lambda k: (m, k, 0)),
+            pl.BlockSpec((None, deep, 2 * state), lambda k: (m, k, 0)),
+            pl.BlockSpec((None, heads, deep), lambda k: (m, 0, k)),
+            whole(bias), whole(rate), whole(skip), whole(seg),
+        ],
+        out_specs=[const(shape) for shape, _ in shapes],
+        out_shape=[jax.ShapeDtypeStruct(shape, kind) for shape, kind in shapes],
+        scratch_shapes=[
+            pltpu.VMEM((rows, inner), F32), pltpu.VMEM((rows, 2 * state), F32), pltpu.VMEM((rows, heads), F32)
+        ],
+        cost_estimate=pl.CostEstimate(flops=5 * 10**9, bytes_accessed=8 * 10**6, transcendentals=10**6),
         name="mix_local",
-    )(val, st, stp, bias, rate, skip, seg)
+    )(hidden, w_inner, w_state, w_step, bias, rate, skip, seg)
 
 
 def gate_kernel(
-    pages_ref, flags_ref, y_ref, gate_ref, c_ref, e_ref, r1_ref, r2_ref, r3_ref, r4_ref,
+    m, pages_ref, flags_ref, y_ref, gate_ref, c_ref, e_ref, r1_ref, r2_ref, r3_ref, r4_ref,
     p0_ref, p1_ref, p2_ref, p3_ref, gain_ref, w_ref, out_ref,
 ):
     rows, inner = y_ref.shape
@@ -152,7 +201,7 @@
     spread = jnp.concatenate([jnp.broadcast_to(e_col[:, h : h + 1], (rows, wide)) for h in range(heads)], axis=1)
     gated = (y_ref[...] + picked * spread) * silu(gate_ref[...])
     square = jnp.sum(gated * gated, axis=1, keepdims=True)
-    mixed = (gated * gain_ref[...]).astype(BF16)
+    mixed = (gated * gain_ref[m : m + 1, :]).astype(BF16)
     out_ref[:, 0:width] = contract(mixed, w_ref[...], ((1,), (0,))).astype(BF16)
     high = square.astype(BF16).astype(F32)
     mid = (square - high).astype(BF16).astype(F32)
@@ -172,7 +221,7 @@
         (None, None, heads, pool.shape[3], state), lambda g, pg, fl: (m, pg[j], 0, 0, 0)
     )
     return pl.pallas_call(
-        gate_kernel,
+        functools.partial(gate_kernel, m),
         grid_spec=pltpu.PrefetchScalarGridSpec(
             num_scalar_prefetch=2,
             grid=(1,),
@@ -180,7 +229,7 @@
             + [whole(r) for r in recv]
             + [page(j) for j in range(4)]
             + [
-                pl.BlockSpec((1, inner), lambda g, pg, fl: (0, 0)),
+                whole(gain),
                 pl.BlockSpec((None, inner, width), lambda g, pg, fl: (m, 0, 0)),
             ],
             out_specs=pl.BlockSpec((rows, width + 128), lambda g, pg, fl: (0, 0)),
@@ -191,89 +240,111 @@
     )(pages, flags, y, gate, c, e, *recv, pool, pool, pool, pool, gain, w_out)
 
 
-def norm_kernel(units, part_ref, hid_ref, gain_ref, out_ref):
+def norm_kernel(m, units, place_ref, part_ref, hid_ref, gain_ref, out_ref):
     width = hid_ref.shape[1]
     total = jnp.sum(part_ref[...].astype(F32), axis=0)
     square = total[:, width : width + 1] + total[:, width + 1 : width + 2] + total[:, width + 2 : width + 3]
     res = hid_ref[...].astype(F32) + total[:, 0:width] * lax.rsqrt(square / units + NORM_EPS)
     mean = jnp.sum(res * res, axis=1, keepdims=True) / width
-    normed = (res * lax.rsqrt(mean + NORM_EPS) * gain_ref[...]).astype(BF16)
+    normed = (res * lax.rsqrt(mean + NORM_EPS) * gain_ref[m : m + 1, :]).astype(BF16)
     out_ref[...] = jnp.broadcast_to(normed[None], out_ref.shape)
 
 
-def final_norm(part, hid, gain, units):
+def final_norm(m, place, part, hidden, gain, units):
+    group, share, _ = part.shape
+    depth = hidden.shape[2]
     return pl.pallas_call(
-        functools.partial(norm_kernel, float(units)),
-        out_shape=jax.ShapeDtypeStruct((part.shape[0],) + hid.shape, BF16),
+        functools.partial(norm_kernel, m, float(units)),
+        grid_spec=pltpu.PrefetchScalarGridSpec(
+            num_scalar_prefetch=1,
+            grid=(1,),
+            in_specs=[
+                pl.BlockSpec(part.shape, lambda g, at: (0, 0, 0)),
+                pl.BlockSpec((None, share, depth), lambda g, at: (m, at[0], 0)),
+                pl.BlockSpec(gain.shape, lambda g, at: (0, 0)),
+            ],
+            out_specs=pl.BlockSpec((group, share, depth), lambda g, at: (0, 0, 0)),
+        ),
+        out_shape=jax.ShapeDtypeStruct((group, share, depth), BF16),
         cost_estimate=pl.CostEstimate(flops=10**7, bytes_accessed=4 * 10**6, transcendentals=100),
         name="final_norm",
-    )(part, hid, gain)
-
-
-def head_kernel(x_ref, w_ref, tgt_ref, out_ref):
+    )(place, part, hidden, gain)
+
+
+def head_kernel(place_ref, x_ref, w_ref, tgt_ref, out_ref):
+    tile = x_ref.shape[0]
+    vocab = w_ref.shape[1]
+    i = pl.program_id(0)
     logits = contract(x_ref[...], w_ref[...], ((1,), (0,)))
     top = jnp.max(logits, axis=1, keepdims=True)
     total = jnp.sum(jnp.exp(logits - top), axis=1, keepdims=True)
     lse = top + jnp.log(total)
-    at = lax.broadcasted_iota(jnp.int32, logits.shape, 1)
-    chosen = jnp.sum(jnp.where(at == tgt_ref[...], logits, 0.0), axis=1, keepdims=True)
-    lane = lax.broadcasted_iota(jnp.int32, (logits.shape[0], 8), 1)
-    out_ref[...] = jnp.transpose(jnp.where(lane == 0, lse, jnp.where(lane == 1, chosen, 0.0)))
-
-
-def head_stats(m, x, head, tgt, tile=256):
+    target = (tgt_ref[...] - place_ref[0] * vocab).astype(F32)
+    target = jnp.transpose(jnp.broadcast_to(target, (8, tile)))[:, 0:1]
+    at = lax.broadcasted_iota(jnp.int32, logits.shape, 1).astype(F32)
+    chosen = jnp.sum(jnp.where(at == target, logits, 0.0), axis=1, keepdims=True)
+    lane = lax.broadcasted_iota(jnp.int32, (tile, 8), 1)
+    flat = jnp.transpose(jnp.where(lane == 0, lse, jnp.where(lane == 1, chosen, 0.0)))
+    count = tile // 128
+    for n in range(count):
+        for which in range(2):
+            piece = flat[which : which + 1, n * 128 : (n + 1) * 128]
+            out_ref[:, pl.ds(which * 4 + i * count + n, 1), :] = jnp.broadcast_to(
+                piece[None], (out_ref.shape[0], 1, 128)
+            )
+
+
+def head_stats(m, place, x, head, tgt, group, tile=256):
     rows, depth = x.shape
     vocab = head.shape[2]
     return pl.pallas_call(
         head_kernel,
-        grid=(rows // tile,),
-        in_specs=[
-            pl.BlockSpec((tile, depth), lambda i: (i, 0)),
-            pl.BlockSpec((None, depth, vocab), lambda i: (m, 0, 0)),
-            pl.BlockSpec((tile, 1), lambda i: (i, 0)),
-        ],
-        out_specs=pl.BlockSpec((8, tile), lambda i: (0, i)),
-        out_shape=jax.ShapeDtypeStruct((8, rows), F32),
+        grid_spec=pltpu.PrefetchScalarGridSpec(
+            num_scalar_prefetch=1,
+            grid=(rows // tile,),
+            in_specs=[
+                pl.BlockSpec((tile, depth), lambda i, at: (i, 0)),
+                pl.BlockSpec((None, depth, vocab), lambda i, at: (m, 0, 0)),
+                pl.BlockSpec((1, tile), lambda i, at: (0, i)),
+            ],
+            out_specs=pl.BlockSpec((group, 8, 128), lambda i, at: (0, 0, 0)),
+        ),
+        out_shape=jax.ShapeDtypeStruct((group, 8, 128), F32),
         cost_estimate=pl.CostEstimate(
             flops=2 * rows * depth * vocab, bytes_accessed=2 * depth * vocab, transcendentals=rows * vocab
         ),
         name="head_stats",
-    )(x, head, tgt)
+    )(place, x, head, tgt)
 
 
 def diff_kernel(s0_ref, s1_ref, live_ref, seg_ref, diff_ref, sums_ref):
     scores = []
     for ref in (s0_ref, s1_ref):
         part = ref[...]
-        lse = part[:, 0, :]
-        top = jnp.max(lse, axis=0, keepdims=True)
-        total = top + jnp.log(jnp.sum(jnp.exp(lse - top), axis=0, keepdims=True))
-        scores.append(jnp.sum(part[:, 1, :], axis=0, keepdims=True) - total)
-    rows = seg_ref.shape[1]
-    alive = jnp.where(
-        lax.broadcasted_iota(jnp.int32, (1, rows), 1) < SPAN, live_ref[0].astype(F32), live_ref[1].astype(F32)
-    )
+        lse = part[:, 0:4, :]
+        top = jnp.max(lse, axis=0)
+        total = top + jnp.log(jnp.sum(jnp.exp(lse - top[None]), axis=0))
+        scores.append(jnp.sum(part[:, 4:8, :], axis=0) - total)
+    lines = lax.broadcasted_iota(jnp.int32, (4, 128), 0)
+    alive = jnp.where(lines < 2, live_ref[0].astype(F32), live_ref[1].astype(F32))
     diff = alive * (scores[0] - scores[1])
     diff_ref[...] = diff
-    which = lax.broadcasted_iota(jnp.int32, (8, rows), 0)
-    sums = jnp.sum(jnp.where(which == seg_ref[...], diff, 0.0), axis=1, keepdims=True)
-    sums_ref[...] = jnp.broadcast_to(sums, sums_ref.shape)
-
-
-def token_diffs(s0, s1, live, seg):
-    rows = seg.shape[1]
+    which = lax.broadcasted_iota(jnp.int32, (8, 128), 0)
+    sums = jnp.zeros((8, 128), F32)
+    for j in range(4):
+        mine = jnp.sum(jnp.where(seg_ref[...] == j, diff, 0.0), axis=1, keepdims=True)
+        sums = jnp.where(which == j, jnp.sum(mine, axis=0, keepdims=True), sums)
+    sums_ref[...] = jnp.broadcast_to(sums[None], sums_ref.shape)
+
+
+def token_diffs(s0, s1, live, seg, devices):
     vm = pl.BlockSpec(memory_space=pltpu.VMEM)
     return pl.pallas_call(
         diff_kernel,
         in_specs=[vm, vm, pl.BlockSpec(memory_space=pltpu.SMEM), vm],
-        out_shape=(jax.ShapeDtypeStruct((1, rows), F32), jax.ShapeDtypeStruct((8, 128), F32)),
+        out_shape=(jax.ShapeDtypeStruct((4, 128), F32), jax.ShapeDtypeStruct((devices, 8, 128), F32)),
         name="token_diffs",
     )(s0, s1, live, seg)
-
-
-def to_all(value, axes):
-    count = lax.axis_size(axes)
-    return lax.all_to_all(jnp.broadcast_to(value[None], (count,) + value.shape), axes, 0, 0)
 
 
 def per_device(
@@ -285,30 +356,27 @@
     inner = w_inner.shape[3]
     group = lax.axis_size(VOC)
     devices = lax.axis_size(SEQ)
-    place = lax.axis_index(VOC)
+    place = lax.axis_index(VOC).astype(jnp.int32).reshape(1)
     share = rows // group
     seg = segment_ids.reshape(1, rows)
-    tgt = (targets - place * head.shape[2]).reshape(rows, 1)
+    tgt = targets.reshape(1, rows)
+    w_inner = w_inner.reshape(2, depth, 2 * inner)
+    w_state = w_state.reshape(2, depth, -1)
+    w_step = jnp.swapaxes(w_step, 1, 2)
+    mixed = [
+        mix_local(m, hidden, w_inner, w_state, w_step, step_bias, rate, skip_gain, seg) for m in range(2)
+    ]
     stats = []
     for m in range(2):
-        tokens = hidden[m]
-        proj = jnp.einsum("td,dgi->gti", tokens, w_inner[m], preferred_element_type=F32)
-        st = jnp.einsum("td,dgn->gtn", tokens, w_state[m], preferred_element_type=F32)
-        stp = jnp.einsum("td,dh->ht", tokens, w_step[m], preferred_element_type=F32)
-        wide = inner // rate.shape[1]
-        y, c, e, pay = mix_local(
-            proj[1], st, stp, step_bias[m][:, None], rate[m][:, None],
-            jnp.broadcast_to(skip_gain[m][:, None], (rate.shape[1], wide)), seg,
-        )
+        y, gate, c, e, pay = mixed[m]
         recv = [lax.ppermute(pay, SEQ, [(i, i + k) for i in range(devices - k)]) for k in range(1, REACH + 1)]
-        part = gate_out(m, pages, flags, y, proj[0], c, e, recv, pool, norm_gain[m][None], w_out)
+        part = gate_out(m, pages, flags, y, gate, c, e, recv, pool, norm_gain, w_out)
         part = lax.all_to_all(part.reshape(group, share, depth + 128), VOC, 0, 0)
-        mine = lax.dynamic_slice_in_dim(tokens, place * share, share, 0)
-        normed = final_norm(part, mine, final_gain[m][None], inner * group)
+        normed = final_norm(m, place, part, hidden, final_gain, inner * group)
         normed = lax.all_to_all(normed, VOC, 0, 0).reshape(rows, depth)
-        stats.append(to_all(head_stats(m, normed, head, tgt), VOC))
-    diff, sums = token_diffs(stats[0], stats[1], live, seg)
-    sums = jnp.sum(to_all(sums, SEQ)[:, 0:4, 0], axis=0)
+        stats.append(lax.all_to_all(head_stats(m, place, normed, head, tgt, group), VOC, 0, 0))
+    diff, sums = token_diffs(stats[0], stats[1], live, segment_ids.reshape(4, 128), devices)
+    sums = jnp.sum(lax.all_to_all(sums, SEQ, 0, 0)[:, 0:4, 0], axis=0)
     owned = jnp.where(owners == lax.axis_index(SEQ), sums, 0.0)
     return diff.reshape(rows), owned[None]
 

time: 256 us -> 226 us (0.88)
  local copies, waits for them, and re-layouts: 44.4 us -> 16 us
  matrix products: 16.1 us -> 0 us
  Pallas kernels: 47 us -> 55.6 us
  waiting for transfers between devices: 69.5 us -> 75.7 us
    dot_general x6 -> x0, matrix products: 16.1 us -> none  [the longest x2 7.15 us: per_device(): jnp.einsum('td,dgi->gti', tokens, w_inner[m], preferred_element_type=F32)]
    unnamed x42 -> x26, local copies, waits for them, and re-layouts: 17.8 us -> 3.98 us
    slice x5 -> x0, local copies, waits for them, and re-layouts: 11.7 us -> none  [the longest x1 4.07 us: per_device(): tokens = hidden[m]]
    reshape x1 -> x2, local copies, waits for them, and re-layouts: 0.87 us -> 12 us  [the longest x1 7.58 us: per_device(): w_inner = w_inner.reshape(2, depth, 2 * inner)]
    pallas_call x8, Pallas kernels: 45.2 us -> 54 us  [the longest x2 18 us: mix_local(): pl.pallas_call(functools.partial(mix_kernel, m), grid=(chunks,), in_specs...]
    all_to_all x2, waiting for transfers between devices: 22.7 us -> 30.1 us  [per_device(): part = lax.all_to_all(part.reshape(group, share, depth + 128), VOC, 0, 0)]
    broadcast_in_dim x6 -> x0, local copies, waits for them, and re-layouts: 5.5 us -> none  [the longest x3 3.48 us: to_all(): jnp.broadcast_to(value[None], (count,) + value.shape)]
    another operation x6 -> x0, local copies, waits for them, and re-layouts: 4.15 us -> none  [the longest x3 2.08 us: per_device(): step_bias[m][:, None]]
  transfers between devices with their start and end apart: 14 -> 14, of which waited for: 6 -> 7; matrix products, arithmetic and copies ran while one was open for 10% -> 0% of each run, Pallas kernels for 14% -> 18%
where the time goes in v2:
time: 226 us; the launch traced here: 225 us
  waiting for transfers between devices  75.7 us (33%)
  starting transfers between devices  62.6 us (28%)
  Pallas kernels  55.6 us (25%)
  local copies, waits for them, and re-layouts  16 us (7%)
  blocking collectives  13.3 us (6%)
    all_to_all x2, waiting for transfers between devices, per_device(): normed = lax.all_to_all(normed, VOC, 0, 0).reshape(rows, depth)  37.7 us
    all_to_all x2, waiting for transfers between devices, per_device(): part = lax.all_to_all(part.reshape(group, share, depth + 128), VOC, 0, 0)  30.1 us
    ppermute x8, starting transfers between devices, per_device(): lax.ppermute(pay, SEQ, [(i, i + k) for i in range(devices - k)])  21.6 us
    pallas_call x2, Pallas kernels, mix_local(): pl.pallas_call(functools.partial(mix_kernel, m), grid=(chunks,), in_specs...  18 us
    pallas_call x2, Pallas kernels, head_stats(): pl.pallas_call(head_kernel, grid_spec=pltpu.PrefetchScalarGridSpec(num_sc...  17.8 us
    all_to_all x2, starting transfers between devices, per_device(): part = lax.all_to_all(part.reshape(group, share, depth + 128), VOC, 0, 0)  14.7 us
    all_to_all x1, blocking collectives, per_device(): lax.all_to_all(head_stats(m, place, normed, head, tgt, group), VOC, 0, 0)  13.3 us
    all_to_all x2, starting transfers between devices, per_device(): normed = lax.all_to_all(normed, VOC, 0, 0).reshape(rows, depth)  11.1 us
  transfers between devices with their start and end apart: 14, of which 7 were waited for; matrix products, arithmetic and copies ran while one was open for 0% of the time, Pallas kernels for 18%

profile of v2, /device:TPU:1, one launch (start us, length us, event | category | flops | bytes accessed | tf_op | source)
XLA Modules:
  0.0 224.7 jit_solution(9363289291028977356)
XLA Ops:
  0.6 4.4 %reshape.39.ws_ref = bf16[2,2048,256]{2,1,0:T(8,128)(2,1)} reshape(bf16[2,2048,2,128]{3,2,1,0:T(2,128)(2,1)} %param.20) | data formatting | bytes 4194304 | tf_op jit(solution)/shard_map/reshape | solution.py:364
  5.1 7.6 %reshape.38.wi_ref = bf16[2,2048,512]{2,1,0:T(8,128)(2,1)} reshape(bf16[2,2048,2,256]{3,2,1,0:T(2,128)(2,1)} %param.19) | data formatting | bytes 8388608 | tf_op jit(solution)/shard_map/reshape | solution.py:363
  12.6 9.0 %mix_local.2 = (f32[512,256]{1,0:T(8,128)}, f32[512,256]{1,0:T(8,128)}, bf16[512,128]{1,0:T(8,128)(2,1)}, f32[512,8]{1,0:T(8,128)}, bf16[272,128]{1,0:T(8,128)(2,1)}) custom-call(bf16[2,512,2048]{2,1,0:T(8,128)(2,1)} %hid_ref.3, bf16[2,2048,512]{2,1,0:T(8,128)(2,1)} %reshape.38.wi_ref, bf16[2,2048,256]{2,1,0:T(8,128)(2,1)} %reshape.39.ws_ref, ...), custom_call_target="tpu_custom_call" | custom-call | flops 5000000000 | bytes 8000000 | tf_op jit(solution)/shard_map/mix_local/pallas_call | solution.py:145
  21.6 5.6 %collective-permute-start.3 = (bf16[272,128]{1,0:T(8,128)(2,1)}, bf16[272,128]{1,0:T(8,128)(2,1)S(1)}, u32[]{:S(2)}, u32[]{:S(2)}) collective-permute-start(bf16[272,128]{1,0:T(8,128)(2,1)} %get-tuple-element.18), channel_id=1, source_target_pairs={{0,64},{16,80},{32,96},{48,112},{1,65},{17,81},{33,97},{49,113},{2... | collective-permute-start | bytes 208904 | tf_op jit(solution)/shard_map/ppermute | solution.py:372
  27.3 1.9 collective-permute-start.2
  29.2 2.4 %collective-permute-start.1 = (bf16[272,128]{1,0:T(8,128)(2,1)}, bf16[272,128]{1,0:T(8,128)(2,1)S(1)}, u32[]{:S(2)}, u32[]{:S(2)}) collective-permute-start(bf16[272,128]{1,0:T(8,128)(2,1)} %get-tuple-element.18), channel_id=1, source_target_pairs={{0,32},{16,48},{32,64},{48,80},{64,96},{80,112},{1,33},{17,49},{33... | collective-permute-start | bytes 208904 | tf_op jit(solution)/shard_map/ppermute | solution.py:372
  31.5 2.1 collective-permute-start
  33.7 0.0 collective-permute-done.3.r4_ref
  33.7 0.0 copy-start.4
  33.7 0.0 collective-permute-done.2.r3_ref
  33.7 0.0 copy-start.6
  33.7 0.0 collective-permute-done.1.r2_ref
  33.7 0.0 copy-start.8
  33.7 1.6 collective-permute-done.r1_ref
  35.3 0.0 copy-start.10
  35.3 0.0 copy-done.4
  35.3 0.0 copy-done.6
  35.4 0.0 copy-done.8
  35.4 0.6 copy-done.10
  36.0 5.4 %gate_out.2 = bf16[512,2176]{1,0:T(8,128)(2,1)} custom-call(s32[4]{0:T(128)} %pages_ref.3, s32[4]{0:T(128)} %flags_ref.3, f32[512,256]{1,0:T(8,128)} %get-tuple-element.14.y_ref, f32[512,256]{1,0:T(8,128)} %get-tuple-element.15.gate_ref, bf16[512,128]{1,0:T(8,128)(2,1)} %get-tuple-element.16.c_ref, f32[512,8]{1,0:T(8,128)} %get-tuple-element.17.e_ref, ...), custom_call_target="tpu_custom_call" | custom-call | flops 3000000000 | bytes 6000000 | tf_op jit(solution)/shard_map/gate_out/pallas_call | solution.py:223
  41.4 7.6 %all-to-all-start = ((bf16[16,32,2176]{2,1,0:T(8,128)(2,1)}), bf16[16,32,2176]{2,1,0:T(8,128)(2,1)S(1)}, u32[]{:S(2)}, u32[]{:S(2)}) async-start(bf16[16,32,2176]{2,1,0:T(8,128)(2,1)} %bitcast.12), calls=%async_computation | async-start | bytes 4456448 | tf_op jit(solution)/shard_map/all_to_all | solution.py:374
  49.0 9.0 %mix_local.3 = (f32[512,256]{1,0:T(8,128)}, f32[512,256]{1,0:T(8,128)}, bf16[512,128]{1,0:T(8,128)(2,1)}, f32[512,8]{1,0:T(8,128)}, bf16[272,128]{1,0:T(8,128)(2,1)}) custom-call(bf16[2,512,2048]{2,1,0:T(8,128)(2,1)} %hid_ref.3, bf16[2,2048,512]{2,1,0:T(8,128)(2,1)} %reshape.38.wi_ref, bf16[2,2048,256]{2,1,0:T(8,128)(2,1)} %reshape.39.ws_ref, ...), custom_call_target="tpu_custom_call" | custom-call | flops 5000000000 | bytes 8000000 | tf_op jit(solution)/shard_map/mix_local/pallas_call | solution.py:145
  58.0 2.9 %collective-permute-start.7 = (bf16[272,128]{1,0:T(8,128)(2,1)}, bf16[272,128]{1,0:T(8,128)(2,1)S(1)}, u32[]{:S(2)}, u32[]{:S(2)}) collective-permute-start(bf16[272,128]{1,0:T(8,128)(2,1)} %get-tuple-element.23), channel_id=1, source_target_pairs={{0,64},{16,80},{32,96},{48,112},{1,65},{17,81},{33,97},{49,113},{2... | collective-permute-start | bytes 208904 | tf_op jit(solution)/shard_map/ppermute | solution.py:372
  60.9 2.9 %collective-permute-start.6 = (bf16[272,128]{1,0:T(8,128)(2,1)}, bf16[272,128]{1,0:T(8,128)(2,1)S(1)}, u32[]{:S(2)}, u32[]{:S(2)}) collective-permute-start(bf16[272,128]{1,0:T(8,128)(2,1)} %get-tuple-element.23), channel_id=1, source_target_pairs={{0,48},{16,64},{32,80},{48,96},{64,112},{1,49},{17,65},{33,81},{49... | collective-permute-start | bytes 208904 | tf_op jit(solution)/shard_map/ppermute | solution.py:372
  63.9 1.3 collective-permute-start.5
  65.2 2.5 %collective-permute-start.4 = (bf16[272,128]{1,0:T(8,128)(2,1)}, bf16[272,128]{1,0:T(8,128)(2,1)S(1)}, u32[]{:S(2)}, u32[]{:S(2)}) collective-permute-start(bf16[272,128]{1,0:T(8,128)(2,1)} %get-tuple-element.23), channel_id=1, source_target_pairs={{0,16},{16,32},{32,48},{48,64},{64,80},{80,96},{96,112},{1,17},{17... | collective-permute-start | bytes 208904 | tf_op jit(solution)/shard_map/ppermute | solution.py:372
  67.7 0.0 collective-permute-done.7.r4_ref
  67.7 0.0 copy-start.5
  67.7 0.0 collective-permute-done.6.r3_ref
  67.7 0.0 copy-start.7
  67.7 0.0 collective-permute-done.5.r2_ref
  67.7 0.0 copy-start.9
  67.7 1.6 collective-permute-done.4.r1_ref
  69.3 0.0 copy-start.11
  69.3 0.0 copy-done.5
  69.3 0.0 copy-done.7
  69.3 0.0 copy-done.9
  69.3 0.6 copy-done.11
  70.0 5.4 %gate_out.3 = bf16[512,2176]{1,0:T(8,128)(2,1)} custom-call(s32[4]{0:T(128)} %pages_ref.3, s32[4]{0:T(128)} %flags_ref.3, f32[512,256]{1,0:T(8,128)} %get-tuple-element.19.y_ref, f32[512,256]{1,0:T(8,128)} %get-tuple-element.20.gate_ref, bf16[512,128]{1,0:T(8,128)(2,1)} %get-tuple-element.21.c_ref, f32[512,8]{1,0:T(8,128)} %get-tuple-element.22.e_ref, ...), custom_call_target="tpu_custom_call" | custom-call | flops 3000000000 | bytes 6000000 | tf_op jit(solution)/shard_map/gate_out/pallas_call | solution.py:223
  75.4 4.6 %all-to-all-done.part_ref = bf16[16,32,2176]{2,1,0:T(8,128)(2,1)S(1)} async-done(((bf16[16,32,2176]{2,1,0:T(8,128)(2,1)}), bf16[16,32,2176]{2,1,0:T(8,128)(2,1)S(1)}, u32[]{:S(2)}, u32[]{:S(2)}) %all-to-all-start) | async-done | bytes 2228256 | tf_op jit(solution)/shard_map/all_to_all | solution.py:374
  80.0 1.4 copy-done
  81.4 7.1 %all-to-all-start.3 = ((bf16[16,32,2176]{2,1,0:T(8,128)(2,1)}), bf16[16,32,2176]{2,1,0:T(8,128)(2,1)}, u32[]{:S(2)}, u32[]{:S(2)}) async-start(bf16[16,32,2176]{2,1,0:T(8,128)(2,1)} %bitcast.13), calls=%async_computation.3 | async-start | bytes 4456448 | tf_op jit(solution)/shard_map/all_to_all | solution.py:374
  88.4 3.7 %final_norm.2 = bf16[16,32,2048]{2,1,0:T(8,128)(2,1)} custom-call(s32[1]{0:T(128)} %bitcast.place_ref, bf16[16,32,2176]{2,1,0:T(8,128)(2,1)} %copy-done, bf16[2,512,2048]{2,1,0:T(8,128)(2,1)} %hid_ref.3, f32[2,2048]{1,0:T(2,128)} %gain_ref.7), custom_call_target="tpu_custom_call" | custom-call | flops 10000000 | bytes 4000000 | tf_op jit(solution)/shard_map/final_norm/pallas_call | solution.py:256
  92.1 25.5 %all-to-all-done.3.part_ref = bf16[16,32,2176]{2,1,0:T(8,128)(2,1)} async-done(((bf16[16,32,2176]{2,1,0:T(8,128)(2,1)}), bf16[16,32,2176]{2,1,0:T(8,128)(2,1)}, u32[]{:S(2)}, u32[]{:S(2)}) %all-to-all-start.3) | async-done | bytes 2228256 | tf_op jit(solution)/shard_map/all_to_all | solution.py:374
  117.6 4.1 %all-to-all-start.1 = ((bf16[16,32,2048]{2,1,0:T(8,128)(2,1)}), bf16[16,32,2048]{2,1,0:T(8,128)(2,1)S(1)}, u32[]{:S(2)}, u32[]{:S(2)}) async-start(bf16[16,32,2048]{2,1,0:T(8,128)(2,1)} %final_norm.2), calls=%async_computation.1 | async-start | bytes 4194304 | tf_op jit(solution)/shard_map/all_to_all | solution.py:376
  121.7 3.7 %final_norm.3 = bf16[16,32,2048]{2,1,0:T(8,128)(2,1)} custom-call(s32[1]{0:T(128)} %bitcast.place_ref, bf16[16,32,2176]{2,1,0:T(8,128)(2,1)} %all-to-all-done.3.part_ref, bf16[2,512,2048]{2,1,0:T(8,128)(2,1)} %hid_ref.3, f32[2,2048]{1,0:T(2,128)} %gain_ref.7), custom_call_target="tpu_custom_call" | custom-call | flops 10000000 | bytes 4000000 | tf_op jit(solution)/shard_map/final_norm/pallas_call | solution.py:256
  125.3 21.4 %all-to-all-done.1 = bf16[16,32,2048]{2,1,0:T(8,128)(2,1)S(1)} async-done(((bf16[16,32,2048]{2,1,0:T(8,128)(2,1)}), bf16[16,32,2048]{2,1,0:T(8,128)(2,1)S(1)}, u32[]{:S(2)}, u32[]{:S(2)}) %all-to-all-start.1) | async-done | bytes 2097184 | tf_op jit(solution)/shard_map/all_to_all | solution.py:376
  146.8 1.3 copy-done.2
  148.1 7.0 %all-to-all-start.4 = ((bf16[16,32,2048]{2,1,0:T(8,128)(2,1)}), bf16[16,32,2048]{2,1,0:T(8,128)(2,1)S(1)}, u32[]{:S(2)}, u32[]{:S(2)}) async-start(bf16[16,32,2048]{2,1,0:T(8,128)(2,1)} %final_norm.3), calls=%async_computation.4 | async-start | bytes 4194304 | tf_op jit(solution)/shard_map/all_to_all | solution.py:376
  155.1 8.9 %head_stats.2 = f32[16,8,128]{2,1,0:T(8,128)} custom-call(s32[1]{0:T(128)} %bitcast.place_ref, bf16[512,2048]{1,0:T(8,128)(2,1)} %bitcast.15, bf16[2,2048,1664]{2,1,0:T(8,128)(2,1)} %w_ref.7, s32[1,512]{1,0:T(1,128)} %bitcast.16), custom_call_target="tpu_custom_call" | custom-call | flops 3489660928 | bytes 6815744 | tf_op jit(solution)/shard_map/head_stats/pallas_call | solution.py:300
  164.0 16.3 %all-to-all-done.4 = bf16[16,32,2048]{2,1,0:T(8,128)(2,1)S(1)} async-done(((bf16[16,32,2048]{2,1,0:T(8,128)(2,1)}), bf16[16,32,2048]{2,1,0:T(8,128)(2,1)S(1)}, u32[]{:S(2)}, u32[]{:S(2)}) %all-to-all-start.4) | async-done | bytes 2097184 | tf_op jit(solution)/shard_map/all_to_all | solution.py:376
  180.3 6.9 %all-to-all-start.2 = ((f32[16,8,128]{2,1,0:T(8,128)}), f32[16,8,128]{2,1,0:T(8,128)S(1)}, u32[]{:S(2)}, u32[]{:S(2)}) async-start(f32[16,8,128]{2,1,0:T(8,128)} %head_stats.2), calls=%async_computation.2 | async-start | bytes 131072 | tf_op jit(solution)/shard_map/all_to_all | solution.py:377
  187.2 0.0 copy-done.1
  187.2 0.0 copy-start.12
  187.2 8.9 %head_stats.3 = f32[16,8,128]{2,1,0:T(8,128)} custom-call(s32[1]{0:T(128)} %bitcast.place_ref, bf16[512,2048]{1,0:T(8,128)(2,1)} %bitcast.14, bf16[2,2048,1664]{2,1,0:T(8,128)(2,1)} %w_ref.7, s32[1,512]{1,0:T(1,128)} %bitcast.17), custom_call_target="tpu_custom_call" | custom-call | flops 3489660928 | bytes 6815744 | tf_op jit(solution)/shard_map/head_stats/pallas_call | solution.py:300
  196.1 0.0 all-to-all-done.2.s0_ref
  196.1 13.3 %all_to_all.35.s1_ref = f32[16,8,128]{2,1,0:T(8,128)} all-to-all(f32[16,8,128]{2,1,0:T(8,128)} %head_stats.3), channel_id=1, replica_groups=mesh['y'=4,'core'=2,'x'=4,'z'=4] {'x','z'}, dimensions={0} | all-to-all | bytes 131072 | tf_op jit(solution)/shard_map/all_to_all | solution.py:377
  209.3 0.0 copy-done.3
  209.3 1.6 token_diffs.1
  211.0 8.3 %all-to-all-start.6 = ((f32[8,8,128]{2,1,0:T(8,128)}), f32[8,8,128]{2,1,0:T(8,128)S(1)}, u32[]{:S(2)}, u32[]{:S(2)}) async-start(f32[8,8,128]{2,1,0:T(8,128)} %get-tuple-element.25), calls=%async_computation.6 | async-start | bytes 65536 | tf_op jit(solution)/shard_map/all_to_all | solution.py:379
  219.3 4.7 %all-to-all-done.6 = f32[8,8,128]{2,1,0:T(8,128)S(1)} async-done(((f32[8,8,128]{2,1,0:T(8,128)}), f32[8,8,128]{2,1,0:T(8,128)S(1)}, u32[]{:S(2)}, u32[]{:S(2)}) %all-to-all-start.6) | async-done | bytes 32800 | tf_op jit(solution)/shard_map/all_to_all | solution.py:379
  224.0 0.1 slice_reduce_fusion
  224.2 0.0 copy-done.12
  224.2 0.5 fusion
  (4 shorter events, 0.0 us)
Async XLA Ops:
  21.6 12.0 %collective-permute-start.3 = (bf16[272,128]{1,0:T(8,128)(2,1)}, bf16[272,128]{1,0:T(8,128)(2,1)S(1)}, u32[]{:S(2)}, u32[]{:S(2)}) collective-permute-start(bf16[272,128]{1,0:T(8,128)(2,1)} %get-tuple-element.18), channel_id=1, source_target_pairs={{0,64},{16,80},{32,96},{48,112},{1,65},{17,81},{33,97},{49,113},{2... | collective-permute-start | bytes 208904 | tf_op jit(solution)/shard_map/ppermute | solution.py:372
  27.3 6.4 %collective-permute-start.2 = (bf16[272,128]{1,0:T(8,128)(2,1)}, bf16[272,128]{1,0:T(8,128)(2,1)S(1)}, u32[]{:S(2)}, u32[]{:S(2)}) collective-permute-start(bf16[272,128]{1,0:T(8,128)(2,1)} %get-tuple-element.18), channel_id=1, source_target_pairs={{0,48},{16,64},{32,80},{48,96},{64,112},{1,49},{17,65},{33,81},{49... | collective-permute-start | bytes 208904 | tf_op jit(solution)/shard_map/ppermute | solution.py:372
  29.2 4.6 %collective-permute-start.1 = (bf16[272,128]{1,0:T(8,128)(2,1)}, bf16[272,128]{1,0:T(8,128)(2,1)S(1)}, u32[]{:S(2)}, u32[]{:S(2)}) collective-permute-start(bf16[272,128]{1,0:T(8,128)(2,1)} %get-tuple-element.18), channel_id=1, source_target_pairs={{0,32},{16,48},{32,64},{48,80},{64,96},{80,112},{1,33},{17,49},{33... | collective-permute-start | bytes 208904 | tf_op jit(solution)/shard_map/ppermute | solution.py:372
  31.5 3.8 %collective-permute-start = (bf16[272,128]{1,0:T(8,128)(2,1)}, bf16[272,128]{1,0:T(8,128)(2,1)S(1)}, u32[]{:S(2)}, u32[]{:S(2)}) collective-permute-start(bf16[272,128]{1,0:T(8,128)(2,1)} %get-tuple-element.18), channel_id=1, source_target_pairs={{0,16},{16,32},{32,48},{48,64},{64,80},{80,96},{96,112},{1,17},{17... | collective-permute-start | bytes 208904 | tf_op jit(solution)/shard_map/ppermute | solution.py:372
  33.7 1.7 copy-start.4
  33.7 1.6 copy-start.6
  33.7 1.6 copy-start.8
  35.3 0.6 copy-start.10
  41.4 38.6 %all-to-all-start = ((bf16[16,32,2176]{2,1,0:T(8,128)(2,1)}), bf16[16,32,2176]{2,1,0:T(8,128)(2,1)S(1)}, u32[]{:S(2)}, u32[]{:S(2)}) async-start(bf16[16,32,2176]{2,1,0:T(8,128)(2,1)} %bitcast.12), calls=%async_computation | async-start | bytes 4456448 | tf_op jit(solution)/shard_map/all_to_all | solution.py:374
  58.0 9.7 %collective-permute-start.7 = (bf16[272,128]{1,0:T(8,128)(2,1)}, bf16[272,128]{1,0:T(8,128)(2,1)S(1)}, u32[]{:S(2)}, u32[]{:S(2)}) collective-permute-start(bf16[272,128]{1,0:T(8,128)(2,1)} %get-tuple-element.23), channel_id=1, source_target_pairs={{0,64},{16,80},{32,96},{48,112},{1,65},{17,81},{33,97},{49,113},{2... | collective-permute-start | bytes 208904 | tf_op jit(solution)/shard_map/ppermute | solution.py:372
  60.9 6.8 %collective-permute-start.6 = (bf16[272,128]{1,0:T(8,128)(2,1)}, bf16[272,128]{1,0:T(8,128)(2,1)S(1)}, u32[]{:S(2)}, u32[]{:S(2)}) collective-permute-start(bf16[272,128]{1,0:T(8,128)(2,1)} %get-tuple-element.23), channel_id=1, source_target_pairs={{0,48},{16,64},{32,80},{48,96},{64,112},{1,49},{17,65},{33,81},{49... | collective-permute-start | bytes 208904 | tf_op jit(solution)/shard_map/ppermute | solution.py:372
  63.9 3.8 %collective-permute-start.5 = (bf16[272,128]{1,0:T(8,128)(2,1)}, bf16[272,128]{1,0:T(8,128)(2,1)S(1)}, u32[]{:S(2)}, u32[]{:S(2)}) collective-permute-start(bf16[272,128]{1,0:T(8,128)(2,1)} %get-tuple-element.23), channel_id=1, source_target_pairs={{0,32},{16,48},{32,64},{48,80},{64,96},{80,112},{1,33},{17,49},{33... | collective-permute-start | bytes 208904 | tf_op jit(solution)/shard_map/ppermute | solution.py:372
  65.2 4.2 %collective-permute-start.4 = (bf16[272,128]{1,0:T(8,128)(2,1)}, bf16[272,128]{1,0:T(8,128)(2,1)S(1)}, u32[]{:S(2)}, u32[]{:S(2)}) collective-permute-start(bf16[272,128]{1,0:T(8,128)(2,1)} %get-tuple-element.23), channel_id=1, source_target_pairs={{0,16},{16,32},{32,48},{48,64},{64,80},{80,96},{96,112},{1,17},{17... | collective-permute-start | bytes 208904 | tf_op jit(solution)/shard_map/ppermute | solution.py:372
  67.7 1.7 copy-start.5
  67.7 1.6 copy-start.7
  67.7 1.6 copy-start.9
  69.3 0.6 copy-start.11
  80.0 1.4 copy-start
  81.4 36.2 %all-to-all-start.3 = ((bf16[16,32,2176]{2,1,0:T(8,128)(2,1)}), bf16[16,32,2176]{2,1,0:T(8,128)(2,1)}, u32[]{:S(2)}, u32[]{:S(2)}) async-start(bf16[16,32,2176]{2,1,0:T(8,128)(2,1)} %bitcast.13), calls=%async_computation.3 | async-start | bytes 4456448 | tf_op jit(solution)/shard_map/all_to_all | solution.py:374
  117.6 29.2 %all-to-all-start.1 = ((bf16[16,32,2048]{2,1,0:T(8,128)(2,1)}), bf16[16,32,2048]{2,1,0:T(8,128)(2,1)S(1)}, u32[]{:S(2)}, u32[]{:S(2)}) async-start(bf16[16,32,2048]{2,1,0:T(8,128)(2,1)} %final_norm.2), calls=%async_computation.1 | async-start | bytes 4194304 | tf_op jit(solution)/shard_map/all_to_all | solution.py:376
  146.8 1.3 copy-start.2
  148.1 32.2 %all-to-all-start.4 = ((bf16[16,32,2048]{2,1,0:T(8,128)(2,1)}), bf16[16,32,2048]{2,1,0:T(8,128)(2,1)S(1)}, u32[]{:S(2)}, u32[]{:S(2)}) async-start(bf16[16,32,2048]{2,1,0:T(8,128)(2,1)} %final_norm.3), calls=%async_computation.4 | async-start | bytes 4194304 | tf_op jit(solution)/shard_map/all_to_all | solution.py:376
  180.3 6.9 %copy-start.1 = (bf16[16,32,2048]{2,1,0:T(8,128)(2,1)}, bf16[16,32,2048]{2,1,0:T(8,128)(2,1)S(1)}, u32[]{:S(2)}) copy-start(bf16[16,32,2048]{2,1,0:T(8,128)(2,1)S(1)} %all-to-all-done.4) | copy-start | bytes 6291460
  180.3 15.8 %all-to-all-start.2 = ((f32[16,8,128]{2,1,0:T(8,128)}), f32[16,8,128]{2,1,0:T(8,128)S(1)}, u32[]{:S(2)}, u32[]{:S(2)}) async-start(f32[16,8,128]{2,1,0:T(8,128)} %head_stats.2), calls=%async_computation.2 | async-start | bytes 131072 | tf_op jit(solution)/shard_map/all_to_all | solution.py:377
  187.2 37.0 %copy-start.12 = (s32[4]{0:T(128)S(1)}, s32[4]{0:T(128)}, u32[]{:S(2)}) copy-start(s32[4]{0:T(128)} %param.35) | copy-start | bytes 52
  196.1 13.3 %copy-start.3 = (f32[16,8,128]{2,1,0:T(8,128)}, f32[16,8,128]{2,1,0:T(8,128)S(1)}, u32[]{:S(2)}) copy-start(f32[16,8,128]{2,1,0:T(8,128)S(1)} %all-to-all-done.2.s0_ref) | copy-start | bytes 196612
  211.0 13.0 %all-to-all-start.6 = ((f32[8,8,128]{2,1,0:T(8,128)}), f32[8,8,128]{2,1,0:T(8,128)S(1)}, u32[]{:S(2)}, u32[]{:S(2)}) async-start(f32[8,8,128]{2,1,0:T(8,128)} %get-tuple-element.25), calls=%async_computation.6 | async-start | bytes 65536 | tf_op jit(solution)/shard_map/all_to_all | solution.py:379

commit v3 on v2

--- a/solution.py
+++ b/solution.py
@@ -24,6 +24,20 @@
 
 def contract(a, b, dims):
     return lax.dot_general(a, b, (dims, ((), ())), preferred_element_type=F32)
+
+
+def pieces(value):
+    high = value.astype(BF16).astype(F32)
+    mid = (value - high).astype(BF16).astype(F32)
+    return [high, mid, value - high - mid]
+
+
+def to_column(row):
+    return jnp.transpose(jnp.broadcast_to(row, (8, row.shape[1])))[:, 0:1]
+
+
+def to_row(column):
+    return jnp.transpose(jnp.broadcast_to(column, (column.shape[0], 8)))[0:1, :]
 
 
 def as_column(row):
@@ -164,13 +178,12 @@
 
 def gate_kernel(
     m, pages_ref, flags_ref, y_ref, gate_ref, c_ref, e_ref, r1_ref, r2_ref, r3_ref, r4_ref,
-    p0_ref, p1_ref, p2_ref, p3_ref, gain_ref, w_ref, out_ref,
+    p0_ref, p1_ref, p2_ref, p3_ref, gain_ref, out_ref,
 ):
     rows, inner = y_ref.shape
     heads = p0_ref.shape[0]
     wide = inner // heads
     state = c_ref.shape[1]
-    width = w_ref.shape[1]
     e_col = e_ref[...]
     seg_col = e_col[:, heads : heads + 1]
     seg_first = e_col[0:1, heads : heads + 1]
@@ -201,21 +214,17 @@
     spread = jnp.concatenate([jnp.broadcast_to(e_col[:, h : h + 1], (rows, wide)) for h in range(heads)], axis=1)
     gated = (y_ref[...] + picked * spread) * silu(gate_ref[...])
     square = jnp.sum(gated * gated, axis=1, keepdims=True)
-    mixed = (gated * gain_ref[m : m + 1, :]).astype(BF16)
-    out_ref[:, 0:width] = contract(mixed, w_ref[...], ((1,), (0,))).astype(BF16)
-    high = square.astype(BF16).astype(F32)
-    mid = (square - high).astype(BF16).astype(F32)
-    low = square - high - mid
-    lane = lax.broadcasted_iota(jnp.int32, (rows, 128), 1)
-    extra = jnp.where(lane == 0, high, jnp.where(lane == 1, mid, jnp.where(lane == 2, low, 0.0)))
-    out_ref[:, width : width + 128] = extra.astype(BF16)
-
-
-def gate_out(m, pages, flags, y, gate, c, e, recv, pool, gain, w_out):
+    out_ref[0:rows, :] = (gated * gain_ref[m : m + 1, :]).astype(BF16)
+    lines = jnp.transpose(jnp.broadcast_to(square, (rows, 8)))[0:1, :]
+    halves = jnp.concatenate([lines[:, 0:inner], lines[:, inner:]], axis=0)
+    extra = jnp.concatenate(pieces(halves) + [jnp.zeros((10, inner), F32)], axis=0)
+    out_ref[rows : rows + 16, :] = extra.astype(BF16)
+
+
+def gate_out(m, pages, flags, y, gate, c, e, recv, pool, gain):
     rows, inner = y.shape
     heads = pool.shape[2]
     state = c.shape[1]
-    width = w_out.shape[2]
     whole = lambda a: pl.BlockSpec(a.shape, lambda g, pg, fl: (0,) * a.ndim)
     page = lambda j: pl.BlockSpec(
         (None, None, heads, pool.shape[3], state), lambda g, pg, fl: (m, pg[j], 0, 0, 0)
@@ -228,93 +237,158 @@
             in_specs=[whole(y), whole(gate), whole(c), whole(e)]
             + [whole(r) for r in recv]
             + [page(j) for j in range(4)]
-            + [
-                whole(gain),
-                pl.BlockSpec((None, inner, width), lambda g, pg, fl: (m, 0, 0)),
-            ],
-            out_specs=pl.BlockSpec((rows, width + 128), lambda g, pg, fl: (0, 0)),
+            + [whole(gain)],
+            out_specs=pl.BlockSpec((rows + 16, inner), lambda g, pg, fl: (0, 0)),
         ),
-        out_shape=jax.ShapeDtypeStruct((rows, width + 128), BF16),
-        cost_estimate=pl.CostEstimate(flops=3 * 10**9, bytes_accessed=6 * 10**6, transcendentals=10**5),
+        out_shape=jax.ShapeDtypeStruct((rows + 16, inner), BF16),
+        cost_estimate=pl.CostEstimate(flops=10**9, bytes_accessed=4 * 10**6, transcendentals=10**5),
         name="gate_out",
-    )(pages, flags, y, gate, c, e, *recv, pool, pool, pool, pool, gain, w_out)
-
-
-def norm_kernel(m, units, place_ref, part_ref, hid_ref, gain_ref, out_ref):
-    width = hid_ref.shape[1]
-    total = jnp.sum(part_ref[...].astype(F32), axis=0)
-    square = total[:, width : width + 1] + total[:, width + 1 : width + 2] + total[:, width + 2 : width + 3]
-    res = hid_ref[...].astype(F32) + total[:, 0:width] * lax.rsqrt(square / units + NORM_EPS)
-    mean = jnp.sum(res * res, axis=1, keepdims=True) / width
-    normed = (res * lax.rsqrt(mean + NORM_EPS) * gain_ref[m : m + 1, :]).astype(BF16)
-    out_ref[...] = jnp.broadcast_to(normed[None], out_ref.shape)
-
-
-def final_norm(m, place, part, hidden, gain, units):
-    group, share, _ = part.shape
-    depth = hidden.shape[2]
-    return pl.pallas_call(
-        functools.partial(norm_kernel, m, float(units)),
+    )(pages, flags, y, gate, c, e, *recv, pool, pool, pool, pool, gain)
+
+
+def out_kernel(at_ref, g0_ref, g1_ref, g2_ref, g3_ref, w_ref, o0_ref, o1_ref, o2_ref, o3_ref, acc_ref, sq_ref):
+    rows, width = acc_ref.shape
+    inner = g0_ref.shape[1]
+    block = rows // 4
+    along, across = at_ref[0], at_ref[1]
+    gathered = (g0_ref, g1_ref, g2_ref, g3_ref)
+    extra = sum(g[rows : rows + 16, :].astype(F32) for g in gathered)
+    square = extra[0:2] + extra[2:4] + extra[4:6]
+    for n in range(4):
+        sq_ref[n : n + 1, :] = square[n // 2 : n // 2 + 1, (n % 2) * block : (n % 2 + 1) * block]
+    acc_ref[...] = sum(
+        contract(g[0:rows, :], w_ref[lax.rem(along + 4 - k, 4)], ((1,), (0,))) for k, g in enumerate(gathered)
+    )
+    for k, out in enumerate((o0_ref, o1_ref, o2_ref, o3_ref)):
+        at = lax.rem(across + k, 4)
+        out[0:block, :] = acc_ref[pl.ds(pl.multiple_of(at * block, block), block), :].astype(BF16)
+        line = jnp.concatenate(pieces(sq_ref[pl.ds(at, 1), :]) + [jnp.zeros((1, width - 3 * block), F32)], axis=1)
+        out[block : block + 16, :] = jnp.broadcast_to(line, (16, width)).astype(BF16)
+
+
+def out_blocks(at, gathered, w):
+    rows = gathered[0].shape[0] - 16
+    width = w.shape[2]
+    block = rows // 4
+    vm = pl.BlockSpec(memory_space=pltpu.VMEM)
+    return pl.pallas_call(
+        out_kernel,
+        in_specs=[pl.BlockSpec(memory_space=pltpu.SMEM)] + [vm] * 5,
+        out_specs=[vm] * 4,
+        out_shape=[jax.ShapeDtypeStruct((block + 16, width), BF16)] * 4,
+        scratch_shapes=[pltpu.VMEM((rows, width), F32), pltpu.VMEM((4, block), F32)],
+        cost_estimate=pl.CostEstimate(flops=10**9, bytes_accessed=3 * 10**6, transcendentals=0),
+        name="out_blocks",
+    )(at, *gathered, w)
+
+
+def residual_kernel(m, units, at_ref, o0_ref, o1_ref, o2_ref, o3_ref, hid_ref, gain_ref, out_ref):
+    block, width = hid_ref.shape
+    total = sum(o[...].astype(F32) for o in (o0_ref, o1_ref, o2_ref, o3_ref))
+    line = total[block : block + 1, :]
+    square = line[:, 0:block] + line[:, block : 2 * block] + line[:, 2 * block : 3 * block]
+    scale = to_column(lax.rsqrt(square / units + NORM_EPS))
+    res = hid_ref[...].astype(F32) + total[0:block, :] * scale
+    out_ref[0:block, :] = (res * gain_ref[m : m + 1, :]).astype(BF16)
+    line = jnp.concatenate(
+        pieces(to_row(jnp.sum(res * res, axis=1, keepdims=True))) + [jnp.zeros((1, width - 3 * block), F32)], axis=1
+    )
+    out_ref[block : block + 16, :] = jnp.broadcast_to(line, (16, width)).astype(BF16)
+
+
+def residual_block(m, at, parts, hidden, gain, units):
+    block, width = parts[0].shape[0] - 16, parts[0].shape[1]
+    whole = pl.BlockSpec((block + 16, width), lambda g, at: (0, 0))
+    return pl.pallas_call(
+        functools.partial(residual_kernel, m, float(units)),
         grid_spec=pltpu.PrefetchScalarGridSpec(
             num_scalar_prefetch=1,
             grid=(1,),
-            in_specs=[
-                pl.BlockSpec(part.shape, lambda g, at: (0, 0, 0)),
-                pl.BlockSpec((None, share, depth), lambda g, at: (m, at[0], 0)),
-                pl.BlockSpec(gain.shape, lambda g, at: (0, 0)),
+            in_specs=[whole] * 4
+            + [
+                pl.BlockSpec((None, block, width), lambda g, at: (m, at[1], at[0])),
+                pl.BlockSpec((2, width), lambda g, at: (0, at[0])),
             ],
-            out_specs=pl.BlockSpec((group, share, depth), lambda g, at: (0, 0, 0)),
+            out_specs=whole,
         ),
-        out_shape=jax.ShapeDtypeStruct((group, share, depth), BF16),
-        cost_estimate=pl.CostEstimate(flops=10**7, bytes_accessed=4 * 10**6, transcendentals=100),
-        name="final_norm",
-    )(place, part, hidden, gain)
-
-
-def head_kernel(place_ref, x_ref, w_ref, tgt_ref, out_ref):
-    tile = x_ref.shape[0]
+        out_shape=jax.ShapeDtypeStruct((block + 16, width), BF16),
+        cost_estimate=pl.CostEstimate(flops=10**6, bytes_accessed=10**6, transcendentals=100),
+        name="residual_block",
+    )(at, *parts, hidden, gain)
+
+
+def join_kernel(at_ref, u0_ref, u1_ref, u2_ref, u3_ref, out_ref):
+    block, width = u0_ref.shape[0] - 16, u0_ref.shape[1]
+    square = jnp.zeros((1, block), F32)
+    for k, u in enumerate((u0_ref, u1_ref, u2_ref, u3_ref)):
+        at = pl.multiple_of(lax.rem(at_ref[0] + 4 - k, 4) * width, width)
+        out_ref[0:block, pl.ds(at, width)] = u[0:block, :]
+        line = u[block : block + 16, :].astype(F32)[0:1, :]
+        square = square + line[:, 0:block] + line[:, block : 2 * block] + line[:, 2 * block : 3 * block]
+    scale = lax.rsqrt(square / out_ref.shape[1] + NORM_EPS)
+    out_ref[block : block + 16, :] = jnp.zeros((16, out_ref.shape[1]), BF16)
+    line = jnp.concatenate(pieces(scale), axis=1)
+    out_ref[block : block + 16, 0 : 3 * block] = jnp.broadcast_to(line, (16, 3 * block)).astype(BF16)
+
+
+def join_columns(at, parts):
+    tall, width = parts[0].shape
+    vm = pl.BlockSpec(memory_space=pltpu.VMEM)
+    return pl.pallas_call(
+        join_kernel,
+        in_specs=[pl.BlockSpec(memory_space=pltpu.SMEM)] + [vm] * 4,
+        out_specs=vm,
+        out_shape=jax.ShapeDtypeStruct((tall, 4 * width), BF16),
+        cost_estimate=pl.CostEstimate(flops=10**5, bytes_accessed=10**6, transcendentals=100),
+        name="join_columns",
+    )(at, *parts)
+
+
+def head_kernel(place_ref, at_ref, x0_ref, x1_ref, x2_ref, x3_ref, w_ref, tgt_ref, out_ref):
+    block = x0_ref.shape[0] - 16
     vocab = w_ref.shape[1]
-    i = pl.program_id(0)
-    logits = contract(x_ref[...], w_ref[...], ((1,), (0,)))
-    top = jnp.max(logits, axis=1, keepdims=True)
-    total = jnp.sum(jnp.exp(logits - top), axis=1, keepdims=True)
-    lse = top + jnp.log(total)
-    target = (tgt_ref[...] - place_ref[0] * vocab).astype(F32)
-    target = jnp.transpose(jnp.broadcast_to(target, (8, tile)))[:, 0:1]
-    at = lax.broadcasted_iota(jnp.int32, logits.shape, 1).astype(F32)
-    chosen = jnp.sum(jnp.where(at == target, logits, 0.0), axis=1, keepdims=True)
-    lane = lax.broadcasted_iota(jnp.int32, (tile, 8), 1)
-    flat = jnp.transpose(jnp.where(lane == 0, lse, jnp.where(lane == 1, chosen, 0.0)))
-    count = tile // 128
-    for n in range(count):
-        for which in range(2):
-            piece = flat[which : which + 1, n * 128 : (n + 1) * 128]
-            out_ref[:, pl.ds(which * 4 + i * count + n, 1), :] = jnp.broadcast_to(
-                piece[None], (out_ref.shape[0], 1, 128)
-            )
-
-
-def head_stats(m, place, x, head, tgt, group, tile=256):
-    rows, depth = x.shape
+    for pair in (((0, x0_ref), (1, x1_ref)), ((2, x2_ref), (3, x3_ref))):
+        rows = jnp.concatenate([x[0:block, :] for _, x in pair], axis=0)
+        raw = contract(rows, w_ref[...], ((1,), (0,)))
+        for n, (k, x) in enumerate(pair):
+            at = lax.rem(at_ref[1] + 4 - k, 4)
+            line = x[block : block + 16, 0 : 3 * block].astype(F32)[0:1, :]
+            scale = to_column(line[:, 0:block] + line[:, block : 2 * block] + line[:, 2 * block : 3 * block])
+            logits = raw[n * block : (n + 1) * block, :] * scale
+            top = jnp.max(logits, axis=1, keepdims=True)
+            lse = top + jnp.log(jnp.sum(jnp.exp(logits - top), axis=1, keepdims=True))
+            target = to_column((tgt_ref[pl.ds(at, 1), :] - place_ref[0] * vocab).astype(F32))
+            column = lax.broadcasted_iota(jnp.int32, logits.shape, 1).astype(F32)
+            chosen = jnp.sum(jnp.where(column == target, logits, 0.0), axis=1, keepdims=True)
+            for which, value in enumerate((lse, chosen)):
+                out_ref[:, pl.ds(which * 4 + at, 1), :] = jnp.broadcast_to(
+                    to_row(value)[None], (out_ref.shape[0], 1, block)
+                )
+
+
+def head_stats(m, place, at, parts, head, tgt, group):
+    tall, depth = parts[0].shape
+    block = tall - 16
     vocab = head.shape[2]
+    whole = pl.BlockSpec((tall, depth), lambda i, pf, at: (0, 0))
     return pl.pallas_call(
         head_kernel,
         grid_spec=pltpu.PrefetchScalarGridSpec(
-            num_scalar_prefetch=1,
-            grid=(rows // tile,),
-            in_specs=[
-                pl.BlockSpec((tile, depth), lambda i, at: (i, 0)),
-                pl.BlockSpec((None, depth, vocab), lambda i, at: (m, 0, 0)),
-                pl.BlockSpec((1, tile), lambda i, at: (0, i)),
+            num_scalar_prefetch=2,
+            grid=(1,),
+            in_specs=[whole] * 4
+            + [
+                pl.BlockSpec((None, depth, vocab), lambda i, pf, at: (m, 0, 0)),
+                pl.BlockSpec(tgt.shape, lambda i, pf, at: (0, 0)),
             ],
-            out_specs=pl.BlockSpec((group, 8, 128), lambda i, at: (0, 0, 0)),
+            out_specs=pl.BlockSpec((group, 8, block), lambda i, pf, at: (0, 0, 0)),
         ),
-        out_shape=jax.ShapeDtypeStruct((group, 8, 128), F32),
+        out_shape=jax.ShapeDtypeStruct((group, 8, block), F32),
         cost_estimate=pl.CostEstimate(
-            flops=2 * rows * depth * vocab, bytes_accessed=2 * depth * vocab, transcendentals=rows * vocab
+            flops=8 * block * depth * vocab, bytes_accessed=2 * depth * vocab, transcendentals=4 * block * vocab
         ),
         name="head_stats",
-    )(place, x, head, tgt)
+    )(place, at, *parts, head, tgt)
 
 
 def diff_kernel(s0_ref, s1_ref, live_ref, seg_ref, diff_ref, sums_ref):
@@ -347,6 +421,14 @@
     )(s0, s1, live, seg)
 
 
+def ring(value, axis, by):
+    return lax.ppermute(value, axis, [(i, (i + by) % 4) for i in range(4)])
+
+
+def gathered(value, axis):
+    return [value] + [ring(value, axis, k) for k in (1, 2, 3)]
+
+
 def per_device(
     hidden, w_inner, w_state, w_step, step_bias, rate, skip_gain, norm_gain, w_out, final_gain, head, pool,
     targets, segment_ids, flags, pages, live, owners,
@@ -357,24 +439,30 @@
     group = lax.axis_size(VOC)
     devices = lax.axis_size(SEQ)
     place = lax.axis_index(VOC).astype(jnp.int32).reshape(1)
-    share = rows // group
     seg = segment_ids.reshape(1, rows)
-    tgt = targets.reshape(1, rows)
+    tgt = targets.reshape(4, rows // 4)
     w_inner = w_inner.reshape(2, depth, 2 * inner)
     w_state = w_state.reshape(2, depth, -1)
     w_step = jnp.swapaxes(w_step, 1, 2)
+    ways = (("x", "z"), ("z", "x"))
+    turned = jnp.swapaxes(w_out.reshape(2, inner, 4, depth // 4), 1, 2)
+    weights = [lax.all_to_all(turned[m], ways[m][0], 0, 0) for m in range(2)]
     mixed = [
         mix_local(m, hidden, w_inner, w_state, w_step, step_bias, rate, skip_gain, seg) for m in range(2)
     ]
     stats = []
     for m in range(2):
+        along, across = ways[m]
+        at = jnp.stack([lax.axis_index(along), lax.axis_index(across)]).astype(jnp.int32)
         y, gate, c, e, pay = mixed[m]
         recv = [lax.ppermute(pay, SEQ, [(i, i + k) for i in range(devices - k)]) for k in range(1, REACH + 1)]
-        part = gate_out(m, pages, flags, y, gate, c, e, recv, pool, norm_gain, w_out)
-        part = lax.all_to_all(part.reshape(group, share, depth + 128), VOC, 0, 0)
-        normed = final_norm(m, place, part, hidden, final_gain, inner * group)
-        normed = lax.all_to_all(normed, VOC, 0, 0).reshape(rows, depth)
-        stats.append(lax.all_to_all(head_stats(m, place, normed, head, tgt, group), VOC, 0, 0))
+        gated = gate_out(m, pages, flags, y, gate, c, e, recv, pool, norm_gain)
+        parts = out_blocks(at, gathered(gated, along), weights[m])
+        parts = [parts[0]] + [ring(parts[k], across, k) for k in (1, 2, 3)]
+        res = residual_block(m, at, parts, hidden, final_gain, inner * group)
+        full = join_columns(at, gathered(res, along))
+        stat = head_stats(m, place, at, gathered(full, across), head, tgt, group)
+        stats.append(lax.all_to_all(stat, VOC, 0, 0))
     diff, sums = token_diffs(stats[0], stats[1], live, segment_ids.reshape(4, 128), devices)
     sums = jnp.sum(lax.all_to_all(sums, SEQ, 0, 0)[:, 0:4, 0], axis=0)
     owned = jnp.where(owners == lax.axis_index(SEQ), sums, 0.0)

time: 226 us -> 236 us (1.044)
  local copies, waits for them, and re-layouts: 16 us -> 26.2 us
  waiting for transfers between devices: 75.7 us -> 65.6 us
  Pallas kernels: 55.6 us -> 63.1 us
  starting transfers between devices: 62.6 us -> 65.8 us
  blocking collectives: 13.3 us -> 10.6 us
    all_to_all x5 -> x3, waiting for transfers between devices: 67.8 us -> 0.01 us  [the longest x2 0.01 us: per_device(): weights = [lax.all_to_all(turned[m], ways[m][0], 0, 0) for m in range(2)]]
    ppermute x0 -> x24, waiting for transfers between devices: none -> 59.2 us  [ring(): return lax.ppermute(value, axis, [(i, (i + by) % 4) for i in range(4)])]
    ppermute x0 -> x24, starting transfers between devices: none -> 26.7 us  [ring(): return lax.ppermute(value, axis, [(i, (i + by) % 4) for i in range(4)])]
    all_to_all x5 -> x3, starting transfers between devices: 32.6 us -> 13.7 us  [the longest x2 9.99 us: per_device(): weights = [lax.all_to_all(turned[m], ways[m][0], 0, 0) for m in range(2)]]
    pallas_call x2 -> x6, Pallas kernels: 7.34 us -> 16.1 us  [the longest x2 6.38 us: out_blocks(): pl.pallas_call(out_kernel, in_specs=[pl.BlockSpec(memory_space=pltpu.SMEM...]
    unnamed x26 -> x75, local copies, waits for them, and re-layouts: 3.98 us -> 11.6 us
    all_to_all x1, starting transfers between devices: 8.31 us -> 4.92 us  [per_device(): sums = jnp.sum(lax.all_to_all(sums, SEQ, 0, 0)[:, 0:4, 0], axis=0)]
    reshape x0 -> x1, local copies, waits for them, and re-layouts: none -> 2.79 us  [per_device(): turned = jnp.swapaxes(w_out.reshape(2, inner, 4, depth // 4), 1, 2)]
  transfers between devices with their start and end apart: 14 -> 36, of which waited for: 7 -> 11; matrix products, arithmetic and copies ran while one was open for 0% -> 5% of each run, Pallas kernels for 18% -> 26%
where the time goes in v3:
time: 236 us; the launch traced here: 234 us
  starting transfers between devices  65.8 us (28%)
  waiting for transfers between devices  65.6 us (28%)
  Pallas kernels  63.1 us (27%)
  local copies, waits for them, and re-layouts  26.2 us (11%)
  blocking collectives  10.6 us (4%)
    ppermute x24, waiting for transfers between devices, ring(): return lax.ppermute(value, axis, [(i, (i + by) % 4) for i in range(4)])  59.2 us
    ppermute x24, starting transfers between devices, ring(): return lax.ppermute(value, axis, [(i, (i + by) % 4) for i in range(4)])  26.7 us
    ppermute x8, starting transfers between devices, per_device(): lax.ppermute(pay, SEQ, [(i, i + k) for i in range(devices - k)])  20.5 us
    pallas_call x2, Pallas kernels, head_stats(): pl.pallas_call(head_kernel, grid_spec=pltpu.PrefetchScalarGridSpec(num_sc...  19.2 us
    pallas_call x2, Pallas kernels, mix_local(): pl.pallas_call(functools.partial(mix_kernel, m), grid=(chunks,), in_specs...  18 us
    unnamed x75, local copies, waits for them, and re-layouts  11.6 us
    all_to_all x1, blocking collectives, per_device(): stats.append(lax.all_to_all(stat, VOC, 0, 0))  10.6 us
    all_to_all x2, starting transfers between devices, per_device(): weights = [lax.all_to_all(turned[m], ways[m][0], 0, 0) for m in range(2)]  9.99 us
  transfers between devices with their start and end apart: 36, of which 11 were waited for; matrix products, arithmetic and copies ran while one was open for 5% of the time, Pallas kernels for 26%

profile of v3, /device:TPU:1, one launch (start us, length us, event | category | flops | bytes accessed | tf_op | source)
XLA Modules:
  0.0 234.3 jit_solution(12467804058938993070)
XLA Ops:
  0.6 3.9 %copy.20 = bf16[2,256,2048]{1,2,0:T(8,128)(2,1)} copy(bf16[2,256,2048]{2,1,0:T(8,128)(2,1)} %param.26) | data formatting | bytes 4194304 | tf_op args[8]
  4.6 2.8 %copy.21 = bf16[2,256,4,512]{3,1,2,0:T(8,128)(2,1)S(1)} copy(bf16[2,256,4,512]{1,3,2,0:T(8,128)(2,1)} %bitcast.17) | data formatting | bytes 4194304 | tf_op jit(solution)/shard_map/reshape | solution.py:448
  7.4 1.6 slice_bitcast_fusion
  9.0 6.0 %all-to-all-start.2 = ((bf16[4,256,512]{2,1,0:T(8,128)(2,1)}), bf16[4,256,512]{2,1,0:T(8,128)(2,1)S(1)}, u32[]{:S(2)}, u32[]{:S(2)}) async-start(bf16[4,256,512]{2,1,0:T(8,128)(2,1)} %get-tuple-element.42), calls=%async_computation.2 | async-start | bytes 2097152 | tf_op jit(solution)/shard_map/all_to_all | solution.py:449
  15.0 2.6 %reshape.30.ws_ref = bf16[2,2048,256]{2,1,0:T(8,128)(2,1)} reshape(bf16[2,2048,2,128]{3,2,1,0:T(2,128)(2,1)S(1)} %copy-done.1) | data formatting | bytes 4194304 | tf_op jit(solution)/shard_map/reshape | solution.py:445
  17.6 7.6 %reshape.29.wi_ref = bf16[2,2048,512]{2,1,0:T(8,128)(2,1)} reshape(bf16[2,2048,2,256]{3,2,1,0:T(2,128)(2,1)} %param.19) | data formatting | bytes 8388608 | tf_op jit(solution)/shard_map/reshape | solution.py:444
  25.2 9.0 %mix_local.3 = (f32[512,256]{1,0:T(8,128)}, f32[512,256]{1,0:T(8,128)}, bf16[512,128]{1,0:T(8,128)(2,1)}, f32[512,8]{1,0:T(8,128)}, bf16[272,128]{1,0:T(8,128)(2,1)}) custom-call(bf16[2,512,2048]{2,1,0:T(8,128)(2,1)} %hid_ref.3, bf16[2,2048,512]{2,1,0:T(8,128)(2,1)} %reshape.29.wi_ref, bf16[2,2048,256]{2,1,0:T(8,128)(2,1)} %reshape.30.ws_ref, ...), custom_call_target="tpu_custom_call" | custom-call | flops 5000000000 | bytes 8000000 | tf_op jit(solution)/shard_map/mix_local/pallas_call | solution.py:159
  34.2 4.8 %collective-permute-start.19 = (bf16[272,128]{1,0:T(8,128)(2,1)}, bf16[272,128]{1,0:T(8,128)(2,1)S(1)}, u32[]{:S(2)}, u32[]{:S(2)}) collective-permute-start(bf16[272,128]{1,0:T(8,128)(2,1)} %get-tuple-element.35), channel_id=1, source_target_pairs={{0,64},{16,80},{32,96},{48,112},{1,65},{17,81},{33,97},{49,113},{2... | collective-permute-start | bytes 208904 | tf_op jit(solution)/shard_map/ppermute | solution.py:458
  39.0 2.1 collective-permute-start.18
  41.1 2.3 collective-permute-start.17
  43.5 2.2 collective-permute-start.16
  45.7 1.6 collective-permute-done.16.r1_ref
  47.3 0.6 copy-done.29
  48.0 4.0 %gate_out.3.g0_ref = bf16[528,256]{1,0:T(8,128)(2,1)} custom-call(s32[4]{0:T(128)} %pages_ref.3, s32[4]{0:T(128)} %flags_ref.3, f32[512,256]{1,0:T(8,128)} %get-tuple-element.31.y_ref, f32[512,256]{1,0:T(8,128)} %get-tuple-element.32.gate_ref, bf16[512,128]{1,0:T(8,128)(2,1)} %get-tuple-element.33.c_ref, f32[512,8]{1,0:T(8,128)} %get-tuple-element.34.e_ref, ...), custom_call_target="tpu_custom_call" | custom-call | flops 1000000000 | bytes 4000000 | tf_op jit(solution)/shard_map/gate_out/pallas_call | solution.py:232
  52.0 3.0 %collective-permute-start.22 = (bf16[528,256]{1,0:T(8,128)(2,1)}, bf16[528,256]{1,0:T(8,128)(2,1)S(1)}, u32[]{:S(2)}, u32[]{:S(2)}) collective-permute-start(bf16[528,256]{1,0:T(8,128)(2,1)} %gate_out.3.g0_ref), channel_id=1, source_target_pairs={{0,3},{1,0},{2,1},{3,2},{4,7},{5,4},{6,5},{7,6},{8,11},{9,8},{10,9... | collective-permute-start | bytes 811016 | tf_op jit(solution)/shard_map/ppermute | solution.py:425
  56.1 0.7 pad_add_fusion.1.at_ref
  56.8 4.0 %all-to-all-start = ((bf16[4,256,512]{2,1,0:T(8,128)(2,1)}), bf16[4,256,512]{2,1,0:T(8,128)(2,1)S(1)}, u32[]{:S(2)}, u32[]{:S(2)}) async-start(bf16[4,256,512]{2,1,0:T(8,128)(2,1)} %get-tuple-element.43), calls=%async_computation | async-start | bytes 2097152 | tf_op jit(solution)/shard_map/all_to_all | solution.py:449
  60.8 6.5 %collective-permute-done.22.g3_ref = bf16[528,256]{1,0:T(8,128)(2,1)S(1)} collective-permute-done((bf16[528,256]{1,0:T(8,128)(2,1)}, bf16[528,256]{1,0:T(8,128)(2,1)S(1)}, u32[]{:S(2)}, u32[]{:S(2)}) %collective-permute-start.22) | collective-permute-done | bytes 270368 | tf_op jit(solution)/shard_map/ppermute | solution.py:425
  67.2 3.6 %collective-permute-done.20.g1_ref = bf16[528,256]{1,0:T(8,128)(2,1)S(1)} collective-permute-done((bf16[528,256]{1,0:T(8,128)(2,1)}, bf16[528,256]{1,0:T(8,128)(2,1)S(1)}, u32[]{:S(2)}, u32[]{:S(2)}) %collective-permute-start.20) | collective-permute-done | bytes 270368 | tf_op jit(solution)/shard_map/ppermute | solution.py:425
  70.9 0.7 copy-done.36
  71.6 3.2 %out_blocks.3 = (bf16[144,512]{1,0:T(8,128)(2,1)}, bf16[144,512]{1,0:T(8,128)(2,1)}, bf16[144,512]{1,0:T(8,128)(2,1)}, bf16[144,512]{1,0:T(8,128)(2,1)}) custom-call(s32[2]{0:T(128)} %pad_add_fusion.1.at_ref, bf16[528,256]{1,0:T(8,128)(2,1)} %gate_out.3.g0_ref, bf16[528,256]{1,0:T(8,128)(2,1)} %copy-done.36, bf16[528,256]{1,0:T(8,128)(2,1)} %copy-done.35, ...), custom_call_target="tpu_custom_call" | custom-call | flops 1000000000 | bytes 3000000 | tf_op jit(solution)/shard_map/out_blocks/pallas_call | solution.py:274
  74.8 1.2 collective-permute-start.23
  76.0 2.4 %collective-permute-start.24 = (bf16[144,512]{1,0:T(8,128)(2,1)}, bf16[144,512]{1,0:T(8,128)(2,1)S(1)}, u32[]{:S(2)}, u32[]{:S(2)}) collective-permute-start(bf16[144,512]{1,0:T(8,128)(2,1)} %get-tuple-element.38), channel_id=1, source_target_pairs={{0,8},{4,12},{8,0},{12,4},{1,9},{5,13},{9,1},{13,5},{2,10},{6,14},... | collective-permute-start | bytes 442376 | tf_op jit(solution)/shard_map/ppermute | solution.py:425
  78.5 1.2 collective-permute-start.25
  79.6 9.0 %mix_local.2 = (f32[512,256]{1,0:T(8,128)}, f32[512,256]{1,0:T(8,128)}, bf16[512,128]{1,0:T(8,128)(2,1)}, f32[512,8]{1,0:T(8,128)}, bf16[272,128]{1,0:T(8,128)(2,1)}) custom-call(bf16[2,512,2048]{2,1,0:T(8,128)(2,1)} %hid_ref.3, bf16[2,2048,512]{2,1,0:T(8,128)(2,1)} %reshape.29.wi_ref, bf16[2,2048,256]{2,1,0:T(8,128)(2,1)} %reshape.30.ws_ref, ...), custom_call_target="tpu_custom_call" | custom-call | flops 5000000000 | bytes 8000000 | tf_op jit(solution)/shard_map/mix_local/pallas_call | solution.py:159
  88.6 2.8 %collective-permute-start.3 = (bf16[272,128]{1,0:T(8,128)(2,1)}, bf16[272,128]{1,0:T(8,128)(2,1)S(1)}, u32[]{:S(2)}, u32[]{:S(2)}) collective-permute-start(bf16[272,128]{1,0:T(8,128)(2,1)} %get-tuple-element.26), channel_id=1, source_target_pairs={{0,64},{16,80},{32,96},{48,112},{1,65},{17,81},{33,97},{49,113},{2... | collective-permute-start | bytes 208904 | tf_op jit(solution)/shard_map/ppermute | solution.py:458
  91.4 2.5 %collective-permute-start.2 = (bf16[272,128]{1,0:T(8,128)(2,1)}, bf16[272,128]{1,0:T(8,128)(2,1)S(1)}, u32[]{:S(2)}, u32[]{:S(2)}) collective-permute-start(bf16[272,128]{1,0:T(8,128)(2,1)} %get-tuple-element.26), channel_id=1, source_target_pairs={{0,48},{16,64},{32,80},{48,96},{64,112},{1,49},{17,65},{33,81},{49... | collective-permute-start | bytes 208904 | tf_op jit(solution)/shard_map/ppermute | solution.py:458
  94.0 1.3 collective-permute-start.1
  95.3 2.5 %collective-permute-start = (bf16[272,128]{1,0:T(8,128)(2,1)}, bf16[272,128]{1,0:T(8,128)(2,1)S(1)}, u32[]{:S(2)}, u32[]{:S(2)}) collective-permute-start(bf16[272,128]{1,0:T(8,128)(2,1)} %get-tuple-element.26), channel_id=1, source_target_pairs={{0,16},{16,32},{32,48},{48,64},{64,80},{80,96},{96,112},{1,17},{17... | collective-permute-start | bytes 208904 | tf_op jit(solution)/shard_map/ppermute | solution.py:458
  97.8 0.6 copy-done.12
  98.5 2.8 %residual_block.3.u0_ref = bf16[144,512]{1,0:T(8,128)(2,1)} custom-call(s32[2]{0:T(128)} %pad_add_fusion.1.at_ref, bf16[144,512]{1,0:T(8,128)(2,1)} %get-tuple-element.36.o0_ref, bf16[144,512]{1,0:T(8,128)(2,1)} %copy-done.10, bf16[144,512]{1,0:T(8,128)(2,1)} %copy-done.11, bf16[144,512]{1,0:T(8,128)(2,1)} %copy-done.12, bf16[2,512,2048]{2,1,0:T(8,128)(2,1)} %hid_ref.3, ...), custom_call_target="tpu_custom_call" | custom-call | flops 1000000 | bytes 1000000 | tf_op jit(solution)/shard_map/residual_block/pallas_call | solution.py:302
  102.6 4.1 %gate_out.2.g0_ref = bf16[528,256]{1,0:T(8,128)(2,1)} custom-call(s32[4]{0:T(128)} %pages_ref.3, s32[4]{0:T(128)} %flags_ref.3, f32[512,256]{1,0:T(8,128)} %get-tuple-element.22.y_ref, f32[512,256]{1,0:T(8,128)} %get-tuple-element.23.gate_ref, bf16[512,128]{1,0:T(8,128)(2,1)} %get-tuple-element.24.c_ref, f32[512,8]{1,0:T(8,128)} %get-tuple-element.25.e_ref, ...), custom_call_target="tpu_custom_call" | custom-call | flops 1000000000 | bytes 4000000 | tf_op jit(solution)/shard_map/gate_out/pallas_call | solution.py:232
  106.7 2.1 collective-permute-start.5
  109.2 0.7 collective-permute-start.26
  109.9 5.1 %collective-permute-done.27.u2_ref = bf16[144,512]{1,0:T(8,128)(2,1)S(1)} collective-permute-done((bf16[144,512]{1,0:T(8,128)(2,1)S(1)}, bf16[144,512]{1,0:T(8,128)(2,1)S(1)}, u32[]{:S(2)}, u32[]{:S(2)}) %collective-permute-start.27) | collective-permute-done | bytes 147488 | tf_op jit(solution)/shard_map/ppermute | solution.py:425
  114.9 4.3 %collective-permute-done.26.u1_ref = bf16[144,512]{1,0:T(8,128)(2,1)S(1)} collective-permute-done((bf16[144,512]{1,0:T(8,128)(2,1)S(1)}, bf16[144,512]{1,0:T(8,128)(2,1)S(1)}, u32[]{:S(2)}, u32[]{:S(2)}) %collective-permute-start.26) | collective-permute-done | bytes 147488 | tf_op jit(solution)/shard_map/ppermute | solution.py:425
  119.2 0.6 copy-done.20
  119.9 2.0 join_columns.3.x0_ref
  121.9 2.6 %collective-permute-start.31 = (bf16[144,2048]{1,0:T(8,128)(2,1)}, bf16[144,2048]{1,0:T(8,128)(2,1)S(1)}, u32[]{:S(2)}, u32[]{:S(2)}) collective-permute-start(bf16[144,2048]{1,0:T(8,128)(2,1)} %join_columns.3.x0_ref), channel_id=1, source_target_pairs={{0,12},{4,0},{8,4},{12,8},{1,13},{5,1},{9,5},{13,9},{2,14},{6,2},{... | collective-permute-start | bytes 1769480 | tf_op jit(solution)/shard_map/ppermute | solution.py:425
  125.2 0.6 copy-done.31
  126.0 1.0 copy-done.2
  127.0 3.2 %out_blocks.2 = (bf16[144,512]{1,0:T(8,128)(2,1)}, bf16[144,512]{1,0:T(8,128)(2,1)}, bf16[144,512]{1,0:T(8,128)(2,1)}, bf16[144,512]{1,0:T(8,128)(2,1)}) custom-call(s32[2]{0:T(128)} %pad_add_fusion.at_ref, bf16[528,256]{1,0:T(8,128)(2,1)} %gate_out.2.g0_ref, bf16[528,256]{1,0:T(8,128)(2,1)} %copy-done.33, bf16[528,256]{1,0:T(8,128)(2,1)} %copy-done.32, ...), custom_call_target="tpu_custom_call" | custom-call | flops 1000000000 | bytes 3000000 | tf_op jit(solution)/shard_map/out_blocks/pallas_call | solution.py:274
  130.6 2.2 collective-permute-start.9
  133.1 6.6 %collective-permute-done.7.o1_ref = bf16[144,512]{1,0:T(8,128)(2,1)S(1)} collective-permute-done((bf16[144,512]{1,0:T(8,128)(2,1)}, bf16[144,512]{1,0:T(8,128)(2,1)S(1)}, u32[]{:S(2)}, u32[]{:S(2)}) %collective-permute-start.7) | collective-permute-done | bytes 147488 | tf_op jit(solution)/shard_map/ppermute | solution.py:425
  139.8 0.6 copy-done.13
  140.6 2.9 %residual_block.2.u0_ref = bf16[144,512]{1,0:T(8,128)(2,1)} custom-call(s32[2]{0:T(128)} %pad_add_fusion.at_ref, bf16[144,512]{1,0:T(8,128)(2,1)} %get-tuple-element.27.o0_ref, bf16[144,512]{1,0:T(8,128)(2,1)} %copy-done.13, bf16[144,512]{1,0:T(8,128)(2,1)} %copy-done.14, bf16[144,512]{1,0:T(8,128)(2,1)} %copy-done.15, bf16[2,512,2048]{2,1,0:T(8,128)(2,1)} %hid_ref.3, ...), custom_call_target="tpu_custom_call" | custom-call | flops 1000000 | bytes 1000000 | tf_op jit(solution)/shard_map/residual_block/pallas_call | solution.py:302
  143.4 2.6 %collective-permute-start.12 = (bf16[144,512]{1,0:T(8,128)(2,1)}, bf16[144,512]{1,0:T(8,128)(2,1)S(1)}, u32[]{:S(2)}, u32[]{:S(2)}) collective-permute-start(bf16[144,512]{1,0:T(8,128)(2,1)} %residual_block.2.u0_ref), channel_id=1, source_target_pairs={{0,12},{4,0},{8,4},{12,8},{1,13},{5,1},{9,5},{13,9},{2,14},{6,2},{... | collective-permute-start | bytes 442376 | tf_op jit(solution)/shard_map/ppermute | solution.py:425
  146.0 7.6 %collective-permute-done.12.u3_ref = bf16[144,512]{1,0:T(8,128)(2,1)S(1)} collective-permute-done((bf16[144,512]{1,0:T(8,128)(2,1)}, bf16[144,512]{1,0:T(8,128)(2,1)S(1)}, u32[]{:S(2)}, u32[]{:S(2)}) %collective-permute-start.12) | collective-permute-done | bytes 147488 | tf_op jit(solution)/shard_map/ppermute | solution.py:425
  153.6 2.7 %collective-permute-start.10 = (bf16[144,512]{1,0:T(8,128)(2,1)}, bf16[144,512]{1,0:T(8,128)(2,1)S(1)}, u32[]{:S(2)}, u32[]{:S(2)}) collective-permute-start(bf16[144,512]{1,0:T(8,128)(2,1)} %residual_block.2.u0_ref), channel_id=1, source_target_pairs={{0,4},{4,8},{8,12},{12,0},{1,5},{5,9},{9,13},{13,1},{2,6},{6,10},{... | collective-permute-start | bytes 442376 | tf_op jit(solution)/shard_map/ppermute | solution.py:425
  156.3 6.9 %collective-permute-done.11.u2_ref = bf16[144,512]{1,0:T(8,128)(2,1)S(1)} collective-permute-done((bf16[144,512]{1,0:T(8,128)(2,1)}, bf16[144,512]{1,0:T(8,128)(2,1)S(1)}, u32[]{:S(2)}, u32[]{:S(2)}) %collective-permute-start.11) | collective-permute-done | bytes 147488 | tf_op jit(solution)/shard_map/ppermute | solution.py:425
  163.2 5.3 %collective-permute-done.10.u1_ref = bf16[144,512]{1,0:T(8,128)(2,1)S(1)} collective-permute-done((bf16[144,512]{1,0:T(8,128)(2,1)}, bf16[144,512]{1,0:T(8,128)(2,1)S(1)}, u32[]{:S(2)}, u32[]{:S(2)}) %collective-permute-start.10) | collective-permute-done | bytes 147488 | tf_op jit(solution)/shard_map/ppermute | solution.py:425
  168.6 0.7 copy-done.21
  169.2 2.0 join_columns.2.x0_ref
  171.8 1.8 collective-permute-start.14
  173.6 0.8 collective-permute-start.13
  174.5 0.8 copy-done.5
  175.5 9.6 %head_stats.3 = f32[16,8,128]{2,1,0:T(8,128)} custom-call(s32[1]{0:T(128)} %bitcast.place_ref, s32[2]{0:T(128)} %pad_add_fusion.1.at_ref, bf16[144,2048]{1,0:T(8,128)(2,1)} %join_columns.3.x0_ref, bf16[144,2048]{1,0:T(8,128)(2,1)} %copy-done.6, bf16[144,2048]{1,0:T(8,128)(2,1)} %copy-done.5, bf16[144,2048]{1,0:T(8,128)(2,1)} %copy-done.4, ...), custom_call_target="tpu_custom_call" | custom-call | flops 3489660928 | bytes 6815744 | tf_op jit(solution)/shard_map/head_stats/pallas_call | solution.py:374
  185.1 3.7 %all-to-all-start.3 = ((f32[16,8,128]{2,1,0:T(8,128)}), f32[16,8,128]{2,1,0:T(8,128)S(1)}, u32[]{:S(2)}, u32[]{:S(2)}) async-start(f32[16,8,128]{2,1,0:T(8,128)} %head_stats.3), calls=%async_computation.3 | async-start | bytes 131072 | tf_op jit(solution)/shard_map/all_to_all | solution.py:465
  188.9 13.2 %collective-permute-done.13.x1_ref = bf16[144,2048]{1,0:T(8,128)(2,1)} collective-permute-done((bf16[144,2048]{1,0:T(8,128)(2,1)}, bf16[144,2048]{1,0:T(8,128)(2,1)}, u32[]{:S(2)}, u32[]{:S(2)}) %collective-permute-start.13) | collective-permute-done | bytes 589856 | tf_op jit(solution)/shard_map/ppermute | solution.py:425
  202.1 9.6 %head_stats.2 = f32[16,8,128]{2,1,0:T(8,128)} custom-call(s32[1]{0:T(128)} %bitcast.place_ref, s32[2]{0:T(128)} %pad_add_fusion.at_ref, bf16[144,2048]{1,0:T(8,128)(2,1)} %join_columns.2.x0_ref, bf16[144,2048]{1,0:T(8,128)(2,1)} %collective-permute-done.13.x1_ref, bf16[144,2048]{1,0:T(8,128)(2,1)} %collective-permute-done.14.x2_ref, ...), custom_call_target="tpu_custom_call" | custom-call | flops 3489660928 | bytes 6815744 | tf_op jit(solution)/shard_map/head_stats/pallas_call | solution.py:374
  211.7 10.6 %all_to_all.25.s0_ref = f32[16,8,128]{2,1,0:T(8,128)} all-to-all(f32[16,8,128]{2,1,0:T(8,128)} %head_stats.2), channel_id=1, replica_groups=mesh['y'=4,'core'=2,'x'=4,'z'=4] {'x','z'}, dimensions={0} | all-to-all | bytes 131072 | tf_op jit(solution)/shard_map/all_to_all | solution.py:465
  222.4 1.6 token_diffs.1
  224.0 4.9 %all-to-all-start.4 = ((f32[8,8,128]{2,1,0:T(8,128)}), f32[8,8,128]{2,1,0:T(8,128)S(1)}, u32[]{:S(2)}, u32[]{:S(2)}) async-start(f32[8,8,128]{2,1,0:T(8,128)} %get-tuple-element.41), calls=%async_computation.4 | async-start | bytes 65536 | tf_op jit(solution)/shard_map/all_to_all | solution.py:467
  228.9 4.7 %all-to-all-done.4 = f32[8,8,128]{2,1,0:T(8,128)S(1)} async-done(((f32[8,8,128]{2,1,0:T(8,128)}), f32[8,8,128]{2,1,0:T(8,128)S(1)}, u32[]{:S(2)}, u32[]{:S(2)}) %all-to-all-start.4) | async-done | bytes 32800 | tf_op jit(solution)/shard_map/all_to_all | solution.py:467
  (105 shorter events, 6.0 us)
Async XLA Ops:
  9.0 6.0 %copy-start.1 = (bf16[2,2048,2,128]{3,2,1,0:T(2,128)(2,1)S(1)}, bf16[2,2048,2,128]{3,2,1,0:T(2,128)(2,1)}, u32[]{:S(2)}) copy-start(bf16[2,2048,2,128]{3,2,1,0:T(2,128)(2,1)} %param.20) | copy-start | bytes 6291460
  9.0 47.8 %all-to-all-start.2 = ((bf16[4,256,512]{2,1,0:T(8,128)(2,1)}), bf16[4,256,512]{2,1,0:T(8,128)(2,1)S(1)}, u32[]{:S(2)}, u32[]{:S(2)}) async-start(bf16[4,256,512]{2,1,0:T(8,128)(2,1)} %get-tuple-element.42), calls=%async_computation.2 | async-start | bytes 2097152 | tf_op jit(solution)/shard_map/all_to_all | solution.py:449
  34.2 11.5 %collective-permute-start.19 = (bf16[272,128]{1,0:T(8,128)(2,1)}, bf16[272,128]{1,0:T(8,128)(2,1)S(1)}, u32[]{:S(2)}, u32[]{:S(2)}) collective-permute-start(bf16[272,128]{1,0:T(8,128)(2,1)} %get-tuple-element.35), channel_id=1, source_target_pairs={{0,64},{16,80},{32,96},{48,112},{1,65},{17,81},{33,97},{49,113},{2... | collective-permute-start | bytes 208904 | tf_op jit(solution)/shard_map/ppermute | solution.py:458
  39.0 6.7 %collective-permute-start.18 = (bf16[272,128]{1,0:T(8,128)(2,1)}, bf16[272,128]{1,0:T(8,128)(2,1)S(1)}, u32[]{:S(2)}, u32[]{:S(2)}) collective-permute-start(bf16[272,128]{1,0:T(8,128)(2,1)} %get-tuple-element.35), channel_id=1, source_target_pairs={{0,48},{16,64},{32,80},{48,96},{64,112},{1,49},{17,65},{33,81},{49... | collective-permute-start | bytes 208904 | tf_op jit(solution)/shard_map/ppermute | solution.py:458
  41.1 4.6 %collective-permute-start.17 = (bf16[272,128]{1,0:T(8,128)(2,1)}, bf16[272,128]{1,0:T(8,128)(2,1)S(1)}, u32[]{:S(2)}, u32[]{:S(2)}) collective-permute-start(bf16[272,128]{1,0:T(8,128)(2,1)} %get-tuple-element.35), channel_id=1, source_target_pairs={{0,32},{16,48},{32,64},{48,80},{64,96},{80,112},{1,33},{17,49},{33... | collective-permute-start | bytes 208904 | tf_op jit(solution)/shard_map/ppermute | solution.py:458
  43.5 3.9 %collective-permute-start.16 = (bf16[272,128]{1,0:T(8,128)(2,1)}, bf16[272,128]{1,0:T(8,128)(2,1)S(1)}, u32[]{:S(2)}, u32[]{:S(2)}) collective-permute-start(bf16[272,128]{1,0:T(8,128)(2,1)} %get-tuple-element.35), channel_id=1, source_target_pairs={{0,16},{16,32},{32,48},{48,64},{64,80},{80,96},{96,112},{1,17},{17... | collective-permute-start | bytes 208904 | tf_op jit(solution)/shard_map/ppermute | solution.py:458
  45.7 1.7 copy-start.26
  45.7 1.6 copy-start.27
  45.7 1.6 copy-start.28
  52.0 15.3 %collective-permute-start.22 = (bf16[528,256]{1,0:T(8,128)(2,1)}, bf16[528,256]{1,0:T(8,128)(2,1)S(1)}, u32[]{:S(2)}, u32[]{:S(2)}) collective-permute-start(bf16[528,256]{1,0:T(8,128)(2,1)} %gate_out.3.g0_ref), channel_id=1, source_target_pairs={{0,3},{1,0},{2,1},{3,2},{4,7},{5,4},{6,5},{7,6},{8,11},{9,8},{10,9... | collective-permute-start | bytes 811016 | tf_op jit(solution)/shard_map/ppermute | solution.py:425
  54.9 12.3 %collective-permute-start.21 = (bf16[528,256]{1,0:T(8,128)(2,1)}, bf16[528,256]{1,0:T(8,128)(2,1)S(1)}, u32[]{:S(2)}, u32[]{:S(2)}) collective-permute-start(bf16[528,256]{1,0:T(8,128)(2,1)} %gate_out.3.g0_ref), channel_id=1, source_target_pairs={{0,2},{1,3},{2,0},{3,1},{4,6},{5,7},{6,4},{7,5},{8,10},{9,11},{10,... | collective-permute-start | bytes 811016 | tf_op jit(solution)/shard_map/ppermute | solution.py:425
  55.5 15.4 %collective-permute-start.20 = (bf16[528,256]{1,0:T(8,128)(2,1)}, bf16[528,256]{1,0:T(8,128)(2,1)S(1)}, u32[]{:S(2)}, u32[]{:S(2)}) collective-permute-start(bf16[528,256]{1,0:T(8,128)(2,1)} %gate_out.3.g0_ref), channel_id=1, source_target_pairs={{0,1},{1,2},{2,3},{3,0},{4,5},{5,6},{6,7},{7,4},{8,9},{9,10},{10,1... | collective-permute-start | bytes 811016 | tf_op jit(solution)/shard_map/ppermute | solution.py:425
  56.8 14.1 %copy-start.3 = (bf16[4,256,512]{2,1,0:T(8,128)(2,1)}, bf16[4,256,512]{2,1,0:T(8,128)(2,1)S(1)}, u32[]{:S(2)}) copy-start(bf16[4,256,512]{2,1,0:T(8,128)(2,1)S(1)} %all-to-all-done.2.w_ref) | copy-start | bytes 3145732
  56.8 68.4 %all-to-all-start = ((bf16[4,256,512]{2,1,0:T(8,128)(2,1)}), bf16[4,256,512]{2,1,0:T(8,128)(2,1)S(1)}, u32[]{:S(2)}, u32[]{:S(2)}) async-start(bf16[4,256,512]{2,1,0:T(8,128)(2,1)} %get-tuple-element.43), calls=%async_computation | async-start | bytes 2097152 | tf_op jit(solution)/shard_map/all_to_all | solution.py:449
  67.2 3.6 %copy-start.34 = (bf16[528,256]{1,0:T(8,128)(2,1)}, bf16[528,256]{1,0:T(8,128)(2,1)S(1)}, u32[]{:S(2)}) copy-start(bf16[528,256]{1,0:T(8,128)(2,1)S(1)} %collective-permute-done.22.g3_ref) | copy-start | bytes 811012
  67.2 3.6 %copy-start.35 = (bf16[528,256]{1,0:T(8,128)(2,1)}, bf16[528,256]{1,0:T(8,128)(2,1)S(1)}, u32[]{:S(2)}) copy-start(bf16[528,256]{1,0:T(8,128)(2,1)S(1)} %collective-permute-done.21.g2_ref) | copy-start | bytes 811012
  70.9 0.7 copy-start.36
  74.8 19.2 %collective-permute-start.23 = (bf16[144,512]{1,0:T(8,128)(2,1)}, bf16[144,512]{1,0:T(8,128)(2,1)S(1)}, u32[]{:S(2)}, u32[]{:S(2)}) collective-permute-start(bf16[144,512]{1,0:T(8,128)(2,1)} %get-tuple-element.37), channel_id=1, source_target_pairs={{0,4},{4,8},{8,12},{12,0},{1,5},{5,9},{9,13},{13,1},{2,6},{6,10},{... | collective-permute-start | bytes 442376 | tf_op jit(solution)/shard_map/ppermute | solution.py:425
  76.0 19.3 %collective-permute-start.24 = (bf16[144,512]{1,0:T(8,128)(2,1)}, bf16[144,512]{1,0:T(8,128)(2,1)S(1)}, u32[]{:S(2)}, u32[]{:S(2)}) collective-permute-start(bf16[144,512]{1,0:T(8,128)(2,1)} %get-tuple-element.38), channel_id=1, source_target_pairs={{0,8},{4,12},{8,0},{12,4},{1,9},{5,13},{9,1},{13,5},{2,10},{6,14},... | collective-permute-start | bytes 442376 | tf_op jit(solution)/shard_map/ppermute | solution.py:425
  78.5 19.3 %collective-permute-start.25 = (bf16[144,512]{1,0:T(8,128)(2,1)}, bf16[144,512]{1,0:T(8,128)(2,1)S(1)}, u32[]{:S(2)}, u32[]{:S(2)}) collective-permute-start(bf16[144,512]{1,0:T(8,128)(2,1)} %get-tuple-element.39), channel_id=1, source_target_pairs={{0,12},{4,0},{8,4},{12,8},{1,13},{5,1},{9,5},{13,9},{2,14},{6,2},{... | collective-permute-start | bytes 442376 | tf_op jit(solution)/shard_map/ppermute | solution.py:425
  88.6 13.2 %collective-permute-start.3 = (bf16[272,128]{1,0:T(8,128)(2,1)}, bf16[272,128]{1,0:T(8,128)(2,1)S(1)}, u32[]{:S(2)}, u32[]{:S(2)}) collective-permute-start(bf16[272,128]{1,0:T(8,128)(2,1)} %get-tuple-element.26), channel_id=1, source_target_pairs={{0,64},{16,80},{32,96},{48,112},{1,65},{17,81},{33,97},{49,113},{2... | collective-permute-start | bytes 208904 | tf_op jit(solution)/shard_map/ppermute | solution.py:458
  91.4 10.4 %collective-permute-start.2 = (bf16[272,128]{1,0:T(8,128)(2,1)}, bf16[272,128]{1,0:T(8,128)(2,1)S(1)}, u32[]{:S(2)}, u32[]{:S(2)}) collective-permute-start(bf16[272,128]{1,0:T(8,128)(2,1)} %get-tuple-element.26), channel_id=1, source_target_pairs={{0,48},{16,64},{32,80},{48,96},{64,112},{1,49},{17,65},{33,81},{49... | collective-permute-start | bytes 208904 | tf_op jit(solution)/shard_map/ppermute | solution.py:458
  94.0 3.9 %copy-start.10 = (bf16[144,512]{1,0:T(8,128)(2,1)}, bf16[144,512]{1,0:T(8,128)(2,1)S(1)}, u32[]{:S(2)}) copy-start(bf16[144,512]{1,0:T(8,128)(2,1)S(1)} %collective-permute-done.23.o1_ref) | copy-start | bytes 442372
  94.0 7.9 %collective-permute-start.1 = (bf16[272,128]{1,0:T(8,128)(2,1)}, bf16[272,128]{1,0:T(8,128)(2,1)S(1)}, u32[]{:S(2)}, u32[]{:S(2)}) collective-permute-start(bf16[272,128]{1,0:T(8,128)(2,1)} %get-tuple-element.26), channel_id=1, source_target_pairs={{0,32},{16,48},{32,64},{48,80},{64,96},{80,112},{1,33},{17,49},{33... | collective-permute-start | bytes 208904 | tf_op jit(solution)/shard_map/ppermute | solution.py:458
  95.3 2.5 %copy-start.11 = (bf16[144,512]{1,0:T(8,128)(2,1)}, bf16[144,512]{1,0:T(8,128)(2,1)S(1)}, u32[]{:S(2)}) copy-start(bf16[144,512]{1,0:T(8,128)(2,1)S(1)} %collective-permute-done.24.o2_ref) | copy-start | bytes 442372
  95.3 6.6 %collective-permute-start = (bf16[272,128]{1,0:T(8,128)(2,1)}, bf16[272,128]{1,0:T(8,128)(2,1)S(1)}, u32[]{:S(2)}, u32[]{:S(2)}) collective-permute-start(bf16[272,128]{1,0:T(8,128)(2,1)} %get-tuple-element.26), channel_id=1, source_target_pairs={{0,16},{16,32},{32,48},{48,64},{64,80},{80,96},{96,112},{1,17},{17... | collective-permute-start | bytes 208904 | tf_op jit(solution)/shard_map/ppermute | solution.py:458
  101.3 7.9 %collective-permute-start.28 = (bf16[144,512]{1,0:T(8,128)(2,1)}, bf16[144,512]{1,0:T(8,128)(2,1)S(1)}, u32[]{:S(2)}, u32[]{:S(2)}) collective-permute-start(bf16[144,512]{1,0:T(8,128)(2,1)} %residual_block.3.u0_ref), channel_id=1, source_target_pairs={{0,3},{1,0},{2,1},{3,2},{4,7},{5,4},{6,5},{7,6},{8,11},{9,8},{10,9... | collective-permute-start | bytes 442376 | tf_op jit(solution)/shard_map/ppermute | solution.py:425
  102.5 6.3 %copy-start.8 = (bf16[144,512]{1,0:T(8,128)(2,1)S(1)}, bf16[144,512]{1,0:T(8,128)(2,1)}, u32[]{:S(2)}) copy-start(bf16[144,512]{1,0:T(8,128)(2,1)} %residual_block.3.u0_ref) | copy-start | bytes 442372
  106.7 18.4 %collective-permute-start.6 = (bf16[528,256]{1,0:T(8,128)(2,1)}, bf16[528,256]{1,0:T(8,128)(2,1)S(1)}, u32[]{:S(2)}, u32[]{:S(2)}) collective-permute-start(bf16[528,256]{1,0:T(8,128)(2,1)} %gate_out.2.g0_ref), channel_id=1, source_target_pairs={{0,12},{4,0},{8,4},{12,8},{1,13},{5,1},{9,5},{13,9},{2,14},{6,2},{... | collective-permute-start | bytes 811016 | tf_op jit(solution)/shard_map/ppermute | solution.py:425
  106.7 18.4 %collective-permute-start.5 = (bf16[528,256]{1,0:T(8,128)(2,1)}, bf16[528,256]{1,0:T(8,128)(2,1)S(1)}, u32[]{:S(2)}, u32[]{:S(2)}) collective-permute-start(bf16[528,256]{1,0:T(8,128)(2,1)} %gate_out.2.g0_ref), channel_id=1, source_target_pairs={{0,8},{4,12},{8,0},{12,4},{1,9},{5,13},{9,1},{13,5},{2,10},{6,14},... | collective-permute-start | bytes 811016 | tf_op jit(solution)/shard_map/ppermute | solution.py:425
  108.8 16.3 %collective-permute-start.4 = (bf16[528,256]{1,0:T(8,128)(2,1)}, bf16[528,256]{1,0:T(8,128)(2,1)S(1)}, u32[]{:S(2)}, u32[]{:S(2)}) collective-permute-start(bf16[528,256]{1,0:T(8,128)(2,1)} %gate_out.2.g0_ref), channel_id=1, source_target_pairs={{0,4},{4,8},{8,12},{12,0},{1,5},{5,9},{9,13},{13,1},{2,6},{6,10},{... | collective-permute-start | bytes 811016 | tf_op jit(solution)/shard_map/ppermute | solution.py:425
  108.8 6.1 %collective-permute-start.27 = (bf16[144,512]{1,0:T(8,128)(2,1)S(1)}, bf16[144,512]{1,0:T(8,128)(2,1)S(1)}, u32[]{:S(2)}, u32[]{:S(2)}) collective-permute-start(bf16[144,512]{1,0:T(8,128)(2,1)S(1)} %copy-done.8), channel_id=1, source_target_pairs={{0,2},{1,3},{2,0},{3,1},{4,6},{5,7},{6,4},{7,5},{8,10},{9,11},{10,... | collective-permute-start | bytes 442376 | tf_op jit(solution)/shard_map/ppermute | solution.py:425
  109.2 10.0 %copy-start.16 = (bf16[144,512]{1,0:T(8,128)(2,1)}, bf16[144,512]{1,0:T(8,128)(2,1)S(1)}, u32[]{:S(2)}) copy-start(bf16[144,512]{1,0:T(8,128)(2,1)S(1)} %collective-permute-done.28.u3_ref) | copy-start | bytes 442372
  109.2 10.0 %collective-permute-start.26 = (bf16[144,512]{1,0:T(8,128)(2,1)S(1)}, bf16[144,512]{1,0:T(8,128)(2,1)S(1)}, u32[]{:S(2)}, u32[]{:S(2)}) collective-permute-start(bf16[144,512]{1,0:T(8,128)(2,1)S(1)} %copy-done.8), channel_id=1, source_target_pairs={{0,1},{1,2},{2,3},{3,0},{4,5},{5,6},{6,7},{7,4},{8,9},{9,10},{10,1... | collective-permute-start | bytes 442376 | tf_op jit(solution)/shard_map/ppermute | solution.py:425
  114.9 4.3 %copy-start.18 = (bf16[144,512]{1,0:T(8,128)(2,1)}, bf16[144,512]{1,0:T(8,128)(2,1)S(1)}, u32[]{:S(2)}) copy-start(bf16[144,512]{1,0:T(8,128)(2,1)S(1)} %collective-permute-done.27.u2_ref) | copy-start | bytes 442372
  121.9 10.9 %copy-start = (bf16[144,2048]{1,0:T(8,128)(2,1)S(1)}, bf16[144,2048]{1,0:T(8,128)(2,1)}, u32[]{:S(2)}) copy-start(bf16[144,2048]{1,0:T(8,128)(2,1)} %join_columns.3.x0_ref) | copy-start | bytes 1769476
  121.9 51.7 %collective-permute-start.31 = (bf16[144,2048]{1,0:T(8,128)(2,1)}, bf16[144,2048]{1,0:T(8,128)(2,1)S(1)}, u32[]{:S(2)}, u32[]{:S(2)}) collective-permute-start(bf16[144,2048]{1,0:T(8,128)(2,1)} %join_columns.3.x0_ref), channel_id=1, source_target_pairs={{0,12},{4,0},{8,4},{12,8},{1,13},{5,1},{9,5},{13,9},{2,14},{6,2},{... | collective-permute-start | bytes 1769480 | tf_op jit(solution)/shard_map/ppermute | solution.py:425
  125.1 0.7 copy-start.31
  125.1 0.8 copy-start.32
  125.1 0.8 copy-start.33
  126.0 1.0 copy-start.2
  130.1 9.6 %collective-permute-start.7 = (bf16[144,512]{1,0:T(8,128)(2,1)}, bf16[144,512]{1,0:T(8,128)(2,1)S(1)}, u32[]{:S(2)}, u32[]{:S(2)}) collective-permute-start(bf16[144,512]{1,0:T(8,128)(2,1)} %get-tuple-element.28), channel_id=1, source_target_pairs={{0,1},{1,2},{2,3},{3,0},{4,5},{5,6},{6,7},{7,4},{8,9},{9,10},{10,1... | collective-permute-start | bytes 442376 | tf_op jit(solution)/shard_map/ppermute | solution.py:425
  130.2 9.6 %collective-permute-start.8 = (bf16[144,512]{1,0:T(8,128)(2,1)}, bf16[144,512]{1,0:T(8,128)(2,1)S(1)}, u32[]{:S(2)}, u32[]{:S(2)}) collective-permute-start(bf16[144,512]{1,0:T(8,128)(2,1)} %get-tuple-element.29), channel_id=1, source_target_pairs={{0,2},{1,3},{2,0},{3,1},{4,6},{5,7},{6,4},{7,5},{8,10},{9,11},{10,... | collective-permute-start | bytes 442376 | tf_op jit(solution)/shard_map/ppermute | solution.py:425
  130.6 9.2 %collective-permute-start.9 = (bf16[144,512]{1,0:T(8,128)(2,1)}, bf16[144,512]{1,0:T(8,128)(2,1)S(1)}, u32[]{:S(2)}, u32[]{:S(2)}) collective-permute-start(bf16[144,512]{1,0:T(8,128)(2,1)} %get-tuple-element.30), channel_id=1, source_target_pairs={{0,3},{1,0},{2,1},{3,2},{4,7},{5,4},{6,5},{7,6},{8,11},{9,8},{10,9... | collective-permute-start | bytes 442376 | tf_op jit(solution)/shard_map/ppermute | solution.py:425
  132.8 41.6 %collective-permute-start.30 = (bf16[144,2048]{1,0:T(8,128)(2,1)S(1)}, bf16[144,2048]{1,0:T(8,128)(2,1)S(1)}, u32[]{:S(2)}, u32[]{:S(2)}) collective-permute-start(bf16[144,2048]{1,0:T(8,128)(2,1)S(1)} %copy-done), channel_id=1, source_target_pairs={{0,8},{4,12},{8,0},{12,4},{1,9},{5,13},{9,1},{13,5},{2,10},{6,14},... | collective-permute-start | bytes 1769480 | tf_op jit(solution)/shard_map/ppermute | solution.py:425
  139.8 34.7 %collective-permute-start.29 = (bf16[144,2048]{1,0:T(8,128)(2,1)S(1)}, bf16[144,2048]{1,0:T(8,128)(2,1)S(1)}, u32[]{:S(2)}, u32[]{:S(2)}) collective-permute-start(bf16[144,2048]{1,0:T(8,128)(2,1)S(1)} %copy-done), channel_id=1, source_target_pairs={{0,4},{4,8},{8,12},{12,0},{1,5},{5,9},{9,13},{13,1},{2,6},{6,10},{... | collective-permute-start | bytes 1769480 | tf_op jit(solution)/shard_map/ppermute | solution.py:425
  139.8 0.7 copy-start.14
  139.8 0.8 copy-start.15
  143.4 10.1 %collective-permute-start.12 = (bf16[144,512]{1,0:T(8,128)(2,1)}, bf16[144,512]{1,0:T(8,128)(2,1)S(1)}, u32[]{:S(2)}, u32[]{:S(2)}) collective-permute-start(bf16[144,512]{1,0:T(8,128)(2,1)} %residual_block.2.u0_ref), channel_id=1, source_target_pairs={{0,12},{4,0},{8,4},{12,8},{1,13},{5,1},{9,5},{13,9},{2,14},{6,2},{... | collective-permute-start | bytes 442376 | tf_op jit(solution)/shard_map/ppermute | solution.py:425
  146.0 17.2 %collective-permute-start.11 = (bf16[144,512]{1,0:T(8,128)(2,1)}, bf16[144,512]{1,0:T(8,128)(2,1)S(1)}, u32[]{:S(2)}, u32[]{:S(2)}) collective-permute-start(bf16[144,512]{1,0:T(8,128)(2,1)} %residual_block.2.u0_ref), channel_id=1, source_target_pairs={{0,8},{4,12},{8,0},{12,4},{1,9},{5,13},{9,1},{13,5},{2,10},{6,14},... | collective-permute-start | bytes 442376 | tf_op jit(solution)/shard_map/ppermute | solution.py:425
  153.6 15.0 %copy-start.17 = (bf16[144,512]{1,0:T(8,128)(2,1)}, bf16[144,512]{1,0:T(8,128)(2,1)S(1)}, u32[]{:S(2)}) copy-start(bf16[144,512]{1,0:T(8,128)(2,1)S(1)} %collective-permute-done.12.u3_ref) | copy-start | bytes 442372
  153.6 15.0 %collective-permute-start.10 = (bf16[144,512]{1,0:T(8,128)(2,1)}, bf16[144,512]{1,0:T(8,128)(2,1)S(1)}, u32[]{:S(2)}, u32[]{:S(2)}) collective-permute-start(bf16[144,512]{1,0:T(8,128)(2,1)} %residual_block.2.u0_ref), channel_id=1, source_target_pairs={{0,4},{4,8},{8,12},{12,0},{1,5},{5,9},{9,13},{13,1},{2,6},{6,10},{... | collective-permute-start | bytes 442376 | tf_op jit(solution)/shard_map/ppermute | solution.py:425
  163.2 5.3 %copy-start.19 = (bf16[144,512]{1,0:T(8,128)(2,1)}, bf16[144,512]{1,0:T(8,128)(2,1)S(1)}, u32[]{:S(2)}) copy-start(bf16[144,512]{1,0:T(8,128)(2,1)S(1)} %collective-permute-done.11.u2_ref) | copy-start | bytes 442372
  171.3 17.6 %collective-permute-start.15 = (bf16[144,2048]{1,0:T(8,128)(2,1)}, bf16[144,2048]{1,0:T(8,128)(2,1)S(1)}, u32[]{:S(2)}, u32[]{:S(2)}) collective-permute-start(bf16[144,2048]{1,0:T(8,128)(2,1)} %join_columns.2.x0_ref), channel_id=1, source_target_pairs={{0,3},{1,0},{2,1},{3,2},{4,7},{5,4},{6,5},{7,6},{8,11},{9,8},{10,9... | collective-permute-start | bytes 1769480 | tf_op jit(solution)/shard_map/ppermute | solution.py:425
  171.8 17.0 %collective-permute-start.14 = (bf16[144,2048]{1,0:T(8,128)(2,1)}, bf16[144,2048]{1,0:T(8,128)(2,1)}, u32[]{:S(2)}, u32[]{:S(2)}) collective-permute-start(bf16[144,2048]{1,0:T(8,128)(2,1)} %join_columns.2.x0_ref), channel_id=1, source_target_pairs={{0,2},{1,3},{2,0},{3,1},{4,6},{5,7},{6,4},{7,5},{8,10},{9,11},{10,... | collective-permute-start | bytes 1769480 | tf_op jit(solution)/shard_map/ppermute | solution.py:425
  173.6 0.9 copy-start.4
  173.6 28.5 %collective-permute-start.13 = (bf16[144,2048]{1,0:T(8,128)(2,1)}, bf16[144,2048]{1,0:T(8,128)(2,1)}, u32[]{:S(2)}, u32[]{:S(2)}) collective-permute-start(bf16[144,2048]{1,0:T(8,128)(2,1)} %join_columns.2.x0_ref), channel_id=1, source_target_pairs={{0,1},{1,2},{2,3},{3,0},{4,5},{5,6},{6,7},{7,4},{8,9},{9,10},{10,1... | collective-permute-start | bytes 1769480 | tf_op jit(solution)/shard_map/ppermute | solution.py:425
  174.5 0.8 copy-start.5
  174.5 1.1 copy-start.6
  185.1 26.6 %all-to-all-start.3 = ((f32[16,8,128]{2,1,0:T(8,128)}), f32[16,8,128]{2,1,0:T(8,128)S(1)}, u32[]{:S(2)}, u32[]{:S(2)}) async-start(f32[16,8,128]{2,1,0:T(8,128)} %head_stats.3), calls=%async_computation.3 | async-start | bytes 131072 | tf_op jit(solution)/shard_map/all_to_all | solution.py:465
  188.8 45.0 %copy-start.30 = (s32[4]{0:T(128)S(1)}, s32[4]{0:T(128)}, u32[]{:S(2)}) copy-start(s32[4]{0:T(128)} %param.35) | copy-start | bytes 52
  188.9 13.3 %copy-start.7 = (bf16[144,2048]{1,0:T(8,128)(2,1)}, bf16[144,2048]{1,0:T(8,128)(2,1)S(1)}, u32[]{:S(2)}) copy-start(bf16[144,2048]{1,0:T(8,128)(2,1)S(1)} %collective-permute-done.15.x3_ref) | copy-start | bytes 1769476
  211.7 10.6 %copy-start.9 = (f32[16,8,128]{2,1,0:T(8,128)}, f32[16,8,128]{2,1,0:T(8,128)S(1)}, u32[]{:S(2)}) copy-start(f32[16,8,128]{2,1,0:T(8,128)S(1)} %all-to-all-done.3.s1_ref) | copy-start | bytes 196612
  224.0 9.7 %all-to-all-start.4 = ((f32[8,8,128]{2,1,0:T(8,128)}), f32[8,8,128]{2,1,0:T(8,128)S(1)}, u32[]{:S(2)}, u32[]{:S(2)}) async-start(f32[8,8,128]{2,1,0:T(8,128)} %get-tuple-element.41), calls=%async_computation.4 | async-start | bytes 65536 | tf_op jit(solution)/shard_map/all_to_all | solution.py:467
  (9 other events, 5.8 us)

commit v4 on v3

--- a/solution.py
+++ b/solution.py
@@ -26,6 +26,16 @@
     return lax.dot_general(a, b, (dims, ((), ())), preferred_element_type=F32)
 
 
+def drop(kernel, inputs, count):
+    def body(*refs):
+        return kernel(*refs[:inputs], *refs[inputs + count :])
+
+    return body
+
+
+ANYWHERE = pl.BlockSpec(memory_space=pl.ANY)
+
+
 def pieces(value):
     high = value.astype(BF16).astype(F32)
     mid = (value - high).astype(BF16).astype(F32)
@@ -62,9 +72,11 @@
         stp_ref[...] = jnp.zeros_like(stp_ref)
 
     tokens = tok_ref[...]
-    gate_ref[...] += contract(tokens, wi_ref[:, 0:inner], ((1,), (0,)))
-    val_ref[...] += contract(tokens, wi_ref[:, inner:], ((1,), (0,)))
-    st_ref[...] += contract(tokens, ws_ref[...], ((1,), (0,)))
+    gate_ref[...] += contract(tokens, wi_ref[:, 0, :], ((1,), (0,)))
+    val_ref[...] += contract(tokens, wi_ref[:, 1, :], ((1,), (0,)))
+    state = c_ref.shape[1]
+    st_ref[:, 0:state] += contract(tokens, ws_ref[:, 0, :], ((1,), (0,)))
+    st_ref[:, state:] += contract(tokens, ws_ref[:, 1, :], ((1,), (0,)))
     stp_ref[...] += contract(tokens, wp_ref[...], ((1,), (1,)))
 
     @pl.when(k == pl.num_programs(0) - 1)
@@ -146,10 +158,10 @@
         y_ref[t0 : t0 + SPAN, :] = jnp.concatenate(acc, axis=1)
 
 
-def mix_local(m, hidden, w_inner, w_state, w_step, bias, rate, skip, seg, chunks=4):
+def mix_local(m, hidden, w_inner, w_state, w_step, bias, rate, skip, seg, after=(), chunks=4):
     rows, depth = hidden.shape[1:]
-    inner = w_inner.shape[2] // 2
-    state = w_state.shape[2] // 2
+    inner = w_inner.shape[3]
+    state = w_state.shape[3]
     heads = bias.shape[1]
     deep = depth // chunks
     whole = lambda a: pl.BlockSpec(a.shape, lambda k: (0,) * a.ndim)
@@ -157,15 +169,16 @@
     shapes = ((rows, inner), F32), ((rows, inner), F32), ((rows, state), BF16), ((rows, 2 * heads), F32), (
         (inner + 16, state), BF16)
     return pl.pallas_call(
-        functools.partial(mix_kernel, m),
+        drop(functools.partial(mix_kernel, m), 8, len(after)),
         grid=(chunks,),
         in_specs=[
             pl.BlockSpec((None, rows, deep), lambda k: (m, 0, k)),
-            pl.BlockSpec((None, deep, 2 * inner), lambda k: (m, k, 0)),
-            pl.BlockSpec((None, deep, 2 * state), lambda k: (m, k, 0)),
+            pl.BlockSpec((None, deep, 2, inner), lambda k: (m, k, 0, 0)),
+            pl.BlockSpec((None, deep, 2, state), lambda k: (m, k, 0, 0)),
             pl.BlockSpec((None, heads, deep), lambda k: (m, 0, k)),
             whole(bias), whole(rate), whole(skip), whole(seg),
-        ],
+        ]
+        + [ANYWHERE] * len(after),
         out_specs=[const(shape) for shape, _ in shapes],
         out_shape=[jax.ShapeDtypeStruct(shape, kind) for shape, kind in shapes],
         scratch_shapes=[
@@ -173,7 +186,7 @@
         ],
         cost_estimate=pl.CostEstimate(flops=5 * 10**9, bytes_accessed=8 * 10**6, transcendentals=10**6),
         name="mix_local",
-    )(hidden, w_inner, w_state, w_step, bias, rate, skip, seg)
+    )(hidden, w_inner, w_state, w_step, bias, rate, skip, seg, *after)
 
 
 def gate_kernel(
@@ -221,7 +234,7 @@
     out_ref[rows : rows + 16, :] = extra.astype(BF16)
 
 
-def gate_out(m, pages, flags, y, gate, c, e, recv, pool, gain):
+def gate_out(m, pages, flags, y, gate, c, e, recv, pool, gain, after=()):
     rows, inner = y.shape
     heads = pool.shape[2]
     state = c.shape[1]
@@ -230,20 +243,21 @@
         (None, None, heads, pool.shape[3], state), lambda g, pg, fl: (m, pg[j], 0, 0, 0)
     )
     return pl.pallas_call(
-        functools.partial(gate_kernel, m),
+        drop(functools.partial(gate_kernel, m), 15, len(after)),
         grid_spec=pltpu.PrefetchScalarGridSpec(
             num_scalar_prefetch=2,
             grid=(1,),
             in_specs=[whole(y), whole(gate), whole(c), whole(e)]
             + [whole(r) for r in recv]
             + [page(j) for j in range(4)]
-            + [whole(gain)],
+            + [whole(gain)]
+            + [ANYWHERE] * len(after),
             out_specs=pl.BlockSpec((rows + 16, inner), lambda g, pg, fl: (0, 0)),
         ),
         out_shape=jax.ShapeDtypeStruct((rows + 16, inner), BF16),
         cost_estimate=pl.CostEstimate(flops=10**9, bytes_accessed=4 * 10**6, transcendentals=10**5),
         name="gate_out",
-    )(pages, flags, y, gate, c, e, *recv, pool, pool, pool, pool, gain)
+    )(pages, flags, y, gate, c, e, *recv, pool, pool, pool, pool, gain, *after)
 
 
 def out_kernel(at_ref, g0_ref, g1_ref, g2_ref, g3_ref, w_ref, o0_ref, o1_ref, o2_ref, o3_ref, acc_ref, sq_ref):
@@ -266,20 +280,20 @@
         out[block : block + 16, :] = jnp.broadcast_to(line, (16, width)).astype(BF16)
 
 
-def out_blocks(at, gathered, w):
+def out_blocks(at, gathered, w, after=()):
     rows = gathered[0].shape[0] - 16
     width = w.shape[2]
     block = rows // 4
     vm = pl.BlockSpec(memory_space=pltpu.VMEM)
     return pl.pallas_call(
-        out_kernel,
-        in_specs=[pl.BlockSpec(memory_space=pltpu.SMEM)] + [vm] * 5,
+        drop(out_kernel, 6, len(after)),
+        in_specs=[pl.BlockSpec(memory_space=pltpu.SMEM)] + [vm] * 5 + [ANYWHERE] * len(after),
         out_specs=[vm] * 4,
         out_shape=[jax.ShapeDtypeStruct((block + 16, width), BF16)] * 4,
         scratch_shapes=[pltpu.VMEM((rows, width), F32), pltpu.VMEM((4, block), F32)],
         cost_estimate=pl.CostEstimate(flops=10**9, bytes_accessed=3 * 10**6, transcendentals=0),
         name="out_blocks",
-    )(at, *gathered, w)
+    )(at, *gathered, w, *after)
 
 
 def residual_kernel(m, units, at_ref, o0_ref, o1_ref, o2_ref, o3_ref, hid_ref, gain_ref, out_ref):
@@ -296,11 +310,11 @@
     out_ref[block : block + 16, :] = jnp.broadcast_to(line, (16, width)).astype(BF16)
 
 
-def residual_block(m, at, parts, hidden, gain, units):
+def residual_block(m, at, parts, hidden, gain, units, after=()):
     block, width = parts[0].shape[0] - 16, parts[0].shape[1]
     whole = pl.BlockSpec((block + 16, width), lambda g, at: (0, 0))
     return pl.pallas_call(
-        functools.partial(residual_kernel, m, float(units)),
+        drop(functools.partial(residual_kernel, m, float(units)), 7, len(after)),
         grid_spec=pltpu.PrefetchScalarGridSpec(
             num_scalar_prefetch=1,
             grid=(1,),
@@ -308,13 +322,14 @@
             + [
                 pl.BlockSpec((None, block, width), lambda g, at: (m, at[1], at[0])),
                 pl.BlockSpec((2, width), lambda g, at: (0, at[0])),
-            ],
+            ]
+            + [ANYWHERE] * len(after),
             out_specs=whole,
         ),
         out_shape=jax.ShapeDtypeStruct((block + 16, width), BF16),
         cost_estimate=pl.CostEstimate(flops=10**6, bytes_accessed=10**6, transcendentals=100),
         name="residual_block",
-    )(at, *parts, hidden, gain)
+    )(at, *parts, hidden, gain, *after)
 
 
 def join_kernel(at_ref, u0_ref, u1_ref, u2_ref, u3_ref, out_ref):
@@ -331,30 +346,51 @@
     out_ref[block : block + 16, 0 : 3 * block] = jnp.broadcast_to(line, (16, 3 * block)).astype(BF16)
 
 
-def join_columns(at, parts):
+def join_columns(at, parts, after=()):
     tall, width = parts[0].shape
     vm = pl.BlockSpec(memory_space=pltpu.VMEM)
     return pl.pallas_call(
-        join_kernel,
-        in_specs=[pl.BlockSpec(memory_space=pltpu.SMEM)] + [vm] * 4,
+        drop(join_kernel, 5, len(after)),
+        in_specs=[pl.BlockSpec(memory_space=pltpu.SMEM)] + [vm] * 4 + [ANYWHERE] * len(after),
         out_specs=vm,
         out_shape=jax.ShapeDtypeStruct((tall, 4 * width), BF16),
         cost_estimate=pl.CostEstimate(flops=10**5, bytes_accessed=10**6, transcendentals=100),
         name="join_columns",
-    )(at, *parts)
-
-
-def head_kernel(place_ref, at_ref, x0_ref, x1_ref, x2_ref, x3_ref, w_ref, tgt_ref, out_ref):
+    )(at, *parts, *after)
+
+
+def head_kernel(place_ref, at_ref, x0_ref, x1_ref, x2_ref, x3_ref, w_ref, tgt_ref, out_ref, acc_ref, scale_ref):
     block = x0_ref.shape[0] - 16
     vocab = w_ref.shape[1]
-    for pair in (((0, x0_ref), (1, x1_ref)), ((2, x2_ref), (3, x3_ref))):
-        rows = jnp.concatenate([x[0:block, :] for _, x in pair], axis=0)
+    step = pl.program_id(0)
+    tiles = (x0_ref, x1_ref, x2_ref, x3_ref)
+
+    @pl.when(step == 0)
+    def _():
+        for k, x in enumerate(tiles):
+            line = x[block : block + 16, 0 : 3 * block].astype(F32)[0:1, :]
+            scale_ref[k : k + 1, :] = (
+                line[:, 0:block] + line[:, block : 2 * block] + line[:, 2 * block : 3 * block]
+            )
+
+    for n in range(2):
+        rows = jnp.concatenate([x[0:block, :] for x in tiles[2 * n : 2 * n + 2]], axis=0)
         raw = contract(rows, w_ref[...], ((1,), (0,)))
-        for n, (k, x) in enumerate(pair):
+        span = slice(2 * n * block, 2 * (n + 1) * block)
+
+        @pl.when(step == 0)
+        def _():
+            acc_ref[span, :] = raw
+
+        @pl.when(step > 0)
+        def _():
+            acc_ref[span, :] += raw
+
+    @pl.when(step == pl.num_programs(0) - 1)
+    def _():
+        for k in range(4):
             at = lax.rem(at_ref[1] + 4 - k, 4)
-            line = x[block : block + 16, 0 : 3 * block].astype(F32)[0:1, :]
-            scale = to_column(line[:, 0:block] + line[:, block : 2 * block] + line[:, 2 * block : 3 * block])
-            logits = raw[n * block : (n + 1) * block, :] * scale
+            logits = acc_ref[k * block : (k + 1) * block, :] * to_column(scale_ref[k : k + 1, :])
             top = jnp.max(logits, axis=1, keepdims=True)
             lse = top + jnp.log(jnp.sum(jnp.exp(logits - top), axis=1, keepdims=True))
             target = to_column((tgt_ref[pl.ds(at, 1), :] - place_ref[0] * vocab).astype(F32))
@@ -366,29 +402,31 @@
                 )
 
 
-def head_stats(m, place, at, parts, head, tgt, group):
+def head_stats(m, place, at, parts, head, tgt, group, after=(), chunks=4):
     tall, depth = parts[0].shape
     block = tall - 16
     vocab = head.shape[2]
-    whole = pl.BlockSpec((tall, depth), lambda i, pf, at: (0, 0))
-    return pl.pallas_call(
-        head_kernel,
+    deep = depth // chunks
+    return pl.pallas_call(
+        drop(head_kernel, 8, len(after)),
         grid_spec=pltpu.PrefetchScalarGridSpec(
             num_scalar_prefetch=2,
-            grid=(1,),
-            in_specs=[whole] * 4
+            grid=(chunks,),
+            in_specs=[pl.BlockSpec((tall, deep), lambda i, pf, at: (0, i))] * 4
             + [
-                pl.BlockSpec((None, depth, vocab), lambda i, pf, at: (m, 0, 0)),
+                pl.BlockSpec((None, deep, vocab), lambda i, pf, at: (m, i, 0)),
                 pl.BlockSpec(tgt.shape, lambda i, pf, at: (0, 0)),
-            ],
+            ]
+            + [ANYWHERE] * len(after),
             out_specs=pl.BlockSpec((group, 8, block), lambda i, pf, at: (0, 0, 0)),
+            scratch_shapes=[pltpu.VMEM((4 * block, vocab), F32), pltpu.VMEM((4, block), F32)],
         ),
         out_shape=jax.ShapeDtypeStruct((group, 8, block), F32),
         cost_estimate=pl.CostEstimate(
             flops=8 * block * depth * vocab, bytes_accessed=2 * depth * vocab, transcendentals=4 * block * vocab
         ),
         name="head_stats",
-    )(place, at, *parts, head, tgt)
+    )(place, at, *parts, head, tgt, *after)
 
 
 def diff_kernel(s0_ref, s1_ref, live_ref, seg_ref, diff_ref, sums_ref):
@@ -421,6 +459,32 @@
     )(s0, s1, live, seg)
 
 
+def turn_kernel(w_ref, out0_ref, out1_ref, sems):
+    width = out0_ref.shape[2]
+    copies = [
+        pltpu.make_async_copy(w_ref.at[m, :, pl.ds(j * width, width)], out.at[j], sems.at[m * 4 + j])
+        for m, out in enumerate((out0_ref, out1_ref))
+        for j in range(4)
+    ]
+    for copy in copies:
+        copy.start()
+    for copy in copies:
+        copy.wait()
+
+
+def turned(w_out):
+    _, inner, depth = w_out.shape
+    return pl.pallas_call(
+        turn_kernel,
+        in_specs=[ANYWHERE],
+        out_specs=[ANYWHERE] * 2,
+        out_shape=[jax.ShapeDtypeStruct((4, inner, depth // 4), w_out.dtype)] * 2,
+        scratch_shapes=[pltpu.SemaphoreType.DMA((8,))],
+        cost_estimate=pl.CostEstimate(flops=0, bytes_accessed=4 * 10**6, transcendentals=0),
+        name="turned",
+    )(w_out)
+
+
 def ring(value, axis, by):
     return lax.ppermute(value, axis, [(i, (i + by) % 4) for i in range(4)])
 
@@ -441,27 +505,38 @@
     place = lax.axis_index(VOC).astype(jnp.int32).reshape(1)
     seg = segment_ids.reshape(1, rows)
     tgt = targets.reshape(4, rows // 4)
-    w_inner = w_inner.reshape(2, depth, 2 * inner)
-    w_state = w_state.reshape(2, depth, -1)
     w_step = jnp.swapaxes(w_step, 1, 2)
     ways = (("x", "z"), ("z", "x"))
-    turned = jnp.swapaxes(w_out.reshape(2, inner, 4, depth // 4), 1, 2)
-    weights = [lax.all_to_all(turned[m], ways[m][0], 0, 0) for m in range(2)]
-    mixed = [
-        mix_local(m, hidden, w_inner, w_state, w_step, step_bias, rate, skip_gain, seg) for m in range(2)
+    both = range(2)
+    at = [
+        jnp.stack([lax.axis_index(along), lax.axis_index(across)]).astype(jnp.int32) for along, across in ways
     ]
-    stats = []
-    for m in range(2):
-        along, across = ways[m]
-        at = jnp.stack([lax.axis_index(along), lax.axis_index(across)]).astype(jnp.int32)
-        y, gate, c, e, pay = mixed[m]
+    turns = turned(w_out)
+    weights = [lax.all_to_all(turns[m], ways[m][0], 0, 0) for m in both]
+
+    def mix(m, after):
+        y, gate, c, e, pay = mix_local(
+            m, hidden, w_inner, w_state, w_step, step_bias, rate, skip_gain, seg, after
+        )
         recv = [lax.ppermute(pay, SEQ, [(i, i + k) for i in range(devices - k)]) for k in range(1, REACH + 1)]
-        gated = gate_out(m, pages, flags, y, gate, c, e, recv, pool, norm_gain)
-        parts = out_blocks(at, gathered(gated, along), weights[m])
-        parts = [parts[0]] + [ring(parts[k], across, k) for k in (1, 2, 3)]
-        res = residual_block(m, at, parts, hidden, final_gain, inner * group)
-        full = join_columns(at, gathered(res, along))
-        stat = head_stats(m, place, at, gathered(full, across), head, tgt, group)
+        return y, gate, c, e, recv
+
+    mixed = [None, None]
+    mixed[0] = mix(0, ())
+    mixed[1] = mix(1, (mixed[0][2],))
+    gated, parts, res, full, stats = [], [], [], [], []
+    for m in both:
+        y, gate, c, e, recv = mixed[m]
+        gated.append(gate_out(m, pages, flags, y, gate, c, e, recv, pool, norm_gain, (mixed[1][2],)))
+    for m in both:
+        out = out_blocks(at[m], gathered(gated[m], ways[m][0]), weights[m], (gated[1],))
+        parts.append([out[0]] + [ring(out[k], ways[m][1], k) for k in (1, 2, 3)])
+    for m in both:
+        res.append(residual_block(m, at[m], parts[m], hidden, final_gain, inner * group, (parts[1][0],)))
+    for m in both:
+        full.append(join_columns(at[m], gathered(res[m], ways[m][0]), (res[1],)))
+    for m in both:
+        stat = head_stats(m, place, at[m], gathered(full[m], ways[m][1]), head, tgt, group, (full[1],))
         stats.append(lax.all_to_all(stat, VOC, 0, 0))
     diff, sums = token_diffs(stats[0], stats[1], live, segment_ids.reshape(4, 128), devices)
     sums = jnp.sum(lax.all_to_all(sums, SEQ, 0, 0)[:, 0:4, 0], axis=0)

time: 236 us -> 288 us (1.22)
  Pallas kernels: 63.1 us -> 143 us
  waiting for transfers between devices: 65.6 us -> 47.6 us
  local copies, waits for them, and re-layouts: 26.2 us -> 9.02 us
  starting transfers between devices: 65.8 us -> 73.6 us
    pallas_call x12 -> x13, Pallas kernels: 61.5 us -> 142 us  [the longest x1 64.7 us: turned(): pl.pallas_call(turn_kernel, in_specs=[ANYWHERE], out_specs=[ANYWHERE] * 2...]
    ppermute x24, waiting for transfers between devices: 59.2 us -> 42.7 us  [ring(): return lax.ppermute(value, axis, [(i, (i + by) % 4) for i in range(4)])]
    reshape x3 -> x0, local copies, waits for them, and re-layouts: 13 us -> none  [the longest x1 7.63 us: per_device(): w_inner = w_inner.reshape(2, depth, 2 * inner)]
    ppermute x24, starting transfers between devices: 26.7 us -> 33.6 us  [ring(): return lax.ppermute(value, axis, [(i, (i + by) % 4) for i in range(4)])]
    unnamed x75 -> x74, local copies, waits for them, and re-layouts: 11.6 us -> 9.02 us
  transfers between devices with their start and end apart: 36 -> 36, of which waited for: 11 -> 7; matrix products, arithmetic and copies ran while one was open for 5% -> 0% of each run, Pallas kernels for 26% -> 26%
where the time goes in v4:
time: 288 us; the launch traced here: 287 us
  Pallas kernels  143 us (50%)
  starting transfers between devices  73.6 us (26%)
  waiting for transfers between devices  47.6 us (17%)
  blocking collectives  10.7 us (4%)
  local copies, waits for them, and re-layouts  9.02 us (3%)
    pallas_call x1, Pallas kernels, turned(): pl.pallas_call(turn_kernel, in_specs=[ANYWHERE], out_specs=[ANYWHERE] * 2...  64.7 us
    ppermute x24, waiting for transfers between devices, ring(): return lax.ppermute(value, axis, [(i, (i + by) % 4) for i in range(4)])  42.7 us
    ppermute x24, starting transfers between devices, ring(): return lax.ppermute(value, axis, [(i, (i + by) % 4) for i in range(4)])  33.6 us
    pallas_call x2, Pallas kernels, mix_local(): pl.pallas_call(drop(functools.partial(mix_kernel, m), 8, len(after)), gri...  29.6 us
    pallas_call x2, Pallas kernels, head_stats(): pl.pallas_call(drop(head_kernel, 8, len(after)), grid_spec=pltpu.Prefetch...  23.3 us
    ppermute x8, starting transfers between devices, mix(): lax.ppermute(pay, SEQ, [(i, i + k) for i in range(devices - k)])  19 us
    all_to_all x1, blocking collectives, per_device(): stats.append(lax.all_to_all(stat, VOC, 0, 0))  10.7 us
    all_to_all x2, starting transfers between devices, per_device(): weights = [lax.all_to_all(turns[m], ways[m][0], 0, 0) for m in both]  9.89 us
  transfers between devices with their start and end apart: 36, of which 7 were waited for; matrix products, arithmetic and copies ran while one was open for 0% of the time, Pallas kernels for 26%

profile of v4, /device:TPU:1, one launch (start us, length us, event | category | flops | bytes accessed | tf_op | source)
XLA Modules:
  0.0 287.2 jit_solution(3109628936325638890)
XLA Ops:
  0.6 64.7 %turned.1 = (bf16[4,256,512]{2,1,0:T(8,128)(2,1)}, bf16[4,256,512]{2,1,0:T(8,128)(2,1)}) custom-call(bf16[2,256,2048]{2,1,0:T(8,128)(2,1)} %w_ref.1), custom_call_target="tpu_custom_call" | custom-call | bytes 4000000 | tf_op jit(solution)/shard_map/turned/pallas_call | solution.py:477
  65.3 4.9 %all-to-all-start = ((bf16[4,256,512]{2,1,0:T(8,128)(2,1)}), bf16[4,256,512]{2,1,0:T(8,128)(2,1)S(1)}, u32[]{:S(2)}, u32[]{:S(2)}) async-start(bf16[4,256,512]{2,1,0:T(8,128)(2,1)} %get-tuple-element.30), calls=%async_computation | async-start | bytes 2097152 | tf_op jit(solution)/shard_map/all_to_all | solution.py:515
  70.2 14.8 %mix_local.2 = (f32[512,256]{1,0:T(8,128)}, f32[512,256]{1,0:T(8,128)}, bf16[512,128]{1,0:T(8,128)(2,1)}, f32[512,8]{1,0:T(8,128)}, bf16[272,128]{1,0:T(8,128)(2,1)}) custom-call(bf16[2,512,2048]{2,1,0:T(8,128)(2,1)} %refs_5_.7, bf16[2,2048,2,256]{3,2,1,0:T(2,128)(2,1)} %refs_1_.5, bf16[2,2048,2,128]{3,2,1,0:T(2,128)(2,1)} %refs_2_.3, ...), custom_call_target="tpu_custom_call" | custom-call | flops 5000000000 | bytes 8000000 | tf_op jit(solution)/shard_map/mix_local/pallas_call | solution.py:171
  85.0 4.8 %collective-permute-start.3 = (bf16[272,128]{1,0:T(8,128)(2,1)}, bf16[272,128]{1,0:T(8,128)(2,1)S(1)}, u32[]{:S(2)}, u32[]{:S(2)}) collective-permute-start(bf16[272,128]{1,0:T(8,128)(2,1)} %get-tuple-element.28), channel_id=1, source_target_pairs={{0,64},{16,80},{32,96},{48,112},{1,65},{17,81},{33,97},{49,113},{2... | collective-permute-start | bytes 208904 | tf_op jit(solution)/shard_map/ppermute | solution.py:521
  89.8 2.1 collective-permute-start.2
  92.0 2.3 collective-permute-start.1
  94.3 2.2 collective-permute-start
  96.5 5.0 %all-to-all-start.1 = ((bf16[4,256,512]{2,1,0:T(8,128)(2,1)}), bf16[4,256,512]{2,1,0:T(8,128)(2,1)S(1)}, u32[]{:S(2)}, u32[]{:S(2)}) async-start(bf16[4,256,512]{2,1,0:T(8,128)(2,1)} %get-tuple-element.39), calls=%async_computation.1 | async-start | bytes 2097152 | tf_op jit(solution)/shard_map/all_to_all | solution.py:515
  101.5 14.8 %mix_local.3 = (f32[512,256]{1,0:T(8,128)}, f32[512,256]{1,0:T(8,128)}, bf16[512,128]{1,0:T(8,128)(2,1)}, f32[512,8]{1,0:T(8,128)}, bf16[272,128]{1,0:T(8,128)(2,1)}) custom-call(bf16[2,512,2048]{2,1,0:T(8,128)(2,1)} %refs_5_.7, bf16[2,2048,2,256]{3,2,1,0:T(2,128)(2,1)} %refs_1_.5, bf16[2,2048,2,128]{3,2,1,0:T(2,128)(2,1)} %refs_2_.3, ...), custom_call_target="tpu_custom_call" | custom-call | flops 5000000000 | bytes 8000000 | tf_op jit(solution)/shard_map/mix_local/pallas_call | solution.py:171
  117.1 4.1 %gate_out.2.refs_1_ = bf16[528,256]{1,0:T(8,128)(2,1)} custom-call(s32[4]{0:T(128)} %refs_0_.7, s32[4]{0:T(128)} %refs_1_.7, f32[512,256]{1,0:T(8,128)} %get-tuple-element.24.refs_2_, f32[512,256]{1,0:T(8,128)} %get-tuple-element.25.refs_3_, bf16[512,128]{1,0:T(8,128)(2,1)} %get-tuple-element.26.refs_8_.refs_4_, f32[512,8]{1,0:T(8,128)} %get-tuple-element.27.refs_5_, ...), custom_call_target="tpu_custom_call" | custom-call | flops 1000000000 | bytes 4000000 | tf_op jit(solution)/shard_map/gate_out/pallas_call | solution.py:245
  121.2 3.0 %collective-permute-start.6 = (bf16[528,256]{1,0:T(8,128)(2,1)}, bf16[528,256]{1,0:T(8,128)(2,1)S(1)}, u32[]{:S(2)}, u32[]{:S(2)}) collective-permute-start(bf16[528,256]{1,0:T(8,128)(2,1)} %gate_out.2.refs_1_), channel_id=1, source_target_pairs={{0,12},{4,0},{8,4},{12,8},{1,13},{5,1},{9,5},{13,9},{2,14},{6,2},{... | collective-permute-start | bytes 811016 | tf_op jit(solution)/shard_map/ppermute | solution.py:489
  124.2 1.3 collective-permute-start.10
  125.5 2.5 collective-permute-start.9
  127.9 1.3 collective-permute-start.8
  129.2 2.5 collective-permute-start.7
  131.8 0.7 collective-permute-start.5
  132.4 0.6 collective-permute-start.4
  133.7 4.0 %gate_out.3.refs_6_.refs_1_ = bf16[528,256]{1,0:T(8,128)(2,1)} custom-call(s32[4]{0:T(128)} %refs_0_.7, s32[4]{0:T(128)} %refs_1_.7, f32[512,256]{1,0:T(8,128)} %get-tuple-element.31.refs_2_, f32[512,256]{1,0:T(8,128)} %get-tuple-element.32.refs_3_, bf16[512,128]{1,0:T(8,128)(2,1)} %get-tuple-element.29.refs_15_.refs_4_, ...), custom_call_target="tpu_custom_call" | custom-call | flops 1000000000 | bytes 4000000 | tf_op jit(solution)/shard_map/gate_out/pallas_call | solution.py:245
  137.7 2.9 %collective-permute-start.16 = (bf16[528,256]{1,0:T(8,128)(2,1)}, bf16[528,256]{1,0:T(8,128)(2,1)S(1)}, u32[]{:S(2)}, u32[]{:S(2)}) collective-permute-start(bf16[528,256]{1,0:T(8,128)(2,1)} %gate_out.3.refs_6_.refs_1_), channel_id=1, source_target_pairs={{0,3},{1,0},{2,1},{3,2},{4,7},{5,4},{6,5},{7,6},{8,11},{9,8},{10,9... | collective-permute-start | bytes 811016 | tf_op jit(solution)/shard_map/ppermute | solution.py:489
  140.7 0.6 collective-permute-start.15
  141.2 0.6 collective-permute-start.14
  141.8 0.6 pad_add_fusion.1.refs_0_.refs_1_
  142.4 0.6 pad_add_fusion.refs_0_.refs_1_
  143.0 4.8 %collective-permute-done.4.refs_2_ = bf16[528,256]{1,0:T(8,128)(2,1)S(1)} collective-permute-done((bf16[528,256]{1,0:T(8,128)(2,1)}, bf16[528,256]{1,0:T(8,128)(2,1)S(1)}, u32[]{:S(2)}, u32[]{:S(2)}) %collective-permute-start.4) | collective-permute-done | bytes 270368 | tf_op jit(solution)/shard_map/ppermute | solution.py:489
  147.8 0.7 copy-done.35
  148.5 3.2 %out_blocks.2 = (bf16[144,512]{1,0:T(8,128)(2,1)}, bf16[144,512]{1,0:T(8,128)(2,1)}, bf16[144,512]{1,0:T(8,128)(2,1)}, bf16[144,512]{1,0:T(8,128)(2,1)}) custom-call(s32[2]{0:T(128)} %pad_add_fusion.refs_0_.refs_1_, bf16[528,256]{1,0:T(8,128)(2,1)} %gate_out.2.refs_1_, bf16[528,256]{1,0:T(8,128)(2,1)} %copy-done.35, bf16[528,256]{1,0:T(8,128)(2,1)} %copy-done.33, ...), custom_call_target="tpu_custom_call" | custom-call | flops 1000000000 | bytes 3000000 | tf_op jit(solution)/shard_map/out_blocks/pallas_call | solution.py:288
  151.7 1.7 collective-permute-start.11
  153.4 2.4 collective-permute-start.12
  155.8 1.2 collective-permute-start.13
  157.0 0.7 copy-done.32
  157.8 1.0 copy-done
  158.8 3.2 %out_blocks.3 = (bf16[144,512]{1,0:T(8,128)(2,1)}, bf16[144,512]{1,0:T(8,128)(2,1)}, bf16[144,512]{1,0:T(8,128)(2,1)}, bf16[144,512]{1,0:T(8,128)(2,1)}) custom-call(s32[2]{0:T(128)} %pad_add_fusion.1.refs_0_.refs_1_, bf16[528,256]{1,0:T(8,128)(2,1)} %gate_out.3.refs_6_.refs_1_, bf16[528,256]{1,0:T(8,128)(2,1)} %copy-done.34, bf16[528,256]{1,0:T(8,128)(2,1)} %copy-done.32, ...), custom_call_target="tpu_custom_call" | custom-call | flops 1000000000 | bytes 3000000 | tf_op jit(solution)/shard_map/out_blocks/pallas_call | solution.py:288
  162.0 0.9 collective-permute-start.20
  162.9 1.8 collective-permute-start.21
  164.7 0.6 collective-permute-start.22
  165.4 0.6 copy-done.16
  166.1 2.8 residual_block.2.refs_1_
  168.9 0.8 collective-permute-start.19
  169.7 1.8 collective-permute-start.18
  171.6 0.6 copy-done.17
  172.3 0.6 copy-done.20
  172.9 2.8 residual_block.3.refs_5_.refs_1_
  175.8 2.5 collective-permute-done.17.refs_2_
  178.3 0.7 copy-done.11
  178.9 2.0 join_columns.2.refs_2_
  180.9 3.6 %collective-permute-start.24 = (bf16[144,2048]{1,0:T(8,128)(2,1)}, bf16[144,2048]{1,0:T(8,128)(2,1)S(1)}, u32[]{:S(2)}, u32[]{:S(2)}) collective-permute-start(bf16[144,2048]{1,0:T(8,128)(2,1)} %join_columns.2.refs_2_), channel_id=1, source_target_pairs={{0,2},{1,3},{2,0},{3,1},{4,6},{5,7},{6,4},{7,5},{8,10},{9,11},{10,... | collective-permute-start | bytes 1769480 | tf_op jit(solution)/shard_map/ppermute | solution.py:489
  184.6 2.7 collective-permute-start.28
  187.2 22.7 %collective-permute-done.28.refs_4_ = bf16[144,512]{1,0:T(8,128)(2,1)S(1)} collective-permute-done((bf16[144,512]{1,0:T(8,128)(2,1)}, bf16[144,512]{1,0:T(8,128)(2,1)S(1)}, u32[]{:S(2)}, u32[]{:S(2)}) %collective-permute-start.28) | collective-permute-done | bytes 147488 | tf_op jit(solution)/shard_map/ppermute | solution.py:489
  209.9 5.7 %collective-permute-start.26 = (bf16[144,512]{1,0:T(8,128)(2,1)}, bf16[144,512]{1,0:T(8,128)(2,1)S(1)}, u32[]{:S(2)}, u32[]{:S(2)}) collective-permute-start(bf16[144,512]{1,0:T(8,128)(2,1)} %residual_block.3.refs_5_.refs_1_), channel_id=1, source_target_pairs={{0,1},{1,2},{2,3},{3,0},{4,5},{5,6},{6,7},{7,4},{8,9},{9,10},{10,1... | collective-permute-start | bytes 442376 | tf_op jit(solution)/shard_map/ppermute | solution.py:489
  215.6 2.4 collective-permute-done.26.refs_2_
  218.0 0.7 copy-done.14
  218.7 2.0 join_columns.3.refs_8_.refs_2_
  220.7 1.5 collective-permute-start.31
  222.3 0.6 collective-permute-start.29
  223.1 0.6 copy-done.3
  223.9 11.6 %head_stats.2 = f32[16,8,128]{2,1,0:T(8,128)} custom-call(s32[1]{0:T(128)} %bitcast.refs_0_, s32[2]{0:T(128)} %pad_add_fusion.refs_0_.refs_1_, bf16[144,2048]{1,0:T(8,128)(2,1)} %join_columns.2.refs_2_, bf16[144,2048]{1,0:T(8,128)(2,1)} %copy-done.4, bf16[144,2048]{1,0:T(8,128)(2,1)} %copy-done.3, bf16[144,2048]{1,0:T(8,128)(2,1)} %copy-done.2, ...), custom_call_target="tpu_custom_call" | custom-call | flops 3489660928 | bytes 6815744 | tf_op jit(solution)/shard_map/head_stats/pallas_call | solution.py:410
  235.5 6.2 %all-to-all-start.2 = ((f32[16,8,128]{2,1,0:T(8,128)}), f32[16,8,128]{2,1,0:T(8,128)S(1)}, u32[]{:S(2)}, u32[]{:S(2)}) async-start(f32[16,8,128]{2,1,0:T(8,128)} %head_stats.2), calls=%async_computation.2 | async-start | bytes 131072 | tf_op jit(solution)/shard_map/all_to_all | solution.py:540
  241.7 10.3 %collective-permute-done.29.refs_3_ = bf16[144,2048]{1,0:T(8,128)(2,1)S(1)} collective-permute-done((bf16[144,2048]{1,0:T(8,128)(2,1)}, bf16[144,2048]{1,0:T(8,128)(2,1)S(1)}, u32[]{:S(2)}, u32[]{:S(2)}) %collective-permute-start.29) | collective-permute-done | bytes 589856 | tf_op jit(solution)/shard_map/ppermute | solution.py:489
  252.0 0.8 copy-done.7
  252.9 11.7 %head_stats.3 = f32[16,8,128]{2,1,0:T(8,128)} custom-call(s32[1]{0:T(128)} %bitcast.refs_0_, s32[2]{0:T(128)} %pad_add_fusion.1.refs_0_.refs_1_, bf16[144,2048]{1,0:T(8,128)(2,1)} %join_columns.3.refs_8_.refs_2_, bf16[144,2048]{1,0:T(8,128)(2,1)} %copy-done.7, bf16[144,2048]{1,0:T(8,128)(2,1)} %copy-done.6, bf16[144,2048]{1,0:T(8,128)(2,1)} %copy-done.5, ...), custom_call_target="tpu_custom_call" | custom-call | flops 3489660928 | bytes 6815744 | tf_op jit(solution)/shard_map/head_stats/pallas_call | solution.py:410
  264.5 10.7 %all_to_all.25.s1_ref = f32[16,8,128]{2,1,0:T(8,128)} all-to-all(f32[16,8,128]{2,1,0:T(8,128)} %head_stats.3), channel_id=1, replica_groups=mesh['y'=4,'core'=2,'x'=4,'z'=4] {'x','z'}, dimensions={0} | all-to-all | bytes 131072 | tf_op jit(solution)/shard_map/all_to_all | solution.py:540
  275.2 1.6 token_diffs.1
  276.8 5.0 %all-to-all-start.4 = ((f32[8,8,128]{2,1,0:T(8,128)}), f32[8,8,128]{2,1,0:T(8,128)S(1)}, u32[]{:S(2)}, u32[]{:S(2)}) async-start(f32[8,8,128]{2,1,0:T(8,128)} %get-tuple-element.45), calls=%async_computation.4 | async-start | bytes 65536 | tf_op jit(solution)/shard_map/all_to_all | solution.py:542
  281.8 4.7 %all-to-all-done.4 = f32[8,8,128]{2,1,0:T(8,128)S(1)} async-done(((f32[8,8,128]{2,1,0:T(8,128)}), f32[8,8,128]{2,1,0:T(8,128)S(1)}, u32[]{:S(2)}, u32[]{:S(2)}) %all-to-all-start.4) | async-done | bytes 32800 | tf_op jit(solution)/shard_map/all_to_all | solution.py:542
  (101 shorter events, 2.8 us)
Async XLA Ops:
  65.3 31.1 %all-to-all-start = ((bf16[4,256,512]{2,1,0:T(8,128)(2,1)}), bf16[4,256,512]{2,1,0:T(8,128)(2,1)S(1)}, u32[]{:S(2)}, u32[]{:S(2)}) async-start(bf16[4,256,512]{2,1,0:T(8,128)(2,1)} %get-tuple-element.30), calls=%async_computation | async-start | bytes 2097152 | tf_op jit(solution)/shard_map/all_to_all | solution.py:515
  85.0 31.3 %collective-permute-start.3 = (bf16[272,128]{1,0:T(8,128)(2,1)}, bf16[272,128]{1,0:T(8,128)(2,1)S(1)}, u32[]{:S(2)}, u32[]{:S(2)}) collective-permute-start(bf16[272,128]{1,0:T(8,128)(2,1)} %get-tuple-element.28), channel_id=1, source_target_pairs={{0,64},{16,80},{32,96},{48,112},{1,65},{17,81},{33,97},{49,113},{2... | collective-permute-start | bytes 208904 | tf_op jit(solution)/shard_map/ppermute | solution.py:521
  89.8 26.5 %collective-permute-start.2 = (bf16[272,128]{1,0:T(8,128)(2,1)}, bf16[272,128]{1,0:T(8,128)(2,1)S(1)}, u32[]{:S(2)}, u32[]{:S(2)}) collective-permute-start(bf16[272,128]{1,0:T(8,128)(2,1)} %get-tuple-element.28), channel_id=1, source_target_pairs={{0,48},{16,64},{32,80},{48,96},{64,112},{1,49},{17,65},{33,81},{49... | collective-permute-start | bytes 208904 | tf_op jit(solution)/shard_map/ppermute | solution.py:521
  92.0 24.4 %collective-permute-start.1 = (bf16[272,128]{1,0:T(8,128)(2,1)}, bf16[272,128]{1,0:T(8,128)(2,1)S(1)}, u32[]{:S(2)}, u32[]{:S(2)}) collective-permute-start(bf16[272,128]{1,0:T(8,128)(2,1)} %get-tuple-element.28), channel_id=1, source_target_pairs={{0,32},{16,48},{32,64},{48,80},{64,96},{80,112},{1,33},{17,49},{33... | collective-permute-start | bytes 208904 | tf_op jit(solution)/shard_map/ppermute | solution.py:521
  94.3 22.1 %collective-permute-start = (bf16[272,128]{1,0:T(8,128)(2,1)}, bf16[272,128]{1,0:T(8,128)(2,1)S(1)}, u32[]{:S(2)}, u32[]{:S(2)}) collective-permute-start(bf16[272,128]{1,0:T(8,128)(2,1)} %get-tuple-element.28), channel_id=1, source_target_pairs={{0,16},{16,32},{32,48},{48,64},{64,80},{80,96},{96,112},{1,17},{17... | collective-permute-start | bytes 208904 | tf_op jit(solution)/shard_map/ppermute | solution.py:521
  96.5 19.8 %copy-start.1 = (bf16[4,256,512]{2,1,0:T(8,128)(2,1)}, bf16[4,256,512]{2,1,0:T(8,128)(2,1)S(1)}, u32[]{:S(2)}) copy-start(bf16[4,256,512]{2,1,0:T(8,128)(2,1)S(1)} %all-to-all-done.refs_5_) | copy-start | bytes 3145732
  96.5 60.5 %all-to-all-start.1 = ((bf16[4,256,512]{2,1,0:T(8,128)(2,1)}), bf16[4,256,512]{2,1,0:T(8,128)(2,1)S(1)}, u32[]{:S(2)}, u32[]{:S(2)}) async-start(bf16[4,256,512]{2,1,0:T(8,128)(2,1)} %get-tuple-element.39), calls=%async_computation.1 | async-start | bytes 2097152 | tf_op jit(solution)/shard_map/all_to_all | solution.py:515
  116.4 0.7 copy-start.28
  117.1 7.1 %copy-start.36 = (bf16[272,128]{1,0:T(8,128)(2,1)S(1)}, bf16[272,128]{1,0:T(8,128)(2,1)}, u32[]{:S(2)}) copy-start(bf16[272,128]{1,0:T(8,128)(2,1)} %get-tuple-element.34) | copy-start | bytes 208900
  121.2 20.0 %collective-permute-start.6 = (bf16[528,256]{1,0:T(8,128)(2,1)}, bf16[528,256]{1,0:T(8,128)(2,1)S(1)}, u32[]{:S(2)}, u32[]{:S(2)}) collective-permute-start(bf16[528,256]{1,0:T(8,128)(2,1)} %gate_out.2.refs_1_), channel_id=1, source_target_pairs={{0,12},{4,0},{8,4},{12,8},{1,13},{5,1},{9,5},{13,9},{2,14},{6,2},{... | collective-permute-start | bytes 811016 | tf_op jit(solution)/shard_map/ppermute | solution.py:489
  124.2 7.6 %collective-permute-start.10 = (bf16[272,128]{1,0:T(8,128)(2,1)S(1)}, bf16[272,128]{1,0:T(8,128)(2,1)S(1)}, u32[]{:S(2)}, u32[]{:S(2)}) collective-permute-start(bf16[272,128]{1,0:T(8,128)(2,1)S(1)} %copy-done.36), channel_id=1, source_target_pairs={{0,64},{16,80},{32,96},{48,112},{1,65},{17,81},{33,97},{49,113},{2... | collective-permute-start | bytes 208904 | tf_op jit(solution)/shard_map/ppermute | solution.py:521
  125.5 7.0 %collective-permute-start.9 = (bf16[272,128]{1,0:T(8,128)(2,1)S(1)}, bf16[272,128]{1,0:T(8,128)(2,1)S(1)}, u32[]{:S(2)}, u32[]{:S(2)}) collective-permute-start(bf16[272,128]{1,0:T(8,128)(2,1)S(1)} %copy-done.36), channel_id=1, source_target_pairs={{0,48},{16,64},{32,80},{48,96},{64,112},{1,49},{17,65},{33,81},{49... | collective-permute-start | bytes 208904 | tf_op jit(solution)/shard_map/ppermute | solution.py:521
  127.9 5.1 %collective-permute-start.8 = (bf16[272,128]{1,0:T(8,128)(2,1)S(1)}, bf16[272,128]{1,0:T(8,128)(2,1)S(1)}, u32[]{:S(2)}, u32[]{:S(2)}) collective-permute-start(bf16[272,128]{1,0:T(8,128)(2,1)S(1)} %copy-done.36), channel_id=1, source_target_pairs={{0,32},{16,48},{32,64},{48,80},{64,96},{80,112},{1,33},{17,49},{33... | collective-permute-start | bytes 208904 | tf_op jit(solution)/shard_map/ppermute | solution.py:521
  129.2 3.9 %collective-permute-start.7 = (bf16[272,128]{1,0:T(8,128)(2,1)S(1)}, bf16[272,128]{1,0:T(8,128)(2,1)S(1)}, u32[]{:S(2)}, u32[]{:S(2)}) collective-permute-start(bf16[272,128]{1,0:T(8,128)(2,1)S(1)} %copy-done.36), channel_id=1, source_target_pairs={{0,16},{16,32},{32,48},{48,64},{64,80},{80,96},{96,112},{1,17},{17... | collective-permute-start | bytes 208904 | tf_op jit(solution)/shard_map/ppermute | solution.py:521
  131.7 1.3 copy-start.21
  131.8 11.2 %collective-permute-start.5 = (bf16[528,256]{1,0:T(8,128)(2,1)}, bf16[528,256]{1,0:T(8,128)(2,1)S(1)}, u32[]{:S(2)}, u32[]{:S(2)}) collective-permute-start(bf16[528,256]{1,0:T(8,128)(2,1)} %gate_out.2.refs_1_), channel_id=1, source_target_pairs={{0,8},{4,12},{8,0},{12,4},{1,9},{5,13},{9,1},{13,5},{2,10},{6,14},... | collective-permute-start | bytes 811016 | tf_op jit(solution)/shard_map/ppermute | solution.py:489
  132.4 0.7 copy-start.23
  132.4 15.4 %collective-permute-start.4 = (bf16[528,256]{1,0:T(8,128)(2,1)}, bf16[528,256]{1,0:T(8,128)(2,1)S(1)}, u32[]{:S(2)}, u32[]{:S(2)}) collective-permute-start(bf16[528,256]{1,0:T(8,128)(2,1)} %gate_out.2.refs_1_), channel_id=1, source_target_pairs={{0,4},{4,8},{8,12},{12,0},{1,5},{5,9},{9,13},{13,1},{2,6},{6,10},{... | collective-permute-start | bytes 811016 | tf_op jit(solution)/shard_map/ppermute | solution.py:489
  137.7 18.1 %collective-permute-start.16 = (bf16[528,256]{1,0:T(8,128)(2,1)}, bf16[528,256]{1,0:T(8,128)(2,1)S(1)}, u32[]{:S(2)}, u32[]{:S(2)}) collective-permute-start(bf16[528,256]{1,0:T(8,128)(2,1)} %gate_out.3.refs_6_.refs_1_), channel_id=1, source_target_pairs={{0,3},{1,0},{2,1},{3,2},{4,7},{5,4},{6,5},{7,6},{8,11},{9,8},{10,9... | collective-permute-start | bytes 811016 | tf_op jit(solution)/shard_map/ppermute | solution.py:489
  140.7 16.3 %collective-permute-start.15 = (bf16[528,256]{1,0:T(8,128)(2,1)}, bf16[528,256]{1,0:T(8,128)(2,1)S(1)}, u32[]{:S(2)}, u32[]{:S(2)}) collective-permute-start(bf16[528,256]{1,0:T(8,128)(2,1)} %gate_out.3.refs_6_.refs_1_), channel_id=1, source_target_pairs={{0,2},{1,3},{2,0},{3,1},{4,6},{5,7},{6,4},{7,5},{8,10},{9,11},{10,... | collective-permute-start | bytes 811016 | tf_op jit(solution)/shard_map/ppermute | solution.py:489
  141.2 6.5 %copy-start.30 = (bf16[528,256]{1,0:T(8,128)(2,1)}, bf16[528,256]{1,0:T(8,128)(2,1)S(1)}, u32[]{:S(2)}) copy-start(bf16[528,256]{1,0:T(8,128)(2,1)S(1)} %collective-permute-done.6.refs_4_) | copy-start | bytes 811012
  141.2 15.8 %collective-permute-start.14 = (bf16[528,256]{1,0:T(8,128)(2,1)}, bf16[528,256]{1,0:T(8,128)(2,1)S(1)}, u32[]{:S(2)}, u32[]{:S(2)}) collective-permute-start(bf16[528,256]{1,0:T(8,128)(2,1)} %gate_out.3.refs_6_.refs_1_), channel_id=1, source_target_pairs={{0,1},{1,2},{2,3},{3,0},{4,5},{5,6},{6,7},{7,4},{8,9},{9,10},{10,1... | collective-permute-start | bytes 811016 | tf_op jit(solution)/shard_map/ppermute | solution.py:489
  143.0 4.8 %copy-start.33 = (bf16[528,256]{1,0:T(8,128)(2,1)}, bf16[528,256]{1,0:T(8,128)(2,1)S(1)}, u32[]{:S(2)}) copy-start(bf16[528,256]{1,0:T(8,128)(2,1)S(1)} %collective-permute-done.5.refs_3_) | copy-start | bytes 811012
  147.8 0.7 copy-start.35
  151.7 13.0 %collective-permute-start.11 = (bf16[144,512]{1,0:T(8,128)(2,1)}, bf16[144,512]{1,0:T(8,128)(2,1)S(1)}, u32[]{:S(2)}, u32[]{:S(2)}) collective-permute-start(bf16[144,512]{1,0:T(8,128)(2,1)} %get-tuple-element.36), channel_id=1, source_target_pairs={{0,1},{1,2},{2,3},{3,0},{4,5},{5,6},{6,7},{7,4},{8,9},{9,10},{10,1... | collective-permute-start | bytes 442376 | tf_op jit(solution)/shard_map/ppermute | solution.py:489
  153.4 11.9 %collective-permute-start.12 = (bf16[144,512]{1,0:T(8,128)(2,1)}, bf16[144,512]{1,0:T(8,128)(2,1)S(1)}, u32[]{:S(2)}, u32[]{:S(2)}) collective-permute-start(bf16[144,512]{1,0:T(8,128)(2,1)} %get-tuple-element.37), channel_id=1, source_target_pairs={{0,2},{1,3},{2,0},{3,1},{4,6},{5,7},{6,4},{7,5},{8,10},{9,11},{10,... | collective-permute-start | bytes 442376 | tf_op jit(solution)/shard_map/ppermute | solution.py:489
  155.8 1.2 copy-start.31
  155.8 9.5 %collective-permute-start.13 = (bf16[144,512]{1,0:T(8,128)(2,1)}, bf16[144,512]{1,0:T(8,128)(2,1)S(1)}, u32[]{:S(2)}, u32[]{:S(2)}) collective-permute-start(bf16[144,512]{1,0:T(8,128)(2,1)} %get-tuple-element.38), channel_id=1, source_target_pairs={{0,3},{1,0},{2,1},{3,2},{4,7},{5,4},{6,5},{7,6},{8,11},{9,8},{10,9... | collective-permute-start | bytes 442376 | tf_op jit(solution)/shard_map/ppermute | solution.py:489
  157.0 0.7 copy-start.32
  157.0 0.8 copy-start.34
  157.8 1.0 copy-start
  162.0 9.5 %collective-permute-start.20 = (bf16[144,512]{1,0:T(8,128)(2,1)}, bf16[144,512]{1,0:T(8,128)(2,1)S(1)}, u32[]{:S(2)}, u32[]{:S(2)}) collective-permute-start(bf16[144,512]{1,0:T(8,128)(2,1)} %get-tuple-element.41), channel_id=1, source_target_pairs={{0,4},{4,8},{8,12},{12,0},{1,5},{5,9},{9,13},{13,1},{2,6},{6,10},{... | collective-permute-start | bytes 442376 | tf_op jit(solution)/shard_map/ppermute | solution.py:489
  162.9 8.6 %collective-permute-start.21 = (bf16[144,512]{1,0:T(8,128)(2,1)}, bf16[144,512]{1,0:T(8,128)(2,1)S(1)}, u32[]{:S(2)}, u32[]{:S(2)}) collective-permute-start(bf16[144,512]{1,0:T(8,128)(2,1)} %get-tuple-element.42), channel_id=1, source_target_pairs={{0,8},{4,12},{8,0},{12,4},{1,9},{5,13},{9,1},{13,5},{2,10},{6,14},... | collective-permute-start | bytes 442376 | tf_op jit(solution)/shard_map/ppermute | solution.py:489
  164.7 6.9 %collective-permute-start.22 = (bf16[144,512]{1,0:T(8,128)(2,1)}, bf16[144,512]{1,0:T(8,128)(2,1)S(1)}, u32[]{:S(2)}, u32[]{:S(2)}) collective-permute-start(bf16[144,512]{1,0:T(8,128)(2,1)} %get-tuple-element.43), channel_id=1, source_target_pairs={{0,12},{4,0},{8,4},{12,8},{1,13},{5,1},{9,5},{13,9},{2,14},{6,2},{... | collective-permute-start | bytes 442376 | tf_op jit(solution)/shard_map/ppermute | solution.py:489
  165.3 0.7 copy-start.18
  168.9 6.8 %collective-permute-start.19 = (bf16[144,512]{1,0:T(8,128)(2,1)}, bf16[144,512]{1,0:T(8,128)(2,1)S(1)}, u32[]{:S(2)}, u32[]{:S(2)}) collective-permute-start(bf16[144,512]{1,0:T(8,128)(2,1)} %residual_block.2.refs_1_), channel_id=1, source_target_pairs={{0,12},{4,0},{8,4},{12,8},{1,13},{5,1},{9,5},{13,9},{2,14},{6,2},{... | collective-permute-start | bytes 442376 | tf_op jit(solution)/shard_map/ppermute | solution.py:489
  169.7 6.0 %collective-permute-start.18 = (bf16[144,512]{1,0:T(8,128)(2,1)}, bf16[144,512]{1,0:T(8,128)(2,1)S(1)}, u32[]{:S(2)}, u32[]{:S(2)}) collective-permute-start(bf16[144,512]{1,0:T(8,128)(2,1)} %residual_block.2.refs_1_), channel_id=1, source_target_pairs={{0,8},{4,12},{8,0},{12,4},{1,9},{5,13},{9,1},{13,5},{2,10},{6,14},... | collective-permute-start | bytes 442376 | tf_op jit(solution)/shard_map/ppermute | solution.py:489
  171.5 0.7 copy-start.17
  171.5 6.7 %collective-permute-start.17 = (bf16[144,512]{1,0:T(8,128)(2,1)}, bf16[144,512]{1,0:T(8,128)(2,1)S(1)}, u32[]{:S(2)}, u32[]{:S(2)}) collective-permute-start(bf16[144,512]{1,0:T(8,128)(2,1)} %residual_block.2.refs_1_), channel_id=1, source_target_pairs={{0,4},{4,8},{8,12},{12,0},{1,5},{5,9},{9,13},{13,1},{2,6},{6,10},{... | collective-permute-start | bytes 442376 | tf_op jit(solution)/shard_map/ppermute | solution.py:489
  171.5 0.7 copy-start.19
  175.8 2.5 copy-start.9
  175.8 2.5 copy-start.10
  178.2 0.7 copy-start.11
  180.9 41.3 %collective-permute-start.25 = (bf16[144,2048]{1,0:T(8,128)(2,1)}, bf16[144,2048]{1,0:T(8,128)(2,1)S(1)}, u32[]{:S(2)}, u32[]{:S(2)}) collective-permute-start(bf16[144,2048]{1,0:T(8,128)(2,1)} %join_columns.2.refs_2_), channel_id=1, source_target_pairs={{0,3},{1,0},{2,1},{3,2},{4,7},{5,4},{6,5},{7,6},{8,11},{9,8},{10,9... | collective-permute-start | bytes 1769480 | tf_op jit(solution)/shard_map/ppermute | solution.py:489
  180.9 41.9 %collective-permute-start.24 = (bf16[144,2048]{1,0:T(8,128)(2,1)}, bf16[144,2048]{1,0:T(8,128)(2,1)S(1)}, u32[]{:S(2)}, u32[]{:S(2)}) collective-permute-start(bf16[144,2048]{1,0:T(8,128)(2,1)} %join_columns.2.refs_2_), channel_id=1, source_target_pairs={{0,2},{1,3},{2,0},{3,1},{4,6},{5,7},{6,4},{7,5},{8,10},{9,11},{10,... | collective-permute-start | bytes 1769480 | tf_op jit(solution)/shard_map/ppermute | solution.py:489
  184.6 38.3 %collective-permute-start.23 = (bf16[144,2048]{1,0:T(8,128)(2,1)}, bf16[144,2048]{1,0:T(8,128)(2,1)S(1)}, u32[]{:S(2)}, u32[]{:S(2)}) collective-permute-start(bf16[144,2048]{1,0:T(8,128)(2,1)} %join_columns.2.refs_2_), channel_id=1, source_target_pairs={{0,1},{1,2},{2,3},{3,0},{4,5},{5,6},{6,7},{7,4},{8,9},{9,10},{10,1... | collective-permute-start | bytes 1769480 | tf_op jit(solution)/shard_map/ppermute | solution.py:489
  184.6 25.4 %collective-permute-start.28 = (bf16[144,512]{1,0:T(8,128)(2,1)}, bf16[144,512]{1,0:T(8,128)(2,1)S(1)}, u32[]{:S(2)}, u32[]{:S(2)}) collective-permute-start(bf16[144,512]{1,0:T(8,128)(2,1)} %residual_block.3.refs_5_.refs_1_), channel_id=1, source_target_pairs={{0,3},{1,0},{2,1},{3,2},{4,7},{5,4},{6,5},{7,6},{8,11},{9,8},{10,9... | collective-permute-start | bytes 442376 | tf_op jit(solution)/shard_map/ppermute | solution.py:489
  187.2 28.4 %collective-permute-start.27 = (bf16[144,512]{1,0:T(8,128)(2,1)}, bf16[144,512]{1,0:T(8,128)(2,1)S(1)}, u32[]{:S(2)}, u32[]{:S(2)}) collective-permute-start(bf16[144,512]{1,0:T(8,128)(2,1)} %residual_block.3.refs_5_.refs_1_), channel_id=1, source_target_pairs={{0,2},{1,3},{2,0},{3,1},{4,6},{5,7},{6,4},{7,5},{8,10},{9,11},{10,... | collective-permute-start | bytes 442376 | tf_op jit(solution)/shard_map/ppermute | solution.py:489
  209.9 8.1 %copy-start.12 = (bf16[144,512]{1,0:T(8,128)(2,1)}, bf16[144,512]{1,0:T(8,128)(2,1)S(1)}, u32[]{:S(2)}) copy-start(bf16[144,512]{1,0:T(8,128)(2,1)S(1)} %collective-permute-done.28.refs_4_) | copy-start | bytes 442372
  209.9 8.1 %collective-permute-start.26 = (bf16[144,512]{1,0:T(8,128)(2,1)}, bf16[144,512]{1,0:T(8,128)(2,1)S(1)}, u32[]{:S(2)}, u32[]{:S(2)}) collective-permute-start(bf16[144,512]{1,0:T(8,128)(2,1)} %residual_block.3.refs_5_.refs_1_), channel_id=1, source_target_pairs={{0,1},{1,2},{2,3},{3,0},{4,5},{5,6},{6,7},{7,4},{8,9},{9,10},{10,1... | collective-permute-start | bytes 442376 | tf_op jit(solution)/shard_map/ppermute | solution.py:489
  215.6 2.4 copy-start.13
  220.7 21.0 %collective-permute-start.31 = (bf16[144,2048]{1,0:T(8,128)(2,1)}, bf16[144,2048]{1,0:T(8,128)(2,1)S(1)}, u32[]{:S(2)}, u32[]{:S(2)}) collective-permute-start(bf16[144,2048]{1,0:T(8,128)(2,1)} %join_columns.3.refs_8_.refs_2_), channel_id=1, source_target_pairs={{0,12},{4,0},{8,4},{12,8},{1,13},{5,1},{9,5},{13,9},{2,14},{6,2},{... | collective-permute-start | bytes 1769480 | tf_op jit(solution)/shard_map/ppermute | solution.py:489
  222.2 19.5 %collective-permute-start.30 = (bf16[144,2048]{1,0:T(8,128)(2,1)}, bf16[144,2048]{1,0:T(8,128)(2,1)S(1)}, u32[]{:S(2)}, u32[]{:S(2)}) collective-permute-start(bf16[144,2048]{1,0:T(8,128)(2,1)} %join_columns.3.refs_8_.refs_2_), channel_id=1, source_target_pairs={{0,8},{4,12},{8,0},{12,4},{1,9},{5,13},{9,1},{13,5},{2,10},{6,14},... | collective-permute-start | bytes 1769480 | tf_op jit(solution)/shard_map/ppermute | solution.py:489
  222.3 0.8 copy-start.2
  222.3 29.8 %collective-permute-start.29 = (bf16[144,2048]{1,0:T(8,128)(2,1)}, bf16[144,2048]{1,0:T(8,128)(2,1)S(1)}, u32[]{:S(2)}, u32[]{:S(2)}) collective-permute-start(bf16[144,2048]{1,0:T(8,128)(2,1)} %join_columns.3.refs_8_.refs_2_), channel_id=1, source_target_pairs={{0,4},{4,8},{8,12},{12,0},{1,5},{5,9},{9,13},{13,1},{2,6},{6,10},{... | collective-permute-start | bytes 1769480 | tf_op jit(solution)/shard_map/ppermute | solution.py:489
  222.8 0.8 copy-start.3
  222.8 1.0 copy-start.4
  235.5 29.0 %all-to-all-start.2 = ((f32[16,8,128]{2,1,0:T(8,128)}), f32[16,8,128]{2,1,0:T(8,128)S(1)}, u32[]{:S(2)}, u32[]{:S(2)}) async-start(f32[16,8,128]{2,1,0:T(8,128)} %head_stats.2), calls=%async_computation.2 | async-start | bytes 131072 | tf_op jit(solution)/shard_map/all_to_all | solution.py:540
  241.7 45.0 %copy-start.29 = (s32[4]{0:T(128)S(1)}, s32[4]{0:T(128)}, u32[]{:S(2)}) copy-start(s32[4]{0:T(128)} %param.35) | copy-start | bytes 52
  241.7 10.3 %copy-start.5 = (bf16[144,2048]{1,0:T(8,128)(2,1)}, bf16[144,2048]{1,0:T(8,128)(2,1)S(1)}, u32[]{:S(2)}) copy-start(bf16[144,2048]{1,0:T(8,128)(2,1)S(1)} %collective-permute-done.31.refs_5_) | copy-start | bytes 1769476
  241.7 10.3 %copy-start.6 = (bf16[144,2048]{1,0:T(8,128)(2,1)}, bf16[144,2048]{1,0:T(8,128)(2,1)S(1)}, u32[]{:S(2)}) copy-start(bf16[144,2048]{1,0:T(8,128)(2,1)S(1)} %collective-permute-done.30.refs_4_) | copy-start | bytes 1769476
  252.0 0.8 copy-start.7
  264.5 10.7 %copy-start.8 = (f32[16,8,128]{2,1,0:T(8,128)}, f32[16,8,128]{2,1,0:T(8,128)S(1)}, u32[]{:S(2)}) copy-start(f32[16,8,128]{2,1,0:T(8,128)S(1)} %all-to-all-done.2.s0_ref) | copy-start | bytes 196612
  276.8 9.7 %all-to-all-start.4 = ((f32[8,8,128]{2,1,0:T(8,128)}), f32[8,8,128]{2,1,0:T(8,128)S(1)}, u32[]{:S(2)}, u32[]{:S(2)}) async-start(f32[8,8,128]{2,1,0:T(8,128)} %get-tuple-element.45), calls=%async_computation.4 | async-start | bytes 65536 | tf_op jit(solution)/shard_map/all_to_all | solution.py:542
  (9 other events, 5.8 us)

commit v5 on v4

--- a/solution.py
+++ b/solution.py
@@ -58,10 +58,11 @@
 
 
 def mix_kernel(
-    m, tok_ref, wi_ref, ws_ref, wp_ref, bias_ref, rate_ref, skip_ref, seg_ref,
+    tok_ref, wi_ref, ws_ref, wp_ref, bias_ref, rate_ref, skip_ref, seg_ref,
     y_ref, gate_ref, c_ref, e_ref, pay_ref, val_ref, st_ref, stp_ref,
 ):
-    k = pl.program_id(0)
+    m = pl.program_id(0)
+    k = pl.program_id(1)
     inner = y_ref.shape[1]
 
     @pl.when(k == 0)
@@ -72,14 +73,12 @@
         stp_ref[...] = jnp.zeros_like(stp_ref)
 
     tokens = tok_ref[...]
-    gate_ref[...] += contract(tokens, wi_ref[:, 0, :], ((1,), (0,)))
-    val_ref[...] += contract(tokens, wi_ref[:, 1, :], ((1,), (0,)))
-    state = c_ref.shape[1]
-    st_ref[:, 0:state] += contract(tokens, ws_ref[:, 0, :], ((1,), (0,)))
-    st_ref[:, state:] += contract(tokens, ws_ref[:, 1, :], ((1,), (0,)))
+    gate_ref[...] += contract(tokens, wi_ref[:, 0:inner], ((1,), (0,)))
+    val_ref[...] += contract(tokens, wi_ref[:, inner:], ((1,), (0,)))
+    st_ref[...] += contract(tokens, ws_ref[...], ((1,), (0,)))
     stp_ref[...] += contract(tokens, wp_ref[...], ((1,), (1,)))
 
-    @pl.when(k == pl.num_programs(0) - 1)
+    @pl.when(k == pl.num_programs(1) - 1)
     def _():
         scan_rows(
             m, bias_ref, rate_ref, skip_ref, seg_ref, y_ref, c_ref, e_ref, pay_ref, val_ref, st_ref, stp_ref
@@ -92,10 +91,10 @@
     wide = inner // heads
     state = c_ref.shape[1]
     seg = seg_ref[...]
-    raw = jnp.transpose(stp_ref[...])[0:heads, :] + as_column(bias_ref[m : m + 1, :])
+    raw = jnp.transpose(stp_ref[...])[0:heads, :] + as_column(bias_ref[pl.ds(m, 1), :])
     dt = jnp.maximum(raw, 0.0) + jnp.log1p(jnp.exp(-jnp.abs(raw)))
-    la = -dt * as_column(rate_ref[m : m + 1, :])
-    skip = as_column(skip_ref[m : m + 1, :])
+    la = -dt * as_column(rate_ref[pl.ds(m, 1), :])
+    skip = as_column(skip_ref[pl.ds(m, 1), :])
     lane = lax.broadcasted_iota(jnp.int32, la.shape, 1)
     run = la
     step = 1
@@ -158,35 +157,33 @@
         y_ref[t0 : t0 + SPAN, :] = jnp.concatenate(acc, axis=1)
 
 
-def mix_local(m, hidden, w_inner, w_state, w_step, bias, rate, skip, seg, after=(), chunks=4):
-    rows, depth = hidden.shape[1:]
-    inner = w_inner.shape[3]
-    state = w_state.shape[3]
+def mix_local(hidden, w_inner, w_state, w_step, bias, rate, skip, seg, chunks=4):
+    models, rows, depth = hidden.shape
+    inner = w_inner.shape[2] // 2
+    state = w_state.shape[2] // 2
     heads = bias.shape[1]
     deep = depth // chunks
-    whole = lambda a: pl.BlockSpec(a.shape, lambda k: (0,) * a.ndim)
-    const = lambda shape: pl.BlockSpec(shape, lambda k: (0, 0))
+    whole = lambda a: pl.BlockSpec(a.shape, lambda m, k: (0,) * a.ndim)
     shapes = ((rows, inner), F32), ((rows, inner), F32), ((rows, state), BF16), ((rows, 2 * heads), F32), (
         (inner + 16, state), BF16)
     return pl.pallas_call(
-        drop(functools.partial(mix_kernel, m), 8, len(after)),
-        grid=(chunks,),
+        mix_kernel,
+        grid=(models, chunks),
         in_specs=[
-            pl.BlockSpec((None, rows, deep), lambda k: (m, 0, k)),
-            pl.BlockSpec((None, deep, 2, inner), lambda k: (m, k, 0, 0)),
-            pl.BlockSpec((None, deep, 2, state), lambda k: (m, k, 0, 0)),
-            pl.BlockSpec((None, heads, deep), lambda k: (m, 0, k)),
+            pl.BlockSpec((None, rows, deep), lambda m, k: (m, 0, k)),
+            pl.BlockSpec((None, deep, 2 * inner), lambda m, k: (m, k, 0)),
+            pl.BlockSpec((None, deep, 2 * state), lambda m, k: (m, k, 0)),
+            pl.BlockSpec((None, heads, deep), lambda m, k: (m, 0, k)),
             whole(bias), whole(rate), whole(skip), whole(seg),
-        ]
-        + [ANYWHERE] * len(after),
-        out_specs=[const(shape) for shape, _ in shapes],
-        out_shape=[jax.ShapeDtypeStruct(shape, kind) for shape, kind in shapes],
+        ],
+        out_specs=[pl.BlockSpec((None,) + shape, lambda m, k: (m, 0, 0)) for shape, _ in shapes],
+        out_shape=[jax.ShapeDtypeStruct((models,) + shape, kind) for shape, kind in shapes],
         scratch_shapes=[
             pltpu.VMEM((rows, inner), F32), pltpu.VMEM((rows, 2 * state), F32), pltpu.VMEM((rows, heads), F32)
         ],
-        cost_estimate=pl.CostEstimate(flops=5 * 10**9, bytes_accessed=8 * 10**6, transcendentals=10**6),
+        cost_estimate=pl.CostEstimate(flops=10**10, bytes_accessed=16 * 10**6, transcendentals=2 * 10**6),
         name="mix_local",
-    )(hidden, w_inner, w_state, w_step, bias, rate, skip, seg, *after)
+    )(hidden, w_inner, w_state, w_step, bias, rate, skip, seg)
 
 
 def gate_kernel(
@@ -235,10 +232,11 @@
 
 
 def gate_out(m, pages, flags, y, gate, c, e, recv, pool, gain, after=()):
-    rows, inner = y.shape
+    rows, inner = y.shape[1:]
     heads = pool.shape[2]
-    state = c.shape[1]
+    state = c.shape[2]
     whole = lambda a: pl.BlockSpec(a.shape, lambda g, pg, fl: (0,) * a.ndim)
+    mine = lambda a: pl.BlockSpec((None,) + a.shape[1:], lambda g, pg, fl: (m, 0, 0))
     page = lambda j: pl.BlockSpec(
         (None, None, heads, pool.shape[3], state), lambda g, pg, fl: (m, pg[j], 0, 0, 0)
     )
@@ -247,8 +245,8 @@
         grid_spec=pltpu.PrefetchScalarGridSpec(
             num_scalar_prefetch=2,
             grid=(1,),
-            in_specs=[whole(y), whole(gate), whole(c), whole(e)]
-            + [whole(r) for r in recv]
+            in_specs=[mine(y), mine(gate), mine(c), mine(e)]
+            + [mine(r) for r in recv]
             + [page(j) for j in range(4)]
             + [whole(gain)]
             + [ANYWHERE] * len(after),
@@ -359,68 +357,51 @@
     )(at, *parts, *after)
 
 
-def head_kernel(place_ref, at_ref, x0_ref, x1_ref, x2_ref, x3_ref, w_ref, tgt_ref, out_ref, acc_ref, scale_ref):
+def head_kernel(m, place_ref, at_ref, x0_ref, x1_ref, x2_ref, x3_ref, w_ref, tgt_ref, out_ref, wv_ref, acc_ref, sems):
     block = x0_ref.shape[0] - 16
-    vocab = w_ref.shape[1]
-    step = pl.program_id(0)
+    vocab = w_ref.shape[2]
+    cut = 768
+    spans = (pl.ds(0, cut), pl.ds(cut, vocab - cut))
+    copies = [
+        pltpu.make_async_copy(w_ref.at[m, :, span], wv_ref.at[:, span], sems.at[n]) for n, span in enumerate(spans)
+    ]
+    for copy in copies:
+        copy.start()
     tiles = (x0_ref, x1_ref, x2_ref, x3_ref)
-
-    @pl.when(step == 0)
-    def _():
-        for k, x in enumerate(tiles):
-            line = x[block : block + 16, 0 : 3 * block].astype(F32)[0:1, :]
-            scale_ref[k : k + 1, :] = (
-                line[:, 0:block] + line[:, block : 2 * block] + line[:, 2 * block : 3 * block]
+    for copy, span in zip(copies, spans):
+        copy.wait()
+        for n in range(2):
+            rows = jnp.concatenate([x[0:block, :] for x in tiles[2 * n : 2 * n + 2]], axis=0)
+            acc_ref[2 * n * block : 2 * (n + 1) * block, span] = contract(rows, wv_ref[:, span], ((1,), (0,)))
+    for k, x in enumerate(tiles):
+        at = lax.rem(at_ref[1] + 4 - k, 4)
+        line = x[block : block + 16, 0 : 3 * block].astype(F32)[0:1, :]
+        scale = to_column(line[:, 0:block] + line[:, block : 2 * block] + line[:, 2 * block : 3 * block])
+        logits = acc_ref[k * block : (k + 1) * block, :] * scale
+        top = jnp.max(logits, axis=1, keepdims=True)
+        lse = top + jnp.log(jnp.sum(jnp.exp(logits - top), axis=1, keepdims=True))
+        target = to_column((tgt_ref[pl.ds(at, 1), :] - place_ref[0] * vocab).astype(F32)).astype(jnp.int32)
+        column = lax.broadcasted_iota(jnp.int32, logits.shape, 1)
+        chosen = jnp.sum(jnp.where(column == target, logits, 0.0), axis=1, keepdims=True)
+        for which, value in enumerate((lse, chosen)):
+            out_ref[:, pl.ds(which * 4 + at, 1), :] = jnp.broadcast_to(
+                to_row(value)[None], (out_ref.shape[0], 1, block)
             )
 
-    for n in range(2):
-        rows = jnp.concatenate([x[0:block, :] for x in tiles[2 * n : 2 * n + 2]], axis=0)
-        raw = contract(rows, w_ref[...], ((1,), (0,)))
-        span = slice(2 * n * block, 2 * (n + 1) * block)
-
-        @pl.when(step == 0)
-        def _():
-            acc_ref[span, :] = raw
-
-        @pl.when(step > 0)
-        def _():
-            acc_ref[span, :] += raw
-
-    @pl.when(step == pl.num_programs(0) - 1)
-    def _():
-        for k in range(4):
-            at = lax.rem(at_ref[1] + 4 - k, 4)
-            logits = acc_ref[k * block : (k + 1) * block, :] * to_column(scale_ref[k : k + 1, :])
-            top = jnp.max(logits, axis=1, keepdims=True)
-            lse = top + jnp.log(jnp.sum(jnp.exp(logits - top), axis=1, keepdims=True))
-            target = to_column((tgt_ref[pl.ds(at, 1), :] - place_ref[0] * vocab).astype(F32))
-            column = lax.broadcasted_iota(jnp.int32, logits.shape, 1).astype(F32)
-            chosen = jnp.sum(jnp.where(column == target, logits, 0.0), axis=1, keepdims=True)
-            for which, value in enumerate((lse, chosen)):
-                out_ref[:, pl.ds(which * 4 + at, 1), :] = jnp.broadcast_to(
-                    to_row(value)[None], (out_ref.shape[0], 1, block)
-                )
-
-
-def head_stats(m, place, at, parts, head, tgt, group, after=(), chunks=4):
+
+def head_stats(m, place, at, parts, head, tgt, group, after=()):
     tall, depth = parts[0].shape
     block = tall - 16
     vocab = head.shape[2]
-    deep = depth // chunks
-    return pl.pallas_call(
-        drop(head_kernel, 8, len(after)),
-        grid_spec=pltpu.PrefetchScalarGridSpec(
-            num_scalar_prefetch=2,
-            grid=(chunks,),
-            in_specs=[pl.BlockSpec((tall, deep), lambda i, pf, at: (0, i))] * 4
-            + [
-                pl.BlockSpec((None, deep, vocab), lambda i, pf, at: (m, i, 0)),
-                pl.BlockSpec(tgt.shape, lambda i, pf, at: (0, 0)),
-            ]
-            + [ANYWHERE] * len(after),
-            out_specs=pl.BlockSpec((group, 8, block), lambda i, pf, at: (0, 0, 0)),
-            scratch_shapes=[pltpu.VMEM((4 * block, vocab), F32), pltpu.VMEM((4, block), F32)],
-        ),
+    vm = pl.BlockSpec(memory_space=pltpu.VMEM)
+    sm = pl.BlockSpec(memory_space=pltpu.SMEM)
+    return pl.pallas_call(
+        drop(functools.partial(head_kernel, m), 8, len(after)),
+        in_specs=[sm, sm] + [vm] * 4 + [ANYWHERE, vm] + [ANYWHERE] * len(after),
+        out_specs=vm,
+        scratch_shapes=[
+            pltpu.VMEM((depth, vocab), BF16), pltpu.VMEM((4 * block, vocab), F32), pltpu.SemaphoreType.DMA((2,))
+        ],
         out_shape=jax.ShapeDtypeStruct((group, 8, block), F32),
         cost_estimate=pl.CostEstimate(
             flops=8 * block * depth * vocab, bytes_accessed=2 * depth * vocab, transcendentals=4 * block * vocab
@@ -459,28 +440,20 @@
     )(s0, s1, live, seg)
 
 
-def turn_kernel(w_ref, out0_ref, out1_ref, sems):
-    width = out0_ref.shape[2]
-    copies = [
-        pltpu.make_async_copy(w_ref.at[m, :, pl.ds(j * width, width)], out.at[j], sems.at[m * 4 + j])
-        for m, out in enumerate((out0_ref, out1_ref))
-        for j in range(4)
-    ]
-    for copy in copies:
-        copy.start()
-    for copy in copies:
-        copy.wait()
-
-
-def turned(w_out):
+def turn_kernel(w_ref, out_ref):
+    out_ref[...] = w_ref[...]
+
+
+def turned(m, w_out):
     _, inner, depth = w_out.shape
+    width = depth // 4
     return pl.pallas_call(
         turn_kernel,
-        in_specs=[ANYWHERE],
-        out_specs=[ANYWHERE] * 2,
-        out_shape=[jax.ShapeDtypeStruct((4, inner, depth // 4), w_out.dtype)] * 2,
-        scratch_shapes=[pltpu.SemaphoreType.DMA((8,))],
-        cost_estimate=pl.CostEstimate(flops=0, bytes_accessed=4 * 10**6, transcendentals=0),
+        grid=(4,),
+        in_specs=[pl.BlockSpec((None, inner, width), lambda j: (m, 0, j))],
+        out_specs=pl.BlockSpec((None, inner, width), lambda j: (j, 0, 0)),
+        out_shape=jax.ShapeDtypeStruct((4, inner, width), w_out.dtype),
+        cost_estimate=pl.CostEstimate(flops=0, bytes_accessed=2 * 10**6, transcendentals=0),
         name="turned",
     )(w_out)
 
@@ -505,36 +478,28 @@
     place = lax.axis_index(VOC).astype(jnp.int32).reshape(1)
     seg = segment_ids.reshape(1, rows)
     tgt = targets.reshape(4, rows // 4)
+    w_inner = w_inner.reshape(2, depth, 2 * inner)
+    w_state = w_state.reshape(2, depth, -1)
     w_step = jnp.swapaxes(w_step, 1, 2)
     ways = (("x", "z"), ("z", "x"))
     both = range(2)
     at = [
         jnp.stack([lax.axis_index(along), lax.axis_index(across)]).astype(jnp.int32) for along, across in ways
     ]
-    turns = turned(w_out)
-    weights = [lax.all_to_all(turns[m], ways[m][0], 0, 0) for m in both]
-
-    def mix(m, after):
-        y, gate, c, e, pay = mix_local(
-            m, hidden, w_inner, w_state, w_step, step_bias, rate, skip_gain, seg, after
-        )
-        recv = [lax.ppermute(pay, SEQ, [(i, i + k) for i in range(devices - k)]) for k in range(1, REACH + 1)]
-        return y, gate, c, e, recv
-
-    mixed = [None, None]
-    mixed[0] = mix(0, ())
-    mixed[1] = mix(1, (mixed[0][2],))
+    weights = [lax.all_to_all(turned(m, w_out), ways[m][0], 0, 0) for m in both]
+    y, gate, c, e, pay = mix_local(hidden, w_inner, w_state, w_step, step_bias, rate, skip_gain, seg)
+    recv = [lax.ppermute(pay, SEQ, [(i, i + k) for i in range(devices - k)]) for k in range(1, REACH + 1)]
     gated, parts, res, full, stats = [], [], [], [], []
     for m in both:
-        y, gate, c, e, recv = mixed[m]
-        gated.append(gate_out(m, pages, flags, y, gate, c, e, recv, pool, norm_gain, (mixed[1][2],)))
+        gated.append(gate_out(m, pages, flags, y, gate, c, e, recv, pool, norm_gain, tuple(gated)))
     for m in both:
         out = out_blocks(at[m], gathered(gated[m], ways[m][0]), weights[m], (gated[1],))
         parts.append([out[0]] + [ring(out[k], ways[m][1], k) for k in (1, 2, 3)])
     for m in both:
         res.append(residual_block(m, at[m], parts[m], hidden, final_gain, inner * group, (parts[1][0],)))
+    blocks = [gathered(res[m], ways[m][0]) for m in both]
     for m in both:
-        full.append(join_columns(at[m], gathered(res[m], ways[m][0]), (res[1],)))
+        full.append(join_columns(at[m], blocks[m], tuple(blocks[1 - m][1:])))
     for m in both:
         stat = head_stats(m, place, at[m], gathered(full[m], ways[m][1]), head, tgt, group, (full[1],))
         stats.append(lax.all_to_all(stat, VOC, 0, 0))

time: 288 us -> 204 us (0.71)
  Pallas kernels: 143 us -> 67.1 us
  waiting for transfers between devices: 47.6 us -> 32.5 us
  local copies, waits for them, and re-layouts: 9.02 us -> 19.1 us
  starting transfers between devices: 73.6 us -> 67.8 us
    pallas_call x5, Pallas kernels: 118 us -> 41.2 us  [the longest x2 18 us: head_stats(): pl.pallas_call(drop(functools.partial(head_kernel, m), 8, len(after)), in...]
    ppermute x24, waiting for transfers between devices: 42.7 us -> 27.8 us  [ring(): return lax.ppermute(value, axis, [(i, (i + by) % 4) for i in range(4)])]
    reshape x0 -> x2, local copies, waits for them, and re-layouts: none -> 10.4 us  [the longest x1 7.76 us: per_device(): w_inner = w_inner.reshape(2, depth, 2 * inner)]
    ppermute x8 -> x4, starting transfers between devices: 19 us -> 12.1 us  [per_device(): lax.ppermute(pay, SEQ, [(i, i + k) for i in range(devices - k)])]
    unnamed x74 -> x68, local copies, waits for them, and re-layouts: 9.02 us -> 8.68 us
  transfers between devices with their start and end apart: 36 -> 32, of which waited for: 7 -> 8; matrix products, arithmetic and copies ran while one was open for 0% -> 6% of each run, Pallas kernels for 26% -> 30%
where the time goes in v5:
time: 204 us; the launch traced here: 202 us
  starting transfers between devices  67.8 us (33%)
  Pallas kernels  67.1 us (33%)
  waiting for transfers between devices  32.5 us (16%)
  local copies, waits for them, and re-layouts  19.1 us (9%)
  blocking collectives  13.3 us (7%)
    ppermute x24, starting transfers between devices, ring(): return lax.ppermute(value, axis, [(i, (i + by) % 4) for i in range(4)])  33.6 us
    ppermute x24, waiting for transfers between devices, ring(): return lax.ppermute(value, axis, [(i, (i + by) % 4) for i in range(4)])  27.8 us
    pallas_call x2, Pallas kernels, head_stats(): pl.pallas_call(drop(functools.partial(head_kernel, m), 8, len(after)), in...  18 us
    pallas_call x1, Pallas kernels, mix_local(): pl.pallas_call(mix_kernel, grid=(models, chunks), in_specs=[pl.BlockSpec(...  16.5 us
    all_to_all x1, blocking collectives, per_device(): stats.append(lax.all_to_all(stat, VOC, 0, 0))  13.3 us
    ppermute x4, starting transfers between devices, per_device(): lax.ppermute(pay, SEQ, [(i, i + k) for i in range(devices - k)])  12.1 us
    all_to_all x2, starting transfers between devices, per_device(): weights = [lax.all_to_all(turned(m, w_out), ways[m][0], 0, 0) for m in both]  9.87 us
    unnamed x68, local copies, waits for them, and re-layouts  8.68 us
  transfers between devices with their start and end apart: 32, of which 8 were waited for; matrix products, arithmetic and copies ran while one was open for 6% of the time, Pallas kernels for 30%

profile of v5, /device:TPU:1, one launch (start us, length us, event | category | flops | bytes accessed | tf_op | source)
XLA Modules:
  0.0 202.4 jit_solution(10480507724641085431)
XLA Ops:
  0.6 3.3 %turned.3 = bf16[4,256,512]{2,1,0:T(8,128)(2,1)} custom-call(bf16[2,256,2048]{2,1,0:T(8,128)(2,1)} %w_ref.3), custom_call_target="tpu_custom_call" | custom-call | bytes 2000000 | tf_op jit(solution)/shard_map/turned/pallas_call | solution.py:450
  4.0 5.9 %all-to-all-start.1 = ((bf16[4,256,512]{2,1,0:T(8,128)(2,1)}), bf16[4,256,512]{2,1,0:T(8,128)(2,1)S(1)}, u32[]{:S(2)}, u32[]{:S(2)}) async-start(bf16[4,256,512]{2,1,0:T(8,128)(2,1)} %turned.3), calls=%async_computation.1 | async-start | bytes 2097152 | tf_op jit(solution)/shard_map/all_to_all | solution.py:489
  9.8 7.8 %reshape.26.wi_ref = bf16[2,2048,512]{2,1,0:T(8,128)(2,1)} reshape(bf16[2,2048,2,256]{3,2,1,0:T(2,128)(2,1)} %param.19) | data formatting | bytes 8388608 | tf_op jit(solution)/shard_map/reshape | solution.py:481
  17.6 2.6 %reshape.27.ws_ref = bf16[2,2048,256]{2,1,0:T(8,128)(2,1)} reshape(bf16[2,2048,2,128]{3,2,1,0:T(2,128)(2,1)S(1)} %copy-done) | data formatting | bytes 4194304 | tf_op jit(solution)/shard_map/reshape | solution.py:482
  20.2 16.5 %mix_local.1 = (f32[2,512,256]{2,1,0:T(8,128)}, f32[2,512,256]{2,1,0:T(8,128)}, bf16[2,512,128]{2,1,0:T(8,128)(2,1)}, f32[2,512,8]{2,1,0:T(8,128)}, bf16[2,272,128]{2,1,0:T(8,128)(2,1)}) custom-call(bf16[2,512,2048]{2,1,0:T(8,128)(2,1)} %refs_5_.3, bf16[2,2048,512]{2,1,0:T(8,128)(2,1)} %reshape.26.wi_ref, bf16[2,2048,256]{2,1,0:T(8,128)(2,1)} %reshape.27.ws_ref, ...), custom_call_target="tpu_custom_call" | custom-call | flops 10000000000 | bytes 16000000 | tf_op jit(solution)/shard_map/mix_local/pallas_call | solution.py:169
  36.7 4.0 %collective-permute-start = (bf16[2,272,128]{2,1,0:T(8,128)(2,1)}, bf16[2,272,128]{2,1,0:T(8,128)(2,1)S(1)}, u32[]{:S(2)}, u32[]{:S(2)}) collective-permute-start(bf16[2,272,128]{2,1,0:T(8,128)(2,1)} %get-tuple-element.21), channel_id=1, source_target_pairs={{0,16},{16,32},{32,48},{48,64},{64,80},{80,96},{96,112},{1,17},{17... | collective-permute-start | bytes 417800 | tf_op jit(solution)/shard_map/ppermute | solution.py:491
  40.7 3.2 %collective-permute-start.1 = (bf16[2,272,128]{2,1,0:T(8,128)(2,1)}, bf16[2,272,128]{2,1,0:T(8,128)(2,1)S(1)}, u32[]{:S(2)}, u32[]{:S(2)}) collective-permute-start(bf16[2,272,128]{2,1,0:T(8,128)(2,1)} %get-tuple-element.21), channel_id=1, source_target_pairs={{0,32},{16,48},{32,64},{48,80},{64,96},{80,112},{1,33},{17,49},{33... | collective-permute-start | bytes 417800 | tf_op jit(solution)/shard_map/ppermute | solution.py:491
  43.9 3.5 %collective-permute-start.2 = (bf16[2,272,128]{2,1,0:T(8,128)(2,1)}, bf16[2,272,128]{2,1,0:T(8,128)(2,1)S(1)}, u32[]{:S(2)}, u32[]{:S(2)}) collective-permute-start(bf16[2,272,128]{2,1,0:T(8,128)(2,1)} %get-tuple-element.21), channel_id=1, source_target_pairs={{0,48},{16,64},{32,80},{48,96},{64,112},{1,49},{17,65},{33,81},{49... | collective-permute-start | bytes 417800 | tf_op jit(solution)/shard_map/ppermute | solution.py:491
  47.5 1.3 collective-permute-start.3
  48.8 3.4 %turned.2 = bf16[4,256,512]{2,1,0:T(8,128)(2,1)} custom-call(bf16[2,256,2048]{2,1,0:T(8,128)(2,1)} %w_ref.3), custom_call_target="tpu_custom_call" | custom-call | bytes 2000000 | tf_op jit(solution)/shard_map/turned/pallas_call | solution.py:450
  52.1 4.0 %all-to-all-start = ((bf16[4,256,512]{2,1,0:T(8,128)(2,1)}), bf16[4,256,512]{2,1,0:T(8,128)(2,1)S(1)}, u32[]{:S(2)}, u32[]{:S(2)}) async-start(bf16[4,256,512]{2,1,0:T(8,128)(2,1)} %turned.2), calls=%async_computation | async-start | bytes 2097152 | tf_op jit(solution)/shard_map/all_to_all | solution.py:489
  56.2 0.6 copy-done.16
  57.0 4.0 %gate_out.2.refs_15_.refs_1_ = bf16[528,256]{1,0:T(8,128)(2,1)} custom-call(s32[4]{0:T(128)} %refs_0_.3, s32[4]{0:T(128)} %refs_1_.3, f32[2,512,256]{2,1,0:T(8,128)} %get-tuple-element.17.refs_2_, f32[2,512,256]{2,1,0:T(8,128)} %get-tuple-element.18.refs_3_, bf16[2,512,128]{2,1,0:T(8,128)(2,1)} %get-tuple-element.19.refs_4_, ...), custom_call_target="tpu_custom_call" | custom-call | flops 1000000000 | bytes 4000000 | tf_op jit(solution)/shard_map/gate_out/pallas_call | solution.py:243
  60.9 4.1 %gate_out.3.refs_6_.refs_1_ = bf16[528,256]{1,0:T(8,128)(2,1)} custom-call(s32[4]{0:T(128)} %refs_0_.3, s32[4]{0:T(128)} %refs_1_.3, f32[2,512,256]{2,1,0:T(8,128)} %get-tuple-element.17.refs_2_, f32[2,512,256]{2,1,0:T(8,128)} %get-tuple-element.18.refs_3_, bf16[2,512,128]{2,1,0:T(8,128)(2,1)} %get-tuple-element.19.refs_4_, ...), custom_call_target="tpu_custom_call" | custom-call | flops 1000000000 | bytes 4000000 | tf_op jit(solution)/shard_map/gate_out/pallas_call | solution.py:243
  65.1 1.7 collective-permute-start.10
  66.8 2.4 %collective-permute-start.11 = (bf16[528,256]{1,0:T(8,128)(2,1)}, bf16[528,256]{1,0:T(8,128)(2,1)S(1)}, u32[]{:S(2)}, u32[]{:S(2)}) collective-permute-start(bf16[528,256]{1,0:T(8,128)(2,1)} %gate_out.3.refs_6_.refs_1_), channel_id=1, source_target_pairs={{0,2},{1,3},{2,0},{3,1},{4,6},{5,7},{6,4},{7,5},{8,10},{9,11},{10,... | collective-permute-start | bytes 811016 | tf_op jit(solution)/shard_map/ppermute | solution.py:462
  69.2 1.2 collective-permute-start.12
  70.4 1.5 collective-permute-start.4
  71.9 2.4 %collective-permute-start.5 = (bf16[528,256]{1,0:T(8,128)(2,1)S(1)}, bf16[528,256]{1,0:T(8,128)(2,1)S(1)}, u32[]{:S(2)}, u32[]{:S(2)}) collective-permute-start(bf16[528,256]{1,0:T(8,128)(2,1)S(1)} %copy-done.1), channel_id=1, source_target_pairs={{0,8},{4,12},{8,0},{12,4},{1,9},{5,13},{9,1},{13,5},{2,10},{6,14},... | collective-permute-start | bytes 811016 | tf_op jit(solution)/shard_map/ppermute | solution.py:462
  74.3 1.9 collective-permute-start.6
  76.1 0.6 pad_add_fusion.1.refs_0_.refs_1_
  76.7 3.7 %collective-permute-done.11.refs_3_ = bf16[528,256]{1,0:T(8,128)(2,1)S(1)} collective-permute-done((bf16[528,256]{1,0:T(8,128)(2,1)}, bf16[528,256]{1,0:T(8,128)(2,1)S(1)}, u32[]{:S(2)}, u32[]{:S(2)}) %collective-permute-start.11) | collective-permute-done | bytes 270368 | tf_op jit(solution)/shard_map/ppermute | solution.py:462
  80.5 0.6 copy-done.32
  81.1 0.7 copy-done.33
  81.9 3.2 %out_blocks.3 = (bf16[144,512]{1,0:T(8,128)(2,1)}, bf16[144,512]{1,0:T(8,128)(2,1)}, bf16[144,512]{1,0:T(8,128)(2,1)}, bf16[144,512]{1,0:T(8,128)(2,1)}) custom-call(s32[2]{0:T(128)} %pad_add_fusion.1.refs_0_.refs_1_, bf16[528,256]{1,0:T(8,128)(2,1)} %gate_out.3.refs_6_.refs_1_, bf16[528,256]{1,0:T(8,128)(2,1)} %copy-done.31, bf16[528,256]{1,0:T(8,128)(2,1)} %copy-done.32, ...), custom_call_target="tpu_custom_call" | custom-call | flops 1000000000 | bytes 3000000 | tf_op jit(solution)/shard_map/out_blocks/pallas_call | solution.py:286
  85.1 1.2 collective-permute-start.16
  86.2 2.4 %collective-permute-start.17 = (bf16[144,512]{1,0:T(8,128)(2,1)}, bf16[144,512]{1,0:T(8,128)(2,1)S(1)}, u32[]{:S(2)}, u32[]{:S(2)}) collective-permute-start(bf16[144,512]{1,0:T(8,128)(2,1)} %get-tuple-element.28), channel_id=1, source_target_pairs={{0,8},{4,12},{8,0},{12,4},{1,9},{5,13},{9,1},{13,5},{2,10},{6,14},... | collective-permute-start | bytes 442376 | tf_op jit(solution)/shard_map/ppermute | solution.py:462
  88.6 1.2 collective-permute-start.18
  89.8 0.6 pad_add_fusion.refs_0_.refs_1_
  90.4 0.7 copy-done.29
  91.2 1.0 copy-done.3
  92.2 3.2 %out_blocks.2 = (bf16[144,512]{1,0:T(8,128)(2,1)}, bf16[144,512]{1,0:T(8,128)(2,1)}, bf16[144,512]{1,0:T(8,128)(2,1)}, bf16[144,512]{1,0:T(8,128)(2,1)}) custom-call(s32[2]{0:T(128)} %pad_add_fusion.refs_0_.refs_1_, bf16[528,256]{1,0:T(8,128)(2,1)} %gate_out.2.refs_15_.refs_1_, bf16[528,256]{1,0:T(8,128)(2,1)} %copy-done.28, bf16[528,256]{1,0:T(8,128)(2,1)} %copy-done.29, ...), custom_call_target="tpu_custom_call" | custom-call | flops 1000000000 | bytes 3000000 | tf_op jit(solution)/shard_map/out_blocks/pallas_call | solution.py:286
  95.4 1.2 collective-permute-start.7
  96.6 2.6 %collective-permute-start.8 = (bf16[144,512]{1,0:T(8,128)(2,1)}, bf16[144,512]{1,0:T(8,128)(2,1)S(1)}, u32[]{:S(2)}, u32[]{:S(2)}) collective-permute-start(bf16[144,512]{1,0:T(8,128)(2,1)} %get-tuple-element.24), channel_id=1, source_target_pairs={{0,2},{1,3},{2,0},{3,1},{4,6},{5,7},{6,4},{7,5},{8,10},{9,11},{10,... | collective-permute-start | bytes 442376 | tf_op jit(solution)/shard_map/ppermute | solution.py:462
  99.3 0.6 copy-done.21
  100.0 2.8 %residual_block.3.refs_1_ = bf16[144,512]{1,0:T(8,128)(2,1)} custom-call(s32[2]{0:T(128)} %pad_add_fusion.1.refs_0_.refs_1_, bf16[144,512]{1,0:T(8,128)(2,1)} %get-tuple-element.26.refs_7_.refs_1_, bf16[144,512]{1,0:T(8,128)(2,1)} %copy-done.21, bf16[144,512]{1,0:T(8,128)(2,1)} %copy-done.22, bf16[144,512]{1,0:T(8,128)(2,1)} %copy-done.24, ...), custom_call_target="tpu_custom_call" | custom-call | flops 1000000 | bytes 1000000 | tf_op jit(solution)/shard_map/residual_block/pallas_call | solution.py:314
  102.8 1.4 collective-permute-start.19
  104.6 2.0 %collective-permute-start.21 = (bf16[144,512]{1,0:T(8,128)(2,1)}, bf16[144,512]{1,0:T(8,128)(2,1)S(1)}, u32[]{:S(2)}, u32[]{:S(2)}) collective-permute-start(bf16[144,512]{1,0:T(8,128)(2,1)} %residual_block.3.refs_1_), channel_id=1, source_target_pairs={{0,3},{1,0},{2,1},{3,2},{4,7},{5,4},{6,5},{7,6},{8,11},{9,8},{10,9... | collective-permute-start | bytes 442376 | tf_op jit(solution)/shard_map/ppermute | solution.py:462
  106.7 0.6 copy-done.25
  107.4 2.8 %residual_block.2.refs_1_ = bf16[144,512]{1,0:T(8,128)(2,1)} custom-call(s32[2]{0:T(128)} %pad_add_fusion.refs_0_.refs_1_, bf16[144,512]{1,0:T(8,128)(2,1)} %get-tuple-element.22.refs_1_, bf16[144,512]{1,0:T(8,128)(2,1)} %copy-done.23, bf16[144,512]{1,0:T(8,128)(2,1)} %copy-done.25, bf16[144,512]{1,0:T(8,128)(2,1)} %copy-done.26, ...), custom_call_target="tpu_custom_call" | custom-call | flops 1000000 | bytes 1000000 | tf_op jit(solution)/shard_map/residual_block/pallas_call | solution.py:314
  110.5 0.9 collective-permute-start.14
  111.4 1.6 collective-permute-start.15
  113.0 4.2 %collective-permute-done.13.refs_2_.refs_5_ = bf16[144,512]{1,0:T(8,128)(2,1)S(1)} collective-permute-done((bf16[144,512]{1,0:T(8,128)(2,1)}, bf16[144,512]{1,0:T(8,128)(2,1)S(1)}, u32[]{:S(2)}, u32[]{:S(2)}) %collective-permute-start.13) | collective-permute-done | bytes 147488 | tf_op jit(solution)/shard_map/ppermute | solution.py:462
  117.2 0.6 collective-permute-done.15.refs_4_.refs_7_
  117.9 0.7 copy-done.15
  118.6 2.0 %join_columns.3.refs_8_.refs_2_ = bf16[144,2048]{1,0:T(8,128)(2,1)} custom-call(s32[2]{0:T(128)} %pad_add_fusion.1.refs_0_.refs_1_, bf16[144,512]{1,0:T(8,128)(2,1)} %residual_block.3.refs_1_, bf16[144,512]{1,0:T(8,128)(2,1)} %copy-done.10, bf16[144,512]{1,0:T(8,128)(2,1)} %copy-done.11, bf16[144,512]{1,0:T(8,128)(2,1)} %copy-done.12, ...), custom_call_target="tpu_custom_call" | custom-call | flops 100000 | bytes 1000000 | tf_op jit(solution)/shard_map/join_columns/pallas_call | solution.py:350
  120.6 3.2 %collective-permute-start.26 = (bf16[144,2048]{1,0:T(8,128)(2,1)}, bf16[144,2048]{1,0:T(8,128)(2,1)S(1)}, u32[]{:S(2)}, u32[]{:S(2)}) collective-permute-start(bf16[144,2048]{1,0:T(8,128)(2,1)} %join_columns.3.refs_8_.refs_2_), channel_id=1, source_target_pairs={{0,8},{4,12},{8,0},{12,4},{1,9},{5,13},{9,1},{13,5},{2,10},{6,14},... | collective-permute-start | bytes 1769480 | tf_op jit(solution)/shard_map/ppermute | solution.py:462
  123.9 2.0 join_columns.2.refs_2_
  125.9 2.0 %collective-permute-start.23 = (bf16[144,2048]{1,0:T(8,128)(2,1)}, bf16[144,2048]{1,0:T(8,128)(2,1)S(1)}, u32[]{:S(2)}, u32[]{:S(2)}) collective-permute-start(bf16[144,2048]{1,0:T(8,128)(2,1)} %join_columns.2.refs_2_), channel_id=1, source_target_pairs={{0,2},{1,3},{2,0},{3,1},{4,6},{5,7},{6,4},{7,5},{8,10},{9,11},{10,... | collective-permute-start | bytes 1769480 | tf_op jit(solution)/shard_map/ppermute | solution.py:462
  127.9 2.8 %collective-permute-done.25.refs_3_ = bf16[144,2048]{1,0:T(8,128)(2,1)S(1)} collective-permute-done((bf16[144,2048]{1,0:T(8,128)(2,1)}, bf16[144,2048]{1,0:T(8,128)(2,1)S(1)}, u32[]{:S(2)}, u32[]{:S(2)}) %collective-permute-start.25) | collective-permute-done | bytes 589856 | tf_op jit(solution)/shard_map/ppermute | solution.py:462
  130.8 2.1 %collective-permute-start.24 = (bf16[144,2048]{1,0:T(8,128)(2,1)}, bf16[144,2048]{1,0:T(8,128)(2,1)S(1)}, u32[]{:S(2)}, u32[]{:S(2)}) collective-permute-start(bf16[144,2048]{1,0:T(8,128)(2,1)} %join_columns.2.refs_2_), channel_id=1, source_target_pairs={{0,3},{1,0},{2,1},{3,2},{4,7},{5,4},{6,5},{7,6},{8,11},{9,8},{10,9... | collective-permute-start | bytes 1769480 | tf_op jit(solution)/shard_map/ppermute | solution.py:462
  132.9 11.0 %collective-permute-done.26.refs_4_ = bf16[144,2048]{1,0:T(8,128)(2,1)S(1)} collective-permute-done((bf16[144,2048]{1,0:T(8,128)(2,1)}, bf16[144,2048]{1,0:T(8,128)(2,1)S(1)}, u32[]{:S(2)}, u32[]{:S(2)}) %collective-permute-start.26) | collective-permute-done | bytes 589856 | tf_op jit(solution)/shard_map/ppermute | solution.py:462
  143.9 5.3 %collective-permute-done.27.refs_5_ = bf16[144,2048]{1,0:T(8,128)(2,1)S(1)} collective-permute-done((bf16[144,2048]{1,0:T(8,128)(2,1)}, bf16[144,2048]{1,0:T(8,128)(2,1)S(1)}, u32[]{:S(2)}, u32[]{:S(2)}) %collective-permute-start.27) | collective-permute-done | bytes 589856 | tf_op jit(solution)/shard_map/ppermute | solution.py:462
  149.2 0.8 copy-done.8
  150.0 9.0 %head_stats.3 = f32[16,8,128]{2,1,0:T(8,128)} custom-call(s32[1]{0:T(128)} %bitcast.refs_0_, s32[2]{0:T(128)} %pad_add_fusion.1.refs_0_.refs_1_, bf16[144,2048]{1,0:T(8,128)(2,1)} %join_columns.3.refs_8_.refs_2_, bf16[144,2048]{1,0:T(8,128)(2,1)} %copy-done.5, bf16[144,2048]{1,0:T(8,128)(2,1)} %copy-done.7, bf16[144,2048]{1,0:T(8,128)(2,1)} %copy-done.8, ...), custom_call_target="tpu_custom_call" | custom-call | flops 3489660928 | bytes 6815744 | tf_op jit(solution)/shard_map/head_stats/pallas_call | solution.py:398
  159.0 5.7 %all-to-all-start.3 = ((f32[16,8,128]{2,1,0:T(8,128)}), f32[16,8,128]{2,1,0:T(8,128)S(1)}, u32[]{:S(2)}, u32[]{:S(2)}) async-start(f32[16,8,128]{2,1,0:T(8,128)} %head_stats.3), calls=%async_computation.3 | async-start | bytes 131072 | tf_op jit(solution)/shard_map/all_to_all | solution.py:505
  164.8 0.8 copy-done.4
  165.8 0.8 copy-done.9
  166.6 9.0 %head_stats.2 = f32[16,8,128]{2,1,0:T(8,128)} custom-call(s32[1]{0:T(128)} %bitcast.refs_0_, s32[2]{0:T(128)} %pad_add_fusion.refs_0_.refs_1_, bf16[144,2048]{1,0:T(8,128)(2,1)} %join_columns.2.refs_2_, bf16[144,2048]{1,0:T(8,128)(2,1)} %copy-done.4, bf16[144,2048]{1,0:T(8,128)(2,1)} %copy-done.6, bf16[144,2048]{1,0:T(8,128)(2,1)} %copy-done.9, ...), custom_call_target="tpu_custom_call" | custom-call | flops 3489660928 | bytes 6815744 | tf_op jit(solution)/shard_map/head_stats/pallas_call | solution.py:398
  175.6 13.3 %all_to_all.25.s0_ref = f32[16,8,128]{2,1,0:T(8,128)} all-to-all(f32[16,8,128]{2,1,0:T(8,128)} %head_stats.2), channel_id=1, replica_groups=mesh['y'=4,'core'=2,'x'=4,'z'=4] {'x','z'}, dimensions={0} | all-to-all | bytes 131072 | tf_op jit(solution)/shard_map/all_to_all | solution.py:505
  188.9 1.6 token_diffs.1
  190.5 6.5 %all-to-all-start.4 = ((f32[8,8,128]{2,1,0:T(8,128)}), f32[8,8,128]{2,1,0:T(8,128)S(1)}, u32[]{:S(2)}, u32[]{:S(2)}) async-start(f32[8,8,128]{2,1,0:T(8,128)} %get-tuple-element.31), calls=%async_computation.4 | async-start | bytes 65536 | tf_op jit(solution)/shard_map/all_to_all | solution.py:507
  197.0 4.7 %all-to-all-done.4 = f32[8,8,128]{2,1,0:T(8,128)S(1)} async-done(((f32[8,8,128]{2,1,0:T(8,128)}), f32[8,8,128]{2,1,0:T(8,128)S(1)}, u32[]{:S(2)}, u32[]{:S(2)}) %all-to-all-start.4) | async-done | bytes 32800 | tf_op jit(solution)/shard_map/all_to_all | solution.py:507
  201.9 0.5 fusion
  (89 shorter events, 1.7 us)
Async XLA Ops:
  4.0 48.2 %all-to-all-start.1 = ((bf16[4,256,512]{2,1,0:T(8,128)(2,1)}), bf16[4,256,512]{2,1,0:T(8,128)(2,1)S(1)}, u32[]{:S(2)}, u32[]{:S(2)}) async-start(bf16[4,256,512]{2,1,0:T(8,128)(2,1)} %turned.3), calls=%async_computation.1 | async-start | bytes 2097152 | tf_op jit(solution)/shard_map/all_to_all | solution.py:489
  9.8 7.8 %copy-start = (bf16[2,2048,2,128]{3,2,1,0:T(2,128)(2,1)S(1)}, bf16[2,2048,2,128]{3,2,1,0:T(2,128)(2,1)}, u32[]{:S(2)}) copy-start(bf16[2,2048,2,128]{3,2,1,0:T(2,128)(2,1)} %param.20) | copy-start | bytes 6291460
  36.7 19.5 %collective-permute-start = (bf16[2,272,128]{2,1,0:T(8,128)(2,1)}, bf16[2,272,128]{2,1,0:T(8,128)(2,1)S(1)}, u32[]{:S(2)}, u32[]{:S(2)}) collective-permute-start(bf16[2,272,128]{2,1,0:T(8,128)(2,1)} %get-tuple-element.21), channel_id=1, source_target_pairs={{0,16},{16,32},{32,48},{48,64},{64,80},{80,96},{96,112},{1,17},{17... | collective-permute-start | bytes 417800 | tf_op jit(solution)/shard_map/ppermute | solution.py:491
  40.7 15.4 %collective-permute-start.1 = (bf16[2,272,128]{2,1,0:T(8,128)(2,1)}, bf16[2,272,128]{2,1,0:T(8,128)(2,1)S(1)}, u32[]{:S(2)}, u32[]{:S(2)}) collective-permute-start(bf16[2,272,128]{2,1,0:T(8,128)(2,1)} %get-tuple-element.21), channel_id=1, source_target_pairs={{0,32},{16,48},{32,64},{48,80},{64,96},{80,112},{1,33},{17,49},{33... | collective-permute-start | bytes 417800 | tf_op jit(solution)/shard_map/ppermute | solution.py:491
  43.9 12.2 %collective-permute-start.2 = (bf16[2,272,128]{2,1,0:T(8,128)(2,1)}, bf16[2,272,128]{2,1,0:T(8,128)(2,1)S(1)}, u32[]{:S(2)}, u32[]{:S(2)}) collective-permute-start(bf16[2,272,128]{2,1,0:T(8,128)(2,1)} %get-tuple-element.21), channel_id=1, source_target_pairs={{0,48},{16,64},{32,80},{48,96},{64,112},{1,49},{17,65},{33,81},{49... | collective-permute-start | bytes 417800 | tf_op jit(solution)/shard_map/ppermute | solution.py:491
  47.5 8.7 %collective-permute-start.3 = (bf16[2,272,128]{2,1,0:T(8,128)(2,1)}, bf16[2,272,128]{2,1,0:T(8,128)(2,1)S(1)}, u32[]{:S(2)}, u32[]{:S(2)}) collective-permute-start(bf16[2,272,128]{2,1,0:T(8,128)(2,1)} %get-tuple-element.21), channel_id=1, source_target_pairs={{0,64},{16,80},{32,96},{48,112},{1,65},{17,81},{33,97},{49,113},{2... | collective-permute-start | bytes 417800 | tf_op jit(solution)/shard_map/ppermute | solution.py:491
  52.1 8.8 %copy-start.2 = (bf16[4,256,512]{2,1,0:T(8,128)(2,1)}, bf16[4,256,512]{2,1,0:T(8,128)(2,1)S(1)}, u32[]{:S(2)}) copy-start(bf16[4,256,512]{2,1,0:T(8,128)(2,1)S(1)} %all-to-all-done.1.refs_5_) | copy-start | bytes 3145732
  52.1 38.3 %all-to-all-start = ((bf16[4,256,512]{2,1,0:T(8,128)(2,1)}), bf16[4,256,512]{2,1,0:T(8,128)(2,1)S(1)}, u32[]{:S(2)}, u32[]{:S(2)}) async-start(bf16[4,256,512]{2,1,0:T(8,128)(2,1)} %turned.2), calls=%async_computation | async-start | bytes 2097152 | tf_op jit(solution)/shard_map/all_to_all | solution.py:489
  56.1 0.7 copy-start.16
  56.2 0.7 copy-start.17
  56.2 0.7 copy-start.18
  56.2 0.8 copy-start.19
  60.9 9.5 %copy-start.1 = (bf16[528,256]{1,0:T(8,128)(2,1)S(1)}, bf16[528,256]{1,0:T(8,128)(2,1)}, u32[]{:S(2)}) copy-start(bf16[528,256]{1,0:T(8,128)(2,1)} %gate_out.2.refs_15_.refs_1_) | copy-start | bytes 811012
  65.1 9.2 %collective-permute-start.10 = (bf16[528,256]{1,0:T(8,128)(2,1)}, bf16[528,256]{1,0:T(8,128)(2,1)S(1)}, u32[]{:S(2)}, u32[]{:S(2)}) collective-permute-start(bf16[528,256]{1,0:T(8,128)(2,1)} %gate_out.3.refs_6_.refs_1_), channel_id=1, source_target_pairs={{0,1},{1,2},{2,3},{3,0},{4,5},{5,6},{6,7},{7,4},{8,9},{9,10},{10,1... | collective-permute-start | bytes 811016 | tf_op jit(solution)/shard_map/ppermute | solution.py:462
  66.8 13.6 %collective-permute-start.11 = (bf16[528,256]{1,0:T(8,128)(2,1)}, bf16[528,256]{1,0:T(8,128)(2,1)S(1)}, u32[]{:S(2)}, u32[]{:S(2)}) collective-permute-start(bf16[528,256]{1,0:T(8,128)(2,1)} %gate_out.3.refs_6_.refs_1_), channel_id=1, source_target_pairs={{0,2},{1,3},{2,0},{3,1},{4,6},{5,7},{6,4},{7,5},{8,10},{9,11},{10,... | collective-permute-start | bytes 811016 | tf_op jit(solution)/shard_map/ppermute | solution.py:462
  69.2 11.3 %collective-permute-start.12 = (bf16[528,256]{1,0:T(8,128)(2,1)}, bf16[528,256]{1,0:T(8,128)(2,1)S(1)}, u32[]{:S(2)}, u32[]{:S(2)}) collective-permute-start(bf16[528,256]{1,0:T(8,128)(2,1)} %gate_out.3.refs_6_.refs_1_), channel_id=1, source_target_pairs={{0,3},{1,0},{2,1},{3,2},{4,7},{5,4},{6,5},{7,6},{8,11},{9,8},{10,9... | collective-permute-start | bytes 811016 | tf_op jit(solution)/shard_map/ppermute | solution.py:462
  70.4 18.2 %collective-permute-start.4 = (bf16[528,256]{1,0:T(8,128)(2,1)S(1)}, bf16[528,256]{1,0:T(8,128)(2,1)S(1)}, u32[]{:S(2)}, u32[]{:S(2)}) collective-permute-start(bf16[528,256]{1,0:T(8,128)(2,1)S(1)} %copy-done.1), channel_id=1, source_target_pairs={{0,4},{4,8},{8,12},{12,0},{1,5},{5,9},{9,13},{13,1},{2,6},{6,10},{... | collective-permute-start | bytes 811016 | tf_op jit(solution)/shard_map/ppermute | solution.py:462
  71.9 18.5 %collective-permute-start.5 = (bf16[528,256]{1,0:T(8,128)(2,1)S(1)}, bf16[528,256]{1,0:T(8,128)(2,1)S(1)}, u32[]{:S(2)}, u32[]{:S(2)}) collective-permute-start(bf16[528,256]{1,0:T(8,128)(2,1)S(1)} %copy-done.1), channel_id=1, source_target_pairs={{0,8},{4,12},{8,0},{12,4},{1,9},{5,13},{9,1},{13,5},{2,10},{6,14},... | collective-permute-start | bytes 811016 | tf_op jit(solution)/shard_map/ppermute | solution.py:462
  74.3 6.3 %copy-start.31 = (bf16[528,256]{1,0:T(8,128)(2,1)}, bf16[528,256]{1,0:T(8,128)(2,1)S(1)}, u32[]{:S(2)}) copy-start(bf16[528,256]{1,0:T(8,128)(2,1)S(1)} %collective-permute-done.10.refs_2_) | copy-start | bytes 811012
  74.3 16.1 %collective-permute-start.6 = (bf16[528,256]{1,0:T(8,128)(2,1)S(1)}, bf16[528,256]{1,0:T(8,128)(2,1)S(1)}, u32[]{:S(2)}, u32[]{:S(2)}) collective-permute-start(bf16[528,256]{1,0:T(8,128)(2,1)S(1)} %copy-done.1), channel_id=1, source_target_pairs={{0,12},{4,0},{8,4},{12,8},{1,13},{5,1},{9,5},{13,9},{2,14},{6,2},{... | collective-permute-start | bytes 811016 | tf_op jit(solution)/shard_map/ppermute | solution.py:462
  80.4 0.7 copy-start.32
  81.1 0.7 copy-start.33
  85.1 14.2 %collective-permute-start.16 = (bf16[144,512]{1,0:T(8,128)(2,1)}, bf16[144,512]{1,0:T(8,128)(2,1)S(1)}, u32[]{:S(2)}, u32[]{:S(2)}) collective-permute-start(bf16[144,512]{1,0:T(8,128)(2,1)} %get-tuple-element.27), channel_id=1, source_target_pairs={{0,4},{4,8},{8,12},{12,0},{1,5},{5,9},{9,13},{13,1},{2,6},{6,10},{... | collective-permute-start | bytes 442376 | tf_op jit(solution)/shard_map/ppermute | solution.py:462
  86.2 13.0 %collective-permute-start.17 = (bf16[144,512]{1,0:T(8,128)(2,1)}, bf16[144,512]{1,0:T(8,128)(2,1)S(1)}, u32[]{:S(2)}, u32[]{:S(2)}) collective-permute-start(bf16[144,512]{1,0:T(8,128)(2,1)} %get-tuple-element.28), channel_id=1, source_target_pairs={{0,8},{4,12},{8,0},{12,4},{1,9},{5,13},{9,1},{13,5},{2,10},{6,14},... | collective-permute-start | bytes 442376 | tf_op jit(solution)/shard_map/ppermute | solution.py:462
  88.6 1.8 copy-start.28
  88.6 10.6 %collective-permute-start.18 = (bf16[144,512]{1,0:T(8,128)(2,1)}, bf16[144,512]{1,0:T(8,128)(2,1)S(1)}, u32[]{:S(2)}, u32[]{:S(2)}) collective-permute-start(bf16[144,512]{1,0:T(8,128)(2,1)} %get-tuple-element.29), channel_id=1, source_target_pairs={{0,12},{4,0},{8,4},{12,8},{1,13},{5,1},{9,5},{13,9},{2,14},{6,2},{... | collective-permute-start | bytes 442376 | tf_op jit(solution)/shard_map/ppermute | solution.py:462
  90.4 0.7 copy-start.29
  90.4 0.8 copy-start.30
  91.2 1.0 copy-start.3
  95.4 9.2 %collective-permute-start.7 = (bf16[144,512]{1,0:T(8,128)(2,1)}, bf16[144,512]{1,0:T(8,128)(2,1)S(1)}, u32[]{:S(2)}, u32[]{:S(2)}) collective-permute-start(bf16[144,512]{1,0:T(8,128)(2,1)} %get-tuple-element.23), channel_id=1, source_target_pairs={{0,1},{1,2},{2,3},{3,0},{4,5},{5,6},{6,7},{7,4},{8,9},{9,10},{10,1... | collective-permute-start | bytes 442376 | tf_op jit(solution)/shard_map/ppermute | solution.py:462
  96.6 10.1 %collective-permute-start.8 = (bf16[144,512]{1,0:T(8,128)(2,1)}, bf16[144,512]{1,0:T(8,128)(2,1)S(1)}, u32[]{:S(2)}, u32[]{:S(2)}) collective-permute-start(bf16[144,512]{1,0:T(8,128)(2,1)} %get-tuple-element.24), channel_id=1, source_target_pairs={{0,2},{1,3},{2,0},{3,1},{4,6},{5,7},{6,4},{7,5},{8,10},{9,11},{10,... | collective-permute-start | bytes 442376 | tf_op jit(solution)/shard_map/ppermute | solution.py:462
  99.2 7.4 %collective-permute-start.9 = (bf16[144,512]{1,0:T(8,128)(2,1)}, bf16[144,512]{1,0:T(8,128)(2,1)S(1)}, u32[]{:S(2)}, u32[]{:S(2)}) collective-permute-start(bf16[144,512]{1,0:T(8,128)(2,1)} %get-tuple-element.25), channel_id=1, source_target_pairs={{0,3},{1,0},{2,1},{3,2},{4,7},{5,4},{6,5},{7,6},{8,11},{9,8},{10,9... | collective-permute-start | bytes 442376 | tf_op jit(solution)/shard_map/ppermute | solution.py:462
  99.2 0.7 copy-start.22
  99.3 0.7 copy-start.24
  102.8 8.6 %collective-permute-start.19 = (bf16[144,512]{1,0:T(8,128)(2,1)}, bf16[144,512]{1,0:T(8,128)(2,1)S(1)}, u32[]{:S(2)}, u32[]{:S(2)}) collective-permute-start(bf16[144,512]{1,0:T(8,128)(2,1)} %residual_block.3.refs_1_), channel_id=1, source_target_pairs={{0,1},{1,2},{2,3},{3,0},{4,5},{5,6},{6,7},{7,4},{8,9},{9,10},{10,1... | collective-permute-start | bytes 442376 | tf_op jit(solution)/shard_map/ppermute | solution.py:462
  104.3 8.7 %collective-permute-start.20 = (bf16[144,512]{1,0:T(8,128)(2,1)}, bf16[144,512]{1,0:T(8,128)(2,1)S(1)}, u32[]{:S(2)}, u32[]{:S(2)}) collective-permute-start(bf16[144,512]{1,0:T(8,128)(2,1)} %residual_block.3.refs_1_), channel_id=1, source_target_pairs={{0,2},{1,3},{2,0},{3,1},{4,6},{5,7},{6,4},{7,5},{8,10},{9,11},{10,... | collective-permute-start | bytes 442376 | tf_op jit(solution)/shard_map/ppermute | solution.py:462
  104.6 2.1 %copy-start.23 = (bf16[144,512]{1,0:T(8,128)(2,1)}, bf16[144,512]{1,0:T(8,128)(2,1)S(1)}, u32[]{:S(2)}) copy-start(bf16[144,512]{1,0:T(8,128)(2,1)S(1)} %collective-permute-done.7.refs_2_) | copy-start | bytes 442372
  104.6 8.4 %collective-permute-start.21 = (bf16[144,512]{1,0:T(8,128)(2,1)}, bf16[144,512]{1,0:T(8,128)(2,1)S(1)}, u32[]{:S(2)}, u32[]{:S(2)}) collective-permute-start(bf16[144,512]{1,0:T(8,128)(2,1)} %residual_block.3.refs_1_), channel_id=1, source_target_pairs={{0,3},{1,0},{2,1},{3,2},{4,7},{5,4},{6,5},{7,6},{8,11},{9,8},{10,9... | collective-permute-start | bytes 442376 | tf_op jit(solution)/shard_map/ppermute | solution.py:462
  106.7 0.7 copy-start.25
  106.7 0.7 copy-start.26
  110.2 7.0 %collective-permute-start.13 = (bf16[144,512]{1,0:T(8,128)(2,1)}, bf16[144,512]{1,0:T(8,128)(2,1)S(1)}, u32[]{:S(2)}, u32[]{:S(2)}) collective-permute-start(bf16[144,512]{1,0:T(8,128)(2,1)} %residual_block.2.refs_1_), channel_id=1, source_target_pairs={{0,4},{4,8},{8,12},{12,0},{1,5},{5,9},{9,13},{13,1},{2,6},{6,10},{... | collective-permute-start | bytes 442376 | tf_op jit(solution)/shard_map/ppermute | solution.py:462
  110.5 6.7 %collective-permute-start.14 = (bf16[144,512]{1,0:T(8,128)(2,1)}, bf16[144,512]{1,0:T(8,128)(2,1)S(1)}, u32[]{:S(2)}, u32[]{:S(2)}) collective-permute-start(bf16[144,512]{1,0:T(8,128)(2,1)} %residual_block.2.refs_1_), channel_id=1, source_target_pairs={{0,8},{4,12},{8,0},{12,4},{1,9},{5,13},{9,1},{13,5},{2,10},{6,14},... | collective-permute-start | bytes 442376 | tf_op jit(solution)/shard_map/ppermute | solution.py:462
  111.4 6.4 %copy-start.10 = (bf16[144,512]{1,0:T(8,128)(2,1)}, bf16[144,512]{1,0:T(8,128)(2,1)S(1)}, u32[]{:S(2)}) copy-start(bf16[144,512]{1,0:T(8,128)(2,1)S(1)} %collective-permute-done.19.refs_5_.refs_2_) | copy-start | bytes 442372
  111.4 6.4 %collective-permute-start.15 = (bf16[144,512]{1,0:T(8,128)(2,1)}, bf16[144,512]{1,0:T(8,128)(2,1)S(1)}, u32[]{:S(2)}, u32[]{:S(2)}) collective-permute-start(bf16[144,512]{1,0:T(8,128)(2,1)} %residual_block.2.refs_1_), channel_id=1, source_target_pairs={{0,12},{4,0},{8,4},{12,8},{1,13},{5,1},{9,5},{13,9},{2,14},{6,2},{... | collective-permute-start | bytes 442376 | tf_op jit(solution)/shard_map/ppermute | solution.py:462
  113.0 4.9 %copy-start.11 = (bf16[144,512]{1,0:T(8,128)(2,1)}, bf16[144,512]{1,0:T(8,128)(2,1)S(1)}, u32[]{:S(2)}) copy-start(bf16[144,512]{1,0:T(8,128)(2,1)S(1)} %collective-permute-done.20.refs_6_.refs_3_) | copy-start | bytes 442372
  113.0 4.9 %copy-start.12 = (bf16[144,512]{1,0:T(8,128)(2,1)}, bf16[144,512]{1,0:T(8,128)(2,1)S(1)}, u32[]{:S(2)}) copy-start(bf16[144,512]{1,0:T(8,128)(2,1)S(1)} %collective-permute-done.21.refs_7_.refs_4_) | copy-start | bytes 442372
  117.2 0.7 copy-start.13
  117.2 0.7 copy-start.14
  120.6 10.2 %collective-permute-start.25 = (bf16[144,2048]{1,0:T(8,128)(2,1)}, bf16[144,2048]{1,0:T(8,128)(2,1)S(1)}, u32[]{:S(2)}, u32[]{:S(2)}) collective-permute-start(bf16[144,2048]{1,0:T(8,128)(2,1)} %join_columns.3.refs_8_.refs_2_), channel_id=1, source_target_pairs={{0,4},{4,8},{8,12},{12,0},{1,5},{5,9},{9,13},{13,1},{2,6},{6,10},{... | collective-permute-start | bytes 1769480 | tf_op jit(solution)/shard_map/ppermute | solution.py:462
  120.6 23.3 %collective-permute-start.26 = (bf16[144,2048]{1,0:T(8,128)(2,1)}, bf16[144,2048]{1,0:T(8,128)(2,1)S(1)}, u32[]{:S(2)}, u32[]{:S(2)}) collective-permute-start(bf16[144,2048]{1,0:T(8,128)(2,1)} %join_columns.3.refs_8_.refs_2_), channel_id=1, source_target_pairs={{0,8},{4,12},{8,0},{12,4},{1,9},{5,13},{9,1},{13,5},{2,10},{6,14},... | collective-permute-start | bytes 1769480 | tf_op jit(solution)/shard_map/ppermute | solution.py:462
  123.9 25.3 %collective-permute-start.27 = (bf16[144,2048]{1,0:T(8,128)(2,1)}, bf16[144,2048]{1,0:T(8,128)(2,1)S(1)}, u32[]{:S(2)}, u32[]{:S(2)}) collective-permute-start(bf16[144,2048]{1,0:T(8,128)(2,1)} %join_columns.3.refs_8_.refs_2_), channel_id=1, source_target_pairs={{0,12},{4,0},{8,4},{12,8},{1,13},{5,1},{9,5},{13,9},{2,14},{6,2},{... | collective-permute-start | bytes 1769480 | tf_op jit(solution)/shard_map/ppermute | solution.py:462
  125.9 38.8 %collective-permute-start.22 = (bf16[144,2048]{1,0:T(8,128)(2,1)}, bf16[144,2048]{1,0:T(8,128)(2,1)S(1)}, u32[]{:S(2)}, u32[]{:S(2)}) collective-permute-start(bf16[144,2048]{1,0:T(8,128)(2,1)} %join_columns.2.refs_2_), channel_id=1, source_target_pairs={{0,1},{1,2},{2,3},{3,0},{4,5},{5,6},{6,7},{7,4},{8,9},{9,10},{10,1... | collective-permute-start | bytes 1769480 | tf_op jit(solution)/shard_map/ppermute | solution.py:462
  125.9 38.9 %collective-permute-start.23 = (bf16[144,2048]{1,0:T(8,128)(2,1)}, bf16[144,2048]{1,0:T(8,128)(2,1)S(1)}, u32[]{:S(2)}, u32[]{:S(2)}) collective-permute-start(bf16[144,2048]{1,0:T(8,128)(2,1)} %join_columns.2.refs_2_), channel_id=1, source_target_pairs={{0,2},{1,3},{2,0},{3,1},{4,6},{5,7},{6,4},{7,5},{8,10},{9,11},{10,... | collective-permute-start | bytes 1769480 | tf_op jit(solution)/shard_map/ppermute | solution.py:462
  130.8 18.4 %copy-start.5 = (bf16[144,2048]{1,0:T(8,128)(2,1)}, bf16[144,2048]{1,0:T(8,128)(2,1)S(1)}, u32[]{:S(2)}) copy-start(bf16[144,2048]{1,0:T(8,128)(2,1)S(1)} %collective-permute-done.25.refs_3_) | copy-start | bytes 1769476
  130.8 34.0 %collective-permute-start.24 = (bf16[144,2048]{1,0:T(8,128)(2,1)}, bf16[144,2048]{1,0:T(8,128)(2,1)S(1)}, u32[]{:S(2)}, u32[]{:S(2)}) collective-permute-start(bf16[144,2048]{1,0:T(8,128)(2,1)} %join_columns.2.refs_2_), channel_id=1, source_target_pairs={{0,3},{1,0},{2,1},{3,2},{4,7},{5,4},{6,5},{7,6},{8,11},{9,8},{10,9... | collective-permute-start | bytes 1769480 | tf_op jit(solution)/shard_map/ppermute | solution.py:462
  143.9 5.3 %copy-start.7 = (bf16[144,2048]{1,0:T(8,128)(2,1)}, bf16[144,2048]{1,0:T(8,128)(2,1)S(1)}, u32[]{:S(2)}) copy-start(bf16[144,2048]{1,0:T(8,128)(2,1)S(1)} %collective-permute-done.26.refs_4_) | copy-start | bytes 1769476
  149.2 0.8 copy-start.8
  159.0 16.6 %all-to-all-start.3 = ((f32[16,8,128]{2,1,0:T(8,128)}), f32[16,8,128]{2,1,0:T(8,128)S(1)}, u32[]{:S(2)}, u32[]{:S(2)}) async-start(f32[16,8,128]{2,1,0:T(8,128)} %head_stats.3), calls=%async_computation.3 | async-start | bytes 131072 | tf_op jit(solution)/shard_map/all_to_all | solution.py:505
  164.7 37.2 %copy-start.27 = (s32[4]{0:T(128)S(1)}, s32[4]{0:T(128)}, u32[]{:S(2)}) copy-start(s32[4]{0:T(128)} %param.35) | copy-start | bytes 52
  164.7 0.8 copy-start.4
  164.8 1.0 copy-start.6
  165.8 0.8 copy-start.9
  175.6 13.3 %copy-start.20 = (f32[16,8,128]{2,1,0:T(8,128)}, f32[16,8,128]{2,1,0:T(8,128)S(1)}, u32[]{:S(2)}) copy-start(f32[16,8,128]{2,1,0:T(8,128)S(1)} %all-to-all-done.3.s1_ref) | copy-start | bytes 196612
  190.5 11.2 %all-to-all-start.4 = ((f32[8,8,128]{2,1,0:T(8,128)}), f32[8,8,128]{2,1,0:T(8,128)S(1)}, u32[]{:S(2)}, u32[]{:S(2)}) async-start(f32[8,8,128]{2,1,0:T(8,128)} %get-tuple-element.31), calls=%async_computation.4 | async-start | bytes 65536 | tf_op jit(solution)/shard_map/all_to_all | solution.py:507
  (2 other events, 1.3 us)

commit v6 on v5

--- a/solution.py
+++ b/solution.py
@@ -16,6 +16,7 @@
 F32 = jnp.float32
 BF16 = jnp.bfloat16
 LOW = -1e30
+LOG2E = 1.4426950408889634
 
 
 def silu(v):
@@ -73,9 +74,11 @@
         stp_ref[...] = jnp.zeros_like(stp_ref)
 
     tokens = tok_ref[...]
-    gate_ref[...] += contract(tokens, wi_ref[:, 0:inner], ((1,), (0,)))
-    val_ref[...] += contract(tokens, wi_ref[:, inner:], ((1,), (0,)))
-    st_ref[...] += contract(tokens, ws_ref[...], ((1,), (0,)))
+    state = c_ref.shape[1]
+    gate_ref[...] += contract(tokens, wi_ref[0], ((1,), (0,)))
+    val_ref[...] += contract(tokens, wi_ref[1], ((1,), (0,)))
+    st_ref[:, 0:state] += contract(tokens, ws_ref[0], ((1,), (0,)))
+    st_ref[:, state:] += contract(tokens, ws_ref[1], ((1,), (0,)))
     stp_ref[...] += contract(tokens, wp_ref[...], ((1,), (1,)))
 
     @pl.when(k == pl.num_programs(1) - 1)
@@ -159,8 +162,8 @@
 
 def mix_local(hidden, w_inner, w_state, w_step, bias, rate, skip, seg, chunks=4):
     models, rows, depth = hidden.shape
-    inner = w_inner.shape[2] // 2
-    state = w_state.shape[2] // 2
+    inner = w_inner.shape[3]
+    state = w_state.shape[3]
     heads = bias.shape[1]
     deep = depth // chunks
     whole = lambda a: pl.BlockSpec(a.shape, lambda m, k: (0,) * a.ndim)
@@ -171,8 +174,8 @@
         grid=(models, chunks),
         in_specs=[
             pl.BlockSpec((None, rows, deep), lambda m, k: (m, 0, k)),
-            pl.BlockSpec((None, deep, 2 * inner), lambda m, k: (m, k, 0)),
-            pl.BlockSpec((None, deep, 2 * state), lambda m, k: (m, k, 0)),
+            pl.BlockSpec((None, 2, deep, inner), lambda m, k: (m, 0, k, 0)),
+            pl.BlockSpec((None, 2, deep, state), lambda m, k: (m, 0, k, 0)),
             pl.BlockSpec((None, heads, deep), lambda m, k: (m, 0, k)),
             whole(bias), whole(rate), whole(skip), whole(seg),
         ],
@@ -188,7 +191,7 @@
 
 def gate_kernel(
     m, pages_ref, flags_ref, y_ref, gate_ref, c_ref, e_ref, r1_ref, r2_ref, r3_ref, r4_ref,
-    p0_ref, p1_ref, p2_ref, p3_ref, gain_ref, out_ref,
+    p0_ref, p1_ref, p2_ref, p3_ref, gain_ref, out_ref, pick_ref,
 ):
     rows, inner = y_ref.shape
     heads = p0_ref.shape[0]
@@ -214,13 +217,19 @@
     prior = jnp.concatenate(parts, axis=0)
     through = jnp.concatenate([jnp.broadcast_to(through[h : h + 1, :], (wide, state)) for h in range(heads)], axis=0)
     out_map = c_ref[...]
-    picked = jnp.zeros((rows, inner), F32)
+    low_id, high_id = jnp.min(seg_col), jnp.max(seg_col)
+    pick_ref[...] = jnp.zeros_like(pick_ref)
     for j in range(4):
-        start = jnp.where(seg_first == float(j), prior + through * init[j], init[j])
-        high = start.astype(BF16)
-        low = (start - high.astype(F32)).astype(BF16)
-        from_state = contract(out_map, high, ((1,), (1,))) + contract(out_map, low, ((1,), (1,)))
-        picked = jnp.where(seg_col == float(j), from_state, picked)
+
+        @pl.when((low_id <= j) & (high_id >= j))
+        def _():
+            start = jnp.where(seg_first == float(j), prior + through * init[j], init[j])
+            high = start.astype(BF16)
+            low = (start - high.astype(F32)).astype(BF16)
+            from_state = contract(out_map, high, ((1,), (1,))) + contract(out_map, low, ((1,), (1,)))
+            pick_ref[...] = jnp.where(seg_col == float(j), from_state, pick_ref[...])
+
+    picked = pick_ref[...]
     spread = jnp.concatenate([jnp.broadcast_to(e_col[:, h : h + 1], (rows, wide)) for h in range(heads)], axis=1)
     gated = (y_ref[...] + picked * spread) * silu(gate_ref[...])
     square = jnp.sum(gated * gated, axis=1, keepdims=True)
@@ -251,6 +260,7 @@
             + [whole(gain)]
             + [ANYWHERE] * len(after),
             out_specs=pl.BlockSpec((rows + 16, inner), lambda g, pg, fl: (0, 0)),
+            scratch_shapes=[pltpu.VMEM((rows, inner), F32)],
         ),
         out_shape=jax.ShapeDtypeStruct((rows + 16, inner), BF16),
         cost_estimate=pl.CostEstimate(flops=10**9, bytes_accessed=4 * 10**6, transcendentals=10**5),
@@ -357,63 +367,85 @@
     )(at, *parts, *after)
 
 
-def head_kernel(m, place_ref, at_ref, x0_ref, x1_ref, x2_ref, x3_ref, w_ref, tgt_ref, out_ref, wv_ref, acc_ref, sems):
-    block = x0_ref.shape[0] - 16
-    vocab = w_ref.shape[2]
-    cut = 768
-    spans = (pl.ds(0, cut), pl.ds(cut, vocab - cut))
+def fetch_kernel(w_ref, out_ref, sems):
+    depth = w_ref.shape[1]
+    half = depth // 2
     copies = [
-        pltpu.make_async_copy(w_ref.at[m, :, span], wv_ref.at[:, span], sems.at[n]) for n, span in enumerate(spans)
+        pltpu.make_async_copy(
+            w_ref.at[m, pl.ds(n * half, half), :], out_ref.at[m, pl.ds(n * half, half), :], sems.at[2 * m + n]
+        )
+        for m in range(2)
+        for n in range(2)
     ]
     for copy in copies:
         copy.start()
-    tiles = (x0_ref, x1_ref, x2_ref, x3_ref)
-    for copy, span in zip(copies, spans):
+    for copy in copies:
         copy.wait()
+
+
+def fetched(head, after):
+    return pl.pallas_call(
+        drop(fetch_kernel, 1, len(after)),
+        in_specs=[ANYWHERE] + [ANYWHERE] * len(after),
+        out_specs=pl.BlockSpec(memory_space=pltpu.VMEM),
+        out_shape=pltpu.VMEM(head.shape, head.dtype),
+        scratch_shapes=[pltpu.SemaphoreType.DMA((4,))],
+        compiler_params=pltpu.CompilerParams(vmem_limit_bytes=16 * 2**20),
+        cost_estimate=pl.CostEstimate(flops=0, bytes_accessed=3 * 10**7, transcendentals=0),
+        name="fetched",
+    )(head, *after)
+
+
+def head_kernel(place_ref, at0_ref, at1_ref, *refs):
+    w_ref, tgt_ref, out_ref, acc_ref = refs[8:]
+    block = refs[0].shape[0] - 16
+    vocab = w_ref.shape[2]
+    for m, at_ref in enumerate((at0_ref, at1_ref)):
+        tiles = refs[4 * m : 4 * m + 4]
         for n in range(2):
             rows = jnp.concatenate([x[0:block, :] for x in tiles[2 * n : 2 * n + 2]], axis=0)
-            acc_ref[2 * n * block : 2 * (n + 1) * block, span] = contract(rows, wv_ref[:, span], ((1,), (0,)))
-    for k, x in enumerate(tiles):
-        at = lax.rem(at_ref[1] + 4 - k, 4)
-        line = x[block : block + 16, 0 : 3 * block].astype(F32)[0:1, :]
-        scale = to_column(line[:, 0:block] + line[:, block : 2 * block] + line[:, 2 * block : 3 * block])
-        logits = acc_ref[k * block : (k + 1) * block, :] * scale
-        top = jnp.max(logits, axis=1, keepdims=True)
-        lse = top + jnp.log(jnp.sum(jnp.exp(logits - top), axis=1, keepdims=True))
-        target = to_column((tgt_ref[pl.ds(at, 1), :] - place_ref[0] * vocab).astype(F32)).astype(jnp.int32)
-        column = lax.broadcasted_iota(jnp.int32, logits.shape, 1)
-        chosen = jnp.sum(jnp.where(column == target, logits, 0.0), axis=1, keepdims=True)
-        for which, value in enumerate((lse, chosen)):
-            out_ref[:, pl.ds(which * 4 + at, 1), :] = jnp.broadcast_to(
-                to_row(value)[None], (out_ref.shape[0], 1, block)
-            )
-
-
-def head_stats(m, place, at, parts, head, tgt, group, after=()):
-    tall, depth = parts[0].shape
+            acc_ref[2 * n * block : 2 * (n + 1) * block, :] = contract(rows, w_ref[m], ((1,), (0,)))
+        for k, x in enumerate(tiles):
+            at = lax.rem(at_ref[1] + 4 - k, 4)
+            line = x[block : block + 16, 0 : 3 * block].astype(F32)[0:1, :]
+            scale = to_column(line[:, 0:block] + line[:, block : 2 * block] + line[:, 2 * block : 3 * block])
+            raw = acc_ref[k * block : (k + 1) * block, :]
+            top = jnp.max(raw, axis=1, keepdims=True)
+            total = jnp.sum(jnp.exp2((raw - top) * (scale * LOG2E)), axis=1, keepdims=True)
+            lse = top * scale + jnp.log(total)
+            target = to_column((tgt_ref[pl.ds(at, 1), :] - place_ref[0] * vocab).astype(F32)).astype(jnp.int32)
+            column = lax.broadcasted_iota(jnp.int32, raw.shape, 1)
+            chosen = jnp.sum(jnp.where(column == target, raw, 0.0), axis=1, keepdims=True) * scale
+            for which, value in enumerate((lse, chosen)):
+                out_ref[:, pl.ds(m * 8 + which * 4 + at, 1), :] = jnp.broadcast_to(
+                    to_row(value)[None], (out_ref.shape[0], 1, block)
+                )
+
+
+def head_stats(place, at, parts, head, tgt, group):
+    tall, depth = parts[0][0].shape
     block = tall - 16
     vocab = head.shape[2]
     vm = pl.BlockSpec(memory_space=pltpu.VMEM)
     sm = pl.BlockSpec(memory_space=pltpu.SMEM)
     return pl.pallas_call(
-        drop(functools.partial(head_kernel, m), 8, len(after)),
-        in_specs=[sm, sm] + [vm] * 4 + [ANYWHERE, vm] + [ANYWHERE] * len(after),
+        head_kernel,
+        in_specs=[sm] * 3 + [vm] * 10,
         out_specs=vm,
-        scratch_shapes=[
-            pltpu.VMEM((depth, vocab), BF16), pltpu.VMEM((4 * block, vocab), F32), pltpu.SemaphoreType.DMA((2,))
-        ],
-        out_shape=jax.ShapeDtypeStruct((group, 8, block), F32),
+        scratch_shapes=[pltpu.VMEM((4 * block, vocab), F32)],
+        out_shape=jax.ShapeDtypeStruct((group, 16, block), F32),
+        compiler_params=pltpu.CompilerParams(vmem_limit_bytes=36 * 2**20),
         cost_estimate=pl.CostEstimate(
-            flops=8 * block * depth * vocab, bytes_accessed=2 * depth * vocab, transcendentals=4 * block * vocab
+            flops=16 * block * depth * vocab, bytes_accessed=10**7, transcendentals=8 * block * vocab
         ),
         name="head_stats",
-    )(place, at, *parts, head, tgt, *after)
-
-
-def diff_kernel(s0_ref, s1_ref, live_ref, seg_ref, diff_ref, sums_ref):
+    )(place, *at, *parts[0], *parts[1], head, tgt)
+
+
+def diff_kernel(stat_ref, live_ref, seg_ref, diff_ref, sums_ref):
     scores = []
-    for ref in (s0_ref, s1_ref):
-        part = ref[...]
+    for m in range(2):
+        part = stat_ref[:, 8 * m : 8 * m + 8, :]
         lse = part[:, 0:4, :]
         top = jnp.max(lse, axis=0)
         total = top + jnp.log(jnp.sum(jnp.exp(lse - top[None]), axis=0))
@@ -427,21 +459,23 @@
     for j in range(4):
         mine = jnp.sum(jnp.where(seg_ref[...] == j, diff, 0.0), axis=1, keepdims=True)
         sums = jnp.where(which == j, jnp.sum(mine, axis=0, keepdims=True), sums)
-    sums_ref[...] = jnp.broadcast_to(sums[None], sums_ref.shape)
-
-
-def token_diffs(s0, s1, live, seg, devices):
+    sums_ref[...] = sums
+
+
+def token_diffs(stats, live, seg):
     vm = pl.BlockSpec(memory_space=pltpu.VMEM)
     return pl.pallas_call(
         diff_kernel,
-        in_specs=[vm, vm, pl.BlockSpec(memory_space=pltpu.SMEM), vm],
-        out_shape=(jax.ShapeDtypeStruct((4, 128), F32), jax.ShapeDtypeStruct((devices, 8, 128), F32)),
+        in_specs=[vm, pl.BlockSpec(memory_space=pltpu.SMEM), vm],
+        out_shape=(jax.ShapeDtypeStruct((4, 128), F32), jax.ShapeDtypeStruct((8, 128), F32)),
         name="token_diffs",
-    )(s0, s1, live, seg)
+    )(stats, live, seg)
 
 
 def turn_kernel(w_ref, out_ref):
-    out_ref[...] = w_ref[...]
+    width = out_ref.shape[2]
+    for j in range(4):
+        out_ref[j] = w_ref[:, j * width : (j + 1) * width]
 
 
 def turned(m, w_out):
@@ -449,9 +483,9 @@
     width = depth // 4
     return pl.pallas_call(
         turn_kernel,
-        grid=(4,),
-        in_specs=[pl.BlockSpec((None, inner, width), lambda j: (m, 0, j))],
-        out_specs=pl.BlockSpec((None, inner, width), lambda j: (j, 0, 0)),
+        grid=(1,),
+        in_specs=[pl.BlockSpec((None, inner, depth), lambda j: (m, 0, 0))],
+        out_specs=pl.BlockSpec((4, inner, width), lambda j: (0, 0, 0)),
         out_shape=jax.ShapeDtypeStruct((4, inner, width), w_out.dtype),
         cost_estimate=pl.CostEstimate(flops=0, bytes_accessed=2 * 10**6, transcendentals=0),
         name="turned",
@@ -478,8 +512,8 @@
     place = lax.axis_index(VOC).astype(jnp.int32).reshape(1)
     seg = segment_ids.reshape(1, rows)
     tgt = targets.reshape(4, rows // 4)
-    w_inner = w_inner.reshape(2, depth, 2 * inner)
-    w_state = w_state.reshape(2, depth, -1)
+    w_inner = jnp.swapaxes(w_inner, 1, 2)
+    w_state = jnp.swapaxes(w_state, 1, 2)
     w_step = jnp.swapaxes(w_step, 1, 2)
     ways = (("x", "z"), ("z", "x"))
     both = range(2)
@@ -489,7 +523,7 @@
     weights = [lax.all_to_all(turned(m, w_out), ways[m][0], 0, 0) for m in both]
     y, gate, c, e, pay = mix_local(hidden, w_inner, w_state, w_step, step_bias, rate, skip_gain, seg)
     recv = [lax.ppermute(pay, SEQ, [(i, i + k) for i in range(devices - k)]) for k in range(1, REACH + 1)]
-    gated, parts, res, full, stats = [], [], [], [], []
+    gated, parts, res, full = [], [], [], []
     for m in both:
         gated.append(gate_out(m, pages, flags, y, gate, c, e, recv, pool, norm_gain, tuple(gated)))
     for m in both:
@@ -500,11 +534,12 @@
     blocks = [gathered(res[m], ways[m][0]) for m in both]
     for m in both:
         full.append(join_columns(at[m], blocks[m], tuple(blocks[1 - m][1:])))
-    for m in both:
-        stat = head_stats(m, place, at[m], gathered(full[m], ways[m][1]), head, tgt, group, (full[1],))
-        stats.append(lax.all_to_all(stat, VOC, 0, 0))
-    diff, sums = token_diffs(stats[0], stats[1], live, segment_ids.reshape(4, 128), devices)
-    sums = jnp.sum(lax.all_to_all(sums, SEQ, 0, 0)[:, 0:4, 0], axis=0)
+    ready = fetched(head, tuple(full))
+    last = [gathered(full[m], ways[m][1]) for m in both]
+    merged = lax.all_to_all(head_stats(place, at, last, ready, tgt, group), VOC, 0, 0)
+    diff, sums = token_diffs(merged, live, segment_ids.reshape(4, 128))
+    sums = sums + lax.ppermute(sums, "core", [(0, 1), (1, 0)])
+    sums = sum(gathered(sums, "y"))[0:4, 0]
     owned = jnp.where(owners == lax.axis_index(SEQ), sums, 0.0)
     return diff.reshape(rows), owned[None]
 

time: 204 us -> 189 us (0.926)
  starting transfers between devices: 67.8 us -> 58.2 us
  Pallas kernels: 67.1 us -> 57.8 us
  waiting for transfers between devices: 32.5 us -> 36.2 us
    all_to_all x2 -> x0, starting transfers between devices: 12.2 us -> none  [the longest x1 6.51 us: per_device(): sums = jnp.sum(lax.all_to_all(sums, SEQ, 0, 0)[:, 0:4, 0], axis=0)]
    reshape x2 -> x0, local copies, waits for them, and re-layouts: 10.4 us -> none  [the longest x1 7.76 us: per_device(): w_inner = w_inner.reshape(2, depth, 2 * inner)]
    pallas_call x5, Pallas kernels: 26.4 us -> 16.5 us  [the longest x1 9.19 us: head_stats(): pl.pallas_call(head_kernel, in_specs=[sm] * 3 + [vm] * 10, out_specs=vm,...]
    unnamed x68 -> x74, local copies, waits for them, and re-layouts: 8.68 us -> 17.9 us
    ppermute x0 -> x1, starting transfers between devices: none -> 8.29 us  [per_device(): sums = sums + lax.ppermute(sums, 'core', [(0, 1), (1, 0)])]
    ppermute x24 -> x27, waiting for transfers between devices: 27.8 us -> 35.2 us  [ring(): return lax.ppermute(value, axis, [(i, (i + by) % 4) for i in range(4)])]
    ppermute x24 -> x27, starting transfers between devices: 33.6 us -> 28.6 us  [ring(): return lax.ppermute(value, axis, [(i, (i + by) % 4) for i in range(4)])]
    all_to_all x2 -> x0, waiting for transfers between devices: 4.72 us -> none  [the longest x1 4.72 us: per_device(): sums = jnp.sum(lax.all_to_all(sums, SEQ, 0, 0)[:, 0:4, 0], axis=0)]
  transfers between devices with their start and end apart: 32 -> 34, of which waited for: 8 -> 11; matrix products, arithmetic and copies ran while one was open for 6% -> 3% of each run, Pallas kernels for 30% -> 23%
where the time goes in v6:
time: 189 us; the launch traced here: 187 us
  starting transfers between devices  58.2 us (31%)
  Pallas kernels  57.8 us (31%)
  waiting for transfers between devices  36.2 us (19%)
  local copies, waits for them, and re-layouts  18 us (10%)
  blocking collectives  13.2 us (7%)
  other arithmetic  2.5 us (1%)
    ppermute x27, waiting for transfers between devices, ring(): return lax.ppermute(value, axis, [(i, (i + by) % 4) for i in range(4)])  35.2 us
    ppermute x27, starting transfers between devices, ring(): return lax.ppermute(value, axis, [(i, (i + by) % 4) for i in range(4)])  28.6 us
    unnamed x74, local copies, waits for them, and re-layouts  17.9 us
    pallas_call x1, Pallas kernels, mix_local(): pl.pallas_call(mix_kernel, grid=(models, chunks), in_specs=[pl.BlockSpec(...  17.1 us
    all_to_all x1, blocking collectives, per_device(): lax.all_to_all(head_stats(place, at, last, ready, tgt, group), VOC, 0, 0)  13.2 us
    ppermute x4, starting transfers between devices, per_device(): lax.ppermute(pay, SEQ, [(i, i + k) for i in range(devices - k)])  11.5 us
    all_to_all x2, starting transfers between devices, per_device(): weights = [lax.all_to_all(turned(m, w_out), ways[m][0], 0, 0) for m in both]  9.86 us
    pallas_call x1, Pallas kernels, head_stats(): pl.pallas_call(head_kernel, in_specs=[sm] * 3 + [vm] * 10, out_specs=vm,...  9.19 us
  transfers between devices with their start and end apart: 34, of which 11 were waited for; matrix products, arithmetic and copies ran while one was open for 3% of the time, Pallas kernels for 23%

profile of v6, /device:TPU:1, one launch (start us, length us, event | category | flops | bytes accessed | tf_op | source)
XLA Modules:
  0.0 187.0 jit_solution(5057846122562363285)
XLA Ops:
  0.6 2.4 %turned.3 = bf16[4,256,512]{2,1,0:T(8,128)(2,1)} custom-call(bf16[2,256,2048]{2,1,0:T(8,128)(2,1)} %w_ref.3), custom_call_target="tpu_custom_call" | custom-call | bytes 2000000 | tf_op jit(solution)/shard_map/turned/pallas_call | solution.py:484
  3.1 5.9 %all-to-all-start.1 = ((bf16[4,256,512]{2,1,0:T(8,128)(2,1)}), bf16[4,256,512]{2,1,0:T(8,128)(2,1)S(1)}, u32[]{:S(2)}, u32[]{:S(2)}) async-start(bf16[4,256,512]{2,1,0:T(8,128)(2,1)} %turned.3), calls=%async_computation.1 | async-start | bytes 2097152 | tf_op jit(solution)/shard_map/all_to_all | solution.py:523
  8.9 1.6 copy.27
  10.5 1.3 copy-done.8
  11.9 2.6 %copy.26 = bf16[2,2048,2,256]{3,1,2,0:T(8,128)(2,1)} copy(bf16[2,2048,2,256]{3,2,1,0:T(2,128)(2,1)S(1)} %copy-done.8) | data formatting | bytes 8388608 | tf_op args[1]
  14.4 17.1 %mix_local.1 = (f32[2,512,256]{2,1,0:T(8,128)}, f32[2,512,256]{2,1,0:T(8,128)}, bf16[2,512,128]{2,1,0:T(8,128)(2,1)}, f32[2,512,8]{2,1,0:T(8,128)}, bf16[2,272,128]{2,1,0:T(8,128)(2,1)}) custom-call(bf16[2,512,2048]{2,1,0:T(8,128)(2,1)} %refs_5_.3, bf16[2,2,2048,256]{3,2,1,0:T(8,128)(2,1)} %bitcast.17, bf16[2,2,2048,128]{3,2,1,0:T(8,128)(2,1)} %bitcast.18, ...), custom_call_target="tpu_custom_call" | custom-call | flops 10000000000 | bytes 16000000 | tf_op jit(solution)/shard_map/mix_local/pallas_call | solution.py:172
  31.6 4.8 %collective-permute-start.3 = (bf16[2,272,128]{2,1,0:T(8,128)(2,1)}, bf16[2,272,128]{2,1,0:T(8,128)(2,1)S(1)}, u32[]{:S(2)}, u32[]{:S(2)}) collective-permute-start(bf16[2,272,128]{2,1,0:T(8,128)(2,1)} %get-tuple-element.21), channel_id=1, source_target_pairs={{0,64},{16,80},{32,96},{48,112},{1,65},{17,81},{33,97},{49,113},{2... | collective-permute-start | bytes 417800 | tf_op jit(solution)/shard_map/ppermute | solution.py:525
  36.4 2.1 %collective-permute-start.2 = (bf16[2,272,128]{2,1,0:T(8,128)(2,1)}, bf16[2,272,128]{2,1,0:T(8,128)(2,1)S(1)}, u32[]{:S(2)}, u32[]{:S(2)}) collective-permute-start(bf16[2,272,128]{2,1,0:T(8,128)(2,1)} %get-tuple-element.21), channel_id=1, source_target_pairs={{0,48},{16,64},{32,80},{48,96},{64,112},{1,49},{17,65},{33,81},{49... | collective-permute-start | bytes 417800 | tf_op jit(solution)/shard_map/ppermute | solution.py:525
  38.5 2.3 %collective-permute-start.1 = (bf16[2,272,128]{2,1,0:T(8,128)(2,1)}, bf16[2,272,128]{2,1,0:T(8,128)(2,1)S(1)}, u32[]{:S(2)}, u32[]{:S(2)}) collective-permute-start(bf16[2,272,128]{2,1,0:T(8,128)(2,1)} %get-tuple-element.21), channel_id=1, source_target_pairs={{0,32},{16,48},{32,64},{48,80},{64,96},{80,112},{1,33},{17,49},{33... | collective-permute-start | bytes 417800 | tf_op jit(solution)/shard_map/ppermute | solution.py:525
  40.8 2.2 %collective-permute-start = (bf16[2,272,128]{2,1,0:T(8,128)(2,1)}, bf16[2,272,128]{2,1,0:T(8,128)(2,1)S(1)}, u32[]{:S(2)}, u32[]{:S(2)}) collective-permute-start(bf16[2,272,128]{2,1,0:T(8,128)(2,1)} %get-tuple-element.21), channel_id=1, source_target_pairs={{0,16},{16,32},{32,48},{48,64},{64,80},{80,96},{96,112},{1,17},{17... | collective-permute-start | bytes 417800 | tf_op jit(solution)/shard_map/ppermute | solution.py:525
  43.1 2.3 %turned.2 = bf16[4,256,512]{2,1,0:T(8,128)(2,1)} custom-call(bf16[2,256,2048]{2,1,0:T(8,128)(2,1)} %w_ref.3), custom_call_target="tpu_custom_call" | custom-call | bytes 2000000 | tf_op jit(solution)/shard_map/turned/pallas_call | solution.py:484
  45.4 4.0 %all-to-all-start = ((bf16[4,256,512]{2,1,0:T(8,128)(2,1)}), bf16[4,256,512]{2,1,0:T(8,128)(2,1)S(1)}, u32[]{:S(2)}, u32[]{:S(2)}) async-start(bf16[4,256,512]{2,1,0:T(8,128)(2,1)} %turned.2), calls=%async_computation | async-start | bytes 2097152 | tf_op jit(solution)/shard_map/all_to_all | solution.py:523
  49.5 0.6 copy-done.19
  50.2 3.9 %gate_out.2.refs_15_.refs_1_ = bf16[528,256]{1,0:T(8,128)(2,1)} custom-call(s32[4]{0:T(128)} %refs_0_.4, s32[4]{0:T(128)} %refs_1_.3, f32[2,512,256]{2,1,0:T(8,128)} %get-tuple-element.17.refs_2_, f32[2,512,256]{2,1,0:T(8,128)} %get-tuple-element.18.refs_3_, bf16[2,512,128]{2,1,0:T(8,128)(2,1)} %get-tuple-element.19.refs_4_, ...), custom_call_target="tpu_custom_call" | custom-call | flops 1000000000 | bytes 4000000 | tf_op jit(solution)/shard_map/gate_out/pallas_call | solution.py:252
  54.2 4.1 %gate_out.3.refs_6_.refs_1_ = bf16[528,256]{1,0:T(8,128)(2,1)} custom-call(s32[4]{0:T(128)} %refs_0_.4, s32[4]{0:T(128)} %refs_1_.3, f32[2,512,256]{2,1,0:T(8,128)} %get-tuple-element.17.refs_2_, f32[2,512,256]{2,1,0:T(8,128)} %get-tuple-element.18.refs_3_, bf16[2,512,128]{2,1,0:T(8,128)(2,1)} %get-tuple-element.19.refs_4_, ...), custom_call_target="tpu_custom_call" | custom-call | flops 1000000000 | bytes 4000000 | tf_op jit(solution)/shard_map/gate_out/pallas_call | solution.py:252
  58.3 3.0 %collective-permute-start.12 = (bf16[528,256]{1,0:T(8,128)(2,1)}, bf16[528,256]{1,0:T(8,128)(2,1)S(1)}, u32[]{:S(2)}, u32[]{:S(2)}) collective-permute-start(bf16[528,256]{1,0:T(8,128)(2,1)} %gate_out.3.refs_6_.refs_1_), channel_id=1, source_target_pairs={{0,3},{1,0},{2,1},{3,2},{4,7},{5,4},{6,5},{7,6},{8,11},{9,8},{10,9... | collective-permute-start | bytes 811016 | tf_op jit(solution)/shard_map/ppermute | solution.py:496
  61.8 0.6 collective-permute-start.10
  62.4 2.7 %collective-permute-start.6 = (bf16[528,256]{1,0:T(8,128)(2,1)S(1)}, bf16[528,256]{1,0:T(8,128)(2,1)S(1)}, u32[]{:S(2)}, u32[]{:S(2)}) collective-permute-start(bf16[528,256]{1,0:T(8,128)(2,1)S(1)} %copy-done.10), channel_id=1, source_target_pairs={{0,12},{4,0},{8,4},{12,8},{1,13},{5,1},{9,5},{13,9},{2,14},{6,2},{... | collective-permute-start | bytes 811016 | tf_op jit(solution)/shard_map/ppermute | solution.py:496
  65.6 6.9 %collective-permute-done.12.refs_4_ = bf16[528,256]{1,0:T(8,128)(2,1)S(1)} collective-permute-done((bf16[528,256]{1,0:T(8,128)(2,1)}, bf16[528,256]{1,0:T(8,128)(2,1)S(1)}, u32[]{:S(2)}, u32[]{:S(2)}) %collective-permute-start.12) | collective-permute-done | bytes 270368 | tf_op jit(solution)/shard_map/ppermute | solution.py:496
  72.6 0.7 pad_add_fusion.1.refs_0_.at1_ref
  73.2 3.9 %collective-permute-done.10.refs_2_ = bf16[528,256]{1,0:T(8,128)(2,1)S(1)} collective-permute-done((bf16[528,256]{1,0:T(8,128)(2,1)}, bf16[528,256]{1,0:T(8,128)(2,1)S(1)}, u32[]{:S(2)}, u32[]{:S(2)}) %collective-permute-start.10) | collective-permute-done | bytes 270368 | tf_op jit(solution)/shard_map/ppermute | solution.py:496
  77.2 0.7 copy-done.35
  77.9 3.2 %out_blocks.3 = (bf16[144,512]{1,0:T(8,128)(2,1)}, bf16[144,512]{1,0:T(8,128)(2,1)}, bf16[144,512]{1,0:T(8,128)(2,1)}, bf16[144,512]{1,0:T(8,128)(2,1)}) custom-call(s32[2]{0:T(128)} %pad_add_fusion.1.refs_0_.at1_ref, bf16[528,256]{1,0:T(8,128)(2,1)} %gate_out.3.refs_6_.refs_1_, bf16[528,256]{1,0:T(8,128)(2,1)} %copy-done.35, bf16[528,256]{1,0:T(8,128)(2,1)} %copy-done.34, ...), custom_call_target="tpu_custom_call" | custom-call | flops 1000000000 | bytes 3000000 | tf_op jit(solution)/shard_map/out_blocks/pallas_call | solution.py:296
  81.0 1.5 collective-permute-start.16
  82.5 2.4 %collective-permute-start.17 = (bf16[144,512]{1,0:T(8,128)(2,1)}, bf16[144,512]{1,0:T(8,128)(2,1)S(1)}, u32[]{:S(2)}, u32[]{:S(2)}) collective-permute-start(bf16[144,512]{1,0:T(8,128)(2,1)} %get-tuple-element.28), channel_id=1, source_target_pairs={{0,8},{4,12},{8,0},{12,4},{1,9},{5,13},{9,1},{13,5},{2,10},{6,14},... | collective-permute-start | bytes 442376 | tf_op jit(solution)/shard_map/ppermute | solution.py:496
  84.9 1.2 collective-permute-start.18
  86.1 0.6 pad_add_fusion.refs_0_.at0_ref
  86.8 0.7 copy-done.31
  87.5 1.0 copy-done.12
  88.6 3.2 %out_blocks.2 = (bf16[144,512]{1,0:T(8,128)(2,1)}, bf16[144,512]{1,0:T(8,128)(2,1)}, bf16[144,512]{1,0:T(8,128)(2,1)}, bf16[144,512]{1,0:T(8,128)(2,1)}) custom-call(s32[2]{0:T(128)} %pad_add_fusion.refs_0_.at0_ref, bf16[528,256]{1,0:T(8,128)(2,1)} %gate_out.2.refs_15_.refs_1_, bf16[528,256]{1,0:T(8,128)(2,1)} %copy-done.32, bf16[528,256]{1,0:T(8,128)(2,1)} %copy-done.31, ...), custom_call_target="tpu_custom_call" | custom-call | flops 1000000000 | bytes 3000000 | tf_op jit(solution)/shard_map/out_blocks/pallas_call | solution.py:296
  91.8 2.0 %collective-permute-start.8 = (bf16[144,512]{1,0:T(8,128)(2,1)}, bf16[144,512]{1,0:T(8,128)(2,1)S(1)}, u32[]{:S(2)}, u32[]{:S(2)}) collective-permute-start(bf16[144,512]{1,0:T(8,128)(2,1)} %get-tuple-element.24), channel_id=1, source_target_pairs={{0,2},{1,3},{2,0},{3,1},{4,6},{5,7},{6,4},{7,5},{8,10},{9,11},{10,... | collective-permute-start | bytes 442376 | tf_op jit(solution)/shard_map/ppermute | solution.py:496
  93.7 0.8 collective-permute-start.9
  94.5 0.6 copy-done.24
  95.2 2.8 %residual_block.3.refs_1_ = bf16[144,512]{1,0:T(8,128)(2,1)} custom-call(s32[2]{0:T(128)} %pad_add_fusion.1.refs_0_.at1_ref, bf16[144,512]{1,0:T(8,128)(2,1)} %get-tuple-element.26.refs_7_.refs_1_, bf16[144,512]{1,0:T(8,128)(2,1)} %copy-done.23, bf16[144,512]{1,0:T(8,128)(2,1)} %copy-done.24, bf16[144,512]{1,0:T(8,128)(2,1)} %copy-done.26, ...), custom_call_target="tpu_custom_call" | custom-call | flops 1000000 | bytes 1000000 | tf_op jit(solution)/shard_map/residual_block/pallas_call | solution.py:324
  98.6 2.0 %collective-permute-start.20 = (bf16[144,512]{1,0:T(8,128)(2,1)}, bf16[144,512]{1,0:T(8,128)(2,1)S(1)}, u32[]{:S(2)}, u32[]{:S(2)}) collective-permute-start(bf16[144,512]{1,0:T(8,128)(2,1)} %residual_block.3.refs_1_), channel_id=1, source_target_pairs={{0,2},{1,3},{2,0},{3,1},{4,6},{5,7},{6,4},{7,5},{8,10},{9,11},{10,... | collective-permute-start | bytes 442376 | tf_op jit(solution)/shard_map/ppermute | solution.py:496
  100.6 0.7 collective-permute-start.19
  101.3 0.6 copy-done.27
  102.0 2.8 %residual_block.2.refs_1_ = bf16[144,512]{1,0:T(8,128)(2,1)} custom-call(s32[2]{0:T(128)} %pad_add_fusion.refs_0_.at0_ref, bf16[144,512]{1,0:T(8,128)(2,1)} %get-tuple-element.22.refs_1_, bf16[144,512]{1,0:T(8,128)(2,1)} %copy-done.25, bf16[144,512]{1,0:T(8,128)(2,1)} %copy-done.27, bf16[144,512]{1,0:T(8,128)(2,1)} %copy-done.28, ...), custom_call_target="tpu_custom_call" | custom-call | flops 1000000 | bytes 1000000 | tf_op jit(solution)/shard_map/residual_block/pallas_call | solution.py:324
  104.8 2.6 %collective-permute-start.14 = (bf16[144,512]{1,0:T(8,128)(2,1)}, bf16[144,512]{1,0:T(8,128)(2,1)S(1)}, u32[]{:S(2)}, u32[]{:S(2)}) collective-permute-start(bf16[144,512]{1,0:T(8,128)(2,1)} %residual_block.2.refs_1_), channel_id=1, source_target_pairs={{0,8},{4,12},{8,0},{12,4},{1,9},{5,13},{9,1},{13,5},{2,10},{6,14},... | collective-permute-start | bytes 442376 | tf_op jit(solution)/shard_map/ppermute | solution.py:496
  107.5 1.5 collective-permute-done.15.refs_4_.refs_7_
  109.0 1.5 collective-permute-done.14.refs_3_.refs_6_
  110.5 2.3 %collective-permute-done.13.refs_2_.refs_5_ = bf16[144,512]{1,0:T(8,128)(2,1)S(1)} collective-permute-done((bf16[144,512]{1,0:T(8,128)(2,1)}, bf16[144,512]{1,0:T(8,128)(2,1)S(1)}, u32[]{:S(2)}, u32[]{:S(2)}) %collective-permute-start.13) | collective-permute-done | bytes 147488 | tf_op jit(solution)/shard_map/ppermute | solution.py:496
  112.9 0.7 copy-done.18
  113.5 2.0 %join_columns.2.refs_1_.refs_0_ = bf16[144,2048]{1,0:T(8,128)(2,1)} custom-call(s32[2]{0:T(128)} %pad_add_fusion.refs_0_.at0_ref, bf16[144,512]{1,0:T(8,128)(2,1)} %residual_block.2.refs_1_, bf16[144,512]{1,0:T(8,128)(2,1)} %copy-done.18, bf16[144,512]{1,0:T(8,128)(2,1)} %copy-done.17, bf16[144,512]{1,0:T(8,128)(2,1)} %copy-done.16, ...), custom_call_target="tpu_custom_call" | custom-call | flops 100000 | bytes 1000000 | tf_op jit(solution)/shard_map/join_columns/pallas_call | solution.py:360
  115.6 2.6 %collective-permute-start.24 = (bf16[144,2048]{1,0:T(8,128)(2,1)}, bf16[144,2048]{1,0:T(8,128)(2,1)S(1)}, u32[]{:S(2)}, u32[]{:S(2)}) collective-permute-start(bf16[144,2048]{1,0:T(8,128)(2,1)} %join_columns.2.refs_1_.refs_0_), channel_id=1, source_target_pairs={{0,3},{1,0},{2,1},{3,2},{4,7},{5,4},{6,5},{7,6},{8,11},{9,8},{10,9... | collective-permute-start | bytes 1769480 | tf_op jit(solution)/shard_map/ppermute | solution.py:496
  118.8 2.0 %join_columns.3.refs_2_.refs_4_ = bf16[144,2048]{1,0:T(8,128)(2,1)} custom-call(s32[2]{0:T(128)} %pad_add_fusion.1.refs_0_.at1_ref, bf16[144,512]{1,0:T(8,128)(2,1)} %residual_block.3.refs_1_, bf16[144,512]{1,0:T(8,128)(2,1)} %copy-done.15, bf16[144,512]{1,0:T(8,128)(2,1)} %copy-done.14, bf16[144,512]{1,0:T(8,128)(2,1)} %copy-done.13, ...), custom_call_target="tpu_custom_call" | custom-call | flops 100000 | bytes 1000000 | tf_op jit(solution)/shard_map/join_columns/pallas_call | solution.py:360
  120.8 0.8 collective-permute-start.27
  121.6 1.7 collective-permute-start.26
  123.3 4.6 %collective-permute-done.24.refs_3_ = bf16[144,2048]{1,0:T(8,128)(2,1)S(1)} collective-permute-done((bf16[144,2048]{1,0:T(8,128)(2,1)}, bf16[144,2048]{1,0:T(8,128)(2,1)S(1)}, u32[]{:S(2)}, u32[]{:S(2)}) %collective-permute-start.24) | collective-permute-done | bytes 589856 | tf_op jit(solution)/shard_map/ppermute | solution.py:496
  128.4 4.9 %copy-done = bf16[2,2048,1664]{2,1,0:T(8,128)(2,1)S(1)} copy-done((bf16[2,2048,1664]{2,1,0:T(8,128)(2,1)S(1)}, bf16[2,2048,1664]{2,1,0:T(8,128)(2,1)}, u32[]{:S(2)}) %copy-start) | copy-done | bytes 13631512
  133.3 1.1 copy-done.1
  134.3 1.1 copy-done.3
  135.4 1.0 fetched.1.refs_8_
  136.4 10.8 %collective-permute-done.22.refs_1_ = bf16[144,2048]{1,0:T(8,128)(2,1)S(1)} collective-permute-done((bf16[144,2048]{1,0:T(8,128)(2,1)}, bf16[144,2048]{1,0:T(8,128)(2,1)S(1)}, u32[]{:S(2)}, u32[]{:S(2)}) %collective-permute-start.22) | collective-permute-done | bytes 589856 | tf_op jit(solution)/shard_map/ppermute | solution.py:496
  147.2 9.2 %head_stats.1 = f32[16,16,128]{2,1,0:T(8,128)S(1)} custom-call(s32[1]{0:T(128)} %bitcast.place_ref, s32[2]{0:T(128)S(1)} %copy-done.6, s32[2]{0:T(128)S(1)} %copy-done.5, bf16[144,2048]{1,0:T(8,128)(2,1)S(1)} %copy-done.2, bf16[144,2048]{1,0:T(8,128)(2,1)S(1)} %collective-permute-done.22.refs_1_, bf16[144,2048]{1,0:T(8,128)(2,1)S(1)} %collective-permute-done.23.refs_2_, ...), custom_call_target="tpu_custom_call" | custom-call | flops 6979321856 | bytes 10000000 | tf_op jit(solution)/shard_map/head_stats/pallas_call | solution.py:431
  156.4 13.2 %all_to_all.15.stat_ref = f32[16,16,128]{2,1,0:T(8,128)} all-to-all(f32[16,16,128]{2,1,0:T(8,128)S(1)} %head_stats.1), channel_id=1, replica_groups=mesh['y'=4,'core'=2,'x'=4,'z'=4] {'x','z'}, dimensions={0} | all-to-all | bytes 262144 | tf_op jit(solution)/shard_map/all_to_all | solution.py:539
  169.7 1.6 token_diffs.1
  171.3 8.3 %collective-permute-start.28 = (f32[8,128]{1,0:T(8,128)}, f32[8,128]{1,0:T(8,128)S(1)}, u32[]{:S(2)}, u32[]{:S(2)}) collective-permute-start(f32[8,128]{1,0:T(8,128)} %get-tuple-element.31), channel_id=1, source_target_pairs={{0,16},{16,0},{1,17},{17,1},{2,18},{18,2},{3,19},{19,3},{4,20},{20... | collective-permute-start | bytes 12296 | tf_op jit(solution)/shard_map/ppermute | solution.py:541
  179.6 1.0 collective-permute-done.28
  180.6 0.7 add.20
  181.3 1.5 collective-permute-start.29
  182.8 1.0 collective-permute-done.31
  183.8 1.5 collective-permute-done.30
  185.3 1.1 collective-permute-done.29
  (99 shorter events, 3.9 us)
Async XLA Ops:
  0.6 8.3 %copy-start.9 = (bf16[2,2048,2,128]{3,2,1,0:T(2,128)(2,1)S(1)}, bf16[2,2048,2,128]{3,2,1,0:T(2,128)(2,1)}, u32[]{:S(2)}) copy-start(bf16[2,2048,2,128]{3,2,1,0:T(2,128)(2,1)} %param.20) | copy-start | bytes 6291460
  3.1 42.3 %all-to-all-start.1 = ((bf16[4,256,512]{2,1,0:T(8,128)(2,1)}), bf16[4,256,512]{2,1,0:T(8,128)(2,1)S(1)}, u32[]{:S(2)}, u32[]{:S(2)}) async-start(bf16[4,256,512]{2,1,0:T(8,128)(2,1)} %turned.3), calls=%async_computation.1 | async-start | bytes 2097152 | tf_op jit(solution)/shard_map/all_to_all | solution.py:523
  8.9 2.9 %copy-start.8 = (bf16[2,2048,2,256]{3,2,1,0:T(2,128)(2,1)S(1)}, bf16[2,2048,2,256]{3,2,1,0:T(2,128)(2,1)}, u32[]{:S(2)}) copy-start(bf16[2,2048,2,256]{3,2,1,0:T(2,128)(2,1)} %param.19) | copy-start | bytes 12582916
  31.6 17.8 %collective-permute-start.3 = (bf16[2,272,128]{2,1,0:T(8,128)(2,1)}, bf16[2,272,128]{2,1,0:T(8,128)(2,1)S(1)}, u32[]{:S(2)}, u32[]{:S(2)}) collective-permute-start(bf16[2,272,128]{2,1,0:T(8,128)(2,1)} %get-tuple-element.21), channel_id=1, source_target_pairs={{0,64},{16,80},{32,96},{48,112},{1,65},{17,81},{33,97},{49,113},{2... | collective-permute-start | bytes 417800 | tf_op jit(solution)/shard_map/ppermute | solution.py:525
  36.4 13.0 %collective-permute-start.2 = (bf16[2,272,128]{2,1,0:T(8,128)(2,1)}, bf16[2,272,128]{2,1,0:T(8,128)(2,1)S(1)}, u32[]{:S(2)}, u32[]{:S(2)}) collective-permute-start(bf16[2,272,128]{2,1,0:T(8,128)(2,1)} %get-tuple-element.21), channel_id=1, source_target_pairs={{0,48},{16,64},{32,80},{48,96},{64,112},{1,49},{17,65},{33,81},{49... | collective-permute-start | bytes 417800 | tf_op jit(solution)/shard_map/ppermute | solution.py:525
  38.5 10.9 %collective-permute-start.1 = (bf16[2,272,128]{2,1,0:T(8,128)(2,1)}, bf16[2,272,128]{2,1,0:T(8,128)(2,1)S(1)}, u32[]{:S(2)}, u32[]{:S(2)}) collective-permute-start(bf16[2,272,128]{2,1,0:T(8,128)(2,1)} %get-tuple-element.21), channel_id=1, source_target_pairs={{0,32},{16,48},{32,64},{48,80},{64,96},{80,112},{1,33},{17,49},{33... | collective-permute-start | bytes 417800 | tf_op jit(solution)/shard_map/ppermute | solution.py:525
  40.8 8.6 %collective-permute-start = (bf16[2,272,128]{2,1,0:T(8,128)(2,1)}, bf16[2,272,128]{2,1,0:T(8,128)(2,1)S(1)}, u32[]{:S(2)}, u32[]{:S(2)}) collective-permute-start(bf16[2,272,128]{2,1,0:T(8,128)(2,1)} %get-tuple-element.21), channel_id=1, source_target_pairs={{0,16},{16,32},{32,48},{48,64},{64,80},{80,96},{96,112},{1,17},{17... | collective-permute-start | bytes 417800 | tf_op jit(solution)/shard_map/ppermute | solution.py:525
  45.4 8.8 %copy-start.11 = (bf16[4,256,512]{2,1,0:T(8,128)(2,1)}, bf16[4,256,512]{2,1,0:T(8,128)(2,1)S(1)}, u32[]{:S(2)}) copy-start(bf16[4,256,512]{2,1,0:T(8,128)(2,1)S(1)} %all-to-all-done.1.refs_5_) | copy-start | bytes 3145732
  45.4 41.4 %all-to-all-start = ((bf16[4,256,512]{2,1,0:T(8,128)(2,1)}), bf16[4,256,512]{2,1,0:T(8,128)(2,1)S(1)}, u32[]{:S(2)}, u32[]{:S(2)}) async-start(bf16[4,256,512]{2,1,0:T(8,128)(2,1)} %turned.2), calls=%async_computation | async-start | bytes 2097152 | tf_op jit(solution)/shard_map/all_to_all | solution.py:523
  49.4 0.7 copy-start.20
  49.4 0.7 copy-start.21
  49.5 0.8 copy-start.22
  54.2 8.2 %copy-start.10 = (bf16[528,256]{1,0:T(8,128)(2,1)S(1)}, bf16[528,256]{1,0:T(8,128)(2,1)}, u32[]{:S(2)}) copy-start(bf16[528,256]{1,0:T(8,128)(2,1)} %gate_out.2.refs_15_.refs_1_) | copy-start | bytes 811012
  58.3 14.3 %collective-permute-start.12 = (bf16[528,256]{1,0:T(8,128)(2,1)}, bf16[528,256]{1,0:T(8,128)(2,1)S(1)}, u32[]{:S(2)}, u32[]{:S(2)}) collective-permute-start(bf16[528,256]{1,0:T(8,128)(2,1)} %gate_out.3.refs_6_.refs_1_), channel_id=1, source_target_pairs={{0,3},{1,0},{2,1},{3,2},{4,7},{5,4},{6,5},{7,6},{8,11},{9,8},{10,9... | collective-permute-start | bytes 811016 | tf_op jit(solution)/shard_map/ppermute | solution.py:496
  61.2 12.0 %collective-permute-start.11 = (bf16[528,256]{1,0:T(8,128)(2,1)}, bf16[528,256]{1,0:T(8,128)(2,1)S(1)}, u32[]{:S(2)}, u32[]{:S(2)}) collective-permute-start(bf16[528,256]{1,0:T(8,128)(2,1)} %gate_out.3.refs_6_.refs_1_), channel_id=1, source_target_pairs={{0,2},{1,3},{2,0},{3,1},{4,6},{5,7},{6,4},{7,5},{8,10},{9,11},{10,... | collective-permute-start | bytes 811016 | tf_op jit(solution)/shard_map/ppermute | solution.py:496
  61.8 15.3 %collective-permute-start.10 = (bf16[528,256]{1,0:T(8,128)(2,1)}, bf16[528,256]{1,0:T(8,128)(2,1)S(1)}, u32[]{:S(2)}, u32[]{:S(2)}) collective-permute-start(bf16[528,256]{1,0:T(8,128)(2,1)} %gate_out.3.refs_6_.refs_1_), channel_id=1, source_target_pairs={{0,1},{1,2},{2,3},{3,0},{4,5},{5,6},{6,7},{7,4},{8,9},{9,10},{10,1... | collective-permute-start | bytes 811016 | tf_op jit(solution)/shard_map/ppermute | solution.py:496
  62.4 22.5 %collective-permute-start.6 = (bf16[528,256]{1,0:T(8,128)(2,1)S(1)}, bf16[528,256]{1,0:T(8,128)(2,1)S(1)}, u32[]{:S(2)}, u32[]{:S(2)}) collective-permute-start(bf16[528,256]{1,0:T(8,128)(2,1)S(1)} %copy-done.10), channel_id=1, source_target_pairs={{0,12},{4,0},{8,4},{12,8},{1,13},{5,1},{9,5},{13,9},{2,14},{6,2},{... | collective-permute-start | bytes 811016 | tf_op jit(solution)/shard_map/ppermute | solution.py:496
  65.1 21.7 %collective-permute-start.5 = (bf16[528,256]{1,0:T(8,128)(2,1)S(1)}, bf16[528,256]{1,0:T(8,128)(2,1)S(1)}, u32[]{:S(2)}, u32[]{:S(2)}) collective-permute-start(bf16[528,256]{1,0:T(8,128)(2,1)S(1)} %copy-done.10), channel_id=1, source_target_pairs={{0,8},{4,12},{8,0},{12,4},{1,9},{5,13},{9,1},{13,5},{2,10},{6,14},... | collective-permute-start | bytes 811016 | tf_op jit(solution)/shard_map/ppermute | solution.py:496
  72.6 4.6 %copy-start.33 = (bf16[528,256]{1,0:T(8,128)(2,1)}, bf16[528,256]{1,0:T(8,128)(2,1)S(1)}, u32[]{:S(2)}) copy-start(bf16[528,256]{1,0:T(8,128)(2,1)S(1)} %collective-permute-done.12.refs_4_) | copy-start | bytes 811012
  72.6 14.2 %collective-permute-start.4 = (bf16[528,256]{1,0:T(8,128)(2,1)S(1)}, bf16[528,256]{1,0:T(8,128)(2,1)S(1)}, u32[]{:S(2)}, u32[]{:S(2)}) collective-permute-start(bf16[528,256]{1,0:T(8,128)(2,1)S(1)} %copy-done.10), channel_id=1, source_target_pairs={{0,4},{4,8},{8,12},{12,0},{1,5},{5,9},{9,13},{13,1},{2,6},{6,10},{... | collective-permute-start | bytes 811016 | tf_op jit(solution)/shard_map/ppermute | solution.py:496
  73.2 3.9 %copy-start.34 = (bf16[528,256]{1,0:T(8,128)(2,1)}, bf16[528,256]{1,0:T(8,128)(2,1)S(1)}, u32[]{:S(2)}) copy-start(bf16[528,256]{1,0:T(8,128)(2,1)S(1)} %collective-permute-done.11.refs_3_) | copy-start | bytes 811012
  77.2 0.7 copy-start.35
  81.0 12.7 %collective-permute-start.16 = (bf16[144,512]{1,0:T(8,128)(2,1)}, bf16[144,512]{1,0:T(8,128)(2,1)S(1)}, u32[]{:S(2)}, u32[]{:S(2)}) collective-permute-start(bf16[144,512]{1,0:T(8,128)(2,1)} %get-tuple-element.27), channel_id=1, source_target_pairs={{0,4},{4,8},{8,12},{12,0},{1,5},{5,9},{9,13},{13,1},{2,6},{6,10},{... | collective-permute-start | bytes 442376 | tf_op jit(solution)/shard_map/ppermute | solution.py:496
  82.5 12.0 %collective-permute-start.17 = (bf16[144,512]{1,0:T(8,128)(2,1)}, bf16[144,512]{1,0:T(8,128)(2,1)S(1)}, u32[]{:S(2)}, u32[]{:S(2)}) collective-permute-start(bf16[144,512]{1,0:T(8,128)(2,1)} %get-tuple-element.28), channel_id=1, source_target_pairs={{0,8},{4,12},{8,0},{12,4},{1,9},{5,13},{9,1},{13,5},{2,10},{6,14},... | collective-permute-start | bytes 442376 | tf_op jit(solution)/shard_map/ppermute | solution.py:496
  84.9 1.9 copy-start.30
  84.9 9.6 %collective-permute-start.18 = (bf16[144,512]{1,0:T(8,128)(2,1)}, bf16[144,512]{1,0:T(8,128)(2,1)S(1)}, u32[]{:S(2)}, u32[]{:S(2)}) collective-permute-start(bf16[144,512]{1,0:T(8,128)(2,1)} %get-tuple-element.29), channel_id=1, source_target_pairs={{0,12},{4,0},{8,4},{12,8},{1,13},{5,1},{9,5},{13,9},{2,14},{6,2},{... | collective-permute-start | bytes 442376 | tf_op jit(solution)/shard_map/ppermute | solution.py:496
  86.7 0.7 copy-start.31
  86.7 0.8 copy-start.32
  87.5 1.0 copy-start.12
  91.8 8.8 %collective-permute-start.7 = (bf16[144,512]{1,0:T(8,128)(2,1)}, bf16[144,512]{1,0:T(8,128)(2,1)S(1)}, u32[]{:S(2)}, u32[]{:S(2)}) collective-permute-start(bf16[144,512]{1,0:T(8,128)(2,1)} %get-tuple-element.23), channel_id=1, source_target_pairs={{0,1},{1,2},{2,3},{3,0},{4,5},{5,6},{6,7},{7,4},{8,9},{9,10},{10,1... | collective-permute-start | bytes 442376 | tf_op jit(solution)/shard_map/ppermute | solution.py:496
  91.8 9.5 %collective-permute-start.8 = (bf16[144,512]{1,0:T(8,128)(2,1)}, bf16[144,512]{1,0:T(8,128)(2,1)S(1)}, u32[]{:S(2)}, u32[]{:S(2)}) collective-permute-start(bf16[144,512]{1,0:T(8,128)(2,1)} %get-tuple-element.24), channel_id=1, source_target_pairs={{0,2},{1,3},{2,0},{3,1},{4,6},{5,7},{6,4},{7,5},{8,10},{9,11},{10,... | collective-permute-start | bytes 442376 | tf_op jit(solution)/shard_map/ppermute | solution.py:496
  93.7 0.8 copy-start.23
  93.7 7.5 %collective-permute-start.9 = (bf16[144,512]{1,0:T(8,128)(2,1)}, bf16[144,512]{1,0:T(8,128)(2,1)S(1)}, u32[]{:S(2)}, u32[]{:S(2)}) collective-permute-start(bf16[144,512]{1,0:T(8,128)(2,1)} %get-tuple-element.25), channel_id=1, source_target_pairs={{0,3},{1,0},{2,1},{3,2},{4,7},{5,4},{6,5},{7,6},{8,11},{9,8},{10,9... | collective-permute-start | bytes 442376 | tf_op jit(solution)/shard_map/ppermute | solution.py:496
  94.5 0.7 copy-start.26
  98.1 9.3 %collective-permute-start.21 = (bf16[144,512]{1,0:T(8,128)(2,1)}, bf16[144,512]{1,0:T(8,128)(2,1)S(1)}, u32[]{:S(2)}, u32[]{:S(2)}) collective-permute-start(bf16[144,512]{1,0:T(8,128)(2,1)} %residual_block.3.refs_1_), channel_id=1, source_target_pairs={{0,3},{1,0},{2,1},{3,2},{4,7},{5,4},{6,5},{7,6},{8,11},{9,8},{10,9... | collective-permute-start | bytes 442376 | tf_op jit(solution)/shard_map/ppermute | solution.py:496
  98.6 8.8 %collective-permute-start.20 = (bf16[144,512]{1,0:T(8,128)(2,1)}, bf16[144,512]{1,0:T(8,128)(2,1)S(1)}, u32[]{:S(2)}, u32[]{:S(2)}) collective-permute-start(bf16[144,512]{1,0:T(8,128)(2,1)} %residual_block.3.refs_1_), channel_id=1, source_target_pairs={{0,2},{1,3},{2,0},{3,1},{4,6},{5,7},{6,4},{7,5},{8,10},{9,11},{10,... | collective-permute-start | bytes 442376 | tf_op jit(solution)/shard_map/ppermute | solution.py:496
  100.6 6.9 %collective-permute-start.19 = (bf16[144,512]{1,0:T(8,128)(2,1)}, bf16[144,512]{1,0:T(8,128)(2,1)S(1)}, u32[]{:S(2)}, u32[]{:S(2)}) collective-permute-start(bf16[144,512]{1,0:T(8,128)(2,1)} %residual_block.3.refs_1_), channel_id=1, source_target_pairs={{0,1},{1,2},{2,3},{3,0},{4,5},{5,6},{6,7},{7,4},{8,9},{9,10},{10,1... | collective-permute-start | bytes 442376 | tf_op jit(solution)/shard_map/ppermute | solution.py:496
  104.8 4.2 %collective-permute-start.15 = (bf16[144,512]{1,0:T(8,128)(2,1)}, bf16[144,512]{1,0:T(8,128)(2,1)S(1)}, u32[]{:S(2)}, u32[]{:S(2)}) collective-permute-start(bf16[144,512]{1,0:T(8,128)(2,1)} %residual_block.2.refs_1_), channel_id=1, source_target_pairs={{0,12},{4,0},{8,4},{12,8},{1,13},{5,1},{9,5},{13,9},{2,14},{6,2},{... | collective-permute-start | bytes 442376 | tf_op jit(solution)/shard_map/ppermute | solution.py:496
  104.8 5.7 %collective-permute-start.14 = (bf16[144,512]{1,0:T(8,128)(2,1)}, bf16[144,512]{1,0:T(8,128)(2,1)S(1)}, u32[]{:S(2)}, u32[]{:S(2)}) collective-permute-start(bf16[144,512]{1,0:T(8,128)(2,1)} %residual_block.2.refs_1_), channel_id=1, source_target_pairs={{0,8},{4,12},{8,0},{12,4},{1,9},{5,13},{9,1},{13,5},{2,10},{6,14},... | collective-permute-start | bytes 442376 | tf_op jit(solution)/shard_map/ppermute | solution.py:496
  107.4 5.4 %copy-start.13 = (bf16[144,512]{1,0:T(8,128)(2,1)}, bf16[144,512]{1,0:T(8,128)(2,1)S(1)}, u32[]{:S(2)}) copy-start(bf16[144,512]{1,0:T(8,128)(2,1)S(1)} %collective-permute-done.21.refs_7_.refs_4_) | copy-start | bytes 442372
  107.4 5.4 %collective-permute-start.13 = (bf16[144,512]{1,0:T(8,128)(2,1)}, bf16[144,512]{1,0:T(8,128)(2,1)S(1)}, u32[]{:S(2)}, u32[]{:S(2)}) collective-permute-start(bf16[144,512]{1,0:T(8,128)(2,1)} %residual_block.2.refs_1_), channel_id=1, source_target_pairs={{0,4},{4,8},{8,12},{12,0},{1,5},{5,9},{9,13},{13,1},{2,6},{6,10},{... | collective-permute-start | bytes 442376 | tf_op jit(solution)/shard_map/ppermute | solution.py:496
  107.4 5.4 %copy-start.14 = (bf16[144,512]{1,0:T(8,128)(2,1)}, bf16[144,512]{1,0:T(8,128)(2,1)S(1)}, u32[]{:S(2)}) copy-start(bf16[144,512]{1,0:T(8,128)(2,1)S(1)} %collective-permute-done.20.refs_6_.refs_3_) | copy-start | bytes 442372
  107.4 5.4 %copy-start.15 = (bf16[144,512]{1,0:T(8,128)(2,1)}, bf16[144,512]{1,0:T(8,128)(2,1)S(1)}, u32[]{:S(2)}) copy-start(bf16[144,512]{1,0:T(8,128)(2,1)S(1)} %collective-permute-done.19.refs_5_.refs_2_) | copy-start | bytes 442372
  109.0 3.8 %copy-start.16 = (bf16[144,512]{1,0:T(8,128)(2,1)}, bf16[144,512]{1,0:T(8,128)(2,1)S(1)}, u32[]{:S(2)}) copy-start(bf16[144,512]{1,0:T(8,128)(2,1)S(1)} %collective-permute-done.15.refs_4_.refs_7_) | copy-start | bytes 442372
  110.5 2.3 %copy-start.17 = (bf16[144,512]{1,0:T(8,128)(2,1)}, bf16[144,512]{1,0:T(8,128)(2,1)S(1)}, u32[]{:S(2)}) copy-start(bf16[144,512]{1,0:T(8,128)(2,1)S(1)} %collective-permute-done.14.refs_3_.refs_6_) | copy-start | bytes 442372
  115.6 12.4 %collective-permute-start.24 = (bf16[144,2048]{1,0:T(8,128)(2,1)}, bf16[144,2048]{1,0:T(8,128)(2,1)S(1)}, u32[]{:S(2)}, u32[]{:S(2)}) collective-permute-start(bf16[144,2048]{1,0:T(8,128)(2,1)} %join_columns.2.refs_1_.refs_0_), channel_id=1, source_target_pairs={{0,3},{1,0},{2,1},{3,2},{4,7},{5,4},{6,5},{7,6},{8,11},{9,8},{10,9... | collective-permute-start | bytes 1769480 | tf_op jit(solution)/shard_map/ppermute | solution.py:496
  118.2 18.2 %collective-permute-start.23 = (bf16[144,2048]{1,0:T(8,128)(2,1)}, bf16[144,2048]{1,0:T(8,128)(2,1)S(1)}, u32[]{:S(2)}, u32[]{:S(2)}) collective-permute-start(bf16[144,2048]{1,0:T(8,128)(2,1)} %join_columns.2.refs_1_.refs_0_), channel_id=1, source_target_pairs={{0,2},{1,3},{2,0},{3,1},{4,6},{5,7},{6,4},{7,5},{8,10},{9,11},{10,... | collective-permute-start | bytes 1769480 | tf_op jit(solution)/shard_map/ppermute | solution.py:496
  118.2 29.0 %collective-permute-start.22 = (bf16[144,2048]{1,0:T(8,128)(2,1)}, bf16[144,2048]{1,0:T(8,128)(2,1)S(1)}, u32[]{:S(2)}, u32[]{:S(2)}) collective-permute-start(bf16[144,2048]{1,0:T(8,128)(2,1)} %join_columns.2.refs_1_.refs_0_), channel_id=1, source_target_pairs={{0,1},{1,2},{2,3},{3,0},{4,5},{5,6},{6,7},{7,4},{8,9},{9,10},{10,1... | collective-permute-start | bytes 1769480 | tf_op jit(solution)/shard_map/ppermute | solution.py:496
  120.8 26.3 %collective-permute-start.27 = (bf16[144,2048]{1,0:T(8,128)(2,1)}, bf16[144,2048]{1,0:T(8,128)(2,1)S(1)}, u32[]{:S(2)}, u32[]{:S(2)}) collective-permute-start(bf16[144,2048]{1,0:T(8,128)(2,1)} %join_columns.3.refs_2_.refs_4_), channel_id=1, source_target_pairs={{0,12},{4,0},{8,4},{12,8},{1,13},{5,1},{9,5},{13,9},{2,14},{6,2},{... | collective-permute-start | bytes 1769480 | tf_op jit(solution)/shard_map/ppermute | solution.py:496
  121.6 25.6 %collective-permute-start.26 = (bf16[144,2048]{1,0:T(8,128)(2,1)}, bf16[144,2048]{1,0:T(8,128)(2,1)S(1)}, u32[]{:S(2)}, u32[]{:S(2)}) collective-permute-start(bf16[144,2048]{1,0:T(8,128)(2,1)} %join_columns.3.refs_2_.refs_4_), channel_id=1, source_target_pairs={{0,8},{4,12},{8,0},{12,4},{1,9},{5,13},{9,1},{13,5},{2,10},{6,14},... | collective-permute-start | bytes 1769480 | tf_op jit(solution)/shard_map/ppermute | solution.py:496
  127.9 19.2 %collective-permute-start.25 = (bf16[144,2048]{1,0:T(8,128)(2,1)}, bf16[144,2048]{1,0:T(8,128)(2,1)S(1)}, u32[]{:S(2)}, u32[]{:S(2)}) collective-permute-start(bf16[144,2048]{1,0:T(8,128)(2,1)} %join_columns.3.refs_2_.refs_4_), channel_id=1, source_target_pairs={{0,4},{4,8},{8,12},{12,0},{1,5},{5,9},{9,13},{13,1},{2,6},{6,10},{... | collective-permute-start | bytes 1769480 | tf_op jit(solution)/shard_map/ppermute | solution.py:496
  128.4 4.9 %copy-start = (bf16[2,2048,1664]{2,1,0:T(8,128)(2,1)S(1)}, bf16[2,2048,1664]{2,1,0:T(8,128)(2,1)}, u32[]{:S(2)}) copy-start(bf16[2,2048,1664]{2,1,0:T(8,128)(2,1)} %refs_0_.5) | copy-start | bytes 40894468
  133.3 1.1 copy-start.1
  134.3 1.1 copy-start.3
  135.4 11.8 %copy-start.2 = (bf16[144,2048]{1,0:T(8,128)(2,1)S(1)}, bf16[144,2048]{1,0:T(8,128)(2,1)}, u32[]{:S(2)}) copy-start(bf16[144,2048]{1,0:T(8,128)(2,1)} %join_columns.2.refs_1_.refs_0_) | copy-start | bytes 1769476
  135.4 11.8 %copy-start.4 = (bf16[144,2048]{1,0:T(8,128)(2,1)S(1)}, bf16[144,2048]{1,0:T(8,128)(2,1)}, u32[]{:S(2)}) copy-start(bf16[144,2048]{1,0:T(8,128)(2,1)} %join_columns.3.refs_2_.refs_4_) | copy-start | bytes 1769476
  135.4 11.8 %copy-start.5 = (s32[2]{0:T(128)S(1)}, s32[2]{0:T(128)}, u32[]{:S(2)}) copy-start(s32[2]{0:T(128)} %pad_add_fusion.1.refs_0_.at1_ref) | copy-start | bytes 28
  135.4 11.8 %copy-start.6 = (s32[2]{0:T(128)S(1)}, s32[2]{0:T(128)}, u32[]{:S(2)}) copy-start(s32[2]{0:T(128)} %pad_add_fusion.refs_0_.at0_ref) | copy-start | bytes 28
  135.4 11.8 %copy-start.7 = (s32[512]{0:T(512)S(1)}, s32[512]{0:T(512)}, u32[]{:S(2)}) copy-start(s32[512]{0:T(512)} %param.30) | copy-start | bytes 6148
  147.2 39.3 %copy-start.29 = (s32[4]{0:T(128)S(1)}, s32[4]{0:T(128)}, u32[]{:S(2)}) copy-start(s32[4]{0:T(128)} %param.35) | copy-start | bytes 52
  171.3 9.3 %collective-permute-start.28 = (f32[8,128]{1,0:T(8,128)}, f32[8,128]{1,0:T(8,128)S(1)}, u32[]{:S(2)}, u32[]{:S(2)}) collective-permute-start(f32[8,128]{1,0:T(8,128)} %get-tuple-element.31), channel_id=1, source_target_pairs={{0,16},{16,0},{1,17},{17,1},{2,18},{18,2},{3,19},{19,3},{4,20},{20... | collective-permute-start | bytes 12296 | tf_op jit(solution)/shard_map/ppermute | solution.py:541
  181.3 2.5 %collective-permute-start.31 = (f32[8,128]{1,0:T(8,128)S(1)}, f32[8,128]{1,0:T(8,128)S(1)}, u32[]{:S(2)}, u32[]{:S(2)}) collective-permute-start(f32[8,128]{1,0:T(8,128)S(1)} %add.20), channel_id=1, source_target_pairs={{0,96},{32,0},{64,32},{96,64},{1,97},{33,1},{65,33},{97,65},{2,98}... | collective-permute-start | bytes 12296 | tf_op jit(solution)/shard_map/ppermute | solution.py:496
  181.3 4.0 %collective-permute-start.30 = (f32[8,128]{1,0:T(8,128)S(1)}, f32[8,128]{1,0:T(8,128)S(1)}, u32[]{:S(2)}, u32[]{:S(2)}) collective-permute-start(f32[8,128]{1,0:T(8,128)S(1)} %add.20), channel_id=1, source_target_pairs={{0,64},{32,96},{64,0},{96,32},{1,65},{33,97},{65,1},{97,33},{2,66}... | collective-permute-start | bytes 12296 | tf_op jit(solution)/shard_map/ppermute | solution.py:496
  181.3 5.1 %collective-permute-start.29 = (f32[8,128]{1,0:T(8,128)S(1)}, f32[8,128]{1,0:T(8,128)S(1)}, u32[]{:S(2)}, u32[]{:S(2)}) collective-permute-start(f32[8,128]{1,0:T(8,128)S(1)} %add.20), channel_id=1, source_target_pairs={{0,32},{32,64},{64,96},{96,0},{1,33},{33,65},{65,97},{97,1},{2,34}... | collective-permute-start | bytes 12296 | tf_op jit(solution)/shard_map/ppermute | solution.py:496
  (6 other events, 4.0 us)

commit v7 on v6

--- a/solution.py
+++ b/solution.py
@@ -263,7 +263,7 @@
             scratch_shapes=[pltpu.VMEM((rows, inner), F32)],
         ),
         out_shape=jax.ShapeDtypeStruct((rows + 16, inner), BF16),
-        cost_estimate=pl.CostEstimate(flops=10**9, bytes_accessed=4 * 10**6, transcendentals=10**5),
+        cost_estimate=pl.CostEstimate(flops=10**9, bytes_accessed=12 * 10**6, transcendentals=10**5),
         name="gate_out",
     )(pages, flags, y, gate, c, e, *recv, pool, pool, pool, pool, gain, *after)
 
@@ -299,7 +299,7 @@
         out_specs=[vm] * 4,
         out_shape=[jax.ShapeDtypeStruct((block + 16, width), BF16)] * 4,
         scratch_shapes=[pltpu.VMEM((rows, width), F32), pltpu.VMEM((4, block), F32)],
-        cost_estimate=pl.CostEstimate(flops=10**9, bytes_accessed=3 * 10**6, transcendentals=0),
+        cost_estimate=pl.CostEstimate(flops=10**9, bytes_accessed=10**7, transcendentals=0),
         name="out_blocks",
     )(at, *gathered, w, *after)
 
@@ -335,7 +335,7 @@
             out_specs=whole,
         ),
         out_shape=jax.ShapeDtypeStruct((block + 16, width), BF16),
-        cost_estimate=pl.CostEstimate(flops=10**6, bytes_accessed=10**6, transcendentals=100),
+        cost_estimate=pl.CostEstimate(flops=10**6, bytes_accessed=9 * 10**6, transcendentals=100),
         name="residual_block",
     )(at, *parts, hidden, gain, *after)
 
@@ -343,15 +343,20 @@
 def join_kernel(at_ref, u0_ref, u1_ref, u2_ref, u3_ref, out_ref):
     block, width = u0_ref.shape[0] - 16, u0_ref.shape[1]
     square = jnp.zeros((1, block), F32)
+    half = block // 2
     for k, u in enumerate((u0_ref, u1_ref, u2_ref, u3_ref)):
         at = pl.multiple_of(lax.rem(at_ref[0] + 4 - k, 4) * width, width)
-        out_ref[0:block, pl.ds(at, width)] = u[0:block, :]
+        for n in range(2):
+            out_ref[n * (half + 8) + 8 : (n + 1) * (half + 8), pl.ds(at, width)] = u[n * half : (n + 1) * half, :]
         line = u[block : block + 16, :].astype(F32)[0:1, :]
         square = square + line[:, 0:block] + line[:, block : 2 * block] + line[:, 2 * block : 3 * block]
-    scale = lax.rsqrt(square / out_ref.shape[1] + NORM_EPS)
-    out_ref[block : block + 16, :] = jnp.zeros((16, out_ref.shape[1]), BF16)
-    line = jnp.concatenate(pieces(scale), axis=1)
-    out_ref[block : block + 16, 0 : 3 * block] = jnp.broadcast_to(line, (16, 3 * block)).astype(BF16)
+    parts = pieces(lax.rsqrt(square / out_ref.shape[1] + NORM_EPS))
+    for n in range(2):
+        line = jnp.concatenate(
+            [p[:, n * half : (n + 1) * half] for p in parts] + [jnp.zeros((1, 256 - 3 * half), F32)], axis=1
+        )
+        out_ref[n * (half + 8) : n * (half + 8) + 8, 0:256] = jnp.broadcast_to(line, (8, 256)).astype(BF16)
+        out_ref[n * (half + 8) : n * (half + 8) + 8, 256:] = jnp.zeros((8, out_ref.shape[1] - 256), BF16)
 
 
 def join_columns(at, parts, after=()):
@@ -362,7 +367,7 @@
         in_specs=[pl.BlockSpec(memory_space=pltpu.SMEM)] + [vm] * 4 + [ANYWHERE] * len(after),
         out_specs=vm,
         out_shape=jax.ShapeDtypeStruct((tall, 4 * width), BF16),
-        cost_estimate=pl.CostEstimate(flops=10**5, bytes_accessed=10**6, transcendentals=100),
+        cost_estimate=pl.CostEstimate(flops=10**5, bytes_accessed=6 * 10**6, transcendentals=100),
         name="join_columns",
     )(at, *parts, *after)
 
@@ -390,56 +395,113 @@
         out_specs=pl.BlockSpec(memory_space=pltpu.VMEM),
         out_shape=pltpu.VMEM(head.shape, head.dtype),
         scratch_shapes=[pltpu.SemaphoreType.DMA((4,))],
-        compiler_params=pltpu.CompilerParams(vmem_limit_bytes=16 * 2**20),
+        compiler_params=pltpu.CompilerParams(vmem_limit_bytes=40 * 2**20),
         cost_estimate=pl.CostEstimate(flops=0, bytes_accessed=3 * 10**7, transcendentals=0),
         name="fetched",
     )(head, *after)
 
 
-def head_kernel(place_ref, at0_ref, at1_ref, *refs):
-    w_ref, tgt_ref, out_ref, acc_ref = refs[8:]
-    block = refs[0].shape[0] - 16
-    vocab = w_ref.shape[2]
+def score_rows(m, halves, places, base, w_ref, tgt_ref, acc_ref, put):
+    half = halves[0].shape[0] - 8
+    block = 2 * half
+    rows = jnp.concatenate([x[8 : half + 8, :] for x in halves], axis=0)
+    acc_ref[0 : rows.shape[0], :] = contract(rows, w_ref[m], ((1,), (0,)))
+    for k, at in enumerate(places):
+        lines = [x[0:8, 0:256].astype(F32)[0:1, :] for x in halves[2 * k : 2 * k + 2]]
+        scale = to_column(
+            jnp.concatenate(
+                [v[:, 0:half] + v[:, half : 2 * half] + v[:, 2 * half : 3 * half] for v in lines], axis=1
+            )
+        )
+        raw = acc_ref[k * block : (k + 1) * block, :]
+        top = jnp.max(raw, axis=1, keepdims=True)
+        total = jnp.sum(jnp.exp2((raw - top) * (scale * LOG2E)), axis=1, keepdims=True)
+        target = to_column((tgt_ref[pl.ds(at, 1), :] - base).astype(F32)).astype(jnp.int32)
+        column = lax.broadcasted_iota(jnp.int32, raw.shape, 1)
+        chosen = jnp.sum(jnp.where(column == target, raw, 0.0), axis=1, keepdims=True) * scale
+        put(m * 8 + at, to_row(top * scale + jnp.log(total)))
+        put(m * 8 + 4 + at, to_row(chosen))
+
+
+def near_kernel(place_ref, at0_ref, at1_ref, *refs):
+    w_ref, tgt_ref, out_ref, acc_ref = refs[6:]
+    half = refs[0].shape[0] // 2
+    base = place_ref[0] * w_ref.shape[2]
+
+    def put(row, value):
+        out_ref[pl.ds(row, 1), :] = value
+
     for m, at_ref in enumerate((at0_ref, at1_ref)):
-        tiles = refs[4 * m : 4 * m + 4]
-        for n in range(2):
-            rows = jnp.concatenate([x[0:block, :] for x in tiles[2 * n : 2 * n + 2]], axis=0)
-            acc_ref[2 * n * block : 2 * (n + 1) * block, :] = contract(rows, w_ref[m], ((1,), (0,)))
-        for k, x in enumerate(tiles):
-            at = lax.rem(at_ref[1] + 4 - k, 4)
-            line = x[block : block + 16, 0 : 3 * block].astype(F32)[0:1, :]
-            scale = to_column(line[:, 0:block] + line[:, block : 2 * block] + line[:, 2 * block : 3 * block])
-            raw = acc_ref[k * block : (k + 1) * block, :]
-            top = jnp.max(raw, axis=1, keepdims=True)
-            total = jnp.sum(jnp.exp2((raw - top) * (scale * LOG2E)), axis=1, keepdims=True)
-            lse = top * scale + jnp.log(total)
-            target = to_column((tgt_ref[pl.ds(at, 1), :] - place_ref[0] * vocab).astype(F32)).astype(jnp.int32)
-            column = lax.broadcasted_iota(jnp.int32, raw.shape, 1)
-            chosen = jnp.sum(jnp.where(column == target, raw, 0.0), axis=1, keepdims=True) * scale
-            for which, value in enumerate((lse, chosen)):
-                out_ref[:, pl.ds(m * 8 + which * 4 + at, 1), :] = jnp.broadcast_to(
-                    to_row(value)[None], (out_ref.shape[0], 1, block)
-                )
-
-
-def head_stats(place, at, parts, head, tgt, group):
-    tall, depth = parts[0][0].shape
+        tiles = refs[3 * m : 3 * m + 3]
+        halves = [x.at[pl.ds(n * half, half), :] for x in tiles for n in range(2)]
+        places = [lax.rem(at_ref[1] + 4 - k, 4) for k in (0, 1, 3)]
+        score_rows(m, halves, places, base, w_ref, tgt_ref, acc_ref, put)
+
+
+def far_kernel(place_ref, at0_ref, at1_ref, *refs):
+    w_ref, tgt_ref, near_ref, out_ref, acc_ref = refs[4:]
+    base = place_ref[0] * w_ref.shape[2]
+    out_ref[...] = jnp.broadcast_to(near_ref[...][None], out_ref.shape)
+
+    def put(row, value):
+        out_ref[:, pl.ds(row, 1), :] = jnp.broadcast_to(value[None], (out_ref.shape[0], 1, value.shape[1]))
+
+    for m, at_ref in enumerate((at0_ref, at1_ref)):
+        places = [lax.rem(at_ref[1] + 2, 4)]
+        score_rows(m, refs[2 * m : 2 * m + 2], places, base, w_ref, tgt_ref, acc_ref, put)
+
+
+def head_stats(place, at, near, cut, head, tgt, group):
+    tall, depth = near[0][0].shape
     block = tall - 16
     vocab = head.shape[2]
     vm = pl.BlockSpec(memory_space=pltpu.VMEM)
     sm = pl.BlockSpec(memory_space=pltpu.SMEM)
-    return pl.pallas_call(
-        head_kernel,
-        in_specs=[sm] * 3 + [vm] * 10,
-        out_specs=vm,
-        scratch_shapes=[pltpu.VMEM((4 * block, vocab), F32)],
+    common = dict(out_specs=vm, compiler_params=pltpu.CompilerParams(vmem_limit_bytes=24 * 2**20))
+    cost = lambda blocks: pl.CostEstimate(
+        flops=4 * blocks * block * depth * vocab, bytes_accessed=10**7, transcendentals=2 * blocks * block * vocab
+    )
+    first = pl.pallas_call(
+        near_kernel,
+        in_specs=[sm] * 3 + [vm] * 8,
+        scratch_shapes=[pltpu.VMEM((3 * block, vocab), F32)],
+        out_shape=jax.ShapeDtypeStruct((16, block), F32),
+        cost_estimate=cost(3),
+        name="head_near",
+        **common,
+    )(place, *at, *near[0], *near[1], head, tgt)
+    return pl.pallas_call(
+        far_kernel,
+        in_specs=[sm] * 3 + [vm] * 7,
+        scratch_shapes=[pltpu.VMEM((block, vocab), F32)],
         out_shape=jax.ShapeDtypeStruct((group, 16, block), F32),
-        compiler_params=pltpu.CompilerParams(vmem_limit_bytes=36 * 2**20),
-        cost_estimate=pl.CostEstimate(
-            flops=16 * block * depth * vocab, bytes_accessed=10**7, transcendentals=8 * block * vocab
-        ),
-        name="head_stats",
-    )(place, *at, *parts[0], *parts[1], head, tgt)
+        cost_estimate=cost(1),
+        name="head_far",
+        **common,
+    )(place, *at, *cut[0], *cut[1], head, tgt, first)
+
+
+def cut_kernel(a_ref, b_ref, c_ref, d_ref, oa_ref, ob_ref, oc_ref, od_ref):
+    oa_ref[...] = a_ref[...]
+    ob_ref[...] = b_ref[...]
+    oc_ref[...] = c_ref[...]
+    od_ref[...] = d_ref[...]
+
+
+def cut_halves(pairs, after):
+    tall, depth = pairs[0][0].shape
+    low = pl.BlockSpec((tall // 2, depth), lambda g: (0, 0))
+    high = pl.BlockSpec((tall // 2, depth), lambda g: (1, 0))
+    return pl.pallas_call(
+        drop(cut_kernel, 4, len(after)),
+        grid=(1,),
+        in_specs=[low, high] * 2 + [ANYWHERE] * len(after),
+        out_specs=[low] * 4,
+        out_shape=[jax.ShapeDtypeStruct((tall // 2, depth), BF16)] * 4,
+        compiler_params=pltpu.CompilerParams(vmem_limit_bytes=8 * 2**20),
+        cost_estimate=pl.CostEstimate(flops=0, bytes_accessed=2 * 10**6, transcendentals=0),
+        name="cut_halves",
+    )(*pairs[0], *pairs[1], *after)
 
 
 def diff_kernel(stat_ref, live_ref, seg_ref, diff_ref, sums_ref):
@@ -535,8 +597,10 @@
     for m in both:
         full.append(join_columns(at[m], blocks[m], tuple(blocks[1 - m][1:])))
     ready = fetched(head, tuple(full))
-    last = [gathered(full[m], ways[m][1]) for m in both]
-    merged = lax.all_to_all(head_stats(place, at, last, ready, tgt, group), VOC, 0, 0)
+    near = [[full[m]] + [ring(full[m], ways[m][1], k) for k in (1, 3)] for m in both]
+    halves = cut_halves([near[m][1:] for m in both], (ready,))
+    cut = [[ring(halves[2 * m], ways[m][1], 1), ring(halves[2 * m + 1], ways[m][1], 3)] for m in both]
+    merged = lax.all_to_all(head_stats(place, at, near, cut, ready, tgt, group), VOC, 0, 0)
     diff, sums = token_diffs(merged, live, segment_ids.reshape(4, 128))
     sums = sums + lax.ppermute(sums, "core", [(0, 1), (1, 0)])
     sums = sum(gathered(sums, "y"))[0:4, 0]

time: 189 us -> 179 us (0.947)
  waiting for transfers between devices: 36.2 us -> 24.8 us
  Pallas kernels: 57.8 us -> 63.9 us
  local copies, waits for them, and re-layouts: 18 us -> 12.1 us
  starting transfers between devices: 58.2 us -> 64 us
  blocking collectives: 13.2 us -> 9.94 us
    ppermute x27 -> x29, waiting for transfers between devices: 35.2 us -> 23.8 us  [ring(): return lax.ppermute(value, axis, [(i, (i + by) % 4) for i in range(4)])]
    unnamed x74 -> x68, local copies, waits for them, and re-layouts: 17.9 us -> 12 us
    ppermute x27 -> x29, starting transfers between devices: 28.6 us -> 33.4 us  [ring(): return lax.ppermute(value, axis, [(i, (i + by) % 4) for i in range(4)])]
    pallas_call x1, Pallas kernels: 0.95 us -> 4.98 us  [fetched(): pl.pallas_call(drop(fetch_kernel, 1, len(after)), in_specs=[ANYWHERE] + [...]
    all_to_all x1, blocking collectives: 13.2 us -> 9.94 us  [per_device(): lax.all_to_all(head_stats(place, at, near, cut, ready, tgt, group), VOC,...]
    pallas_call x1 -> x3, Pallas kernels: 9.19 us -> 11.1 us  [the longest x1 7.69 us: head_stats(): pl.pallas_call(near_kernel, in_specs=[sm] * 3 + [vm] * 8, scratch_shapes=...]
  transfers between devices with their start and end apart: 34 -> 36, of which waited for: 11 -> 11; matrix products, arithmetic and copies ran while one was open for 3% -> 3% of each run, Pallas kernels for 23% -> 30%
where the time goes in v7:
time: 179 us; the launch traced here: 178 us
  starting transfers between devices  64 us (36%)
  Pallas kernels  63.9 us (36%)
  waiting for transfers between devices  24.8 us (14%)
  local copies, waits for them, and re-layouts  12.1 us (7%)
  blocking collectives  9.94 us (6%)
  other arithmetic  2.5 us (1%)
    ppermute x29, starting transfers between devices, ring(): return lax.ppermute(value, axis, [(i, (i + by) % 4) for i in range(4)])  33.4 us
    ppermute x29, waiting for transfers between devices, ring(): return lax.ppermute(value, axis, [(i, (i + by) % 4) for i in range(4)])  23.8 us
    pallas_call x1, Pallas kernels, mix_local(): pl.pallas_call(mix_kernel, grid=(models, chunks), in_specs=[pl.BlockSpec(...  17.1 us
    unnamed x68, local copies, waits for them, and re-layouts  12 us
    ppermute x4, starting transfers between devices, per_device(): lax.ppermute(pay, SEQ, [(i, i + k) for i in range(devices - k)])  11.5 us
    all_to_all x1, blocking collectives, per_device(): lax.all_to_all(head_stats(place, at, near, cut, ready, tgt, group), VOC,...  9.94 us
    all_to_all x2, starting transfers between devices, per_device(): weights = [lax.all_to_all(turned(m, w_out), ways[m][0], 0, 0) for m in both]  9.86 us
    ppermute x1, starting transfers between devices, per_device(): sums = sums + lax.ppermute(sums, 'core', [(0, 1), (1, 0)])  9.26 us
  transfers between devices with their start and end apart: 36, of which 11 were waited for; matrix products, arithmetic and copies ran while one was open for 3% of the time, Pallas kernels for 30%

profile of v7, /device:TPU:1, one launch (start us, length us, event | category | flops | bytes accessed | tf_op | source)
XLA Modules:
  0.0 178.3 jit_solution(4982460919149318173)
XLA Ops:
  0.6 2.4 %turned.3 = bf16[4,256,512]{2,1,0:T(8,128)(2,1)} custom-call(bf16[2,256,2048]{2,1,0:T(8,128)(2,1)} %w_ref.3), custom_call_target="tpu_custom_call" | custom-call | bytes 2000000 | tf_op jit(solution)/shard_map/turned/pallas_call | solution.py:546
  3.1 5.9 %all-to-all-start.1 = ((bf16[4,256,512]{2,1,0:T(8,128)(2,1)}), bf16[4,256,512]{2,1,0:T(8,128)(2,1)S(1)}, u32[]{:S(2)}, u32[]{:S(2)}) async-start(bf16[4,256,512]{2,1,0:T(8,128)(2,1)} %turned.3), calls=%async_computation.1 | async-start | bytes 2097152 | tf_op jit(solution)/shard_map/all_to_all | solution.py:585
  8.9 1.6 copy.27
  10.5 1.3 copy-done.5
  11.9 2.6 %copy.26 = bf16[2,2048,2,256]{3,1,2,0:T(8,128)(2,1)} copy(bf16[2,2048,2,256]{3,2,1,0:T(2,128)(2,1)S(1)} %copy-done.5) | data formatting | bytes 8388608 | tf_op args[1]
  14.4 17.1 %mix_local.1 = (f32[2,512,256]{2,1,0:T(8,128)}, f32[2,512,256]{2,1,0:T(8,128)}, bf16[2,512,128]{2,1,0:T(8,128)(2,1)}, f32[2,512,8]{2,1,0:T(8,128)}, bf16[2,272,128]{2,1,0:T(8,128)(2,1)}) custom-call(bf16[2,512,2048]{2,1,0:T(8,128)(2,1)} %refs_5_.3, bf16[2,2,2048,256]{3,2,1,0:T(8,128)(2,1)} %bitcast.18, bf16[2,2,2048,128]{3,2,1,0:T(8,128)(2,1)} %bitcast.19, ...), custom_call_target="tpu_custom_call" | custom-call | flops 10000000000 | bytes 16000000 | tf_op jit(solution)/shard_map/mix_local/pallas_call | solution.py:172
  31.6 4.8 %collective-permute-start.3 = (bf16[2,272,128]{2,1,0:T(8,128)(2,1)}, bf16[2,272,128]{2,1,0:T(8,128)(2,1)S(1)}, u32[]{:S(2)}, u32[]{:S(2)}) collective-permute-start(bf16[2,272,128]{2,1,0:T(8,128)(2,1)} %get-tuple-element.25), channel_id=1, source_target_pairs={{0,64},{16,80},{32,96},{48,112},{1,65},{17,81},{33,97},{49,113},{2... | collective-permute-start | bytes 417800 | tf_op jit(solution)/shard_map/ppermute | solution.py:587
  36.4 2.1 %collective-permute-start.2 = (bf16[2,272,128]{2,1,0:T(8,128)(2,1)}, bf16[2,272,128]{2,1,0:T(8,128)(2,1)S(1)}, u32[]{:S(2)}, u32[]{:S(2)}) collective-permute-start(bf16[2,272,128]{2,1,0:T(8,128)(2,1)} %get-tuple-element.25), channel_id=1, source_target_pairs={{0,48},{16,64},{32,80},{48,96},{64,112},{1,49},{17,65},{33,81},{49... | collective-permute-start | bytes 417800 | tf_op jit(solution)/shard_map/ppermute | solution.py:587
  38.5 2.3 %collective-permute-start.1 = (bf16[2,272,128]{2,1,0:T(8,128)(2,1)}, bf16[2,272,128]{2,1,0:T(8,128)(2,1)S(1)}, u32[]{:S(2)}, u32[]{:S(2)}) collective-permute-start(bf16[2,272,128]{2,1,0:T(8,128)(2,1)} %get-tuple-element.25), channel_id=1, source_target_pairs={{0,32},{16,48},{32,64},{48,80},{64,96},{80,112},{1,33},{17,49},{33... | collective-permute-start | bytes 417800 | tf_op jit(solution)/shard_map/ppermute | solution.py:587
  40.8 2.2 %collective-permute-start = (bf16[2,272,128]{2,1,0:T(8,128)(2,1)}, bf16[2,272,128]{2,1,0:T(8,128)(2,1)S(1)}, u32[]{:S(2)}, u32[]{:S(2)}) collective-permute-start(bf16[2,272,128]{2,1,0:T(8,128)(2,1)} %get-tuple-element.25), channel_id=1, source_target_pairs={{0,16},{16,32},{32,48},{48,64},{64,80},{80,96},{96,112},{1,17},{17... | collective-permute-start | bytes 417800 | tf_op jit(solution)/shard_map/ppermute | solution.py:587
  43.1 2.3 %turned.2 = bf16[4,256,512]{2,1,0:T(8,128)(2,1)} custom-call(bf16[2,256,2048]{2,1,0:T(8,128)(2,1)} %w_ref.3), custom_call_target="tpu_custom_call" | custom-call | bytes 2000000 | tf_op jit(solution)/shard_map/turned/pallas_call | solution.py:546
  45.4 4.0 %all-to-all-start = ((bf16[4,256,512]{2,1,0:T(8,128)(2,1)}), bf16[4,256,512]{2,1,0:T(8,128)(2,1)S(1)}, u32[]{:S(2)}, u32[]{:S(2)}) async-start(bf16[4,256,512]{2,1,0:T(8,128)(2,1)} %turned.2), calls=%async_computation | async-start | bytes 2097152 | tf_op jit(solution)/shard_map/all_to_all | solution.py:585
  49.5 0.6 copy-done.16
  50.2 3.9 %gate_out.2.refs_15_.refs_1_ = bf16[528,256]{1,0:T(8,128)(2,1)} custom-call(s32[4]{0:T(128)} %refs_0_.4, s32[4]{0:T(128)} %refs_1_.3, f32[2,512,256]{2,1,0:T(8,128)} %get-tuple-element.21.refs_2_, f32[2,512,256]{2,1,0:T(8,128)} %get-tuple-element.22.refs_3_, bf16[2,512,128]{2,1,0:T(8,128)(2,1)} %get-tuple-element.23.refs_4_, ...), custom_call_target="tpu_custom_call" | custom-call | flops 1000000000 | bytes 12000000 | tf_op jit(solution)/shard_map/gate_out/pallas_call | solution.py:252
  54.2 4.2 %gate_out.3.refs_6_.refs_1_ = bf16[528,256]{1,0:T(8,128)(2,1)} custom-call(s32[4]{0:T(128)} %refs_0_.4, s32[4]{0:T(128)} %refs_1_.3, f32[2,512,256]{2,1,0:T(8,128)} %get-tuple-element.21.refs_2_, f32[2,512,256]{2,1,0:T(8,128)} %get-tuple-element.22.refs_3_, bf16[2,512,128]{2,1,0:T(8,128)(2,1)} %get-tuple-element.23.refs_4_, ...), custom_call_target="tpu_custom_call" | custom-call | flops 1000000000 | bytes 12000000 | tf_op jit(solution)/shard_map/gate_out/pallas_call | solution.py:252
  58.3 3.0 %collective-permute-start.12 = (bf16[528,256]{1,0:T(8,128)(2,1)}, bf16[528,256]{1,0:T(8,128)(2,1)S(1)}, u32[]{:S(2)}, u32[]{:S(2)}) collective-permute-start(bf16[528,256]{1,0:T(8,128)(2,1)} %gate_out.3.refs_6_.refs_1_), channel_id=1, source_target_pairs={{0,3},{1,0},{2,1},{3,2},{4,7},{5,4},{6,5},{7,6},{8,11},{9,8},{10,9... | collective-permute-start | bytes 811016 | tf_op jit(solution)/shard_map/ppermute | solution.py:558
  62.5 2.7 %collective-permute-start.6 = (bf16[528,256]{1,0:T(8,128)(2,1)S(1)}, bf16[528,256]{1,0:T(8,128)(2,1)S(1)}, u32[]{:S(2)}, u32[]{:S(2)}) collective-permute-start(bf16[528,256]{1,0:T(8,128)(2,1)S(1)} %copy-done.7), channel_id=1, source_target_pairs={{0,12},{4,0},{8,4},{12,8},{1,13},{5,1},{9,5},{13,9},{2,14},{6,2},{... | collective-permute-start | bytes 811016 | tf_op jit(solution)/shard_map/ppermute | solution.py:558
  65.7 6.9 %collective-permute-done.12.refs_4_ = bf16[528,256]{1,0:T(8,128)(2,1)S(1)} collective-permute-done((bf16[528,256]{1,0:T(8,128)(2,1)}, bf16[528,256]{1,0:T(8,128)(2,1)S(1)}, u32[]{:S(2)}, u32[]{:S(2)}) %collective-permute-start.12) | collective-permute-done | bytes 270368 | tf_op jit(solution)/shard_map/ppermute | solution.py:558
  72.6 0.7 pad_add_fusion.1.refs_0_.at1_ref
  73.3 3.9 %collective-permute-done.10.refs_2_ = bf16[528,256]{1,0:T(8,128)(2,1)S(1)} collective-permute-done((bf16[528,256]{1,0:T(8,128)(2,1)}, bf16[528,256]{1,0:T(8,128)(2,1)S(1)}, u32[]{:S(2)}, u32[]{:S(2)}) %collective-permute-start.10) | collective-permute-done | bytes 270368 | tf_op jit(solution)/shard_map/ppermute | solution.py:558
  77.2 0.7 copy-done.32
  77.9 3.2 %out_blocks.3 = (bf16[144,512]{1,0:T(8,128)(2,1)}, bf16[144,512]{1,0:T(8,128)(2,1)}, bf16[144,512]{1,0:T(8,128)(2,1)}, bf16[144,512]{1,0:T(8,128)(2,1)}) custom-call(s32[2]{0:T(128)} %pad_add_fusion.1.refs_0_.at1_ref, bf16[528,256]{1,0:T(8,128)(2,1)} %gate_out.3.refs_6_.refs_1_, bf16[528,256]{1,0:T(8,128)(2,1)} %copy-done.32, bf16[528,256]{1,0:T(8,128)(2,1)} %copy-done.31, ...), custom_call_target="tpu_custom_call" | custom-call | flops 1000000000 | bytes 10000000 | tf_op jit(solution)/shard_map/out_blocks/pallas_call | solution.py:296
  81.1 1.5 collective-permute-start.16
  82.6 2.4 %collective-permute-start.17 = (bf16[144,512]{1,0:T(8,128)(2,1)}, bf16[144,512]{1,0:T(8,128)(2,1)S(1)}, u32[]{:S(2)}, u32[]{:S(2)}) collective-permute-start(bf16[144,512]{1,0:T(8,128)(2,1)} %get-tuple-element.32), channel_id=1, source_target_pairs={{0,8},{4,12},{8,0},{12,4},{1,9},{5,13},{9,1},{13,5},{2,10},{6,14},... | collective-permute-start | bytes 442376 | tf_op jit(solution)/shard_map/ppermute | solution.py:558
  85.0 1.2 collective-permute-start.18
  86.2 0.6 pad_add_fusion.refs_0_.at0_ref
  86.8 0.7 copy-done.28
  87.6 1.0 copy-done.9
  88.6 3.2 %out_blocks.2 = (bf16[144,512]{1,0:T(8,128)(2,1)}, bf16[144,512]{1,0:T(8,128)(2,1)}, bf16[144,512]{1,0:T(8,128)(2,1)}, bf16[144,512]{1,0:T(8,128)(2,1)}) custom-call(s32[2]{0:T(128)} %pad_add_fusion.refs_0_.at0_ref, bf16[528,256]{1,0:T(8,128)(2,1)} %gate_out.2.refs_15_.refs_1_, bf16[528,256]{1,0:T(8,128)(2,1)} %copy-done.29, bf16[528,256]{1,0:T(8,128)(2,1)} %copy-done.28, ...), custom_call_target="tpu_custom_call" | custom-call | flops 1000000000 | bytes 10000000 | tf_op jit(solution)/shard_map/out_blocks/pallas_call | solution.py:296
  91.8 2.0 %collective-permute-start.8 = (bf16[144,512]{1,0:T(8,128)(2,1)}, bf16[144,512]{1,0:T(8,128)(2,1)S(1)}, u32[]{:S(2)}, u32[]{:S(2)}) collective-permute-start(bf16[144,512]{1,0:T(8,128)(2,1)} %get-tuple-element.28), channel_id=1, source_target_pairs={{0,2},{1,3},{2,0},{3,1},{4,6},{5,7},{6,4},{7,5},{8,10},{9,11},{10,... | collective-permute-start | bytes 442376 | tf_op jit(solution)/shard_map/ppermute | solution.py:558
  93.8 0.8 collective-permute-start.9
  94.6 0.6 copy-done.21
  95.3 2.8 %residual_block.3.refs_1_ = bf16[144,512]{1,0:T(8,128)(2,1)} custom-call(s32[2]{0:T(128)} %pad_add_fusion.1.refs_0_.at1_ref, bf16[144,512]{1,0:T(8,128)(2,1)} %get-tuple-element.30.refs_7_.refs_1_, bf16[144,512]{1,0:T(8,128)(2,1)} %copy-done.20, bf16[144,512]{1,0:T(8,128)(2,1)} %copy-done.21, bf16[144,512]{1,0:T(8,128)(2,1)} %copy-done.23, ...), custom_call_target="tpu_custom_call" | custom-call | flops 1000000 | bytes 9000000 | tf_op jit(solution)/shard_map/residual_block/pallas_call | solution.py:324
  98.7 2.0 %collective-permute-start.20 = (bf16[144,512]{1,0:T(8,128)(2,1)}, bf16[144,512]{1,0:T(8,128)(2,1)S(1)}, u32[]{:S(2)}, u32[]{:S(2)}) collective-permute-start(bf16[144,512]{1,0:T(8,128)(2,1)} %residual_block.3.refs_1_), channel_id=1, source_target_pairs={{0,2},{1,3},{2,0},{3,1},{4,6},{5,7},{6,4},{7,5},{8,10},{9,11},{10,... | collective-permute-start | bytes 442376 | tf_op jit(solution)/shard_map/ppermute | solution.py:558
  100.6 0.7 collective-permute-start.19
  101.3 0.6 copy-done.24
  102.0 2.8 %residual_block.2.refs_1_ = bf16[144,512]{1,0:T(8,128)(2,1)} custom-call(s32[2]{0:T(128)} %pad_add_fusion.refs_0_.at0_ref, bf16[144,512]{1,0:T(8,128)(2,1)} %get-tuple-element.26.refs_1_, bf16[144,512]{1,0:T(8,128)(2,1)} %copy-done.22, bf16[144,512]{1,0:T(8,128)(2,1)} %copy-done.24, bf16[144,512]{1,0:T(8,128)(2,1)} %copy-done.25, ...), custom_call_target="tpu_custom_call" | custom-call | flops 1000000 | bytes 9000000 | tf_op jit(solution)/shard_map/residual_block/pallas_call | solution.py:324
  104.9 2.6 %collective-permute-start.14 = (bf16[144,512]{1,0:T(8,128)(2,1)}, bf16[144,512]{1,0:T(8,128)(2,1)S(1)}, u32[]{:S(2)}, u32[]{:S(2)}) collective-permute-start(bf16[144,512]{1,0:T(8,128)(2,1)} %residual_block.2.refs_1_), channel_id=1, source_target_pairs={{0,8},{4,12},{8,0},{12,4},{1,9},{5,13},{9,1},{13,5},{2,10},{6,14},... | collective-permute-start | bytes 442376 | tf_op jit(solution)/shard_map/ppermute | solution.py:558
  107.5 1.5 collective-permute-done.15.refs_4_.refs_7_
  109.1 1.5 collective-permute-done.14.refs_3_.refs_6_
  110.6 2.3 %collective-permute-done.13.refs_2_.refs_5_ = bf16[144,512]{1,0:T(8,128)(2,1)S(1)} collective-permute-done((bf16[144,512]{1,0:T(8,128)(2,1)}, bf16[144,512]{1,0:T(8,128)(2,1)S(1)}, u32[]{:S(2)}, u32[]{:S(2)}) %collective-permute-start.13) | collective-permute-done | bytes 147488 | tf_op jit(solution)/shard_map/ppermute | solution.py:558
  112.9 0.7 copy-done.15
  113.6 2.1 %join_columns.2.refs_1_.refs_0_ = bf16[144,2048]{1,0:T(8,128)(2,1)} custom-call(s32[2]{0:T(128)} %pad_add_fusion.refs_0_.at0_ref, bf16[144,512]{1,0:T(8,128)(2,1)} %residual_block.2.refs_1_, bf16[144,512]{1,0:T(8,128)(2,1)} %copy-done.15, bf16[144,512]{1,0:T(8,128)(2,1)} %copy-done.14, bf16[144,512]{1,0:T(8,128)(2,1)} %copy-done.13, ...), custom_call_target="tpu_custom_call" | custom-call | flops 100000 | bytes 6000000 | tf_op jit(solution)/shard_map/join_columns/pallas_call | solution.py:365
  115.7 2.6 %collective-permute-start.23 = (bf16[144,2048]{1,0:T(8,128)(2,1)}, bf16[144,2048]{1,0:T(8,128)(2,1)S(1)}, u32[]{:S(2)}, u32[]{:S(2)}) collective-permute-start(bf16[144,2048]{1,0:T(8,128)(2,1)} %join_columns.2.refs_1_.refs_0_), channel_id=1, source_target_pairs={{0,3},{1,0},{2,1},{3,2},{4,7},{5,4},{6,5},{7,6},{8,11},{9,8},{10,9... | collective-permute-start | bytes 1769480 | tf_op jit(solution)/shard_map/ppermute | solution.py:558
  118.3 2.1 %join_columns.3.refs_2_.refs_3_ = bf16[144,2048]{1,0:T(8,128)(2,1)} custom-call(s32[2]{0:T(128)} %pad_add_fusion.1.refs_0_.at1_ref, bf16[144,512]{1,0:T(8,128)(2,1)} %residual_block.3.refs_1_, bf16[144,512]{1,0:T(8,128)(2,1)} %copy-done.12, bf16[144,512]{1,0:T(8,128)(2,1)} %copy-done.11, bf16[144,512]{1,0:T(8,128)(2,1)} %copy-done.10, ...), custom_call_target="tpu_custom_call" | custom-call | flops 100000 | bytes 6000000 | tf_op jit(solution)/shard_map/join_columns/pallas_call | solution.py:365
  120.4 0.8 collective-permute-start.25
  121.1 0.7 collective-permute-start.24
  121.8 1.1 copy-done
  122.9 5.0 %fetched.1.refs_4_.refs_6_ = bf16[2,2048,1664]{2,1,0:T(8,128)(2,1)S(1)} custom-call(bf16[2,2048,1664]{2,1,0:T(8,128)(2,1)} %refs_0_.5, bf16[144,2048]{1,0:T(8,128)(2,1)S(1)} %copy-done, bf16[144,2048]{1,0:T(8,128)(2,1)} %join_columns.3.refs_2_.refs_3_), custom_call_target="tpu_custom_call" | custom-call | bytes 30000000 | tf_op jit(solution)/shard_map/fetched/pallas_call | solution.py:392
  127.9 1.8 %collective-permute-done.22.refs_0_.refs_1_ = bf16[144,2048]{1,0:T(8,128)(2,1)S(1)} collective-permute-done((bf16[144,2048]{1,0:T(8,128)(2,1)}, bf16[144,2048]{1,0:T(8,128)(2,1)S(1)}, u32[]{:S(2)}, u32[]{:S(2)}) %collective-permute-start.22) | collective-permute-done | bytes 589856 | tf_op jit(solution)/shard_map/ppermute | solution.py:558
  129.8 0.9 collective-permute-done.25.refs_3_.refs_5_
  130.6 1.2 collective-permute-done.24.refs_2_.refs_4_
  132.0 2.7 %collective-permute-start.27 = (bf16[72,2048]{1,0:T(8,128)(2,1)S(1)}, bf16[72,2048]{1,0:T(8,128)(2,1)S(1)}, u32[]{:S(2)}, u32[]{:S(2)}) collective-permute-start(bf16[72,2048]{1,0:T(8,128)(2,1)S(1)} %get-tuple-element.35), channel_id=1, source_target_pairs={{0,3},{1,0},{2,1},{3,2},{4,7},{5,4},{6,5},{7,6},{8,11},{9,8},{10,9... | collective-permute-start | bytes 884744 | tf_op jit(solution)/shard_map/ppermute | solution.py:558
  134.7 2.7 %collective-permute-start.29 = (bf16[72,2048]{1,0:T(8,128)(2,1)S(1)}, bf16[72,2048]{1,0:T(8,128)(2,1)S(1)}, u32[]{:S(2)}, u32[]{:S(2)}) collective-permute-start(bf16[72,2048]{1,0:T(8,128)(2,1)S(1)} %get-tuple-element.37), channel_id=1, source_target_pairs={{0,12},{4,0},{8,4},{12,8},{1,13},{5,1},{9,5},{13,9},{2,14},{6,2},{... | collective-permute-start | bytes 884744 | tf_op jit(solution)/shard_map/ppermute | solution.py:558
  137.4 7.7 %head_near.1.refs_6_ = f32[16,128]{1,0:T(8,128)S(1)} custom-call(s32[1]{0:T(128)} %bitcast.place_ref, s32[2]{0:T(128)S(1)} %copy-done.3, s32[2]{0:T(128)S(1)} %copy-done.2, bf16[144,2048]{1,0:T(8,128)(2,1)S(1)} %copy-done, bf16[144,2048]{1,0:T(8,128)(2,1)S(1)} %collective-permute-done.22.refs_0_.refs_1_, ...), custom_call_target="tpu_custom_call" | custom-call | flops 5234491392 | bytes 10000000 | tf_op jit(solution)/shard_map/head_near/pallas_call | solution.py:464
  145.1 3.3 %head_far.1 = f32[16,16,128]{2,1,0:T(8,128)S(1)} custom-call(s32[1]{0:T(128)} %bitcast.place_ref, s32[2]{0:T(128)S(1)} %copy-done.3, s32[2]{0:T(128)S(1)} %copy-done.2, bf16[72,2048]{1,0:T(8,128)(2,1)S(1)} %collective-permute-done.26.refs_0_, bf16[72,2048]{1,0:T(8,128)(2,1)S(1)} %collective-permute-done.27.refs_1_, ...), custom_call_target="tpu_custom_call" | custom-call | flops 1744830464 | bytes 10000000 | tf_op jit(solution)/shard_map/head_far/pallas_call | solution.py:473
  148.4 9.9 %all_to_all.15.stat_ref = f32[16,16,128]{2,1,0:T(8,128)} all-to-all(f32[16,16,128]{2,1,0:T(8,128)S(1)} %head_far.1), channel_id=1, replica_groups=mesh['y'=4,'core'=2,'x'=4,'z'=4] {'x','z'}, dimensions={0} | all-to-all | bytes 262144 | tf_op jit(solution)/shard_map/all_to_all | solution.py:603
  158.4 1.6 token_diffs.1
  160.0 9.3 %collective-permute-start.30 = (f32[8,128]{1,0:T(8,128)}, f32[8,128]{1,0:T(8,128)S(1)}, u32[]{:S(2)}, u32[]{:S(2)}) collective-permute-start(f32[8,128]{1,0:T(8,128)} %get-tuple-element.39), channel_id=1, source_target_pairs={{0,16},{16,0},{1,17},{17,1},{2,18},{18,2},{3,19},{19,3},{4,20},{20... | collective-permute-start | bytes 12296 | tf_op jit(solution)/shard_map/ppermute | solution.py:605
  169.3 1.0 collective-permute-done.30
  170.3 0.7 add.20
  171.0 3.0 %collective-permute-start.32 = (f32[8,128]{1,0:T(8,128)S(1)}, f32[8,128]{1,0:T(8,128)S(1)}, u32[]{:S(2)}, u32[]{:S(2)}) collective-permute-start(f32[8,128]{1,0:T(8,128)S(1)} %add.20), channel_id=1, source_target_pairs={{0,64},{32,96},{64,0},{96,32},{1,65},{33,97},{65,1},{97,33},{2,66}... | collective-permute-start | bytes 12296 | tf_op jit(solution)/shard_map/ppermute | solution.py:558
  174.0 1.0 collective-permute-done.32
  175.0 2.7 %collective-permute-done.31 = f32[8,128]{1,0:T(8,128)S(1)} collective-permute-done((f32[8,128]{1,0:T(8,128)S(1)}, f32[8,128]{1,0:T(8,128)S(1)}, u32[]{:S(2)}, u32[]{:S(2)}) %collective-permute-start.31) | collective-permute-done | bytes 4128 | tf_op jit(solution)/shard_map/ppermute | solution.py:558
  (99 shorter events, 3.6 us)
Async XLA Ops:
  0.6 8.3 %copy-start.6 = (bf16[2,2048,2,128]{3,2,1,0:T(2,128)(2,1)S(1)}, bf16[2,2048,2,128]{3,2,1,0:T(2,128)(2,1)}, u32[]{:S(2)}) copy-start(bf16[2,2048,2,128]{3,2,1,0:T(2,128)(2,1)} %param.20) | copy-start | bytes 6291460
  3.1 42.3 %all-to-all-start.1 = ((bf16[4,256,512]{2,1,0:T(8,128)(2,1)}), bf16[4,256,512]{2,1,0:T(8,128)(2,1)S(1)}, u32[]{:S(2)}, u32[]{:S(2)}) async-start(bf16[4,256,512]{2,1,0:T(8,128)(2,1)} %turned.3), calls=%async_computation.1 | async-start | bytes 2097152 | tf_op jit(solution)/shard_map/all_to_all | solution.py:585
  8.9 2.9 %copy-start.5 = (bf16[2,2048,2,256]{3,2,1,0:T(2,128)(2,1)S(1)}, bf16[2,2048,2,256]{3,2,1,0:T(2,128)(2,1)}, u32[]{:S(2)}) copy-start(bf16[2,2048,2,256]{3,2,1,0:T(2,128)(2,1)} %param.19) | copy-start | bytes 12582916
  31.6 17.8 %collective-permute-start.3 = (bf16[2,272,128]{2,1,0:T(8,128)(2,1)}, bf16[2,272,128]{2,1,0:T(8,128)(2,1)S(1)}, u32[]{:S(2)}, u32[]{:S(2)}) collective-permute-start(bf16[2,272,128]{2,1,0:T(8,128)(2,1)} %get-tuple-element.25), channel_id=1, source_target_pairs={{0,64},{16,80},{32,96},{48,112},{1,65},{17,81},{33,97},{49,113},{2... | collective-permute-start | bytes 417800 | tf_op jit(solution)/shard_map/ppermute | solution.py:587
  36.4 13.0 %collective-permute-start.2 = (bf16[2,272,128]{2,1,0:T(8,128)(2,1)}, bf16[2,272,128]{2,1,0:T(8,128)(2,1)S(1)}, u32[]{:S(2)}, u32[]{:S(2)}) collective-permute-start(bf16[2,272,128]{2,1,0:T(8,128)(2,1)} %get-tuple-element.25), channel_id=1, source_target_pairs={{0,48},{16,64},{32,80},{48,96},{64,112},{1,49},{17,65},{33,81},{49... | collective-permute-start | bytes 417800 | tf_op jit(solution)/shard_map/ppermute | solution.py:587
  38.5 10.9 %collective-permute-start.1 = (bf16[2,272,128]{2,1,0:T(8,128)(2,1)}, bf16[2,272,128]{2,1,0:T(8,128)(2,1)S(1)}, u32[]{:S(2)}, u32[]{:S(2)}) collective-permute-start(bf16[2,272,128]{2,1,0:T(8,128)(2,1)} %get-tuple-element.25), channel_id=1, source_target_pairs={{0,32},{16,48},{32,64},{48,80},{64,96},{80,112},{1,33},{17,49},{33... | collective-permute-start | bytes 417800 | tf_op jit(solution)/shard_map/ppermute | solution.py:587
  40.8 8.6 %collective-permute-start = (bf16[2,272,128]{2,1,0:T(8,128)(2,1)}, bf16[2,272,128]{2,1,0:T(8,128)(2,1)S(1)}, u32[]{:S(2)}, u32[]{:S(2)}) collective-permute-start(bf16[2,272,128]{2,1,0:T(8,128)(2,1)} %get-tuple-element.25), channel_id=1, source_target_pairs={{0,16},{16,32},{32,48},{48,64},{64,80},{80,96},{96,112},{1,17},{17... | collective-permute-start | bytes 417800 | tf_op jit(solution)/shard_map/ppermute | solution.py:587
  45.4 8.8 %copy-start.8 = (bf16[4,256,512]{2,1,0:T(8,128)(2,1)}, bf16[4,256,512]{2,1,0:T(8,128)(2,1)S(1)}, u32[]{:S(2)}) copy-start(bf16[4,256,512]{2,1,0:T(8,128)(2,1)S(1)} %all-to-all-done.1.refs_5_) | copy-start | bytes 3145732
  45.4 41.4 %all-to-all-start = ((bf16[4,256,512]{2,1,0:T(8,128)(2,1)}), bf16[4,256,512]{2,1,0:T(8,128)(2,1)S(1)}, u32[]{:S(2)}, u32[]{:S(2)}) async-start(bf16[4,256,512]{2,1,0:T(8,128)(2,1)} %turned.2), calls=%async_computation | async-start | bytes 2097152 | tf_op jit(solution)/shard_map/all_to_all | solution.py:585
  49.4 0.7 copy-start.17
  49.4 0.7 copy-start.18
  49.5 0.8 copy-start.19
  54.2 8.3 %copy-start.7 = (bf16[528,256]{1,0:T(8,128)(2,1)S(1)}, bf16[528,256]{1,0:T(8,128)(2,1)}, u32[]{:S(2)}) copy-start(bf16[528,256]{1,0:T(8,128)(2,1)} %gate_out.2.refs_15_.refs_1_) | copy-start | bytes 811012
  58.3 14.3 %collective-permute-start.12 = (bf16[528,256]{1,0:T(8,128)(2,1)}, bf16[528,256]{1,0:T(8,128)(2,1)S(1)}, u32[]{:S(2)}, u32[]{:S(2)}) collective-permute-start(bf16[528,256]{1,0:T(8,128)(2,1)} %gate_out.3.refs_6_.refs_1_), channel_id=1, source_target_pairs={{0,3},{1,0},{2,1},{3,2},{4,7},{5,4},{6,5},{7,6},{8,11},{9,8},{10,9... | collective-permute-start | bytes 811016 | tf_op jit(solution)/shard_map/ppermute | solution.py:558
  61.3 12.0 %collective-permute-start.11 = (bf16[528,256]{1,0:T(8,128)(2,1)}, bf16[528,256]{1,0:T(8,128)(2,1)S(1)}, u32[]{:S(2)}, u32[]{:S(2)}) collective-permute-start(bf16[528,256]{1,0:T(8,128)(2,1)} %gate_out.3.refs_6_.refs_1_), channel_id=1, source_target_pairs={{0,2},{1,3},{2,0},{3,1},{4,6},{5,7},{6,4},{7,5},{8,10},{9,11},{10,... | collective-permute-start | bytes 811016 | tf_op jit(solution)/shard_map/ppermute | solution.py:558
  61.9 15.3 %collective-permute-start.10 = (bf16[528,256]{1,0:T(8,128)(2,1)}, bf16[528,256]{1,0:T(8,128)(2,1)S(1)}, u32[]{:S(2)}, u32[]{:S(2)}) collective-permute-start(bf16[528,256]{1,0:T(8,128)(2,1)} %gate_out.3.refs_6_.refs_1_), channel_id=1, source_target_pairs={{0,1},{1,2},{2,3},{3,0},{4,5},{5,6},{6,7},{7,4},{8,9},{9,10},{10,1... | collective-permute-start | bytes 811016 | tf_op jit(solution)/shard_map/ppermute | solution.py:558
  62.5 22.5 %collective-permute-start.6 = (bf16[528,256]{1,0:T(8,128)(2,1)S(1)}, bf16[528,256]{1,0:T(8,128)(2,1)S(1)}, u32[]{:S(2)}, u32[]{:S(2)}) collective-permute-start(bf16[528,256]{1,0:T(8,128)(2,1)S(1)} %copy-done.7), channel_id=1, source_target_pairs={{0,12},{4,0},{8,4},{12,8},{1,13},{5,1},{9,5},{13,9},{2,14},{6,2},{... | collective-permute-start | bytes 811016 | tf_op jit(solution)/shard_map/ppermute | solution.py:558
  65.1 21.7 %collective-permute-start.5 = (bf16[528,256]{1,0:T(8,128)(2,1)S(1)}, bf16[528,256]{1,0:T(8,128)(2,1)S(1)}, u32[]{:S(2)}, u32[]{:S(2)}) collective-permute-start(bf16[528,256]{1,0:T(8,128)(2,1)S(1)} %copy-done.7), channel_id=1, source_target_pairs={{0,8},{4,12},{8,0},{12,4},{1,9},{5,13},{9,1},{13,5},{2,10},{6,14},... | collective-permute-start | bytes 811016 | tf_op jit(solution)/shard_map/ppermute | solution.py:558
  72.6 4.6 %copy-start.30 = (bf16[528,256]{1,0:T(8,128)(2,1)}, bf16[528,256]{1,0:T(8,128)(2,1)S(1)}, u32[]{:S(2)}) copy-start(bf16[528,256]{1,0:T(8,128)(2,1)S(1)} %collective-permute-done.12.refs_4_) | copy-start | bytes 811012
  72.6 14.2 %collective-permute-start.4 = (bf16[528,256]{1,0:T(8,128)(2,1)S(1)}, bf16[528,256]{1,0:T(8,128)(2,1)S(1)}, u32[]{:S(2)}, u32[]{:S(2)}) collective-permute-start(bf16[528,256]{1,0:T(8,128)(2,1)S(1)} %copy-done.7), channel_id=1, source_target_pairs={{0,4},{4,8},{8,12},{12,0},{1,5},{5,9},{9,13},{13,1},{2,6},{6,10},{... | collective-permute-start | bytes 811016 | tf_op jit(solution)/shard_map/ppermute | solution.py:558
  73.3 3.9 %copy-start.31 = (bf16[528,256]{1,0:T(8,128)(2,1)}, bf16[528,256]{1,0:T(8,128)(2,1)S(1)}, u32[]{:S(2)}) copy-start(bf16[528,256]{1,0:T(8,128)(2,1)S(1)} %collective-permute-done.11.refs_3_) | copy-start | bytes 811012
  77.2 0.7 copy-start.32
  81.1 12.7 %collective-permute-start.16 = (bf16[144,512]{1,0:T(8,128)(2,1)}, bf16[144,512]{1,0:T(8,128)(2,1)S(1)}, u32[]{:S(2)}, u32[]{:S(2)}) collective-permute-start(bf16[144,512]{1,0:T(8,128)(2,1)} %get-tuple-element.31), channel_id=1, source_target_pairs={{0,4},{4,8},{8,12},{12,0},{1,5},{5,9},{9,13},{13,1},{2,6},{6,10},{... | collective-permute-start | bytes 442376 | tf_op jit(solution)/shard_map/ppermute | solution.py:558
  82.6 12.0 %collective-permute-start.17 = (bf16[144,512]{1,0:T(8,128)(2,1)}, bf16[144,512]{1,0:T(8,128)(2,1)S(1)}, u32[]{:S(2)}, u32[]{:S(2)}) collective-permute-start(bf16[144,512]{1,0:T(8,128)(2,1)} %get-tuple-element.32), channel_id=1, source_target_pairs={{0,8},{4,12},{8,0},{12,4},{1,9},{5,13},{9,1},{13,5},{2,10},{6,14},... | collective-permute-start | bytes 442376 | tf_op jit(solution)/shard_map/ppermute | solution.py:558
  85.0 1.9 %copy-start.27 = (bf16[528,256]{1,0:T(8,128)(2,1)}, bf16[528,256]{1,0:T(8,128)(2,1)S(1)}, u32[]{:S(2)}) copy-start(bf16[528,256]{1,0:T(8,128)(2,1)S(1)} %collective-permute-done.6.refs_4_) | copy-start | bytes 811012
  85.0 9.6 %collective-permute-start.18 = (bf16[144,512]{1,0:T(8,128)(2,1)}, bf16[144,512]{1,0:T(8,128)(2,1)S(1)}, u32[]{:S(2)}, u32[]{:S(2)}) collective-permute-start(bf16[144,512]{1,0:T(8,128)(2,1)} %get-tuple-element.33), channel_id=1, source_target_pairs={{0,12},{4,0},{8,4},{12,8},{1,13},{5,1},{9,5},{13,9},{2,14},{6,2},{... | collective-permute-start | bytes 442376 | tf_op jit(solution)/shard_map/ppermute | solution.py:558
  86.8 0.7 copy-start.28
  86.8 0.8 copy-start.29
  87.6 1.0 copy-start.9
  91.8 8.8 %collective-permute-start.7 = (bf16[144,512]{1,0:T(8,128)(2,1)}, bf16[144,512]{1,0:T(8,128)(2,1)S(1)}, u32[]{:S(2)}, u32[]{:S(2)}) collective-permute-start(bf16[144,512]{1,0:T(8,128)(2,1)} %get-tuple-element.27), channel_id=1, source_target_pairs={{0,1},{1,2},{2,3},{3,0},{4,5},{5,6},{6,7},{7,4},{8,9},{9,10},{10,1... | collective-permute-start | bytes 442376 | tf_op jit(solution)/shard_map/ppermute | solution.py:558
  91.8 9.5 %collective-permute-start.8 = (bf16[144,512]{1,0:T(8,128)(2,1)}, bf16[144,512]{1,0:T(8,128)(2,1)S(1)}, u32[]{:S(2)}, u32[]{:S(2)}) collective-permute-start(bf16[144,512]{1,0:T(8,128)(2,1)} %get-tuple-element.28), channel_id=1, source_target_pairs={{0,2},{1,3},{2,0},{3,1},{4,6},{5,7},{6,4},{7,5},{8,10},{9,11},{10,... | collective-permute-start | bytes 442376 | tf_op jit(solution)/shard_map/ppermute | solution.py:558
  93.8 0.8 copy-start.20
  93.8 7.5 %collective-permute-start.9 = (bf16[144,512]{1,0:T(8,128)(2,1)}, bf16[144,512]{1,0:T(8,128)(2,1)S(1)}, u32[]{:S(2)}, u32[]{:S(2)}) collective-permute-start(bf16[144,512]{1,0:T(8,128)(2,1)} %get-tuple-element.29), channel_id=1, source_target_pairs={{0,3},{1,0},{2,1},{3,2},{4,7},{5,4},{6,5},{7,6},{8,11},{9,8},{10,9... | collective-permute-start | bytes 442376 | tf_op jit(solution)/shard_map/ppermute | solution.py:558
  94.6 0.7 copy-start.23
  98.2 9.3 %collective-permute-start.21 = (bf16[144,512]{1,0:T(8,128)(2,1)}, bf16[144,512]{1,0:T(8,128)(2,1)S(1)}, u32[]{:S(2)}, u32[]{:S(2)}) collective-permute-start(bf16[144,512]{1,0:T(8,128)(2,1)} %residual_block.3.refs_1_), channel_id=1, source_target_pairs={{0,3},{1,0},{2,1},{3,2},{4,7},{5,4},{6,5},{7,6},{8,11},{9,8},{10,9... | collective-permute-start | bytes 442376 | tf_op jit(solution)/shard_map/ppermute | solution.py:558
  98.7 8.8 %collective-permute-start.20 = (bf16[144,512]{1,0:T(8,128)(2,1)}, bf16[144,512]{1,0:T(8,128)(2,1)S(1)}, u32[]{:S(2)}, u32[]{:S(2)}) collective-permute-start(bf16[144,512]{1,0:T(8,128)(2,1)} %residual_block.3.refs_1_), channel_id=1, source_target_pairs={{0,2},{1,3},{2,0},{3,1},{4,6},{5,7},{6,4},{7,5},{8,10},{9,11},{10,... | collective-permute-start | bytes 442376 | tf_op jit(solution)/shard_map/ppermute | solution.py:558
  100.6 6.9 %collective-permute-start.19 = (bf16[144,512]{1,0:T(8,128)(2,1)}, bf16[144,512]{1,0:T(8,128)(2,1)S(1)}, u32[]{:S(2)}, u32[]{:S(2)}) collective-permute-start(bf16[144,512]{1,0:T(8,128)(2,1)} %residual_block.3.refs_1_), channel_id=1, source_target_pairs={{0,1},{1,2},{2,3},{3,0},{4,5},{5,6},{6,7},{7,4},{8,9},{9,10},{10,1... | collective-permute-start | bytes 442376 | tf_op jit(solution)/shard_map/ppermute | solution.py:558
  101.3 0.7 copy-start.25
  104.9 4.2 %collective-permute-start.15 = (bf16[144,512]{1,0:T(8,128)(2,1)}, bf16[144,512]{1,0:T(8,128)(2,1)S(1)}, u32[]{:S(2)}, u32[]{:S(2)}) collective-permute-start(bf16[144,512]{1,0:T(8,128)(2,1)} %residual_block.2.refs_1_), channel_id=1, source_target_pairs={{0,12},{4,0},{8,4},{12,8},{1,13},{5,1},{9,5},{13,9},{2,14},{6,2},{... | collective-permute-start | bytes 442376 | tf_op jit(solution)/shard_map/ppermute | solution.py:558
  104.9 5.7 %collective-permute-start.14 = (bf16[144,512]{1,0:T(8,128)(2,1)}, bf16[144,512]{1,0:T(8,128)(2,1)S(1)}, u32[]{:S(2)}, u32[]{:S(2)}) collective-permute-start(bf16[144,512]{1,0:T(8,128)(2,1)} %residual_block.2.refs_1_), channel_id=1, source_target_pairs={{0,8},{4,12},{8,0},{12,4},{1,9},{5,13},{9,1},{13,5},{2,10},{6,14},... | collective-permute-start | bytes 442376 | tf_op jit(solution)/shard_map/ppermute | solution.py:558
  107.5 5.4 %copy-start.10 = (bf16[144,512]{1,0:T(8,128)(2,1)}, bf16[144,512]{1,0:T(8,128)(2,1)S(1)}, u32[]{:S(2)}) copy-start(bf16[144,512]{1,0:T(8,128)(2,1)S(1)} %collective-permute-done.21.refs_7_.refs_4_) | copy-start | bytes 442372
  107.5 5.4 %collective-permute-start.13 = (bf16[144,512]{1,0:T(8,128)(2,1)}, bf16[144,512]{1,0:T(8,128)(2,1)S(1)}, u32[]{:S(2)}, u32[]{:S(2)}) collective-permute-start(bf16[144,512]{1,0:T(8,128)(2,1)} %residual_block.2.refs_1_), channel_id=1, source_target_pairs={{0,4},{4,8},{8,12},{12,0},{1,5},{5,9},{9,13},{13,1},{2,6},{6,10},{... | collective-permute-start | bytes 442376 | tf_op jit(solution)/shard_map/ppermute | solution.py:558
  107.5 5.4 %copy-start.11 = (bf16[144,512]{1,0:T(8,128)(2,1)}, bf16[144,512]{1,0:T(8,128)(2,1)S(1)}, u32[]{:S(2)}) copy-start(bf16[144,512]{1,0:T(8,128)(2,1)S(1)} %collective-permute-done.20.refs_6_.refs_3_) | copy-start | bytes 442372
  107.5 5.4 %copy-start.12 = (bf16[144,512]{1,0:T(8,128)(2,1)}, bf16[144,512]{1,0:T(8,128)(2,1)S(1)}, u32[]{:S(2)}) copy-start(bf16[144,512]{1,0:T(8,128)(2,1)S(1)} %collective-permute-done.19.refs_5_.refs_2_) | copy-start | bytes 442372
  109.1 3.8 %copy-start.13 = (bf16[144,512]{1,0:T(8,128)(2,1)}, bf16[144,512]{1,0:T(8,128)(2,1)S(1)}, u32[]{:S(2)}) copy-start(bf16[144,512]{1,0:T(8,128)(2,1)S(1)} %collective-permute-done.15.refs_4_.refs_7_) | copy-start | bytes 442372
  110.6 2.3 %copy-start.14 = (bf16[144,512]{1,0:T(8,128)(2,1)}, bf16[144,512]{1,0:T(8,128)(2,1)S(1)}, u32[]{:S(2)}) copy-start(bf16[144,512]{1,0:T(8,128)(2,1)S(1)} %collective-permute-done.14.refs_3_.refs_6_) | copy-start | bytes 442372
  115.7 12.3 %collective-permute-start.23 = (bf16[144,2048]{1,0:T(8,128)(2,1)}, bf16[144,2048]{1,0:T(8,128)(2,1)S(1)}, u32[]{:S(2)}, u32[]{:S(2)}) collective-permute-start(bf16[144,2048]{1,0:T(8,128)(2,1)} %join_columns.2.refs_1_.refs_0_), channel_id=1, source_target_pairs={{0,3},{1,0},{2,1},{3,2},{4,7},{5,4},{6,5},{7,6},{8,11},{9,8},{10,9... | collective-permute-start | bytes 1769480 | tf_op jit(solution)/shard_map/ppermute | solution.py:558
  118.3 11.5 %collective-permute-start.22 = (bf16[144,2048]{1,0:T(8,128)(2,1)}, bf16[144,2048]{1,0:T(8,128)(2,1)S(1)}, u32[]{:S(2)}, u32[]{:S(2)}) collective-permute-start(bf16[144,2048]{1,0:T(8,128)(2,1)} %join_columns.2.refs_1_.refs_0_), channel_id=1, source_target_pairs={{0,1},{1,2},{2,3},{3,0},{4,5},{5,6},{6,7},{7,4},{8,9},{9,10},{10,1... | collective-permute-start | bytes 1769480 | tf_op jit(solution)/shard_map/ppermute | solution.py:558
  120.4 10.2 %collective-permute-start.25 = (bf16[144,2048]{1,0:T(8,128)(2,1)}, bf16[144,2048]{1,0:T(8,128)(2,1)S(1)}, u32[]{:S(2)}, u32[]{:S(2)}) collective-permute-start(bf16[144,2048]{1,0:T(8,128)(2,1)} %join_columns.3.refs_2_.refs_3_), channel_id=1, source_target_pairs={{0,12},{4,0},{8,4},{12,8},{1,13},{5,1},{9,5},{13,9},{2,14},{6,2},{... | collective-permute-start | bytes 1769480 | tf_op jit(solution)/shard_map/ppermute | solution.py:558
  121.1 10.7 %collective-permute-start.24 = (bf16[144,2048]{1,0:T(8,128)(2,1)}, bf16[144,2048]{1,0:T(8,128)(2,1)S(1)}, u32[]{:S(2)}, u32[]{:S(2)}) collective-permute-start(bf16[144,2048]{1,0:T(8,128)(2,1)} %join_columns.3.refs_2_.refs_3_), channel_id=1, source_target_pairs={{0,4},{4,8},{8,12},{12,0},{1,5},{5,9},{9,13},{13,1},{2,6},{6,10},{... | collective-permute-start | bytes 1769480 | tf_op jit(solution)/shard_map/ppermute | solution.py:558
  121.8 1.1 copy-start
  127.9 9.5 %copy-start.1 = (bf16[144,2048]{1,0:T(8,128)(2,1)S(1)}, bf16[144,2048]{1,0:T(8,128)(2,1)}, u32[]{:S(2)}) copy-start(bf16[144,2048]{1,0:T(8,128)(2,1)} %join_columns.3.refs_2_.refs_3_) | copy-start | bytes 1769476
  127.9 9.4 %copy-start.2 = (s32[2]{0:T(128)S(1)}, s32[2]{0:T(128)}, u32[]{:S(2)}) copy-start(s32[2]{0:T(128)} %pad_add_fusion.1.refs_0_.at1_ref) | copy-start | bytes 28
  127.9 9.4 %copy-start.3 = (s32[2]{0:T(128)S(1)}, s32[2]{0:T(128)}, u32[]{:S(2)}) copy-start(s32[2]{0:T(128)} %pad_add_fusion.refs_0_.at0_ref) | copy-start | bytes 28
  127.9 9.4 %copy-start.4 = (s32[512]{0:T(512)S(1)}, s32[512]{0:T(512)}, u32[]{:S(2)}) copy-start(s32[512]{0:T(512)} %param.30) | copy-start | bytes 6148
  131.9 13.1 %collective-permute-start.26 = (bf16[72,2048]{1,0:T(8,128)(2,1)S(1)}, bf16[72,2048]{1,0:T(8,128)(2,1)S(1)}, u32[]{:S(2)}, u32[]{:S(2)}) collective-permute-start(bf16[72,2048]{1,0:T(8,128)(2,1)S(1)} %get-tuple-element.34), channel_id=1, source_target_pairs={{0,1},{1,2},{2,3},{3,0},{4,5},{5,6},{6,7},{7,4},{8,9},{9,10},{10,1... | collective-permute-start | bytes 884744 | tf_op jit(solution)/shard_map/ppermute | solution.py:558
  132.0 13.1 %collective-permute-start.27 = (bf16[72,2048]{1,0:T(8,128)(2,1)S(1)}, bf16[72,2048]{1,0:T(8,128)(2,1)S(1)}, u32[]{:S(2)}, u32[]{:S(2)}) collective-permute-start(bf16[72,2048]{1,0:T(8,128)(2,1)S(1)} %get-tuple-element.35), channel_id=1, source_target_pairs={{0,3},{1,0},{2,1},{3,2},{4,7},{5,4},{6,5},{7,6},{8,11},{9,8},{10,9... | collective-permute-start | bytes 884744 | tf_op jit(solution)/shard_map/ppermute | solution.py:558
  134.7 10.4 %collective-permute-start.28 = (bf16[72,2048]{1,0:T(8,128)(2,1)S(1)}, bf16[72,2048]{1,0:T(8,128)(2,1)S(1)}, u32[]{:S(2)}, u32[]{:S(2)}) collective-permute-start(bf16[72,2048]{1,0:T(8,128)(2,1)S(1)} %get-tuple-element.36), channel_id=1, source_target_pairs={{0,4},{4,8},{8,12},{12,0},{1,5},{5,9},{9,13},{13,1},{2,6},{6,10},{... | collective-permute-start | bytes 884744 | tf_op jit(solution)/shard_map/ppermute | solution.py:558
  134.7 10.4 %collective-permute-start.29 = (bf16[72,2048]{1,0:T(8,128)(2,1)S(1)}, bf16[72,2048]{1,0:T(8,128)(2,1)S(1)}, u32[]{:S(2)}, u32[]{:S(2)}) collective-permute-start(bf16[72,2048]{1,0:T(8,128)(2,1)S(1)} %get-tuple-element.37), channel_id=1, source_target_pairs={{0,12},{4,0},{8,4},{12,8},{1,13},{5,1},{9,5},{13,9},{2,14},{6,2},{... | collective-permute-start | bytes 884744 | tf_op jit(solution)/shard_map/ppermute | solution.py:558
  145.0 32.8 %copy-start.26 = (s32[4]{0:T(128)S(1)}, s32[4]{0:T(128)}, u32[]{:S(2)}) copy-start(s32[4]{0:T(128)} %param.35) | copy-start | bytes 52
  160.0 10.3 %collective-permute-start.30 = (f32[8,128]{1,0:T(8,128)}, f32[8,128]{1,0:T(8,128)S(1)}, u32[]{:S(2)}, u32[]{:S(2)}) collective-permute-start(f32[8,128]{1,0:T(8,128)} %get-tuple-element.39), channel_id=1, source_target_pairs={{0,16},{16,0},{1,17},{17,1},{2,18},{18,2},{3,19},{19,3},{4,20},{20... | collective-permute-start | bytes 12296 | tf_op jit(solution)/shard_map/ppermute | solution.py:605
  171.0 3.0 %collective-permute-start.33 = (f32[8,128]{1,0:T(8,128)S(1)}, f32[8,128]{1,0:T(8,128)S(1)}, u32[]{:S(2)}, u32[]{:S(2)}) collective-permute-start(f32[8,128]{1,0:T(8,128)S(1)} %add.20), channel_id=1, source_target_pairs={{0,96},{32,0},{64,32},{96,64},{1,97},{33,1},{65,33},{97,65},{2,98}... | collective-permute-start | bytes 12296 | tf_op jit(solution)/shard_map/ppermute | solution.py:558
  171.0 4.0 %collective-permute-start.32 = (f32[8,128]{1,0:T(8,128)S(1)}, f32[8,128]{1,0:T(8,128)S(1)}, u32[]{:S(2)}, u32[]{:S(2)}) collective-permute-start(f32[8,128]{1,0:T(8,128)S(1)} %add.20), channel_id=1, source_target_pairs={{0,64},{32,96},{64,0},{96,32},{1,65},{33,97},{65,1},{97,33},{2,66}... | collective-permute-start | bytes 12296 | tf_op jit(solution)/shard_map/ppermute | solution.py:558
  174.0 3.7 %collective-permute-start.31 = (f32[8,128]{1,0:T(8,128)S(1)}, f32[8,128]{1,0:T(8,128)S(1)}, u32[]{:S(2)}, u32[]{:S(2)}) collective-permute-start(f32[8,128]{1,0:T(8,128)S(1)} %add.20), channel_id=1, source_target_pairs={{0,32},{32,64},{64,96},{96,0},{1,33},{33,65},{65,97},{97,1},{2,34}... | collective-permute-start | bytes 12296 | tf_op jit(solution)/shard_map/ppermute | solution.py:558
  (5 other events, 3.3 us)

commit v8 on v7

--- a/solution.py
+++ b/solution.py
@@ -160,7 +160,7 @@
         y_ref[t0 : t0 + SPAN, :] = jnp.concatenate(acc, axis=1)
 
 
-def mix_local(hidden, w_inner, w_state, w_step, bias, rate, skip, seg, chunks=4):
+def mix_local(hidden, w_inner, w_state, w_step, bias, rate, skip, seg, chunks=2):
     models, rows, depth = hidden.shape
     inner = w_inner.shape[3]
     state = w_state.shape[3]
@@ -190,9 +190,10 @@
 
 
 def gate_kernel(
-    m, pages_ref, flags_ref, y_ref, gate_ref, c_ref, e_ref, r1_ref, r2_ref, r3_ref, r4_ref,
-    p0_ref, p1_ref, p2_ref, p3_ref, gain_ref, out_ref, pick_ref,
+    pages_ref, flags_ref, y_ref, gate_ref, c_ref, e_ref, r1_ref, r2_ref, r3_ref, r4_ref,
+    p0_ref, p1_ref, p2_ref, p3_ref, gain_ref, out0_ref, out1_ref, pick_ref,
 ):
+    m = pl.program_id(0)
     rows, inner = y_ref.shape
     heads = p0_ref.shape[0]
     wide = inner // heads
@@ -233,39 +234,42 @@
     spread = jnp.concatenate([jnp.broadcast_to(e_col[:, h : h + 1], (rows, wide)) for h in range(heads)], axis=1)
     gated = (y_ref[...] + picked * spread) * silu(gate_ref[...])
     square = jnp.sum(gated * gated, axis=1, keepdims=True)
-    out_ref[0:rows, :] = (gated * gain_ref[m : m + 1, :]).astype(BF16)
-    lines = jnp.transpose(jnp.broadcast_to(square, (rows, 8)))[0:1, :]
+    mixed = (gated * gain_ref[pl.ds(m, 1), :]).astype(BF16)
+    lines = to_row(square)
     halves = jnp.concatenate([lines[:, 0:inner], lines[:, inner:]], axis=0)
-    extra = jnp.concatenate(pieces(halves) + [jnp.zeros((10, inner), F32)], axis=0)
-    out_ref[rows : rows + 16, :] = extra.astype(BF16)
-
-
-def gate_out(m, pages, flags, y, gate, c, e, recv, pool, gain, after=()):
-    rows, inner = y.shape[1:]
+    extra = jnp.concatenate(pieces(halves) + [jnp.zeros((10, inner), F32)], axis=0).astype(BF16)
+    for n, out in enumerate((out0_ref, out1_ref)):
+
+        @pl.when(m == n)
+        def _():
+            out[0:rows, :] = mixed
+            out[rows : rows + 16, :] = extra
+
+
+def gate_out(pages, flags, y, gate, c, e, recv, pool, gain):
+    models, rows, inner = y.shape
     heads = pool.shape[2]
     state = c.shape[2]
-    whole = lambda a: pl.BlockSpec(a.shape, lambda g, pg, fl: (0,) * a.ndim)
-    mine = lambda a: pl.BlockSpec((None,) + a.shape[1:], lambda g, pg, fl: (m, 0, 0))
+    mine = lambda a: pl.BlockSpec((None,) + a.shape[1:], lambda m, pg, fl: (m, 0, 0))
     page = lambda j: pl.BlockSpec(
-        (None, None, heads, pool.shape[3], state), lambda g, pg, fl: (m, pg[j], 0, 0, 0)
+        (None, None, heads, pool.shape[3], state), lambda m, pg, fl: (m, pg[j], 0, 0, 0)
     )
     return pl.pallas_call(
-        drop(functools.partial(gate_kernel, m), 15, len(after)),
+        gate_kernel,
         grid_spec=pltpu.PrefetchScalarGridSpec(
             num_scalar_prefetch=2,
-            grid=(1,),
+            grid=(models,),
             in_specs=[mine(y), mine(gate), mine(c), mine(e)]
             + [mine(r) for r in recv]
             + [page(j) for j in range(4)]
-            + [whole(gain)]
-            + [ANYWHERE] * len(after),
-            out_specs=pl.BlockSpec((rows + 16, inner), lambda g, pg, fl: (0, 0)),
+            + [pl.BlockSpec(gain.shape, lambda m, pg, fl: (0, 0))],
+            out_specs=[pl.BlockSpec((rows + 16, inner), lambda m, pg, fl: (0, 0))] * models,
             scratch_shapes=[pltpu.VMEM((rows, inner), F32)],
         ),
-        out_shape=jax.ShapeDtypeStruct((rows + 16, inner), BF16),
-        cost_estimate=pl.CostEstimate(flops=10**9, bytes_accessed=12 * 10**6, transcendentals=10**5),
+        out_shape=[jax.ShapeDtypeStruct((rows + 16, inner), BF16)] * models,
+        cost_estimate=pl.CostEstimate(flops=2 * 10**9, bytes_accessed=2 * 10**7, transcendentals=10**5),
         name="gate_out",
-    )(pages, flags, y, gate, c, e, *recv, pool, pool, pool, pool, gain, *after)
+    )(pages, flags, y, gate, c, e, *recv, pool, pool, pool, pool, gain)
 
 
 def out_kernel(at_ref, g0_ref, g1_ref, g2_ref, g3_ref, w_ref, o0_ref, o1_ref, o2_ref, o3_ref, acc_ref, sq_ref):
@@ -300,6 +304,7 @@
         out_shape=[jax.ShapeDtypeStruct((block + 16, width), BF16)] * 4,
         scratch_shapes=[pltpu.VMEM((rows, width), F32), pltpu.VMEM((4, block), F32)],
         cost_estimate=pl.CostEstimate(flops=10**9, bytes_accessed=10**7, transcendentals=0),
+        compiler_params=pltpu.CompilerParams(vmem_limit_bytes=14 * 2**20),
         name="out_blocks",
     )(at, *gathered, w, *after)
 
@@ -328,7 +333,7 @@
             grid=(1,),
             in_specs=[whole] * 4
             + [
-                pl.BlockSpec((None, block, width), lambda g, at: (m, at[1], at[0])),
+                pl.BlockSpec((block, width), lambda g, at: (0, 0)),
                 pl.BlockSpec((2, width), lambda g, at: (0, at[0])),
             ]
             + [ANYWHERE] * len(after),
@@ -336,6 +341,7 @@
         ),
         out_shape=jax.ShapeDtypeStruct((block + 16, width), BF16),
         cost_estimate=pl.CostEstimate(flops=10**6, bytes_accessed=9 * 10**6, transcendentals=100),
+        compiler_params=pltpu.CompilerParams(vmem_limit_bytes=8 * 2**20),
         name="residual_block",
     )(at, *parts, hidden, gain, *after)
 
@@ -368,6 +374,7 @@
         out_specs=vm,
         out_shape=jax.ShapeDtypeStruct((tall, 4 * width), BF16),
         cost_estimate=pl.CostEstimate(flops=10**5, bytes_accessed=6 * 10**6, transcendentals=100),
+        compiler_params=pltpu.CompilerParams(vmem_limit_bytes=8 * 2**20),
         name="join_columns",
     )(at, *parts, *after)
 
@@ -534,24 +541,38 @@
     )(stats, live, seg)
 
 
-def turn_kernel(w_ref, out_ref):
+def turn_kernel(at_ref, w_ref, hid_ref, out_ref, mine_ref):
     width = out_ref.shape[2]
     for j in range(4):
         out_ref[j] = w_ref[:, j * width : (j + 1) * width]
-
-
-def turned(m, w_out):
+    mine_ref[...] = hid_ref[...]
+
+
+def turned(m, at, w_out, hidden):
     _, inner, depth = w_out.shape
     width = depth // 4
+    block = hidden.shape[1] // 4
     return pl.pallas_call(
         turn_kernel,
-        grid=(1,),
-        in_specs=[pl.BlockSpec((None, inner, depth), lambda j: (m, 0, 0))],
-        out_specs=pl.BlockSpec((4, inner, width), lambda j: (0, 0, 0)),
-        out_shape=jax.ShapeDtypeStruct((4, inner, width), w_out.dtype),
-        cost_estimate=pl.CostEstimate(flops=0, bytes_accessed=2 * 10**6, transcendentals=0),
+        grid_spec=pltpu.PrefetchScalarGridSpec(
+            num_scalar_prefetch=1,
+            grid=(1,),
+            in_specs=[
+                pl.BlockSpec((None, inner, depth), lambda j, at: (m, 0, 0)),
+                pl.BlockSpec((None, block, width), lambda j, at: (m, at[1], at[0])),
+            ],
+            out_specs=[
+                pl.BlockSpec((4, inner, width), lambda j, at: (0, 0, 0)),
+                pl.BlockSpec((block, width), lambda j, at: (0, 0)),
+            ],
+        ),
+        out_shape=[
+            jax.ShapeDtypeStruct((4, inner, width), w_out.dtype),
+            jax.ShapeDtypeStruct((block, width), hidden.dtype),
+        ],
+        cost_estimate=pl.CostEstimate(flops=0, bytes_accessed=6 * 10**6, transcendentals=0),
         name="turned",
-    )(w_out)
+    )(at, w_out, hidden)
 
 
 def ring(value, axis, by):
@@ -582,17 +603,17 @@
     at = [
         jnp.stack([lax.axis_index(along), lax.axis_index(across)]).astype(jnp.int32) for along, across in ways
     ]
-    weights = [lax.all_to_all(turned(m, w_out), ways[m][0], 0, 0) for m in both]
+    turns = [turned(m, at[m], w_out, hidden) for m in both]
+    weights = [lax.all_to_all(turns[m][0], ways[m][0], 0, 0) for m in both]
     y, gate, c, e, pay = mix_local(hidden, w_inner, w_state, w_step, step_bias, rate, skip_gain, seg)
     recv = [lax.ppermute(pay, SEQ, [(i, i + k) for i in range(devices - k)]) for k in range(1, REACH + 1)]
-    gated, parts, res, full = [], [], [], []
+    parts, res, full = [], [], []
+    gated = gate_out(pages, flags, y, gate, c, e, recv, pool, norm_gain)
     for m in both:
-        gated.append(gate_out(m, pages, flags, y, gate, c, e, recv, pool, norm_gain, tuple(gated)))
-    for m in both:
-        out = out_blocks(at[m], gathered(gated[m], ways[m][0]), weights[m], (gated[1],))
+        out = out_blocks(at[m], gathered(gated[m], ways[m][0]), weights[m])
         parts.append([out[0]] + [ring(out[k], ways[m][1], k) for k in (1, 2, 3)])
     for m in both:
-        res.append(residual_block(m, at[m], parts[m], hidden, final_gain, inner * group, (parts[1][0],)))
+        res.append(residual_block(m, at[m], parts[m], turns[m][1], final_gain, inner * group, (parts[1][0],)))
     blocks = [gathered(res[m], ways[m][0]) for m in both]
     for m in both:
         full.append(join_columns(at[m], blocks[m], tuple(blocks[1 - m][1:])))

time: 179 us -> 168 us (0.939)
  Pallas kernels: 63.9 us -> 51.7 us
  waiting for transfers between devices: 24.8 us -> 35.4 us
  starting transfers between devices: 64 us -> 58.4 us
  local copies, waits for them, and re-layouts: 12.1 us -> 8.36 us
    ppermute x29, waiting for transfers between devices: 23.8 us -> 34.4 us  [ring(): return lax.ppermute(value, axis, [(i, (i + by) % 4) for i in range(4)])]
    pallas_call x2, Pallas kernels: 5.68 us -> 1.73 us  [residual_block(): pl.pallas_call(drop(functools.partial(residual_kernel, m, float(units)),...]
    unnamed x68 -> x36, local copies, waits for them, and re-layouts: 12 us -> 8.24 us
    ppermute x1, starting transfers between devices: 9.26 us -> 5.85 us  [per_device(): sums = sums + lax.ppermute(sums, 'core', [(0, 1), (1, 0)])]
    pallas_call x2, Pallas kernels: 6.38 us -> 3.4 us  [out_blocks(): pl.pallas_call(drop(out_kernel, 6, len(after)), in_specs=[pl.BlockSpec(me...]
    pallas_call x2, Pallas kernels: 4.16 us -> 1.29 us  [join_columns(): pl.pallas_call(drop(join_kernel, 5, len(after)), in_specs=[pl.BlockSpec(m...]
    ppermute x29, starting transfers between devices: 33.4 us -> 31.2 us  [ring(): return lax.ppermute(value, axis, [(i, (i + by) % 4) for i in range(4)])]
    pallas_call x4 -> x3, Pallas kernels: 12.9 us -> 12 us  [the longest x2 6.1 us: turned(): pl.pallas_call(turn_kernel, grid_spec=pltpu.PrefetchScalarGridSpec(num_sc...]
  transfers between devices with their start and end apart: 36 -> 36, of which waited for: 11 -> 14; matrix products, arithmetic and copies ran while one was open for 3% -> 3% of each run, Pallas kernels for 30% -> 26%
where the time goes in v8:
time: 168 us; the launch traced here: 167 us
  starting transfers between devices  58.4 us (35%)
  Pallas kernels  51.7 us (31%)
  waiting for transfers between devices  35.4 us (21%)
  blocking collectives  9.94 us (6%)
  local copies, waits for them, and re-layouts  8.36 us (5%)
  other arithmetic  2.4 us (1%)
    ppermute x29, waiting for transfers between devices, ring(): return lax.ppermute(value, axis, [(i, (i + by) % 4) for i in range(4)])  34.4 us
    ppermute x29, starting transfers between devices, ring(): return lax.ppermute(value, axis, [(i, (i + by) % 4) for i in range(4)])  31.2 us
    pallas_call x1, Pallas kernels, mix_local(): pl.pallas_call(mix_kernel, grid=(models, chunks), in_specs=[pl.BlockSpec(...  15.5 us
    ppermute x4, starting transfers between devices, per_device(): lax.ppermute(pay, SEQ, [(i, i + k) for i in range(devices - k)])  11.5 us
    all_to_all x1, blocking collectives, per_device(): lax.all_to_all(head_stats(place, at, near, cut, ready, tgt, group), VOC,...  9.94 us
    all_to_all x2, starting transfers between devices, per_device(): weights = [lax.all_to_all(turns[m][0], ways[m][0], 0, 0) for m in both]  9.89 us
    unnamed x36, local copies, waits for them, and re-layouts  8.24 us
    pallas_call x1, Pallas kernels, head_stats(): pl.pallas_call(near_kernel, in_specs=[sm] * 3 + [vm] * 8, scratch_shapes=...  7.69 us
  transfers between devices with their start and end apart: 36, of which 14 were waited for; matrix products, arithmetic and copies ran while one was open for 3% of the time, Pallas kernels for 26%

profile of v8, /device:TPU:1, one launch (start us, length us, event | category | flops | bytes accessed | tf_op | source)
XLA Modules:
  0.0 167.1 jit_solution(16291546648025862891)
XLA Ops:
  0.6 0.6 pad_add_fusion.1.at_ref.refs_0_.at1_ref
  1.2 3.1 %turned.3 = (bf16[4,256,512]{2,1,0:T(8,128)(2,1)}, bf16[128,512]{1,0:T(8,128)(2,1)}) custom-call(s32[2]{0:T(128)} %pad_add_fusion.1.at_ref.refs_0_.at1_ref, bf16[2,256,2048]{2,1,0:T(8,128)(2,1)} %w_ref.3, bf16[2,512,2048]{2,1,0:T(8,128)(2,1)} %hid_ref.3), custom_call_target="tpu_custom_call" | custom-call | bytes 6000000 | tf_op jit(solution)/shard_map/turned/pallas_call | solution.py:555
  4.3 5.9 %all-to-all-start.1 = ((bf16[4,256,512]{2,1,0:T(8,128)(2,1)}), bf16[4,256,512]{2,1,0:T(8,128)(2,1)S(1)}, u32[]{:S(2)}, u32[]{:S(2)}) async-start(bf16[4,256,512]{2,1,0:T(8,128)(2,1)} %get-tuple-element.40), calls=%async_computation.1 | async-start | bytes 2097152 | tf_op jit(solution)/shard_map/all_to_all | solution.py:607
  10.2 1.6 copy.27
  11.8 1.3 copy-done.10
  13.1 2.6 %copy.26 = bf16[2,2048,2,256]{3,1,2,0:T(8,128)(2,1)} copy(bf16[2,2048,2,256]{3,2,1,0:T(2,128)(2,1)S(1)} %copy-done.10) | data formatting | bytes 8388608 | tf_op args[1]
  15.7 15.5 %mix_local.1 = (f32[2,512,256]{2,1,0:T(8,128)}, f32[2,512,256]{2,1,0:T(8,128)}, bf16[2,512,128]{2,1,0:T(8,128)(2,1)}, f32[2,512,8]{2,1,0:T(8,128)}, bf16[2,272,128]{2,1,0:T(8,128)(2,1)}) custom-call(bf16[2,512,2048]{2,1,0:T(8,128)(2,1)} %hid_ref.3, bf16[2,2,2048,256]{3,2,1,0:T(8,128)(2,1)} %bitcast.18, bf16[2,2,2048,128]{3,2,1,0:T(8,128)(2,1)} %bitcast.19, ...), custom_call_target="tpu_custom_call" | custom-call | flops 10000000000 | bytes 16000000 | tf_op jit(solution)/shard_map/mix_local/pallas_call | solution.py:172
  31.3 4.8 %collective-permute-start.3 = (bf16[2,272,128]{2,1,0:T(8,128)(2,1)}, bf16[2,272,128]{2,1,0:T(8,128)(2,1)S(1)}, u32[]{:S(2)}, u32[]{:S(2)}) collective-permute-start(bf16[2,272,128]{2,1,0:T(8,128)(2,1)} %get-tuple-element.31), channel_id=1, source_target_pairs={{0,64},{16,80},{32,96},{48,112},{1,65},{17,81},{33,97},{49,113},{2... | collective-permute-start | bytes 417800 | tf_op jit(solution)/shard_map/ppermute | solution.py:609
  36.1 2.1 %collective-permute-start.2 = (bf16[2,272,128]{2,1,0:T(8,128)(2,1)}, bf16[2,272,128]{2,1,0:T(8,128)(2,1)S(1)}, u32[]{:S(2)}, u32[]{:S(2)}) collective-permute-start(bf16[2,272,128]{2,1,0:T(8,128)(2,1)} %get-tuple-element.31), channel_id=1, source_target_pairs={{0,48},{16,64},{32,80},{48,96},{64,112},{1,49},{17,65},{33,81},{49... | collective-permute-start | bytes 417800 | tf_op jit(solution)/shard_map/ppermute | solution.py:609
  38.3 2.3 %collective-permute-start.1 = (bf16[2,272,128]{2,1,0:T(8,128)(2,1)}, bf16[2,272,128]{2,1,0:T(8,128)(2,1)S(1)}, u32[]{:S(2)}, u32[]{:S(2)}) collective-permute-start(bf16[2,272,128]{2,1,0:T(8,128)(2,1)} %get-tuple-element.31), channel_id=1, source_target_pairs={{0,32},{16,48},{32,64},{48,80},{64,96},{80,112},{1,33},{17,49},{33... | collective-permute-start | bytes 417800 | tf_op jit(solution)/shard_map/ppermute | solution.py:609
  40.6 2.2 %collective-permute-start = (bf16[2,272,128]{2,1,0:T(8,128)(2,1)}, bf16[2,272,128]{2,1,0:T(8,128)(2,1)S(1)}, u32[]{:S(2)}, u32[]{:S(2)}) collective-permute-start(bf16[2,272,128]{2,1,0:T(8,128)(2,1)} %get-tuple-element.31), channel_id=1, source_target_pairs={{0,16},{16,32},{32,48},{48,64},{64,80},{80,96},{96,112},{1,17},{17... | collective-permute-start | bytes 417800 | tf_op jit(solution)/shard_map/ppermute | solution.py:609
  42.8 0.6 pad_add_fusion.at_ref.refs_0_.at0_ref
  43.4 3.0 %turned.2 = (bf16[4,256,512]{2,1,0:T(8,128)(2,1)}, bf16[128,512]{1,0:T(8,128)(2,1)}) custom-call(s32[2]{0:T(128)} %pad_add_fusion.at_ref.refs_0_.at0_ref, bf16[2,256,2048]{2,1,0:T(8,128)(2,1)} %w_ref.3, bf16[2,512,2048]{2,1,0:T(8,128)(2,1)} %hid_ref.3), custom_call_target="tpu_custom_call" | custom-call | bytes 6000000 | tf_op jit(solution)/shard_map/turned/pallas_call | solution.py:555
  46.4 4.0 %all-to-all-start = ((bf16[4,256,512]{2,1,0:T(8,128)(2,1)}), bf16[4,256,512]{2,1,0:T(8,128)(2,1)S(1)}, u32[]{:S(2)}, u32[]{:S(2)}) async-start(bf16[4,256,512]{2,1,0:T(8,128)(2,1)} %get-tuple-element.33), calls=%async_computation | async-start | bytes 2097152 | tf_op jit(solution)/shard_map/all_to_all | solution.py:607
  50.5 0.6 copy-done.12
  51.2 5.9 %gate_out.1 = (bf16[528,256]{1,0:T(8,128)(2,1)}, bf16[528,256]{1,0:T(8,128)(2,1)}) custom-call(s32[4]{0:T(128)} %pages_ref.1, s32[4]{0:T(128)} %flags_ref.1, f32[2,512,256]{2,1,0:T(8,128)} %get-tuple-element.27.y_ref, f32[2,512,256]{2,1,0:T(8,128)} %get-tuple-element.28.gate_ref, bf16[2,512,128]{2,1,0:T(8,128)(2,1)} %get-tuple-element.29.c_ref, ...), custom_call_target="tpu_custom_call" | custom-call | flops 2000000000 | bytes 20000000 | tf_op jit(solution)/shard_map/gate_out/pallas_call | solution.py:257
  57.1 3.0 %collective-permute-start.12 = (bf16[528,256]{1,0:T(8,128)(2,1)}, bf16[528,256]{1,0:T(8,128)(2,1)S(1)}, u32[]{:S(2)}, u32[]{:S(2)}) collective-permute-start(bf16[528,256]{1,0:T(8,128)(2,1)} %get-tuple-element.39.refs_1_), channel_id=1, source_target_pairs={{0,3},{1,0},{2,1},{3,2},{4,7},{5,4},{6,5},{7,6},{8,11},{9,8},{10,9... | collective-permute-start | bytes 811016 | tf_op jit(solution)/shard_map/ppermute | solution.py:579
  60.1 0.6 collective-permute-start.11
  60.7 0.6 collective-permute-start.10
  61.3 2.7 %collective-permute-start.6 = (bf16[528,256]{1,0:T(8,128)(2,1)}, bf16[528,256]{1,0:T(8,128)(2,1)S(1)}, u32[]{:S(2)}, u32[]{:S(2)}) collective-permute-start(bf16[528,256]{1,0:T(8,128)(2,1)} %get-tuple-element.32.refs_1_), channel_id=1, source_target_pairs={{0,12},{4,0},{8,4},{12,8},{1,13},{5,1},{9,5},{13,9},{2,14},{6,2},{... | collective-permute-start | bytes 811016 | tf_op jit(solution)/shard_map/ppermute | solution.py:579
  64.0 0.6 collective-permute-start.5
  64.6 6.9 %collective-permute-done.12.refs_4_ = bf16[528,256]{1,0:T(8,128)(2,1)S(1)} collective-permute-done((bf16[528,256]{1,0:T(8,128)(2,1)}, bf16[528,256]{1,0:T(8,128)(2,1)S(1)}, u32[]{:S(2)}, u32[]{:S(2)}) %collective-permute-start.12) | collective-permute-done | bytes 270368 | tf_op jit(solution)/shard_map/ppermute | solution.py:579
  71.5 4.6 %collective-permute-done.10.refs_2_ = bf16[528,256]{1,0:T(8,128)(2,1)S(1)} collective-permute-done((bf16[528,256]{1,0:T(8,128)(2,1)}, bf16[528,256]{1,0:T(8,128)(2,1)S(1)}, u32[]{:S(2)}, u32[]{:S(2)}) %collective-permute-start.10) | collective-permute-done | bytes 270368 | tf_op jit(solution)/shard_map/ppermute | solution.py:579
  76.1 1.0 copy-done.9
  77.0 2.1 %out_blocks.3 = (bf16[144,512]{1,0:T(8,128)(2,1)S(1)}, bf16[144,512]{1,0:T(8,128)(2,1)}, bf16[144,512]{1,0:T(8,128)(2,1)}, bf16[144,512]{1,0:T(8,128)(2,1)S(1)}) custom-call(s32[2]{0:T(128)S(1)} %copy-done.5, bf16[528,256]{1,0:T(8,128)(2,1)S(1)} %copy-done.9, bf16[528,256]{1,0:T(8,128)(2,1)S(1)} %collective-permute-done.10.refs_2_, ...), custom_call_target="tpu_custom_call" | custom-call | flops 1000000000 | bytes 10000000 | tf_op jit(solution)/shard_map/out_blocks/pallas_call | solution.py:300
  79.1 1.5 collective-permute-start.16
  80.6 2.4 %collective-permute-start.17 = (bf16[144,512]{1,0:T(8,128)(2,1)}, bf16[144,512]{1,0:T(8,128)(2,1)S(1)}, u32[]{:S(2)}, u32[]{:S(2)}) collective-permute-start(bf16[144,512]{1,0:T(8,128)(2,1)} %get-tuple-element.43), channel_id=1, source_target_pairs={{0,8},{4,12},{8,0},{12,4},{1,9},{5,13},{9,1},{13,5},{2,10},{6,14},... | collective-permute-start | bytes 442376 | tf_op jit(solution)/shard_map/ppermute | solution.py:579
  83.0 1.2 collective-permute-start.18
  84.2 0.9 copy-done.8
  85.1 1.3 out_blocks.2
  86.5 0.8 collective-permute-start.8
  87.4 1.8 %collective-permute-start.9 = (bf16[144,512]{1,0:T(8,128)(2,1)S(1)}, bf16[144,512]{1,0:T(8,128)(2,1)S(1)}, u32[]{:S(2)}, u32[]{:S(2)}) collective-permute-start(bf16[144,512]{1,0:T(8,128)(2,1)S(1)} %get-tuple-element.37), channel_id=1, source_target_pairs={{0,3},{1,0},{2,1},{3,2},{4,7},{5,4},{6,5},{7,6},{8,11},{9,8},{10,9... | collective-permute-start | bytes 442376 | tf_op jit(solution)/shard_map/ppermute | solution.py:579
  89.2 0.6 collective-permute-done.17.refs_3_
  89.8 0.9 residual_block.3.refs_1_
  91.0 1.6 collective-permute-start.20
  92.6 5.0 %collective-permute-done.7.refs_2_ = bf16[144,512]{1,0:T(8,128)(2,1)S(1)} collective-permute-done((bf16[144,512]{1,0:T(8,128)(2,1)S(1)}, bf16[144,512]{1,0:T(8,128)(2,1)S(1)}, u32[]{:S(2)}, u32[]{:S(2)}) %collective-permute-start.7) | collective-permute-done | bytes 147488 | tf_op jit(solution)/shard_map/ppermute | solution.py:579
  97.6 0.9 residual_block.2.refs_1_
  98.5 1.9 %collective-permute-start.14 = (bf16[144,512]{1,0:T(8,128)(2,1)S(1)}, bf16[144,512]{1,0:T(8,128)(2,1)S(1)}, u32[]{:S(2)}, u32[]{:S(2)}) collective-permute-start(bf16[144,512]{1,0:T(8,128)(2,1)S(1)} %residual_block.2.refs_1_), channel_id=1, source_target_pairs={{0,8},{4,12},{8,0},{12,4},{1,9},{5,13},{9,1},{13,5},{2,10},{6,14},... | collective-permute-start | bytes 442376 | tf_op jit(solution)/shard_map/ppermute | solution.py:579
  100.4 2.4 %collective-permute-done.19.refs_5_.refs_2_ = bf16[144,512]{1,0:T(8,128)(2,1)S(1)} collective-permute-done((bf16[144,512]{1,0:T(8,128)(2,1)S(1)}, bf16[144,512]{1,0:T(8,128)(2,1)S(1)}, u32[]{:S(2)}, u32[]{:S(2)}) %collective-permute-start.19) | collective-permute-done | bytes 147488 | tf_op jit(solution)/shard_map/ppermute | solution.py:579
  102.8 1.3 collective-permute-done.14.refs_3_.refs_6_
  104.1 2.2 %collective-permute-done.13.refs_2_.refs_5_ = bf16[144,512]{1,0:T(8,128)(2,1)S(1)} collective-permute-done((bf16[144,512]{1,0:T(8,128)(2,1)S(1)}, bf16[144,512]{1,0:T(8,128)(2,1)S(1)}, u32[]{:S(2)}, u32[]{:S(2)}) %collective-permute-start.13) | collective-permute-done | bytes 147488 | tf_op jit(solution)/shard_map/ppermute | solution.py:579
  106.2 0.6 join_columns.2.refs_1_.refs_0_
  106.9 3.7 %collective-permute-start.23 = (bf16[144,2048]{1,0:T(8,128)(2,1)S(1)}, bf16[144,2048]{1,0:T(8,128)(2,1)S(1)}, u32[]{:S(2)}, u32[]{:S(2)}) collective-permute-start(bf16[144,2048]{1,0:T(8,128)(2,1)S(1)} %join_columns.2.refs_1_.refs_0_), channel_id=1, source_target_pairs={{0,3},{1,0},{2,1},{3,2},{4,7},{5,4},{6,5},{7,6},{8,11},{9,8},{10,9... | collective-permute-start | bytes 1769480 | tf_op jit(solution)/shard_map/ppermute | solution.py:579
  110.6 0.6 join_columns.3.refs_2_.refs_3_
  111.3 1.0 collective-permute-start.25
  112.8 5.0 %fetched.1.refs_4_.refs_6_ = bf16[2,2048,1664]{2,1,0:T(8,128)(2,1)S(1)} custom-call(bf16[2,2048,1664]{2,1,0:T(8,128)(2,1)} %refs_0_.1, bf16[144,2048]{1,0:T(8,128)(2,1)S(1)} %join_columns.2.refs_1_.refs_0_, bf16[144,2048]{1,0:T(8,128)(2,1)} %copy-done), custom_call_target="tpu_custom_call" | custom-call | bytes 30000000 | tf_op jit(solution)/shard_map/fetched/pallas_call | solution.py:399
  117.8 3.1 %collective-permute-done.23.refs_1_.refs_2_ = bf16[144,2048]{1,0:T(8,128)(2,1)S(1)} collective-permute-done((bf16[144,2048]{1,0:T(8,128)(2,1)S(1)}, bf16[144,2048]{1,0:T(8,128)(2,1)S(1)}, u32[]{:S(2)}, u32[]{:S(2)}) %collective-permute-start.23) | collective-permute-done | bytes 589856 | tf_op jit(solution)/shard_map/ppermute | solution.py:579
  120.9 3.1 %collective-permute-done.22.refs_0_.refs_1_ = bf16[144,2048]{1,0:T(8,128)(2,1)S(1)} collective-permute-done((bf16[144,2048]{1,0:T(8,128)(2,1)S(1)}, bf16[144,2048]{1,0:T(8,128)(2,1)S(1)}, u32[]{:S(2)}, u32[]{:S(2)}) %collective-permute-start.22) | collective-permute-done | bytes 589856 | tf_op jit(solution)/shard_map/ppermute | solution.py:579
  124.0 1.6 collective-permute-done.24.refs_2_.refs_4_
  125.8 2.7 %collective-permute-start.27 = (bf16[72,2048]{1,0:T(8,128)(2,1)S(1)}, bf16[72,2048]{1,0:T(8,128)(2,1)S(1)}, u32[]{:S(2)}, u32[]{:S(2)}) collective-permute-start(bf16[72,2048]{1,0:T(8,128)(2,1)S(1)} %get-tuple-element.47), channel_id=1, source_target_pairs={{0,3},{1,0},{2,1},{3,2},{4,7},{5,4},{6,5},{7,6},{8,11},{9,8},{10,9... | collective-permute-start | bytes 884744 | tf_op jit(solution)/shard_map/ppermute | solution.py:579
  128.5 2.7 %collective-permute-start.29 = (bf16[72,2048]{1,0:T(8,128)(2,1)S(1)}, bf16[72,2048]{1,0:T(8,128)(2,1)S(1)}, u32[]{:S(2)}, u32[]{:S(2)}) collective-permute-start(bf16[72,2048]{1,0:T(8,128)(2,1)S(1)} %get-tuple-element.49), channel_id=1, source_target_pairs={{0,12},{4,0},{8,4},{12,8},{1,13},{5,1},{9,5},{13,9},{2,14},{6,2},{... | collective-permute-start | bytes 884744 | tf_op jit(solution)/shard_map/ppermute | solution.py:579
  131.1 7.7 %head_near.1.refs_6_ = f32[16,128]{1,0:T(8,128)S(1)} custom-call(s32[1]{0:T(128)} %bitcast.place_ref, s32[2]{0:T(128)S(1)} %copy-done.6, s32[2]{0:T(128)S(1)} %copy-done.5, bf16[144,2048]{1,0:T(8,128)(2,1)S(1)} %join_columns.2.refs_1_.refs_0_, bf16[144,2048]{1,0:T(8,128)(2,1)S(1)} %collective-permute-done.22.refs_0_.refs_1_, ...), custom_call_target="tpu_custom_call" | custom-call | flops 5234491392 | bytes 10000000 | tf_op jit(solution)/shard_map/head_near/pallas_call | solution.py:471
  138.9 3.3 %head_far.1 = f32[16,16,128]{2,1,0:T(8,128)S(1)} custom-call(s32[1]{0:T(128)} %bitcast.place_ref, s32[2]{0:T(128)S(1)} %copy-done.6, s32[2]{0:T(128)S(1)} %copy-done.5, bf16[72,2048]{1,0:T(8,128)(2,1)S(1)} %collective-permute-done.26.refs_0_, bf16[72,2048]{1,0:T(8,128)(2,1)S(1)} %collective-permute-done.27.refs_1_, ...), custom_call_target="tpu_custom_call" | custom-call | flops 1744830464 | bytes 10000000 | tf_op jit(solution)/shard_map/head_far/pallas_call | solution.py:480
  142.2 9.9 %all_to_all.15.stat_ref = f32[16,16,128]{2,1,0:T(8,128)} all-to-all(f32[16,16,128]{2,1,0:T(8,128)S(1)} %head_far.1), channel_id=1, replica_groups=mesh['y'=4,'core'=2,'x'=4,'z'=4] {'x','z'}, dimensions={0} | all-to-all | bytes 262144 | tf_op jit(solution)/shard_map/all_to_all | solution.py:624
  152.2 1.7 token_diffs.1
  153.8 5.9 %collective-permute-start.30 = (f32[8,128]{1,0:T(8,128)}, f32[8,128]{1,0:T(8,128)S(1)}, u32[]{:S(2)}, u32[]{:S(2)}) collective-permute-start(f32[8,128]{1,0:T(8,128)} %get-tuple-element.51), channel_id=1, source_target_pairs={{0,16},{16,0},{1,17},{17,1},{2,18},{18,2},{3,19},{19,3},{4,20},{20... | collective-permute-start | bytes 12296 | tf_op jit(solution)/shard_map/ppermute | solution.py:626
  159.7 1.0 collective-permute-done.30
  160.7 0.7 add.20
  161.4 0.9 collective-permute-start.32
  162.2 0.6 collective-permute-start.31
  162.9 1.0 collective-permute-done.33
  163.8 1.5 collective-permute-done.32
  165.4 1.1 collective-permute-done.31
  166.6 0.5 fusion
  (66 shorter events, 1.5 us)
Async XLA Ops:
  1.2 9.0 %copy-start.11 = (bf16[2,2048,2,128]{3,2,1,0:T(2,128)(2,1)S(1)}, bf16[2,2048,2,128]{3,2,1,0:T(2,128)(2,1)}, u32[]{:S(2)}) copy-start(bf16[2,2048,2,128]{3,2,1,0:T(2,128)(2,1)} %param.20) | copy-start | bytes 6291460
  4.3 42.0 %all-to-all-start.1 = ((bf16[4,256,512]{2,1,0:T(8,128)(2,1)}), bf16[4,256,512]{2,1,0:T(8,128)(2,1)S(1)}, u32[]{:S(2)}, u32[]{:S(2)}) async-start(bf16[4,256,512]{2,1,0:T(8,128)(2,1)} %get-tuple-element.40), calls=%async_computation.1 | async-start | bytes 2097152 | tf_op jit(solution)/shard_map/all_to_all | solution.py:607
  10.2 2.9 %copy-start.10 = (bf16[2,2048,2,256]{3,2,1,0:T(2,128)(2,1)S(1)}, bf16[2,2048,2,256]{3,2,1,0:T(2,128)(2,1)}, u32[]{:S(2)}) copy-start(bf16[2,2048,2,256]{3,2,1,0:T(2,128)(2,1)} %param.19) | copy-start | bytes 12582916
  31.3 19.1 %collective-permute-start.3 = (bf16[2,272,128]{2,1,0:T(8,128)(2,1)}, bf16[2,272,128]{2,1,0:T(8,128)(2,1)S(1)}, u32[]{:S(2)}, u32[]{:S(2)}) collective-permute-start(bf16[2,272,128]{2,1,0:T(8,128)(2,1)} %get-tuple-element.31), channel_id=1, source_target_pairs={{0,64},{16,80},{32,96},{48,112},{1,65},{17,81},{33,97},{49,113},{2... | collective-permute-start | bytes 417800 | tf_op jit(solution)/shard_map/ppermute | solution.py:609
  36.1 14.3 %collective-permute-start.2 = (bf16[2,272,128]{2,1,0:T(8,128)(2,1)}, bf16[2,272,128]{2,1,0:T(8,128)(2,1)S(1)}, u32[]{:S(2)}, u32[]{:S(2)}) collective-permute-start(bf16[2,272,128]{2,1,0:T(8,128)(2,1)} %get-tuple-element.31), channel_id=1, source_target_pairs={{0,48},{16,64},{32,80},{48,96},{64,112},{1,49},{17,65},{33,81},{49... | collective-permute-start | bytes 417800 | tf_op jit(solution)/shard_map/ppermute | solution.py:609
  38.3 12.2 %collective-permute-start.1 = (bf16[2,272,128]{2,1,0:T(8,128)(2,1)}, bf16[2,272,128]{2,1,0:T(8,128)(2,1)S(1)}, u32[]{:S(2)}, u32[]{:S(2)}) collective-permute-start(bf16[2,272,128]{2,1,0:T(8,128)(2,1)} %get-tuple-element.31), channel_id=1, source_target_pairs={{0,32},{16,48},{32,64},{48,80},{64,96},{80,112},{1,33},{17,49},{33... | collective-permute-start | bytes 417800 | tf_op jit(solution)/shard_map/ppermute | solution.py:609
  40.6 9.9 %collective-permute-start = (bf16[2,272,128]{2,1,0:T(8,128)(2,1)}, bf16[2,272,128]{2,1,0:T(8,128)(2,1)S(1)}, u32[]{:S(2)}, u32[]{:S(2)}) collective-permute-start(bf16[2,272,128]{2,1,0:T(8,128)(2,1)} %get-tuple-element.31), channel_id=1, source_target_pairs={{0,16},{16,32},{32,48},{48,64},{64,80},{80,96},{96,112},{1,17},{17... | collective-permute-start | bytes 417800 | tf_op jit(solution)/shard_map/ppermute | solution.py:609
  46.4 37.8 %all-to-all-start = ((bf16[4,256,512]{2,1,0:T(8,128)(2,1)}), bf16[4,256,512]{2,1,0:T(8,128)(2,1)S(1)}, u32[]{:S(2)}, u32[]{:S(2)}) async-start(bf16[4,256,512]{2,1,0:T(8,128)(2,1)} %get-tuple-element.33), calls=%async_computation | async-start | bytes 2097152 | tf_op jit(solution)/shard_map/all_to_all | solution.py:607
  50.4 0.7 copy-start.12
  50.4 0.7 copy-start.13
  50.4 0.7 copy-start.14
  50.5 0.8 copy-start.15
  51.2 24.8 %copy-start.5 = (s32[2]{0:T(128)S(1)}, s32[2]{0:T(128)}, u32[]{:S(2)}) copy-start(s32[2]{0:T(128)} %pad_add_fusion.1.at_ref.refs_0_.at1_ref) | copy-start | bytes 28
  51.2 32.9 %copy-start.6 = (s32[2]{0:T(128)S(1)}, s32[2]{0:T(128)}, u32[]{:S(2)}) copy-start(s32[2]{0:T(128)} %pad_add_fusion.at_ref.refs_0_.at0_ref) | copy-start | bytes 28
  57.1 32.7 %copy-start.2 = (bf16[128,512]{1,0:T(8,128)(2,1)S(1)}, bf16[128,512]{1,0:T(8,128)(2,1)}, u32[]{:S(2)}) copy-start(bf16[128,512]{1,0:T(8,128)(2,1)} %get-tuple-element.45.refs_5_) | copy-start | bytes 393220
  57.1 32.7 %copy-start.4 = (f32[2,2048]{1,0:T(2,128)S(1)}, f32[2,2048]{1,0:T(2,128)}, u32[]{:S(2)}) copy-start(f32[2,2048]{1,0:T(2,128)} %refs_6_.3) | copy-start | bytes 49156
  57.1 14.3 %collective-permute-start.12 = (bf16[528,256]{1,0:T(8,128)(2,1)}, bf16[528,256]{1,0:T(8,128)(2,1)S(1)}, u32[]{:S(2)}, u32[]{:S(2)}) collective-permute-start(bf16[528,256]{1,0:T(8,128)(2,1)} %get-tuple-element.39.refs_1_), channel_id=1, source_target_pairs={{0,3},{1,0},{2,1},{3,2},{4,7},{5,4},{6,5},{7,6},{8,11},{9,8},{10,9... | collective-permute-start | bytes 811016 | tf_op jit(solution)/shard_map/ppermute | solution.py:579
  60.1 11.3 %collective-permute-start.11 = (bf16[528,256]{1,0:T(8,128)(2,1)}, bf16[528,256]{1,0:T(8,128)(2,1)S(1)}, u32[]{:S(2)}, u32[]{:S(2)}) collective-permute-start(bf16[528,256]{1,0:T(8,128)(2,1)} %get-tuple-element.39.refs_1_), channel_id=1, source_target_pairs={{0,2},{1,3},{2,0},{3,1},{4,6},{5,7},{6,4},{7,5},{8,10},{9,11},{10,... | collective-permute-start | bytes 811016 | tf_op jit(solution)/shard_map/ppermute | solution.py:579
  60.7 15.3 %collective-permute-start.10 = (bf16[528,256]{1,0:T(8,128)(2,1)}, bf16[528,256]{1,0:T(8,128)(2,1)S(1)}, u32[]{:S(2)}, u32[]{:S(2)}) collective-permute-start(bf16[528,256]{1,0:T(8,128)(2,1)} %get-tuple-element.39.refs_1_), channel_id=1, source_target_pairs={{0,1},{1,2},{2,3},{3,0},{4,5},{5,6},{6,7},{7,4},{8,9},{9,10},{10,1... | collective-permute-start | bytes 811016 | tf_op jit(solution)/shard_map/ppermute | solution.py:579
  61.3 36.3 %copy-start.3 = (bf16[128,512]{1,0:T(8,128)(2,1)S(1)}, bf16[128,512]{1,0:T(8,128)(2,1)}, u32[]{:S(2)}) copy-start(bf16[128,512]{1,0:T(8,128)(2,1)} %get-tuple-element.38.refs_5_) | copy-start | bytes 393220
  61.3 21.6 %collective-permute-start.6 = (bf16[528,256]{1,0:T(8,128)(2,1)}, bf16[528,256]{1,0:T(8,128)(2,1)S(1)}, u32[]{:S(2)}, u32[]{:S(2)}) collective-permute-start(bf16[528,256]{1,0:T(8,128)(2,1)} %get-tuple-element.32.refs_1_), channel_id=1, source_target_pairs={{0,12},{4,0},{8,4},{12,8},{1,13},{5,1},{9,5},{13,9},{2,14},{6,2},{... | collective-permute-start | bytes 811016 | tf_op jit(solution)/shard_map/ppermute | solution.py:579
  64.0 20.2 %collective-permute-start.5 = (bf16[528,256]{1,0:T(8,128)(2,1)}, bf16[528,256]{1,0:T(8,128)(2,1)S(1)}, u32[]{:S(2)}, u32[]{:S(2)}) collective-permute-start(bf16[528,256]{1,0:T(8,128)(2,1)} %get-tuple-element.32.refs_1_), channel_id=1, source_target_pairs={{0,8},{4,12},{8,0},{12,4},{1,9},{5,13},{9,1},{13,5},{2,10},{6,14},... | collective-permute-start | bytes 811016 | tf_op jit(solution)/shard_map/ppermute | solution.py:579
  71.5 12.7 %collective-permute-start.4 = (bf16[528,256]{1,0:T(8,128)(2,1)}, bf16[528,256]{1,0:T(8,128)(2,1)S(1)}, u32[]{:S(2)}, u32[]{:S(2)}) collective-permute-start(bf16[528,256]{1,0:T(8,128)(2,1)} %get-tuple-element.32.refs_1_), channel_id=1, source_target_pairs={{0,4},{4,8},{8,12},{12,0},{1,5},{5,9},{9,13},{13,1},{2,6},{6,10},{... | collective-permute-start | bytes 811016 | tf_op jit(solution)/shard_map/ppermute | solution.py:579
  76.1 1.0 copy-start.9
  79.1 8.3 %collective-permute-start.16 = (bf16[144,512]{1,0:T(8,128)(2,1)}, bf16[144,512]{1,0:T(8,128)(2,1)S(1)}, u32[]{:S(2)}, u32[]{:S(2)}) collective-permute-start(bf16[144,512]{1,0:T(8,128)(2,1)} %get-tuple-element.42), channel_id=1, source_target_pairs={{0,4},{4,8},{8,12},{12,0},{1,5},{5,9},{9,13},{13,1},{2,6},{6,10},{... | collective-permute-start | bytes 442376 | tf_op jit(solution)/shard_map/ppermute | solution.py:579
  80.6 9.2 %collective-permute-start.17 = (bf16[144,512]{1,0:T(8,128)(2,1)}, bf16[144,512]{1,0:T(8,128)(2,1)S(1)}, u32[]{:S(2)}, u32[]{:S(2)}) collective-permute-start(bf16[144,512]{1,0:T(8,128)(2,1)} %get-tuple-element.43), channel_id=1, source_target_pairs={{0,8},{4,12},{8,0},{12,4},{1,9},{5,13},{9,1},{13,5},{2,10},{6,14},... | collective-permute-start | bytes 442376 | tf_op jit(solution)/shard_map/ppermute | solution.py:579
  83.0 6.8 %collective-permute-start.18 = (bf16[144,512]{1,0:T(8,128)(2,1)S(1)}, bf16[144,512]{1,0:T(8,128)(2,1)S(1)}, u32[]{:S(2)}, u32[]{:S(2)}) collective-permute-start(bf16[144,512]{1,0:T(8,128)(2,1)S(1)} %get-tuple-element.44), channel_id=1, source_target_pairs={{0,12},{4,0},{8,4},{12,8},{1,13},{5,1},{9,5},{13,9},{2,14},{6,2},{... | collective-permute-start | bytes 442376 | tf_op jit(solution)/shard_map/ppermute | solution.py:579
  84.2 1.0 copy-start.8
  86.4 11.1 %collective-permute-start.7 = (bf16[144,512]{1,0:T(8,128)(2,1)S(1)}, bf16[144,512]{1,0:T(8,128)(2,1)S(1)}, u32[]{:S(2)}, u32[]{:S(2)}) collective-permute-start(bf16[144,512]{1,0:T(8,128)(2,1)S(1)} %get-tuple-element.35), channel_id=1, source_target_pairs={{0,1},{1,2},{2,3},{3,0},{4,5},{5,6},{6,7},{7,4},{8,9},{9,10},{10,1... | collective-permute-start | bytes 442376 | tf_op jit(solution)/shard_map/ppermute | solution.py:579
  86.5 11.0 %collective-permute-start.8 = (bf16[144,512]{1,0:T(8,128)(2,1)S(1)}, bf16[144,512]{1,0:T(8,128)(2,1)S(1)}, u32[]{:S(2)}, u32[]{:S(2)}) collective-permute-start(bf16[144,512]{1,0:T(8,128)(2,1)S(1)} %get-tuple-element.36), channel_id=1, source_target_pairs={{0,2},{1,3},{2,0},{3,1},{4,6},{5,7},{6,4},{7,5},{8,10},{9,11},{10,... | collective-permute-start | bytes 442376 | tf_op jit(solution)/shard_map/ppermute | solution.py:579
  87.4 10.2 %collective-permute-start.9 = (bf16[144,512]{1,0:T(8,128)(2,1)S(1)}, bf16[144,512]{1,0:T(8,128)(2,1)S(1)}, u32[]{:S(2)}, u32[]{:S(2)}) collective-permute-start(bf16[144,512]{1,0:T(8,128)(2,1)S(1)} %get-tuple-element.37), channel_id=1, source_target_pairs={{0,3},{1,0},{2,1},{3,2},{4,7},{5,4},{6,5},{7,6},{8,11},{9,8},{10,9... | collective-permute-start | bytes 442376 | tf_op jit(solution)/shard_map/ppermute | solution.py:579
  90.7 9.7 %collective-permute-start.21 = (bf16[144,512]{1,0:T(8,128)(2,1)S(1)}, bf16[144,512]{1,0:T(8,128)(2,1)S(1)}, u32[]{:S(2)}, u32[]{:S(2)}) collective-permute-start(bf16[144,512]{1,0:T(8,128)(2,1)S(1)} %residual_block.3.refs_1_), channel_id=1, source_target_pairs={{0,3},{1,0},{2,1},{3,2},{4,7},{5,4},{6,5},{7,6},{8,11},{9,8},{10,9... | collective-permute-start | bytes 442376 | tf_op jit(solution)/shard_map/ppermute | solution.py:579
  91.0 9.4 %collective-permute-start.20 = (bf16[144,512]{1,0:T(8,128)(2,1)S(1)}, bf16[144,512]{1,0:T(8,128)(2,1)S(1)}, u32[]{:S(2)}, u32[]{:S(2)}) collective-permute-start(bf16[144,512]{1,0:T(8,128)(2,1)S(1)} %residual_block.3.refs_1_), channel_id=1, source_target_pairs={{0,2},{1,3},{2,0},{3,1},{4,6},{5,7},{6,4},{7,5},{8,10},{9,11},{10,... | collective-permute-start | bytes 442376 | tf_op jit(solution)/shard_map/ppermute | solution.py:579
  97.6 5.2 %collective-permute-start.19 = (bf16[144,512]{1,0:T(8,128)(2,1)S(1)}, bf16[144,512]{1,0:T(8,128)(2,1)S(1)}, u32[]{:S(2)}, u32[]{:S(2)}) collective-permute-start(bf16[144,512]{1,0:T(8,128)(2,1)S(1)} %residual_block.3.refs_1_), channel_id=1, source_target_pairs={{0,1},{1,2},{2,3},{3,0},{4,5},{5,6},{6,7},{7,4},{8,9},{9,10},{10,1... | collective-permute-start | bytes 442376 | tf_op jit(solution)/shard_map/ppermute | solution.py:579
  98.4 4.3 %collective-permute-start.15 = (bf16[144,512]{1,0:T(8,128)(2,1)S(1)}, bf16[144,512]{1,0:T(8,128)(2,1)S(1)}, u32[]{:S(2)}, u32[]{:S(2)}) collective-permute-start(bf16[144,512]{1,0:T(8,128)(2,1)S(1)} %residual_block.2.refs_1_), channel_id=1, source_target_pairs={{0,12},{4,0},{8,4},{12,8},{1,13},{5,1},{9,5},{13,9},{2,14},{6,2},{... | collective-permute-start | bytes 442376 | tf_op jit(solution)/shard_map/ppermute | solution.py:579
  98.5 5.6 %collective-permute-start.14 = (bf16[144,512]{1,0:T(8,128)(2,1)S(1)}, bf16[144,512]{1,0:T(8,128)(2,1)S(1)}, u32[]{:S(2)}, u32[]{:S(2)}) collective-permute-start(bf16[144,512]{1,0:T(8,128)(2,1)S(1)} %residual_block.2.refs_1_), channel_id=1, source_target_pairs={{0,8},{4,12},{8,0},{12,4},{1,9},{5,13},{9,1},{13,5},{2,10},{6,14},... | collective-permute-start | bytes 442376 | tf_op jit(solution)/shard_map/ppermute | solution.py:579
  100.4 5.9 %collective-permute-start.13 = (bf16[144,512]{1,0:T(8,128)(2,1)S(1)}, bf16[144,512]{1,0:T(8,128)(2,1)S(1)}, u32[]{:S(2)}, u32[]{:S(2)}) collective-permute-start(bf16[144,512]{1,0:T(8,128)(2,1)S(1)} %residual_block.2.refs_1_), channel_id=1, source_target_pairs={{0,4},{4,8},{8,12},{12,0},{1,5},{5,9},{9,13},{13,1},{2,6},{6,10},{... | collective-permute-start | bytes 442376 | tf_op jit(solution)/shard_map/ppermute | solution.py:579
  106.9 14.0 %collective-permute-start.23 = (bf16[144,2048]{1,0:T(8,128)(2,1)S(1)}, bf16[144,2048]{1,0:T(8,128)(2,1)S(1)}, u32[]{:S(2)}, u32[]{:S(2)}) collective-permute-start(bf16[144,2048]{1,0:T(8,128)(2,1)S(1)} %join_columns.2.refs_1_.refs_0_), channel_id=1, source_target_pairs={{0,3},{1,0},{2,1},{3,2},{4,7},{5,4},{6,5},{7,6},{8,11},{9,8},{10,9... | collective-permute-start | bytes 1769480 | tf_op jit(solution)/shard_map/ppermute | solution.py:579
  110.6 13.4 %collective-permute-start.22 = (bf16[144,2048]{1,0:T(8,128)(2,1)S(1)}, bf16[144,2048]{1,0:T(8,128)(2,1)S(1)}, u32[]{:S(2)}, u32[]{:S(2)}) collective-permute-start(bf16[144,2048]{1,0:T(8,128)(2,1)S(1)} %join_columns.2.refs_1_.refs_0_), channel_id=1, source_target_pairs={{0,1},{1,2},{2,3},{3,0},{4,5},{5,6},{6,7},{7,4},{8,9},{9,10},{10,1... | collective-permute-start | bytes 1769480 | tf_op jit(solution)/shard_map/ppermute | solution.py:579
  111.2 1.5 copy-start
  111.3 12.8 %collective-permute-start.25 = (bf16[144,2048]{1,0:T(8,128)(2,1)S(1)}, bf16[144,2048]{1,0:T(8,128)(2,1)S(1)}, u32[]{:S(2)}, u32[]{:S(2)}) collective-permute-start(bf16[144,2048]{1,0:T(8,128)(2,1)S(1)} %join_columns.3.refs_2_.refs_3_), channel_id=1, source_target_pairs={{0,12},{4,0},{8,4},{12,8},{1,13},{5,1},{9,5},{13,9},{2,14},{6,2},{... | collective-permute-start | bytes 1769480 | tf_op jit(solution)/shard_map/ppermute | solution.py:579
  112.2 13.4 %collective-permute-start.24 = (bf16[144,2048]{1,0:T(8,128)(2,1)S(1)}, bf16[144,2048]{1,0:T(8,128)(2,1)S(1)}, u32[]{:S(2)}, u32[]{:S(2)}) collective-permute-start(bf16[144,2048]{1,0:T(8,128)(2,1)S(1)} %join_columns.3.refs_2_.refs_3_), channel_id=1, source_target_pairs={{0,4},{4,8},{8,12},{12,0},{1,5},{5,9},{9,13},{13,1},{2,6},{6,10},{... | collective-permute-start | bytes 1769480 | tf_op jit(solution)/shard_map/ppermute | solution.py:579
  117.7 13.4 %copy-start.1 = (bf16[144,2048]{1,0:T(8,128)(2,1)S(1)}, bf16[144,2048]{1,0:T(8,128)(2,1)}, u32[]{:S(2)}) copy-start(bf16[144,2048]{1,0:T(8,128)(2,1)} %copy-done) | copy-start | bytes 1769476
  117.8 13.4 %copy-start.7 = (s32[512]{0:T(512)S(1)}, s32[512]{0:T(512)}, u32[]{:S(2)}) copy-start(s32[512]{0:T(512)} %param.30) | copy-start | bytes 6148
  125.7 13.1 %collective-permute-start.26 = (bf16[72,2048]{1,0:T(8,128)(2,1)S(1)}, bf16[72,2048]{1,0:T(8,128)(2,1)S(1)}, u32[]{:S(2)}, u32[]{:S(2)}) collective-permute-start(bf16[72,2048]{1,0:T(8,128)(2,1)S(1)} %get-tuple-element.46), channel_id=1, source_target_pairs={{0,1},{1,2},{2,3},{3,0},{4,5},{5,6},{6,7},{7,4},{8,9},{9,10},{10,1... | collective-permute-start | bytes 884744 | tf_op jit(solution)/shard_map/ppermute | solution.py:579
  125.8 13.1 %collective-permute-start.27 = (bf16[72,2048]{1,0:T(8,128)(2,1)S(1)}, bf16[72,2048]{1,0:T(8,128)(2,1)S(1)}, u32[]{:S(2)}, u32[]{:S(2)}) collective-permute-start(bf16[72,2048]{1,0:T(8,128)(2,1)S(1)} %get-tuple-element.47), channel_id=1, source_target_pairs={{0,3},{1,0},{2,1},{3,2},{4,7},{5,4},{6,5},{7,6},{8,11},{9,8},{10,9... | collective-permute-start | bytes 884744 | tf_op jit(solution)/shard_map/ppermute | solution.py:579
  128.4 10.4 %collective-permute-start.28 = (bf16[72,2048]{1,0:T(8,128)(2,1)S(1)}, bf16[72,2048]{1,0:T(8,128)(2,1)S(1)}, u32[]{:S(2)}, u32[]{:S(2)}) collective-permute-start(bf16[72,2048]{1,0:T(8,128)(2,1)S(1)} %get-tuple-element.48), channel_id=1, source_target_pairs={{0,4},{4,8},{8,12},{12,0},{1,5},{5,9},{9,13},{13,1},{2,6},{6,10},{... | collective-permute-start | bytes 884744 | tf_op jit(solution)/shard_map/ppermute | solution.py:579
  128.5 10.4 %collective-permute-start.29 = (bf16[72,2048]{1,0:T(8,128)(2,1)S(1)}, bf16[72,2048]{1,0:T(8,128)(2,1)S(1)}, u32[]{:S(2)}, u32[]{:S(2)}) collective-permute-start(bf16[72,2048]{1,0:T(8,128)(2,1)S(1)} %get-tuple-element.49), channel_id=1, source_target_pairs={{0,12},{4,0},{8,4},{12,8},{1,13},{5,1},{9,5},{13,9},{2,14},{6,2},{... | collective-permute-start | bytes 884744 | tf_op jit(solution)/shard_map/ppermute | solution.py:579
  138.8 27.8 %copy-start.16 = (s32[4]{0:T(128)S(1)}, s32[4]{0:T(128)}, u32[]{:S(2)}) copy-start(s32[4]{0:T(128)} %param.35) | copy-start | bytes 52
  153.8 6.9 %collective-permute-start.30 = (f32[8,128]{1,0:T(8,128)}, f32[8,128]{1,0:T(8,128)S(1)}, u32[]{:S(2)}, u32[]{:S(2)}) collective-permute-start(f32[8,128]{1,0:T(8,128)} %get-tuple-element.51), channel_id=1, source_target_pairs={{0,16},{16,0},{1,17},{17,1},{2,18},{18,2},{3,19},{19,3},{4,20},{20... | collective-permute-start | bytes 12296 | tf_op jit(solution)/shard_map/ppermute | solution.py:626
  161.4 2.5 %collective-permute-start.33 = (f32[8,128]{1,0:T(8,128)S(1)}, f32[8,128]{1,0:T(8,128)S(1)}, u32[]{:S(2)}, u32[]{:S(2)}) collective-permute-start(f32[8,128]{1,0:T(8,128)S(1)} %add.20), channel_id=1, source_target_pairs={{0,96},{32,0},{64,32},{96,64},{1,97},{33,1},{65,33},{97,65},{2,98}... | collective-permute-start | bytes 12296 | tf_op jit(solution)/shard_map/ppermute | solution.py:579
  161.4 4.0 %collective-permute-start.32 = (f32[8,128]{1,0:T(8,128)S(1)}, f32[8,128]{1,0:T(8,128)S(1)}, u32[]{:S(2)}, u32[]{:S(2)}) collective-permute-start(f32[8,128]{1,0:T(8,128)S(1)} %add.20), channel_id=1, source_target_pairs={{0,64},{32,96},{64,0},{96,32},{1,65},{33,97},{65,1},{97,33},{2,66}... | collective-permute-start | bytes 12296 | tf_op jit(solution)/shard_map/ppermute | solution.py:579
  162.2 4.2 %collective-permute-start.31 = (f32[8,128]{1,0:T(8,128)S(1)}, f32[8,128]{1,0:T(8,128)S(1)}, u32[]{:S(2)}, u32[]{:S(2)}) collective-permute-start(f32[8,128]{1,0:T(8,128)S(1)} %add.20), channel_id=1, source_target_pairs={{0,32},{32,64},{64,96},{96,0},{1,33},{33,65},{65,97},{97,1},{2,34}... | collective-permute-start | bytes 12296 | tf_op jit(solution)/shard_map/ppermute | solution.py:579

commit v9 on v8

--- a/solution.py
+++ b/solution.py
@@ -160,7 +160,7 @@
         y_ref[t0 : t0 + SPAN, :] = jnp.concatenate(acc, axis=1)
 
 
-def mix_local(hidden, w_inner, w_state, w_step, bias, rate, skip, seg, chunks=2):
+def mix_local(hidden, w_inner, w_state, w_step, bias, rate, skip, seg, chunks=1):
     models, rows, depth = hidden.shape
     inner = w_inner.shape[3]
     state = w_state.shape[3]
@@ -272,11 +272,11 @@
     )(pages, flags, y, gate, c, e, *recv, pool, pool, pool, pool, gain)
 
 
-def out_kernel(at_ref, g0_ref, g1_ref, g2_ref, g3_ref, w_ref, o0_ref, o1_ref, o2_ref, o3_ref, acc_ref, sq_ref):
+def out_kernel(m, at_ref, g0_ref, g1_ref, g2_ref, g3_ref, w_ref, o0_ref, o1_ref, o2_ref, o3_ref, acc_ref, sq_ref):
     rows, width = acc_ref.shape
     inner = g0_ref.shape[1]
     block = rows // 4
-    along, across = at_ref[0], at_ref[1]
+    along, across = at_ref[m], at_ref[1 - m]
     gathered = (g0_ref, g1_ref, g2_ref, g3_ref)
     extra = sum(g[rows : rows + 16, :].astype(F32) for g in gathered)
     square = extra[0:2] + extra[2:4] + extra[4:6]
@@ -292,13 +292,13 @@
         out[block : block + 16, :] = jnp.broadcast_to(line, (16, width)).astype(BF16)
 
 
-def out_blocks(at, gathered, w, after=()):
+def out_blocks(m, at, gathered, w, after=()):
     rows = gathered[0].shape[0] - 16
     width = w.shape[2]
     block = rows // 4
     vm = pl.BlockSpec(memory_space=pltpu.VMEM)
     return pl.pallas_call(
-        drop(out_kernel, 6, len(after)),
+        drop(functools.partial(out_kernel, m), 6, len(after)),
         in_specs=[pl.BlockSpec(memory_space=pltpu.SMEM)] + [vm] * 5 + [ANYWHERE] * len(after),
         out_specs=[vm] * 4,
         out_shape=[jax.ShapeDtypeStruct((block + 16, width), BF16)] * 4,
@@ -334,7 +334,7 @@
             in_specs=[whole] * 4
             + [
                 pl.BlockSpec((block, width), lambda g, at: (0, 0)),
-                pl.BlockSpec((2, width), lambda g, at: (0, at[0])),
+                pl.BlockSpec((2, width), lambda g, at: (0, at[m])),
             ]
             + [ANYWHERE] * len(after),
             out_specs=whole,
@@ -346,12 +346,12 @@
     )(at, *parts, hidden, gain, *after)
 
 
-def join_kernel(at_ref, u0_ref, u1_ref, u2_ref, u3_ref, out_ref):
+def join_kernel(m, at_ref, u0_ref, u1_ref, u2_ref, u3_ref, out_ref):
     block, width = u0_ref.shape[0] - 16, u0_ref.shape[1]
     square = jnp.zeros((1, block), F32)
     half = block // 2
     for k, u in enumerate((u0_ref, u1_ref, u2_ref, u3_ref)):
-        at = pl.multiple_of(lax.rem(at_ref[0] + 4 - k, 4) * width, width)
+        at = pl.multiple_of(lax.rem(at_ref[m] + 4 - k, 4) * width, width)
         for n in range(2):
             out_ref[n * (half + 8) + 8 : (n + 1) * (half + 8), pl.ds(at, width)] = u[n * half : (n + 1) * half, :]
         line = u[block : block + 16, :].astype(F32)[0:1, :]
@@ -365,11 +365,11 @@
         out_ref[n * (half + 8) : n * (half + 8) + 8, 256:] = jnp.zeros((8, out_ref.shape[1] - 256), BF16)
 
 
-def join_columns(at, parts, after=()):
+def join_columns(m, at, parts, after=()):
     tall, width = parts[0].shape
     vm = pl.BlockSpec(memory_space=pltpu.VMEM)
     return pl.pallas_call(
-        drop(join_kernel, 5, len(after)),
+        drop(functools.partial(join_kernel, m), 5, len(after)),
         in_specs=[pl.BlockSpec(memory_space=pltpu.SMEM)] + [vm] * 4 + [ANYWHERE] * len(after),
         out_specs=vm,
         out_shape=jax.ShapeDtypeStruct((tall, 4 * width), BF16),
@@ -430,7 +430,7 @@
         put(m * 8 + 4 + at, to_row(chosen))
 
 
-def near_kernel(place_ref, at0_ref, at1_ref, *refs):
+def near_kernel(place_ref, at_ref, *refs):
     w_ref, tgt_ref, out_ref, acc_ref = refs[6:]
     half = refs[0].shape[0] // 2
     base = place_ref[0] * w_ref.shape[2]
@@ -438,14 +438,14 @@
     def put(row, value):
         out_ref[pl.ds(row, 1), :] = value
 
-    for m, at_ref in enumerate((at0_ref, at1_ref)):
+    for m in range(2):
         tiles = refs[3 * m : 3 * m + 3]
         halves = [x.at[pl.ds(n * half, half), :] for x in tiles for n in range(2)]
-        places = [lax.rem(at_ref[1] + 4 - k, 4) for k in (0, 1, 3)]
+        places = [lax.rem(at_ref[1 - m] + 4 - k, 4) for k in (0, 1, 3)]
         score_rows(m, halves, places, base, w_ref, tgt_ref, acc_ref, put)
 
 
-def far_kernel(place_ref, at0_ref, at1_ref, *refs):
+def far_kernel(place_ref, at_ref, *refs):
     w_ref, tgt_ref, near_ref, out_ref, acc_ref = refs[4:]
     base = place_ref[0] * w_ref.shape[2]
     out_ref[...] = jnp.broadcast_to(near_ref[...][None], out_ref.shape)
@@ -453,8 +453,8 @@
     def put(row, value):
         out_ref[:, pl.ds(row, 1), :] = jnp.broadcast_to(value[None], (out_ref.shape[0], 1, value.shape[1]))
 
-    for m, at_ref in enumerate((at0_ref, at1_ref)):
-        places = [lax.rem(at_ref[1] + 2, 4)]
+    for m in range(2):
+        places = [lax.rem(at_ref[1 - m] + 2, 4)]
         score_rows(m, refs[2 * m : 2 * m + 2], places, base, w_ref, tgt_ref, acc_ref, put)
 
 
@@ -470,22 +470,22 @@
     )
     first = pl.pallas_call(
         near_kernel,
-        in_specs=[sm] * 3 + [vm] * 8,
+        in_specs=[sm] * 2 + [vm] * 8,
         scratch_shapes=[pltpu.VMEM((3 * block, vocab), F32)],
         out_shape=jax.ShapeDtypeStruct((16, block), F32),
         cost_estimate=cost(3),
         name="head_near",
         **common,
-    )(place, *at, *near[0], *near[1], head, tgt)
+    )(place, at, *near[0], *near[1], head, tgt)
     return pl.pallas_call(
         far_kernel,
-        in_specs=[sm] * 3 + [vm] * 7,
+        in_specs=[sm] * 2 + [vm] * 7,
         scratch_shapes=[pltpu.VMEM((block, vocab), F32)],
         out_shape=jax.ShapeDtypeStruct((group, 16, block), F32),
         cost_estimate=cost(1),
         name="head_far",
         **common,
-    )(place, *at, *cut[0], *cut[1], head, tgt, first)
+    )(place, at, *cut[0], *cut[1], head, tgt, first)
 
 
 def cut_kernel(a_ref, b_ref, c_ref, d_ref, oa_ref, ob_ref, oc_ref, od_ref):
@@ -541,36 +541,36 @@
     )(stats, live, seg)
 
 
-def turn_kernel(at_ref, w_ref, hid_ref, out_ref, mine_ref):
-    width = out_ref.shape[2]
-    for j in range(4):
-        out_ref[j] = w_ref[:, j * width : (j + 1) * width]
-    mine_ref[...] = hid_ref[...]
-
-
-def turned(m, at, w_out, hidden):
-    _, inner, depth = w_out.shape
+def turn_kernel(at_ref, w_ref, hid_ref, w0_ref, w1_ref, h0_ref, h1_ref):
+    width = w0_ref.shape[2]
+    for m, (out, mine) in enumerate(((w0_ref, h0_ref), (w1_ref, h1_ref))):
+
+        @pl.when(pl.program_id(0) == m)
+        def _():
+            for j in range(4):
+                out[j] = w_ref[:, j * width : (j + 1) * width]
+            mine[...] = hid_ref[...]
+
+
+def turned(at, w_out, hidden):
+    models, inner, depth = w_out.shape
     width = depth // 4
     block = hidden.shape[1] // 4
     return pl.pallas_call(
         turn_kernel,
         grid_spec=pltpu.PrefetchScalarGridSpec(
             num_scalar_prefetch=1,
-            grid=(1,),
+            grid=(models,),
             in_specs=[
-                pl.BlockSpec((None, inner, depth), lambda j, at: (m, 0, 0)),
-                pl.BlockSpec((None, block, width), lambda j, at: (m, at[1], at[0])),
+                pl.BlockSpec((None, inner, depth), lambda m, at: (m, 0, 0)),
+                pl.BlockSpec((None, block, width), lambda m, at: (m, at[1 - m], at[m])),
             ],
-            out_specs=[
-                pl.BlockSpec((4, inner, width), lambda j, at: (0, 0, 0)),
-                pl.BlockSpec((block, width), lambda j, at: (0, 0)),
-            ],
+            out_specs=[pl.BlockSpec((4, inner, width), lambda m, at: (0, 0, 0))] * 2
+            + [pl.BlockSpec((block, width), lambda m, at: (0, 0))] * 2,
         ),
-        out_shape=[
-            jax.ShapeDtypeStruct((4, inner, width), w_out.dtype),
-            jax.ShapeDtypeStruct((block, width), hidden.dtype),
-        ],
-        cost_estimate=pl.CostEstimate(flops=0, bytes_accessed=6 * 10**6, transcendentals=0),
+        out_shape=[jax.ShapeDtypeStruct((4, inner, width), w_out.dtype)] * 2
+        + [jax.ShapeDtypeStruct((block, width), hidden.dtype)] * 2,
+        cost_estimate=pl.CostEstimate(flops=0, bytes_accessed=10**7, transcendentals=0),
         name="turned",
     )(at, w_out, hidden)
 
@@ -600,23 +600,21 @@
     w_step = jnp.swapaxes(w_step, 1, 2)
     ways = (("x", "z"), ("z", "x"))
     both = range(2)
-    at = [
-        jnp.stack([lax.axis_index(along), lax.axis_index(across)]).astype(jnp.int32) for along, across in ways
-    ]
-    turns = [turned(m, at[m], w_out, hidden) for m in both]
-    weights = [lax.all_to_all(turns[m][0], ways[m][0], 0, 0) for m in both]
+    at = jnp.stack([lax.axis_index("x"), lax.axis_index("z")]).astype(jnp.int32)
+    turns = turned(at, w_out, hidden)
+    weights = [lax.all_to_all(turns[m], ways[m][0], 0, 0) for m in both]
     y, gate, c, e, pay = mix_local(hidden, w_inner, w_state, w_step, step_bias, rate, skip_gain, seg)
     recv = [lax.ppermute(pay, SEQ, [(i, i + k) for i in range(devices - k)]) for k in range(1, REACH + 1)]
     parts, res, full = [], [], []
     gated = gate_out(pages, flags, y, gate, c, e, recv, pool, norm_gain)
     for m in both:
-        out = out_blocks(at[m], gathered(gated[m], ways[m][0]), weights[m])
+        out = out_blocks(m, at, gathered(gated[m], ways[m][0]), weights[m])
         parts.append([out[0]] + [ring(out[k], ways[m][1], k) for k in (1, 2, 3)])
     for m in both:
-        res.append(residual_block(m, at[m], parts[m], turns[m][1], final_gain, inner * group, (parts[1][0],)))
+        res.append(residual_block(m, at, parts[m], turns[2 + m], final_gain, inner * group, (parts[1][0],)))
     blocks = [gathered(res[m], ways[m][0]) for m in both]
     for m in both:
-        full.append(join_columns(at[m], blocks[m], tuple(blocks[1 - m][1:])))
+        full.append(join_columns(m, at, blocks[m], tuple(blocks[1 - m][1:])))
     ready = fetched(head, tuple(full))
     near = [[full[m]] + [ring(full[m], ways[m][1], k) for k in (1, 3)] for m in both]
     halves = cut_halves([near[m][1:] for m in both], (ready,))

time: 168 us -> 165 us (0.982)
  Pallas kernels: 51.7 us -> 48.4 us
    pallas_call x2 -> x1, Pallas kernels: 6.1 us -> 3.92 us  [turned(): pl.pallas_call(turn_kernel, grid_spec=pltpu.PrefetchScalarGridSpec(num_sc...]
    unnamed x36 -> x34, local copies, waits for them, and re-layouts: 8.24 us -> 8.14 us
  transfers between devices with their start and end apart: 36 -> 36, of which waited for: 14 -> 14; matrix products, arithmetic and copies ran while one was open for 3% -> 3% of each run, Pallas kernels for 26% -> 24%
where the time goes in v9:
time: 165 us; the launch traced here: 164 us
  starting transfers between devices  59.1 us (36%)
  Pallas kernels  48.4 us (29%)
  waiting for transfers between devices  35.9 us (22%)
  blocking collectives  9.94 us (6%)
  local copies, waits for them, and re-layouts  8.26 us (5%)
  other arithmetic  1.82 us (1%)
    ppermute x29, waiting for transfers between devices, ring(): return lax.ppermute(value, axis, [(i, (i + by) % 4) for i in range(4)])  34.3 us
    ppermute x29, starting transfers between devices, ring(): return lax.ppermute(value, axis, [(i, (i + by) % 4) for i in range(4)])  30.9 us
    pallas_call x1, Pallas kernels, mix_local(): pl.pallas_call(mix_kernel, grid=(models, chunks), in_specs=[pl.BlockSpec(...  14.9 us
    ppermute x4, starting transfers between devices, per_device(): lax.ppermute(pay, SEQ, [(i, i + k) for i in range(devices - k)])  11.5 us
    all_to_all x1, blocking collectives, per_device(): lax.all_to_all(head_stats(place, at, near, cut, ready, tgt, group), VOC,...  9.94 us
    all_to_all x2, starting transfers between devices, per_device(): weights = [lax.all_to_all(turns[m], ways[m][0], 0, 0) for m in both]  9.88 us
    unnamed x34, local copies, waits for them, and re-layouts  8.14 us
    pallas_call x1, Pallas kernels, head_stats(): pl.pallas_call(near_kernel, in_specs=[sm] * 2 + [vm] * 8, scratch_shapes=...  7.7 us
  transfers between devices with their start and end apart: 36, of which 14 were waited for; matrix products, arithmetic and copies ran while one was open for 3% of the time, Pallas kernels for 24%

profile of v9, /device:TPU:1, one launch (start us, length us, event | category | flops | bytes accessed | tf_op | source)
XLA Modules:
  0.0 164.3 jit_solution(9394853561057355341)
XLA Ops:
  0.6 0.6 pad_add_fusion.at_ref.refs_0_
  1.3 3.9 %turned.1 = (bf16[4,256,512]{2,1,0:T(8,128)(2,1)}, bf16[4,256,512]{2,1,0:T(8,128)(2,1)}, bf16[128,512]{1,0:T(8,128)(2,1)}, bf16[128,512]{1,0:T(8,128)(2,1)}) custom-call(s32[2]{0:T(128)} %pad_add_fusion.at_ref.refs_0_, bf16[2,256,2048]{2,1,0:T(8,128)(2,1)} %w_ref.1, bf16[2,512,2048]{2,1,0:T(8,128)(2,1)} %hid_ref.1), custom_call_target="tpu_custom_call" | custom-call | bytes 10000000 | tf_op jit(solution)/shard_map/turned/pallas_call | solution.py:559
  5.2 5.9 %all-to-all-start.1 = ((bf16[4,256,512]{2,1,0:T(8,128)(2,1)}), bf16[4,256,512]{2,1,0:T(8,128)(2,1)S(1)}, u32[]{:S(2)}, u32[]{:S(2)}) async-start(bf16[4,256,512]{2,1,0:T(8,128)(2,1)} %get-tuple-element.40), calls=%async_computation.1 | async-start | bytes 2097152 | tf_op jit(solution)/shard_map/all_to_all | solution.py:605
  11.0 1.6 copy.27
  12.7 1.3 copy-done.9
  14.0 2.6 %copy.26 = bf16[2,2048,2,256]{3,1,2,0:T(8,128)(2,1)} copy(bf16[2,2048,2,256]{3,2,1,0:T(2,128)(2,1)S(1)} %copy-done.9) | data formatting | bytes 8388608 | tf_op args[1]
  16.6 14.9 %mix_local.1 = (f32[2,512,256]{2,1,0:T(8,128)}, f32[2,512,256]{2,1,0:T(8,128)}, bf16[2,512,128]{2,1,0:T(8,128)(2,1)}, f32[2,512,8]{2,1,0:T(8,128)}, bf16[2,272,128]{2,1,0:T(8,128)(2,1)}) custom-call(bf16[2,512,2048]{2,1,0:T(8,128)(2,1)} %hid_ref.1, bf16[2,2,2048,256]{3,2,1,0:T(8,128)(2,1)} %bitcast.18, bf16[2,2,2048,128]{3,2,1,0:T(8,128)(2,1)} %bitcast.19, ...), custom_call_target="tpu_custom_call" | custom-call | flops 10000000000 | bytes 16000000 | tf_op jit(solution)/shard_map/mix_local/pallas_call | solution.py:172
  31.5 4.8 %collective-permute-start.3 = (bf16[2,272,128]{2,1,0:T(8,128)(2,1)}, bf16[2,272,128]{2,1,0:T(8,128)(2,1)S(1)}, u32[]{:S(2)}, u32[]{:S(2)}) collective-permute-start(bf16[2,272,128]{2,1,0:T(8,128)(2,1)} %get-tuple-element.31), channel_id=1, source_target_pairs={{0,64},{16,80},{32,96},{48,112},{1,65},{17,81},{33,97},{49,113},{2... | collective-permute-start | bytes 417800 | tf_op jit(solution)/shard_map/ppermute | solution.py:607
  36.3 2.1 %collective-permute-start.2 = (bf16[2,272,128]{2,1,0:T(8,128)(2,1)}, bf16[2,272,128]{2,1,0:T(8,128)(2,1)S(1)}, u32[]{:S(2)}, u32[]{:S(2)}) collective-permute-start(bf16[2,272,128]{2,1,0:T(8,128)(2,1)} %get-tuple-element.31), channel_id=1, source_target_pairs={{0,48},{16,64},{32,80},{48,96},{64,112},{1,49},{17,65},{33,81},{49... | collective-permute-start | bytes 417800 | tf_op jit(solution)/shard_map/ppermute | solution.py:607
  38.5 2.3 %collective-permute-start.1 = (bf16[2,272,128]{2,1,0:T(8,128)(2,1)}, bf16[2,272,128]{2,1,0:T(8,128)(2,1)S(1)}, u32[]{:S(2)}, u32[]{:S(2)}) collective-permute-start(bf16[2,272,128]{2,1,0:T(8,128)(2,1)} %get-tuple-element.31), channel_id=1, source_target_pairs={{0,32},{16,48},{32,64},{48,80},{64,96},{80,112},{1,33},{17,49},{33... | collective-permute-start | bytes 417800 | tf_op jit(solution)/shard_map/ppermute | solution.py:607
  40.8 2.2 %collective-permute-start = (bf16[2,272,128]{2,1,0:T(8,128)(2,1)}, bf16[2,272,128]{2,1,0:T(8,128)(2,1)S(1)}, u32[]{:S(2)}, u32[]{:S(2)}) collective-permute-start(bf16[2,272,128]{2,1,0:T(8,128)(2,1)} %get-tuple-element.31), channel_id=1, source_target_pairs={{0,16},{16,32},{32,48},{48,64},{64,80},{80,96},{96,112},{1,17},{17... | collective-permute-start | bytes 417800 | tf_op jit(solution)/shard_map/ppermute | solution.py:607
  43.0 4.0 %all-to-all-start = ((bf16[4,256,512]{2,1,0:T(8,128)(2,1)}), bf16[4,256,512]{2,1,0:T(8,128)(2,1)S(1)}, u32[]{:S(2)}, u32[]{:S(2)}) async-start(bf16[4,256,512]{2,1,0:T(8,128)(2,1)} %get-tuple-element.33), calls=%async_computation | async-start | bytes 2097152 | tf_op jit(solution)/shard_map/all_to_all | solution.py:605
  47.1 0.5 collective-permute-done.r1_ref
  47.8 0.5 copy-done.14
  48.3 5.5 %gate_out.1 = (bf16[528,256]{1,0:T(8,128)(2,1)}, bf16[528,256]{1,0:T(8,128)(2,1)}) custom-call(s32[4]{0:T(128)} %pages_ref.1, s32[4]{0:T(128)} %flags_ref.1, f32[2,512,256]{2,1,0:T(8,128)} %get-tuple-element.27.y_ref, f32[2,512,256]{2,1,0:T(8,128)} %get-tuple-element.28.gate_ref, bf16[2,512,128]{2,1,0:T(8,128)(2,1)} %get-tuple-element.29.c_ref, ...), custom_call_target="tpu_custom_call" | custom-call | flops 2000000000 | bytes 20000000 | tf_op jit(solution)/shard_map/gate_out/pallas_call | solution.py:257
  53.8 2.9 %collective-permute-start.12 = (bf16[528,256]{1,0:T(8,128)(2,1)}, bf16[528,256]{1,0:T(8,128)(2,1)S(1)}, u32[]{:S(2)}, u32[]{:S(2)}) collective-permute-start(bf16[528,256]{1,0:T(8,128)(2,1)} %get-tuple-element.39.refs_1_), channel_id=1, source_target_pairs={{0,3},{1,0},{2,1},{3,2},{4,7},{5,4},{6,5},{7,6},{8,11},{9,8},{10,9... | collective-permute-start | bytes 811016 | tf_op jit(solution)/shard_map/ppermute | solution.py:579
  56.7 0.6 collective-permute-start.11
  57.3 0.6 collective-permute-start.10
  57.8 2.5 %collective-permute-start.6 = (bf16[528,256]{1,0:T(8,128)(2,1)}, bf16[528,256]{1,0:T(8,128)(2,1)S(1)}, u32[]{:S(2)}, u32[]{:S(2)}) collective-permute-start(bf16[528,256]{1,0:T(8,128)(2,1)} %get-tuple-element.32.refs_1_), channel_id=1, source_target_pairs={{0,12},{4,0},{8,4},{12,8},{1,13},{5,1},{9,5},{13,9},{2,14},{6,2},{... | collective-permute-start | bytes 811016 | tf_op jit(solution)/shard_map/ppermute | solution.py:579
  60.3 0.5 collective-permute-start.5
  60.8 7.5 %collective-permute-done.12.refs_4_ = bf16[528,256]{1,0:T(8,128)(2,1)S(1)} collective-permute-done((bf16[528,256]{1,0:T(8,128)(2,1)}, bf16[528,256]{1,0:T(8,128)(2,1)S(1)}, u32[]{:S(2)}, u32[]{:S(2)}) %collective-permute-start.12) | collective-permute-done | bytes 270368 | tf_op jit(solution)/shard_map/ppermute | solution.py:579
  68.4 4.2 %collective-permute-done.10.refs_2_ = bf16[528,256]{1,0:T(8,128)(2,1)S(1)} collective-permute-done((bf16[528,256]{1,0:T(8,128)(2,1)}, bf16[528,256]{1,0:T(8,128)(2,1)S(1)}, u32[]{:S(2)}, u32[]{:S(2)}) %collective-permute-start.10) | collective-permute-done | bytes 270368 | tf_op jit(solution)/shard_map/ppermute | solution.py:579
  72.6 1.0 copy-done.8
  73.6 2.1 %out_blocks.3 = (bf16[144,512]{1,0:T(8,128)(2,1)S(1)}, bf16[144,512]{1,0:T(8,128)(2,1)}, bf16[144,512]{1,0:T(8,128)(2,1)}, bf16[144,512]{1,0:T(8,128)(2,1)S(1)}) custom-call(s32[2]{0:T(128)S(1)} %copy-done.5, bf16[528,256]{1,0:T(8,128)(2,1)S(1)} %copy-done.8, bf16[528,256]{1,0:T(8,128)(2,1)S(1)} %collective-permute-done.10.refs_2_, ...), custom_call_target="tpu_custom_call" | custom-call | flops 1000000000 | bytes 10000000 | tf_op jit(solution)/shard_map/out_blocks/pallas_call | solution.py:300
  75.6 1.2 collective-permute-start.16
  76.8 2.5 %collective-permute-start.17 = (bf16[144,512]{1,0:T(8,128)(2,1)}, bf16[144,512]{1,0:T(8,128)(2,1)S(1)}, u32[]{:S(2)}, u32[]{:S(2)}) collective-permute-start(bf16[144,512]{1,0:T(8,128)(2,1)} %get-tuple-element.43), channel_id=1, source_target_pairs={{0,8},{4,12},{8,0},{12,4},{1,9},{5,13},{9,1},{13,5},{2,10},{6,14},... | collective-permute-start | bytes 442376 | tf_op jit(solution)/shard_map/ppermute | solution.py:579
  79.3 1.2 collective-permute-start.18
  80.5 0.9 copy-done.7
  81.4 1.3 out_blocks.2
  82.8 0.3 collective-permute-start.7
  83.0 0.9 collective-permute-start.8
  83.9 1.7 %collective-permute-start.9 = (bf16[144,512]{1,0:T(8,128)(2,1)S(1)}, bf16[144,512]{1,0:T(8,128)(2,1)S(1)}, u32[]{:S(2)}, u32[]{:S(2)}) collective-permute-start(bf16[144,512]{1,0:T(8,128)(2,1)S(1)} %get-tuple-element.37), channel_id=1, source_target_pairs={{0,3},{1,0},{2,1},{3,2},{4,7},{5,4},{6,5},{7,6},{8,11},{9,8},{10,9... | collective-permute-start | bytes 442376 | tf_op jit(solution)/shard_map/ppermute | solution.py:579
  85.7 0.4 collective-permute-done.17.refs_3_
  86.1 0.9 residual_block.3.refs_1_
  87.0 0.3 collective-permute-start.21
  87.3 1.8 %collective-permute-start.20 = (bf16[144,512]{1,0:T(8,128)(2,1)S(1)}, bf16[144,512]{1,0:T(8,128)(2,1)S(1)}, u32[]{:S(2)}, u32[]{:S(2)}) collective-permute-start(bf16[144,512]{1,0:T(8,128)(2,1)S(1)} %residual_block.3.refs_1_), channel_id=1, source_target_pairs={{0,2},{1,3},{2,0},{3,1},{4,6},{5,7},{6,4},{7,5},{8,10},{9,11},{10,... | collective-permute-start | bytes 442376 | tf_op jit(solution)/shard_map/ppermute | solution.py:579
  89.1 5.2 %collective-permute-done.7.refs_2_ = bf16[144,512]{1,0:T(8,128)(2,1)S(1)} collective-permute-done((bf16[144,512]{1,0:T(8,128)(2,1)S(1)}, bf16[144,512]{1,0:T(8,128)(2,1)S(1)}, u32[]{:S(2)}, u32[]{:S(2)}) %collective-permute-start.7) | collective-permute-done | bytes 147488 | tf_op jit(solution)/shard_map/ppermute | solution.py:579
  94.3 0.9 residual_block.2.refs_1_
  95.2 1.8 %collective-permute-start.14 = (bf16[144,512]{1,0:T(8,128)(2,1)S(1)}, bf16[144,512]{1,0:T(8,128)(2,1)S(1)}, u32[]{:S(2)}, u32[]{:S(2)}) collective-permute-start(bf16[144,512]{1,0:T(8,128)(2,1)S(1)} %residual_block.2.refs_1_), channel_id=1, source_target_pairs={{0,8},{4,12},{8,0},{12,4},{1,9},{5,13},{9,1},{13,5},{2,10},{6,14},... | collective-permute-start | bytes 442376 | tf_op jit(solution)/shard_map/ppermute | solution.py:579
  97.1 2.4 %collective-permute-done.19.refs_5_.refs_2_ = bf16[144,512]{1,0:T(8,128)(2,1)S(1)} collective-permute-done((bf16[144,512]{1,0:T(8,128)(2,1)S(1)}, bf16[144,512]{1,0:T(8,128)(2,1)S(1)}, u32[]{:S(2)}, u32[]{:S(2)}) %collective-permute-start.19) | collective-permute-done | bytes 147488 | tf_op jit(solution)/shard_map/ppermute | solution.py:579
  99.5 1.3 collective-permute-done.14.refs_3_.refs_6_
  100.8 2.5 %collective-permute-done.13.refs_2_.refs_5_ = bf16[144,512]{1,0:T(8,128)(2,1)S(1)} collective-permute-done((bf16[144,512]{1,0:T(8,128)(2,1)S(1)}, bf16[144,512]{1,0:T(8,128)(2,1)S(1)}, u32[]{:S(2)}, u32[]{:S(2)}) %collective-permute-start.13) | collective-permute-done | bytes 147488 | tf_op jit(solution)/shard_map/ppermute | solution.py:579
  103.3 0.6 join_columns.2.refs_1_.refs_0_
  103.9 2.4 %collective-permute-start.23 = (bf16[144,2048]{1,0:T(8,128)(2,1)S(1)}, bf16[144,2048]{1,0:T(8,128)(2,1)S(1)}, u32[]{:S(2)}, u32[]{:S(2)}) collective-permute-start(bf16[144,2048]{1,0:T(8,128)(2,1)S(1)} %join_columns.2.refs_1_.refs_0_), channel_id=1, source_target_pairs={{0,3},{1,0},{2,1},{3,2},{4,7},{5,4},{6,5},{7,6},{8,11},{9,8},{10,9... | collective-permute-start | bytes 1769480 | tf_op jit(solution)/shard_map/ppermute | solution.py:579
  106.3 0.6 join_columns.3.refs_2_.refs_3_
  107.0 1.1 collective-permute-start.25
  108.1 0.4 collective-permute-start.24
  108.5 5.0 %fetched.1.refs_4_.refs_6_ = bf16[2,2048,1664]{2,1,0:T(8,128)(2,1)S(1)} custom-call(bf16[2,2048,1664]{2,1,0:T(8,128)(2,1)} %refs_0_.1, bf16[144,2048]{1,0:T(8,128)(2,1)S(1)} %join_columns.2.refs_1_.refs_0_, bf16[144,2048]{1,0:T(8,128)(2,1)} %copy-done), custom_call_target="tpu_custom_call" | custom-call | bytes 30000000 | tf_op jit(solution)/shard_map/fetched/pallas_call | solution.py:399
  113.5 2.0 %collective-permute-done.23.refs_1_.refs_2_ = bf16[144,2048]{1,0:T(8,128)(2,1)S(1)} collective-permute-done((bf16[144,2048]{1,0:T(8,128)(2,1)S(1)}, bf16[144,2048]{1,0:T(8,128)(2,1)S(1)}, u32[]{:S(2)}, u32[]{:S(2)}) %collective-permute-start.23) | collective-permute-done | bytes 589856 | tf_op jit(solution)/shard_map/ppermute | solution.py:579
  115.5 3.0 %collective-permute-done.22.refs_0_.refs_1_ = bf16[144,2048]{1,0:T(8,128)(2,1)S(1)} collective-permute-done((bf16[144,2048]{1,0:T(8,128)(2,1)S(1)}, bf16[144,2048]{1,0:T(8,128)(2,1)S(1)}, u32[]{:S(2)}, u32[]{:S(2)}) %collective-permute-start.22) | collective-permute-done | bytes 589856 | tf_op jit(solution)/shard_map/ppermute | solution.py:579
  118.4 2.1 %collective-permute-done.24.refs_2_.refs_4_ = bf16[144,2048]{1,0:T(8,128)(2,1)S(1)} collective-permute-done((bf16[144,2048]{1,0:T(8,128)(2,1)S(1)}, bf16[144,2048]{1,0:T(8,128)(2,1)S(1)}, u32[]{:S(2)}, u32[]{:S(2)}) %collective-permute-start.24) | collective-permute-done | bytes 589856 | tf_op jit(solution)/shard_map/ppermute | solution.py:579
  120.7 2.7 %collective-permute-start.27 = (bf16[72,2048]{1,0:T(8,128)(2,1)S(1)}, bf16[72,2048]{1,0:T(8,128)(2,1)S(1)}, u32[]{:S(2)}, u32[]{:S(2)}) collective-permute-start(bf16[72,2048]{1,0:T(8,128)(2,1)S(1)} %get-tuple-element.47), channel_id=1, source_target_pairs={{0,3},{1,0},{2,1},{3,2},{4,7},{5,4},{6,5},{7,6},{8,11},{9,8},{10,9... | collective-permute-start | bytes 884744 | tf_op jit(solution)/shard_map/ppermute | solution.py:579
  123.3 2.7 %collective-permute-start.29 = (bf16[72,2048]{1,0:T(8,128)(2,1)S(1)}, bf16[72,2048]{1,0:T(8,128)(2,1)S(1)}, u32[]{:S(2)}, u32[]{:S(2)}) collective-permute-start(bf16[72,2048]{1,0:T(8,128)(2,1)S(1)} %get-tuple-element.49), channel_id=1, source_target_pairs={{0,12},{4,0},{8,4},{12,8},{1,13},{5,1},{9,5},{13,9},{2,14},{6,2},{... | collective-permute-start | bytes 884744 | tf_op jit(solution)/shard_map/ppermute | solution.py:579
  126.0 7.7 %head_near.1.refs_6_ = f32[16,128]{1,0:T(8,128)S(1)} custom-call(s32[1]{0:T(128)} %bitcast.place_ref, s32[2]{0:T(128)S(1)} %copy-done.5, bf16[144,2048]{1,0:T(8,128)(2,1)S(1)} %join_columns.2.refs_1_.refs_0_, bf16[144,2048]{1,0:T(8,128)(2,1)S(1)} %collective-permute-done.22.refs_0_.refs_1_, bf16[144,2048]{1,0:T(8,128)(2,1)S(1)} %collective-permute-done.23.refs_1_.refs_2_, ...), custom_call_target="tpu_custom_call" | custom-call | flops 5234491392 | bytes 10000000 | tf_op jit(solution)/shard_map/head_near/pallas_call | solution.py:471
  133.8 3.3 %head_far.1 = f32[16,16,128]{2,1,0:T(8,128)S(1)} custom-call(s32[1]{0:T(128)} %bitcast.place_ref, s32[2]{0:T(128)S(1)} %copy-done.5, bf16[72,2048]{1,0:T(8,128)(2,1)S(1)} %collective-permute-done.26.refs_0_, bf16[72,2048]{1,0:T(8,128)(2,1)S(1)} %collective-permute-done.27.refs_1_, bf16[72,2048]{1,0:T(8,128)(2,1)S(1)} %collective-permute-done.28.refs_2_, ...), custom_call_target="tpu_custom_call" | custom-call | flops 1744830464 | bytes 10000000 | tf_op jit(solution)/shard_map/head_far/pallas_call | solution.py:480
  137.1 9.9 %all_to_all.15.stat_ref = f32[16,16,128]{2,1,0:T(8,128)} all-to-all(f32[16,16,128]{2,1,0:T(8,128)S(1)} %head_far.1), channel_id=1, replica_groups=mesh['y'=4,'core'=2,'x'=4,'z'=4] {'x','z'}, dimensions={0} | all-to-all | bytes 262144 | tf_op jit(solution)/shard_map/all_to_all | solution.py:622
  147.0 1.7 %token_diffs.1 = (f32[4,128]{1,0:T(4,128)}, f32[8,128]{1,0:T(8,128)}) custom-call(f32[16,16,128]{2,1,0:T(8,128)} %all_to_all.15.stat_ref, s32[2]{0:T(128)} %live_ref.1, s32[4,128]{1,0:T(4,128)} %bitcast.21), custom_call_target="tpu_custom_call" | custom-call | tf_op jit(solution)/shard_map/token_diffs/pallas_call | solution.py:536
  148.7 6.8 %collective-permute-start.30 = (f32[8,128]{1,0:T(8,128)}, f32[8,128]{1,0:T(8,128)S(1)}, u32[]{:S(2)}, u32[]{:S(2)}) collective-permute-start(f32[8,128]{1,0:T(8,128)} %get-tuple-element.51), channel_id=1, source_target_pairs={{0,16},{16,0},{1,17},{17,1},{2,18},{18,2},{3,19},{19,3},{4,20},{20... | collective-permute-start | bytes 12296 | tf_op jit(solution)/shard_map/ppermute | solution.py:624
  155.5 1.0 collective-permute-done.30
  156.6 0.7 add.20
  157.2 2.8 %collective-permute-start.32 = (f32[8,128]{1,0:T(8,128)S(1)}, f32[8,128]{1,0:T(8,128)S(1)}, u32[]{:S(2)}, u32[]{:S(2)}) collective-permute-start(f32[8,128]{1,0:T(8,128)S(1)} %add.20), channel_id=1, source_target_pairs={{0,64},{32,96},{64,0},{96,32},{1,65},{33,97},{65,1},{97,33},{2,66}... | collective-permute-start | bytes 12296 | tf_op jit(solution)/shard_map/ppermute | solution.py:579
  160.0 1.2 collective-permute-done.32
  161.2 2.5 %collective-permute-done.31 = f32[8,128]{1,0:T(8,128)S(1)} collective-permute-done((f32[8,128]{1,0:T(8,128)S(1)}, f32[8,128]{1,0:T(8,128)S(1)}, u32[]{:S(2)}, u32[]{:S(2)}) %collective-permute-start.31) | collective-permute-done | bytes 4128 | tf_op jit(solution)/shard_map/ppermute | solution.py:579
  163.8 0.5 fusion
  (62 shorter events, 0.6 us)
Async XLA Ops:
  1.3 9.8 %copy-start.10 = (bf16[2,2048,2,128]{3,2,1,0:T(2,128)(2,1)S(1)}, bf16[2,2048,2,128]{3,2,1,0:T(2,128)(2,1)}, u32[]{:S(2)}) copy-start(bf16[2,2048,2,128]{3,2,1,0:T(2,128)(2,1)} %param.20) | copy-start | bytes 6291460
  5.2 37.8 %all-to-all-start.1 = ((bf16[4,256,512]{2,1,0:T(8,128)(2,1)}), bf16[4,256,512]{2,1,0:T(8,128)(2,1)S(1)}, u32[]{:S(2)}, u32[]{:S(2)}) async-start(bf16[4,256,512]{2,1,0:T(8,128)(2,1)} %get-tuple-element.40), calls=%async_computation.1 | async-start | bytes 2097152 | tf_op jit(solution)/shard_map/all_to_all | solution.py:605
  11.0 2.9 %copy-start.9 = (bf16[2,2048,2,256]{3,2,1,0:T(2,128)(2,1)S(1)}, bf16[2,2048,2,256]{3,2,1,0:T(2,128)(2,1)}, u32[]{:S(2)}) copy-start(bf16[2,2048,2,256]{3,2,1,0:T(2,128)(2,1)} %param.19) | copy-start | bytes 12582916
  31.5 15.5 %collective-permute-start.3 = (bf16[2,272,128]{2,1,0:T(8,128)(2,1)}, bf16[2,272,128]{2,1,0:T(8,128)(2,1)S(1)}, u32[]{:S(2)}, u32[]{:S(2)}) collective-permute-start(bf16[2,272,128]{2,1,0:T(8,128)(2,1)} %get-tuple-element.31), channel_id=1, source_target_pairs={{0,64},{16,80},{32,96},{48,112},{1,65},{17,81},{33,97},{49,113},{2... | collective-permute-start | bytes 417800 | tf_op jit(solution)/shard_map/ppermute | solution.py:607
  36.3 10.7 %collective-permute-start.2 = (bf16[2,272,128]{2,1,0:T(8,128)(2,1)}, bf16[2,272,128]{2,1,0:T(8,128)(2,1)S(1)}, u32[]{:S(2)}, u32[]{:S(2)}) collective-permute-start(bf16[2,272,128]{2,1,0:T(8,128)(2,1)} %get-tuple-element.31), channel_id=1, source_target_pairs={{0,48},{16,64},{32,80},{48,96},{64,112},{1,49},{17,65},{33,81},{49... | collective-permute-start | bytes 417800 | tf_op jit(solution)/shard_map/ppermute | solution.py:607
  38.5 8.6 %collective-permute-start.1 = (bf16[2,272,128]{2,1,0:T(8,128)(2,1)}, bf16[2,272,128]{2,1,0:T(8,128)(2,1)S(1)}, u32[]{:S(2)}, u32[]{:S(2)}) collective-permute-start(bf16[2,272,128]{2,1,0:T(8,128)(2,1)} %get-tuple-element.31), channel_id=1, source_target_pairs={{0,32},{16,48},{32,64},{48,80},{64,96},{80,112},{1,33},{17,49},{33... | collective-permute-start | bytes 417800 | tf_op jit(solution)/shard_map/ppermute | solution.py:607
  40.8 6.8 %collective-permute-start = (bf16[2,272,128]{2,1,0:T(8,128)(2,1)}, bf16[2,272,128]{2,1,0:T(8,128)(2,1)S(1)}, u32[]{:S(2)}, u32[]{:S(2)}) collective-permute-start(bf16[2,272,128]{2,1,0:T(8,128)(2,1)} %get-tuple-element.31), channel_id=1, source_target_pairs={{0,16},{16,32},{32,48},{48,64},{64,80},{80,96},{96,112},{1,17},{17... | collective-permute-start | bytes 417800 | tf_op jit(solution)/shard_map/ppermute | solution.py:607
  43.0 37.5 %all-to-all-start = ((bf16[4,256,512]{2,1,0:T(8,128)(2,1)}), bf16[4,256,512]{2,1,0:T(8,128)(2,1)S(1)}, u32[]{:S(2)}, u32[]{:S(2)}) async-start(bf16[4,256,512]{2,1,0:T(8,128)(2,1)} %get-tuple-element.33), calls=%async_computation | async-start | bytes 2097152 | tf_op jit(solution)/shard_map/all_to_all | solution.py:605
  47.0 0.7 copy-start.11
  47.0 0.7 copy-start.12
  47.0 0.7 copy-start.13
  47.6 0.7 copy-start.14
  48.3 24.3 %copy-start.5 = (s32[2]{0:T(128)S(1)}, s32[2]{0:T(128)}, u32[]{:S(2)}) copy-start(s32[2]{0:T(128)} %pad_add_fusion.at_ref.refs_0_) | copy-start | bytes 28
  53.7 32.4 %copy-start.3 = (bf16[128,512]{1,0:T(8,128)(2,1)S(1)}, bf16[128,512]{1,0:T(8,128)(2,1)}, u32[]{:S(2)}) copy-start(bf16[128,512]{1,0:T(8,128)(2,1)} %get-tuple-element.45.refs_5_) | copy-start | bytes 393220
  53.7 32.4 %copy-start.4 = (f32[2,2048]{1,0:T(2,128)S(1)}, f32[2,2048]{1,0:T(2,128)}, u32[]{:S(2)}) copy-start(f32[2,2048]{1,0:T(2,128)} %refs_6_.3) | copy-start | bytes 49156
  53.8 14.6 %collective-permute-start.12 = (bf16[528,256]{1,0:T(8,128)(2,1)}, bf16[528,256]{1,0:T(8,128)(2,1)S(1)}, u32[]{:S(2)}, u32[]{:S(2)}) collective-permute-start(bf16[528,256]{1,0:T(8,128)(2,1)} %get-tuple-element.39.refs_1_), channel_id=1, source_target_pairs={{0,3},{1,0},{2,1},{3,2},{4,7},{5,4},{6,5},{7,6},{8,11},{9,8},{10,9... | collective-permute-start | bytes 811016 | tf_op jit(solution)/shard_map/ppermute | solution.py:579
  56.7 11.7 %collective-permute-start.11 = (bf16[528,256]{1,0:T(8,128)(2,1)}, bf16[528,256]{1,0:T(8,128)(2,1)S(1)}, u32[]{:S(2)}, u32[]{:S(2)}) collective-permute-start(bf16[528,256]{1,0:T(8,128)(2,1)} %get-tuple-element.39.refs_1_), channel_id=1, source_target_pairs={{0,2},{1,3},{2,0},{3,1},{4,6},{5,7},{6,4},{7,5},{8,10},{9,11},{10,... | collective-permute-start | bytes 811016 | tf_op jit(solution)/shard_map/ppermute | solution.py:579
  57.3 15.3 %collective-permute-start.10 = (bf16[528,256]{1,0:T(8,128)(2,1)}, bf16[528,256]{1,0:T(8,128)(2,1)S(1)}, u32[]{:S(2)}, u32[]{:S(2)}) collective-permute-start(bf16[528,256]{1,0:T(8,128)(2,1)} %get-tuple-element.39.refs_1_), channel_id=1, source_target_pairs={{0,1},{1,2},{2,3},{3,0},{4,5},{5,6},{6,7},{7,4},{8,9},{9,10},{10,1... | collective-permute-start | bytes 811016 | tf_op jit(solution)/shard_map/ppermute | solution.py:579
  57.8 36.5 %copy-start.2 = (bf16[128,512]{1,0:T(8,128)(2,1)S(1)}, bf16[128,512]{1,0:T(8,128)(2,1)}, u32[]{:S(2)}) copy-start(bf16[128,512]{1,0:T(8,128)(2,1)} %get-tuple-element.38.refs_5_) | copy-start | bytes 393220
  57.8 21.5 %collective-permute-start.6 = (bf16[528,256]{1,0:T(8,128)(2,1)}, bf16[528,256]{1,0:T(8,128)(2,1)S(1)}, u32[]{:S(2)}, u32[]{:S(2)}) collective-permute-start(bf16[528,256]{1,0:T(8,128)(2,1)} %get-tuple-element.32.refs_1_), channel_id=1, source_target_pairs={{0,12},{4,0},{8,4},{12,8},{1,13},{5,1},{9,5},{13,9},{2,14},{6,2},{... | collective-permute-start | bytes 811016 | tf_op jit(solution)/shard_map/ppermute | solution.py:579
  60.3 20.1 %collective-permute-start.5 = (bf16[528,256]{1,0:T(8,128)(2,1)}, bf16[528,256]{1,0:T(8,128)(2,1)S(1)}, u32[]{:S(2)}, u32[]{:S(2)}) collective-permute-start(bf16[528,256]{1,0:T(8,128)(2,1)} %get-tuple-element.32.refs_1_), channel_id=1, source_target_pairs={{0,8},{4,12},{8,0},{12,4},{1,9},{5,13},{9,1},{13,5},{2,10},{6,14},... | collective-permute-start | bytes 811016 | tf_op jit(solution)/shard_map/ppermute | solution.py:579
  68.4 12.1 %collective-permute-start.4 = (bf16[528,256]{1,0:T(8,128)(2,1)}, bf16[528,256]{1,0:T(8,128)(2,1)S(1)}, u32[]{:S(2)}, u32[]{:S(2)}) collective-permute-start(bf16[528,256]{1,0:T(8,128)(2,1)} %get-tuple-element.32.refs_1_), channel_id=1, source_target_pairs={{0,4},{4,8},{8,12},{12,0},{1,5},{5,9},{9,13},{13,1},{2,6},{6,10},{... | collective-permute-start | bytes 811016 | tf_op jit(solution)/shard_map/ppermute | solution.py:579
  72.6 1.0 copy-start.8
  75.6 8.3 %collective-permute-start.16 = (bf16[144,512]{1,0:T(8,128)(2,1)}, bf16[144,512]{1,0:T(8,128)(2,1)S(1)}, u32[]{:S(2)}, u32[]{:S(2)}) collective-permute-start(bf16[144,512]{1,0:T(8,128)(2,1)} %get-tuple-element.42), channel_id=1, source_target_pairs={{0,4},{4,8},{8,12},{12,0},{1,5},{5,9},{9,13},{13,1},{2,6},{6,10},{... | collective-permute-start | bytes 442376 | tf_op jit(solution)/shard_map/ppermute | solution.py:579
  76.8 9.3 %collective-permute-start.17 = (bf16[144,512]{1,0:T(8,128)(2,1)}, bf16[144,512]{1,0:T(8,128)(2,1)S(1)}, u32[]{:S(2)}, u32[]{:S(2)}) collective-permute-start(bf16[144,512]{1,0:T(8,128)(2,1)} %get-tuple-element.43), channel_id=1, source_target_pairs={{0,8},{4,12},{8,0},{12,4},{1,9},{5,13},{9,1},{13,5},{2,10},{6,14},... | collective-permute-start | bytes 442376 | tf_op jit(solution)/shard_map/ppermute | solution.py:579
  79.3 6.8 %collective-permute-start.18 = (bf16[144,512]{1,0:T(8,128)(2,1)S(1)}, bf16[144,512]{1,0:T(8,128)(2,1)S(1)}, u32[]{:S(2)}, u32[]{:S(2)}) collective-permute-start(bf16[144,512]{1,0:T(8,128)(2,1)S(1)} %get-tuple-element.44), channel_id=1, source_target_pairs={{0,12},{4,0},{8,4},{12,8},{1,13},{5,1},{9,5},{13,9},{2,14},{6,2},{... | collective-permute-start | bytes 442376 | tf_op jit(solution)/shard_map/ppermute | solution.py:579
  80.5 1.0 copy-start.7
  82.8 11.5 %collective-permute-start.7 = (bf16[144,512]{1,0:T(8,128)(2,1)S(1)}, bf16[144,512]{1,0:T(8,128)(2,1)S(1)}, u32[]{:S(2)}, u32[]{:S(2)}) collective-permute-start(bf16[144,512]{1,0:T(8,128)(2,1)S(1)} %get-tuple-element.35), channel_id=1, source_target_pairs={{0,1},{1,2},{2,3},{3,0},{4,5},{5,6},{6,7},{7,4},{8,9},{9,10},{10,1... | collective-permute-start | bytes 442376 | tf_op jit(solution)/shard_map/ppermute | solution.py:579
  83.0 11.3 %collective-permute-start.8 = (bf16[144,512]{1,0:T(8,128)(2,1)S(1)}, bf16[144,512]{1,0:T(8,128)(2,1)S(1)}, u32[]{:S(2)}, u32[]{:S(2)}) collective-permute-start(bf16[144,512]{1,0:T(8,128)(2,1)S(1)} %get-tuple-element.36), channel_id=1, source_target_pairs={{0,2},{1,3},{2,0},{3,1},{4,6},{5,7},{6,4},{7,5},{8,10},{9,11},{10,... | collective-permute-start | bytes 442376 | tf_op jit(solution)/shard_map/ppermute | solution.py:579
  83.9 10.3 %collective-permute-start.9 = (bf16[144,512]{1,0:T(8,128)(2,1)S(1)}, bf16[144,512]{1,0:T(8,128)(2,1)S(1)}, u32[]{:S(2)}, u32[]{:S(2)}) collective-permute-start(bf16[144,512]{1,0:T(8,128)(2,1)S(1)} %get-tuple-element.37), channel_id=1, source_target_pairs={{0,3},{1,0},{2,1},{3,2},{4,7},{5,4},{6,5},{7,6},{8,11},{9,8},{10,9... | collective-permute-start | bytes 442376 | tf_op jit(solution)/shard_map/ppermute | solution.py:579
  87.0 10.0 %collective-permute-start.21 = (bf16[144,512]{1,0:T(8,128)(2,1)S(1)}, bf16[144,512]{1,0:T(8,128)(2,1)S(1)}, u32[]{:S(2)}, u32[]{:S(2)}) collective-permute-start(bf16[144,512]{1,0:T(8,128)(2,1)S(1)} %residual_block.3.refs_1_), channel_id=1, source_target_pairs={{0,3},{1,0},{2,1},{3,2},{4,7},{5,4},{6,5},{7,6},{8,11},{9,8},{10,9... | collective-permute-start | bytes 442376 | tf_op jit(solution)/shard_map/ppermute | solution.py:579
  87.3 9.8 %collective-permute-start.20 = (bf16[144,512]{1,0:T(8,128)(2,1)S(1)}, bf16[144,512]{1,0:T(8,128)(2,1)S(1)}, u32[]{:S(2)}, u32[]{:S(2)}) collective-permute-start(bf16[144,512]{1,0:T(8,128)(2,1)S(1)} %residual_block.3.refs_1_), channel_id=1, source_target_pairs={{0,2},{1,3},{2,0},{3,1},{4,6},{5,7},{6,4},{7,5},{8,10},{9,11},{10,... | collective-permute-start | bytes 442376 | tf_op jit(solution)/shard_map/ppermute | solution.py:579
  94.3 5.2 %collective-permute-start.19 = (bf16[144,512]{1,0:T(8,128)(2,1)S(1)}, bf16[144,512]{1,0:T(8,128)(2,1)S(1)}, u32[]{:S(2)}, u32[]{:S(2)}) collective-permute-start(bf16[144,512]{1,0:T(8,128)(2,1)S(1)} %residual_block.3.refs_1_), channel_id=1, source_target_pairs={{0,1},{1,2},{2,3},{3,0},{4,5},{5,6},{6,7},{7,4},{8,9},{9,10},{10,1... | collective-permute-start | bytes 442376 | tf_op jit(solution)/shard_map/ppermute | solution.py:579
  95.2 4.3 %collective-permute-start.15 = (bf16[144,512]{1,0:T(8,128)(2,1)S(1)}, bf16[144,512]{1,0:T(8,128)(2,1)S(1)}, u32[]{:S(2)}, u32[]{:S(2)}) collective-permute-start(bf16[144,512]{1,0:T(8,128)(2,1)S(1)} %residual_block.2.refs_1_), channel_id=1, source_target_pairs={{0,12},{4,0},{8,4},{12,8},{1,13},{5,1},{9,5},{13,9},{2,14},{6,2},{... | collective-permute-start | bytes 442376 | tf_op jit(solution)/shard_map/ppermute | solution.py:579
  95.2 5.6 %collective-permute-start.14 = (bf16[144,512]{1,0:T(8,128)(2,1)S(1)}, bf16[144,512]{1,0:T(8,128)(2,1)S(1)}, u32[]{:S(2)}, u32[]{:S(2)}) collective-permute-start(bf16[144,512]{1,0:T(8,128)(2,1)S(1)} %residual_block.2.refs_1_), channel_id=1, source_target_pairs={{0,8},{4,12},{8,0},{12,4},{1,9},{5,13},{9,1},{13,5},{2,10},{6,14},... | collective-permute-start | bytes 442376 | tf_op jit(solution)/shard_map/ppermute | solution.py:579
  97.0 6.3 %collective-permute-start.13 = (bf16[144,512]{1,0:T(8,128)(2,1)S(1)}, bf16[144,512]{1,0:T(8,128)(2,1)S(1)}, u32[]{:S(2)}, u32[]{:S(2)}) collective-permute-start(bf16[144,512]{1,0:T(8,128)(2,1)S(1)} %residual_block.2.refs_1_), channel_id=1, source_target_pairs={{0,4},{4,8},{8,12},{12,0},{1,5},{5,9},{9,13},{13,1},{2,6},{6,10},{... | collective-permute-start | bytes 442376 | tf_op jit(solution)/shard_map/ppermute | solution.py:579
  103.9 11.5 %collective-permute-start.23 = (bf16[144,2048]{1,0:T(8,128)(2,1)S(1)}, bf16[144,2048]{1,0:T(8,128)(2,1)S(1)}, u32[]{:S(2)}, u32[]{:S(2)}) collective-permute-start(bf16[144,2048]{1,0:T(8,128)(2,1)S(1)} %join_columns.2.refs_1_.refs_0_), channel_id=1, source_target_pairs={{0,3},{1,0},{2,1},{3,2},{4,7},{5,4},{6,5},{7,6},{8,11},{9,8},{10,9... | collective-permute-start | bytes 1769480 | tf_op jit(solution)/shard_map/ppermute | solution.py:579
  106.3 12.1 %collective-permute-start.22 = (bf16[144,2048]{1,0:T(8,128)(2,1)S(1)}, bf16[144,2048]{1,0:T(8,128)(2,1)S(1)}, u32[]{:S(2)}, u32[]{:S(2)}) collective-permute-start(bf16[144,2048]{1,0:T(8,128)(2,1)S(1)} %join_columns.2.refs_1_.refs_0_), channel_id=1, source_target_pairs={{0,1},{1,2},{2,3},{3,0},{4,5},{5,6},{6,7},{7,4},{8,9},{9,10},{10,1... | collective-permute-start | bytes 1769480 | tf_op jit(solution)/shard_map/ppermute | solution.py:579
  107.0 1.5 copy-start
  107.0 11.5 %collective-permute-start.25 = (bf16[144,2048]{1,0:T(8,128)(2,1)S(1)}, bf16[144,2048]{1,0:T(8,128)(2,1)S(1)}, u32[]{:S(2)}, u32[]{:S(2)}) collective-permute-start(bf16[144,2048]{1,0:T(8,128)(2,1)S(1)} %join_columns.3.refs_2_.refs_3_), channel_id=1, source_target_pairs={{0,12},{4,0},{8,4},{12,8},{1,13},{5,1},{9,5},{13,9},{2,14},{6,2},{... | collective-permute-start | bytes 1769480 | tf_op jit(solution)/shard_map/ppermute | solution.py:579
  108.1 12.4 %collective-permute-start.24 = (bf16[144,2048]{1,0:T(8,128)(2,1)S(1)}, bf16[144,2048]{1,0:T(8,128)(2,1)S(1)}, u32[]{:S(2)}, u32[]{:S(2)}) collective-permute-start(bf16[144,2048]{1,0:T(8,128)(2,1)S(1)} %join_columns.3.refs_2_.refs_3_), channel_id=1, source_target_pairs={{0,4},{4,8},{8,12},{12,0},{1,5},{5,9},{9,13},{13,1},{2,6},{6,10},{... | collective-permute-start | bytes 1769480 | tf_op jit(solution)/shard_map/ppermute | solution.py:579
  113.5 12.5 %copy-start.1 = (bf16[144,2048]{1,0:T(8,128)(2,1)S(1)}, bf16[144,2048]{1,0:T(8,128)(2,1)}, u32[]{:S(2)}) copy-start(bf16[144,2048]{1,0:T(8,128)(2,1)} %copy-done) | copy-start | bytes 1769476
  113.5 12.5 %copy-start.6 = (s32[512]{0:T(512)S(1)}, s32[512]{0:T(512)}, u32[]{:S(2)}) copy-start(s32[512]{0:T(512)} %param.30) | copy-start | bytes 6148
  120.6 13.1 %collective-permute-start.26 = (bf16[72,2048]{1,0:T(8,128)(2,1)S(1)}, bf16[72,2048]{1,0:T(8,128)(2,1)S(1)}, u32[]{:S(2)}, u32[]{:S(2)}) collective-permute-start(bf16[72,2048]{1,0:T(8,128)(2,1)S(1)} %get-tuple-element.46), channel_id=1, source_target_pairs={{0,1},{1,2},{2,3},{3,0},{4,5},{5,6},{6,7},{7,4},{8,9},{9,10},{10,1... | collective-permute-start | bytes 884744 | tf_op jit(solution)/shard_map/ppermute | solution.py:579
  120.7 13.1 %collective-permute-start.27 = (bf16[72,2048]{1,0:T(8,128)(2,1)S(1)}, bf16[72,2048]{1,0:T(8,128)(2,1)S(1)}, u32[]{:S(2)}, u32[]{:S(2)}) collective-permute-start(bf16[72,2048]{1,0:T(8,128)(2,1)S(1)} %get-tuple-element.47), channel_id=1, source_target_pairs={{0,3},{1,0},{2,1},{3,2},{4,7},{5,4},{6,5},{7,6},{8,11},{9,8},{10,9... | collective-permute-start | bytes 884744 | tf_op jit(solution)/shard_map/ppermute | solution.py:579
  123.3 10.4 %collective-permute-start.28 = (bf16[72,2048]{1,0:T(8,128)(2,1)S(1)}, bf16[72,2048]{1,0:T(8,128)(2,1)S(1)}, u32[]{:S(2)}, u32[]{:S(2)}) collective-permute-start(bf16[72,2048]{1,0:T(8,128)(2,1)S(1)} %get-tuple-element.48), channel_id=1, source_target_pairs={{0,4},{4,8},{8,12},{12,0},{1,5},{5,9},{9,13},{13,1},{2,6},{6,10},{... | collective-permute-start | bytes 884744 | tf_op jit(solution)/shard_map/ppermute | solution.py:579
  123.3 10.4 %collective-permute-start.29 = (bf16[72,2048]{1,0:T(8,128)(2,1)S(1)}, bf16[72,2048]{1,0:T(8,128)(2,1)S(1)}, u32[]{:S(2)}, u32[]{:S(2)}) collective-permute-start(bf16[72,2048]{1,0:T(8,128)(2,1)S(1)} %get-tuple-element.49), channel_id=1, source_target_pairs={{0,12},{4,0},{8,4},{12,8},{1,13},{5,1},{9,5},{13,9},{2,14},{6,2},{... | collective-permute-start | bytes 884744 | tf_op jit(solution)/shard_map/ppermute | solution.py:579
  133.7 30.1 %copy-start.15 = (s32[4]{0:T(128)S(1)}, s32[4]{0:T(128)}, u32[]{:S(2)}) copy-start(s32[4]{0:T(128)} %param.35) | copy-start | bytes 52
  148.7 7.9 %collective-permute-start.30 = (f32[8,128]{1,0:T(8,128)}, f32[8,128]{1,0:T(8,128)S(1)}, u32[]{:S(2)}, u32[]{:S(2)}) collective-permute-start(f32[8,128]{1,0:T(8,128)} %get-tuple-element.51), channel_id=1, source_target_pairs={{0,16},{16,0},{1,17},{17,1},{2,18},{18,2},{3,19},{19,3},{4,20},{20... | collective-permute-start | bytes 12296 | tf_op jit(solution)/shard_map/ppermute | solution.py:624
  157.2 2.8 %collective-permute-start.33 = (f32[8,128]{1,0:T(8,128)S(1)}, f32[8,128]{1,0:T(8,128)S(1)}, u32[]{:S(2)}, u32[]{:S(2)}) collective-permute-start(f32[8,128]{1,0:T(8,128)S(1)} %add.20), channel_id=1, source_target_pairs={{0,96},{32,0},{64,32},{96,64},{1,97},{33,1},{65,33},{97,65},{2,98}... | collective-permute-start | bytes 12296 | tf_op jit(solution)/shard_map/ppermute | solution.py:579
  157.2 4.0 %collective-permute-start.32 = (f32[8,128]{1,0:T(8,128)S(1)}, f32[8,128]{1,0:T(8,128)S(1)}, u32[]{:S(2)}, u32[]{:S(2)}) collective-permute-start(f32[8,128]{1,0:T(8,128)S(1)} %add.20), channel_id=1, source_target_pairs={{0,64},{32,96},{64,0},{96,32},{1,65},{33,97},{65,1},{97,33},{2,66}... | collective-permute-start | bytes 12296 | tf_op jit(solution)/shard_map/ppermute | solution.py:579
  160.0 3.7 %collective-permute-start.31 = (f32[8,128]{1,0:T(8,128)S(1)}, f32[8,128]{1,0:T(8,128)S(1)}, u32[]{:S(2)}, u32[]{:S(2)}) collective-permute-start(f32[8,128]{1,0:T(8,128)S(1)} %add.20), channel_id=1, source_target_pairs={{0,32},{32,64},{64,96},{96,0},{1,33},{33,65},{65,97},{97,1},{2,34}... | collective-permute-start | bytes 12296 | tf_op jit(solution)/shard_map/ppermute | solution.py:579

commit v10 on v9

--- a/solution.py
+++ b/solution.py
@@ -113,7 +113,8 @@
     grow = jnp.exp(run - base)
     keep = jnp.where(seg == last, jnp.exp(jnp.minimum(total - run, 0.0)) * dt, 0.0)
     tail = jnp.exp(jnp.sum(jnp.where(seg == last, la, 0.0), axis=1, keepdims=True))
-    cols = jnp.transpose(jnp.concatenate([run, keep], axis=0))
+    run = run * LOG2E
+    cols = jnp.transpose(jnp.concatenate([run, keep, dt, dt], axis=0))
     segf = jnp.broadcast_to(seg.astype(F32), (heads, rows))
     ecol = jnp.transpose(jnp.concatenate([grow, segf], axis=0))
     e_ref[...] = ecol
@@ -138,6 +139,9 @@
         axis=0,
     )
     pay_ref[inner : inner + 16, :] = meta.astype(BF16)
+    timed = jnp.concatenate(
+        [vf[:, h * wide : (h + 1) * wide] * cols[:, 2 * heads + h : 2 * heads + h + 1] for h in range(heads)], axis=1
+    ).astype(BF16)
     blocks = rows // SPAN
     for i in range(blocks):
         t0 = i * SPAN
@@ -153,9 +157,9 @@
                 )
             for h in range(heads):
                 gap = cols[t0 : t0 + SPAN, h : h + 1] - run[h : h + 1, s0 : s0 + SPAN]
-                weight = jnp.exp(jnp.where(same, gap, LOW)) * (scores * dt[h : h + 1, s0 : s0 + SPAN])
+                weight = jnp.exp2(jnp.where(same, gap, LOW)) * scores
                 acc[h] = acc[h] + contract(
-                    weight.astype(BF16), values[s0 : s0 + SPAN, h * wide : (h + 1) * wide], ((1,), (0,))
+                    weight.astype(BF16), timed[s0 : s0 + SPAN, h * wide : (h + 1) * wide], ((1,), (0,))
                 )
         y_ref[t0 : t0 + SPAN, :] = jnp.concatenate(acc, axis=1)
 
@@ -430,18 +434,32 @@
         put(m * 8 + 4 + at, to_row(chosen))
 
 
+def own_kernel(place_ref, at_ref, x0_ref, x1_ref, w_ref, tgt_ref, out_ref, acc_ref):
+    half = x0_ref.shape[0] // 2
+    base = place_ref[0] * w_ref.shape[2]
+    out_ref[...] = jnp.zeros_like(out_ref)
+
+    def put(row, value):
+        out_ref[pl.ds(row, 1), :] = value
+
+    for m, x in enumerate((x0_ref, x1_ref)):
+        halves = [x.at[pl.ds(n * half, half), :] for n in range(2)]
+        score_rows(m, halves, [at_ref[1 - m]], base, w_ref, tgt_ref, acc_ref, put)
+
+
 def near_kernel(place_ref, at_ref, *refs):
-    w_ref, tgt_ref, out_ref, acc_ref = refs[6:]
+    w_ref, tgt_ref, own_ref, out_ref, acc_ref = refs[4:]
     half = refs[0].shape[0] // 2
     base = place_ref[0] * w_ref.shape[2]
+    out_ref[...] = own_ref[...]
 
     def put(row, value):
         out_ref[pl.ds(row, 1), :] = value
 
     for m in range(2):
-        tiles = refs[3 * m : 3 * m + 3]
+        tiles = refs[2 * m : 2 * m + 2]
         halves = [x.at[pl.ds(n * half, half), :] for x in tiles for n in range(2)]
-        places = [lax.rem(at_ref[1 - m] + 4 - k, 4) for k in (0, 1, 3)]
+        places = [lax.rem(at_ref[1 - m] + 4 - k, 4) for k in (1, 3)]
         score_rows(m, halves, places, base, w_ref, tgt_ref, acc_ref, put)
 
 
@@ -468,15 +486,24 @@
     cost = lambda blocks: pl.CostEstimate(
         flops=4 * blocks * block * depth * vocab, bytes_accessed=10**7, transcendentals=2 * blocks * block * vocab
     )
+    own = pl.pallas_call(
+        own_kernel,
+        in_specs=[sm] * 2 + [vm] * 4,
+        scratch_shapes=[pltpu.VMEM((block, vocab), F32)],
+        out_shape=jax.ShapeDtypeStruct((16, block), F32),
+        cost_estimate=cost(1),
+        name="head_own",
+        **common,
+    )(place, at, near[0][0], near[1][0], head, tgt)
     first = pl.pallas_call(
         near_kernel,
-        in_specs=[sm] * 2 + [vm] * 8,
-        scratch_shapes=[pltpu.VMEM((3 * block, vocab), F32)],
+        in_specs=[sm] * 2 + [vm] * 7,
+        scratch_shapes=[pltpu.VMEM((2 * block, vocab), F32)],
         out_shape=jax.ShapeDtypeStruct((16, block), F32),
-        cost_estimate=cost(3),
+        cost_estimate=cost(2),
         name="head_near",
         **common,
-    )(place, at, *near[0], *near[1], head, tgt)
+    )(place, at, *near[0][1:], *near[1][1:], head, tgt, own)
     return pl.pallas_call(
         far_kernel,
         in_specs=[sm] * 2 + [vm] * 7,

time: 165 us -> 165 us (level)
  waiting for transfers between devices: 35.9 us -> 27 us
  starting transfers between devices: 59.1 us -> 63.7 us
  Pallas kernels: 48.4 us -> 50.3 us
    ppermute x29, waiting for transfers between devices: 34.3 us -> 25.4 us  [ring(): return lax.ppermute(value, axis, [(i, (i + by) % 4) for i in range(4)])]
    ppermute x29, starting transfers between devices: 30.9 us -> 35.8 us  [ring(): return lax.ppermute(value, axis, [(i, (i + by) % 4) for i in range(4)])]
    pallas_call x1 -> x2, Pallas kernels: 7.7 us -> 8.54 us  [the longest x1 5.23 us: head_stats(): pl.pallas_call(near_kernel, in_specs=[sm] * 2 + [vm] * 7, scratch_shapes=...]
  transfers between devices with their start and end apart: 36 -> 36, of which waited for: 14 -> 16; matrix products, arithmetic and copies ran while one was open for 3% -> 3% of each run, Pallas kernels for 24% -> 25%
where the time goes in v10:
time: 165 us; the launch traced here: 164 us
  starting transfers between devices  63.7 us (39%)
  Pallas kernels  50.3 us (30%)
  waiting for transfers between devices  27 us (16%)
  blocking collectives  10.7 us (6%)
  local copies, waits for them, and re-layouts  9.31 us (6%)
  other arithmetic  1.82 us (1%)
    ppermute x29, starting transfers between devices, ring(): return lax.ppermute(value, axis, [(i, (i + by) % 4) for i in range(4)])  35.8 us
    ppermute x29, waiting for transfers between devices, ring(): return lax.ppermute(value, axis, [(i, (i + by) % 4) for i in range(4)])  25.4 us
    pallas_call x1, Pallas kernels, mix_local(): pl.pallas_call(mix_kernel, grid=(models, chunks), in_specs=[pl.BlockSpec(...  15.2 us
    ppermute x4, starting transfers between devices, per_device(): lax.ppermute(pay, SEQ, [(i, i + k) for i in range(devices - k)])  11.5 us
    all_to_all x1, blocking collectives, per_device(): lax.all_to_all(head_stats(place, at, near, cut, ready, tgt, group), VOC,...  10.7 us
    all_to_all x2, starting transfers between devices, per_device(): weights = [lax.all_to_all(turns[m], ways[m][0], 0, 0) for m in both]  9.88 us
    unnamed x34, local copies, waits for them, and re-layouts  9.19 us
    ppermute x1, starting transfers between devices, per_device(): sums = sums + lax.ppermute(sums, 'core', [(0, 1), (1, 0)])  6.61 us
  transfers between devices with their start and end apart: 36, of which 16 were waited for; matrix products, arithmetic and copies ran while one was open for 3% of the time, Pallas kernels for 25%

profile of v10, /device:TPU:1, one launch (start us, length us, event | category | flops | bytes accessed | tf_op | source)
XLA Modules:
  0.0 163.8 jit_solution(109021397794171979)
XLA Ops:
  0.6 0.6 pad_add_fusion.at_ref.refs_0_
  1.3 3.9 %turned.1 = (bf16[4,256,512]{2,1,0:T(8,128)(2,1)}, bf16[4,256,512]{2,1,0:T(8,128)(2,1)}, bf16[128,512]{1,0:T(8,128)(2,1)}, bf16[128,512]{1,0:T(8,128)(2,1)}) custom-call(s32[2]{0:T(128)} %pad_add_fusion.at_ref.refs_0_, bf16[2,256,2048]{2,1,0:T(8,128)(2,1)} %w_ref.1, bf16[2,512,2048]{2,1,0:T(8,128)(2,1)} %hid_ref.1), custom_call_target="tpu_custom_call" | custom-call | bytes 10000000 | tf_op jit(solution)/shard_map/turned/pallas_call | solution.py:586
  5.2 5.9 %all-to-all-start.1 = ((bf16[4,256,512]{2,1,0:T(8,128)(2,1)}), bf16[4,256,512]{2,1,0:T(8,128)(2,1)S(1)}, u32[]{:S(2)}, u32[]{:S(2)}) async-start(bf16[4,256,512]{2,1,0:T(8,128)(2,1)} %get-tuple-element.40), calls=%async_computation.1 | async-start | bytes 2097152 | tf_op jit(solution)/shard_map/all_to_all | solution.py:632
  11.0 1.6 copy.27
  12.7 1.3 copy-done.9
  14.0 2.6 %copy.26 = bf16[2,2048,2,256]{3,1,2,0:T(8,128)(2,1)} copy(bf16[2,2048,2,256]{3,2,1,0:T(2,128)(2,1)S(1)} %copy-done.9) | data formatting | bytes 8388608 | tf_op args[1]
  16.6 15.2 %mix_local.1 = (f32[2,512,256]{2,1,0:T(8,128)}, f32[2,512,256]{2,1,0:T(8,128)}, bf16[2,512,128]{2,1,0:T(8,128)(2,1)}, f32[2,512,8]{2,1,0:T(8,128)}, bf16[2,272,128]{2,1,0:T(8,128)(2,1)}) custom-call(bf16[2,512,2048]{2,1,0:T(8,128)(2,1)} %hid_ref.1, bf16[2,2,2048,256]{3,2,1,0:T(8,128)(2,1)} %bitcast.19, bf16[2,2,2048,128]{3,2,1,0:T(8,128)(2,1)} %bitcast.20, ...), custom_call_target="tpu_custom_call" | custom-call | flops 10000000000 | bytes 16000000 | tf_op jit(solution)/shard_map/mix_local/pallas_call | solution.py:176
  31.7 4.8 %collective-permute-start.3 = (bf16[2,272,128]{2,1,0:T(8,128)(2,1)}, bf16[2,272,128]{2,1,0:T(8,128)(2,1)S(1)}, u32[]{:S(2)}, u32[]{:S(2)}) collective-permute-start(bf16[2,272,128]{2,1,0:T(8,128)(2,1)} %get-tuple-element.31), channel_id=1, source_target_pairs={{0,64},{16,80},{32,96},{48,112},{1,65},{17,81},{33,97},{49,113},{2... | collective-permute-start | bytes 417800 | tf_op jit(solution)/shard_map/ppermute | solution.py:634
  36.6 2.1 %collective-permute-start.2 = (bf16[2,272,128]{2,1,0:T(8,128)(2,1)}, bf16[2,272,128]{2,1,0:T(8,128)(2,1)S(1)}, u32[]{:S(2)}, u32[]{:S(2)}) collective-permute-start(bf16[2,272,128]{2,1,0:T(8,128)(2,1)} %get-tuple-element.31), channel_id=1, source_target_pairs={{0,48},{16,64},{32,80},{48,96},{64,112},{1,49},{17,65},{33,81},{49... | collective-permute-start | bytes 417800 | tf_op jit(solution)/shard_map/ppermute | solution.py:634
  38.7 2.3 %collective-permute-start.1 = (bf16[2,272,128]{2,1,0:T(8,128)(2,1)}, bf16[2,272,128]{2,1,0:T(8,128)(2,1)S(1)}, u32[]{:S(2)}, u32[]{:S(2)}) collective-permute-start(bf16[2,272,128]{2,1,0:T(8,128)(2,1)} %get-tuple-element.31), channel_id=1, source_target_pairs={{0,32},{16,48},{32,64},{48,80},{64,96},{80,112},{1,33},{17,49},{33... | collective-permute-start | bytes 417800 | tf_op jit(solution)/shard_map/ppermute | solution.py:634
  41.0 2.2 %collective-permute-start = (bf16[2,272,128]{2,1,0:T(8,128)(2,1)}, bf16[2,272,128]{2,1,0:T(8,128)(2,1)S(1)}, u32[]{:S(2)}, u32[]{:S(2)}) collective-permute-start(bf16[2,272,128]{2,1,0:T(8,128)(2,1)} %get-tuple-element.31), channel_id=1, source_target_pairs={{0,16},{16,32},{32,48},{48,64},{64,80},{80,96},{96,112},{1,17},{17... | collective-permute-start | bytes 417800 | tf_op jit(solution)/shard_map/ppermute | solution.py:634
  43.2 4.0 %all-to-all-start = ((bf16[4,256,512]{2,1,0:T(8,128)(2,1)}), bf16[4,256,512]{2,1,0:T(8,128)(2,1)S(1)}, u32[]{:S(2)}, u32[]{:S(2)}) async-start(bf16[4,256,512]{2,1,0:T(8,128)(2,1)} %get-tuple-element.33), calls=%async_computation | async-start | bytes 2097152 | tf_op jit(solution)/shard_map/all_to_all | solution.py:632
  47.3 0.5 collective-permute-done.r1_ref
  48.0 0.5 copy-done.14
  48.5 6.3 %gate_out.1 = (bf16[528,256]{1,0:T(8,128)(2,1)}, bf16[528,256]{1,0:T(8,128)(2,1)}) custom-call(s32[4]{0:T(128)} %pages_ref.1, s32[4]{0:T(128)} %flags_ref.1, f32[2,512,256]{2,1,0:T(8,128)} %get-tuple-element.27.y_ref, f32[2,512,256]{2,1,0:T(8,128)} %get-tuple-element.28.gate_ref, bf16[2,512,128]{2,1,0:T(8,128)(2,1)} %get-tuple-element.29.c_ref, ...), custom_call_target="tpu_custom_call" | custom-call | flops 2000000000 | bytes 20000000 | tf_op jit(solution)/shard_map/gate_out/pallas_call | solution.py:261
  54.8 2.9 %collective-permute-start.12 = (bf16[528,256]{1,0:T(8,128)(2,1)}, bf16[528,256]{1,0:T(8,128)(2,1)S(1)}, u32[]{:S(2)}, u32[]{:S(2)}) collective-permute-start(bf16[528,256]{1,0:T(8,128)(2,1)} %get-tuple-element.39.refs_1_), channel_id=1, source_target_pairs={{0,3},{1,0},{2,1},{3,2},{4,7},{5,4},{6,5},{7,6},{8,11},{9,8},{10,9... | collective-permute-start | bytes 811016 | tf_op jit(solution)/shard_map/ppermute | solution.py:606
  57.7 0.6 collective-permute-start.11
  58.3 0.6 collective-permute-start.10
  58.9 2.5 %collective-permute-start.6 = (bf16[528,256]{1,0:T(8,128)(2,1)}, bf16[528,256]{1,0:T(8,128)(2,1)S(1)}, u32[]{:S(2)}, u32[]{:S(2)}) collective-permute-start(bf16[528,256]{1,0:T(8,128)(2,1)} %get-tuple-element.32.refs_1_), channel_id=1, source_target_pairs={{0,12},{4,0},{8,4},{12,8},{1,13},{5,1},{9,5},{13,9},{2,14},{6,2},{... | collective-permute-start | bytes 811016 | tf_op jit(solution)/shard_map/ppermute | solution.py:606
  61.4 0.5 collective-permute-start.5
  61.9 8.1 %collective-permute-done.12.refs_4_ = bf16[528,256]{1,0:T(8,128)(2,1)S(1)} collective-permute-done((bf16[528,256]{1,0:T(8,128)(2,1)}, bf16[528,256]{1,0:T(8,128)(2,1)S(1)}, u32[]{:S(2)}, u32[]{:S(2)}) %collective-permute-start.12) | collective-permute-done | bytes 270368 | tf_op jit(solution)/shard_map/ppermute | solution.py:606
  70.0 1.0 collective-permute-start.4
  71.0 2.8 %collective-permute-done.10.refs_2_ = bf16[528,256]{1,0:T(8,128)(2,1)S(1)} collective-permute-done((bf16[528,256]{1,0:T(8,128)(2,1)}, bf16[528,256]{1,0:T(8,128)(2,1)S(1)}, u32[]{:S(2)}, u32[]{:S(2)}) %collective-permute-start.10) | collective-permute-done | bytes 270368 | tf_op jit(solution)/shard_map/ppermute | solution.py:606
  73.7 1.0 copy-done.8
  74.7 2.1 %out_blocks.3 = (bf16[144,512]{1,0:T(8,128)(2,1)S(1)}, bf16[144,512]{1,0:T(8,128)(2,1)}, bf16[144,512]{1,0:T(8,128)(2,1)}, bf16[144,512]{1,0:T(8,128)(2,1)S(1)}) custom-call(s32[2]{0:T(128)S(1)} %copy-done.5, bf16[528,256]{1,0:T(8,128)(2,1)S(1)} %copy-done.8, bf16[528,256]{1,0:T(8,128)(2,1)S(1)} %collective-permute-done.10.refs_2_, ...), custom_call_target="tpu_custom_call" | custom-call | flops 1000000000 | bytes 10000000 | tf_op jit(solution)/shard_map/out_blocks/pallas_call | solution.py:304
  76.8 1.2 collective-permute-start.16
  77.9 2.4 %collective-permute-start.17 = (bf16[144,512]{1,0:T(8,128)(2,1)}, bf16[144,512]{1,0:T(8,128)(2,1)S(1)}, u32[]{:S(2)}, u32[]{:S(2)}) collective-permute-start(bf16[144,512]{1,0:T(8,128)(2,1)} %get-tuple-element.43), channel_id=1, source_target_pairs={{0,8},{4,12},{8,0},{12,4},{1,9},{5,13},{9,1},{13,5},{2,10},{6,14},... | collective-permute-start | bytes 442376 | tf_op jit(solution)/shard_map/ppermute | solution.py:606
  80.4 1.2 collective-permute-start.18
  81.6 0.9 copy-done.7
  82.5 1.3 out_blocks.2
  83.9 2.2 %collective-permute-start.8 = (bf16[144,512]{1,0:T(8,128)(2,1)S(1)}, bf16[144,512]{1,0:T(8,128)(2,1)S(1)}, u32[]{:S(2)}, u32[]{:S(2)}) collective-permute-start(bf16[144,512]{1,0:T(8,128)(2,1)S(1)} %get-tuple-element.36), channel_id=1, source_target_pairs={{0,2},{1,3},{2,0},{3,1},{4,6},{5,7},{6,4},{7,5},{8,10},{9,11},{10,... | collective-permute-start | bytes 442376 | tf_op jit(solution)/shard_map/ppermute | solution.py:606
  86.1 0.5 collective-permute-start.9
  86.6 0.6 collective-permute-done.17.refs_3_
  87.2 0.9 residual_block.3.refs_1_
  88.1 2.0 %collective-permute-start.21 = (bf16[144,512]{1,0:T(8,128)(2,1)S(1)}, bf16[144,512]{1,0:T(8,128)(2,1)S(1)}, u32[]{:S(2)}, u32[]{:S(2)}) collective-permute-start(bf16[144,512]{1,0:T(8,128)(2,1)S(1)} %residual_block.3.refs_1_), channel_id=1, source_target_pairs={{0,3},{1,0},{2,1},{3,2},{4,7},{5,4},{6,5},{7,6},{8,11},{9,8},{10,9... | collective-permute-start | bytes 442376 | tf_op jit(solution)/shard_map/ppermute | solution.py:606
  90.3 0.7 collective-permute-done.7.refs_2_
  91.2 1.5 collective-permute-done.9.refs_4_
  92.7 0.9 residual_block.2.refs_1_
  93.6 3.0 %collective-permute-start.14 = (bf16[144,512]{1,0:T(8,128)(2,1)S(1)}, bf16[144,512]{1,0:T(8,128)(2,1)S(1)}, u32[]{:S(2)}, u32[]{:S(2)}) collective-permute-start(bf16[144,512]{1,0:T(8,128)(2,1)S(1)} %residual_block.2.refs_1_), channel_id=1, source_target_pairs={{0,8},{4,12},{8,0},{12,4},{1,9},{5,13},{9,1},{13,5},{2,10},{6,14},... | collective-permute-start | bytes 442376 | tf_op jit(solution)/shard_map/ppermute | solution.py:606
  96.6 1.6 collective-permute-done.19.refs_5_.refs_2_
  98.2 0.9 collective-permute-done.14.refs_3_.refs_6_
  99.2 2.6 %collective-permute-done.13.refs_2_.refs_5_ = bf16[144,512]{1,0:T(8,128)(2,1)S(1)} collective-permute-done((bf16[144,512]{1,0:T(8,128)(2,1)S(1)}, bf16[144,512]{1,0:T(8,128)(2,1)S(1)}, u32[]{:S(2)}, u32[]{:S(2)}) %collective-permute-start.13) | collective-permute-done | bytes 147488 | tf_op jit(solution)/shard_map/ppermute | solution.py:606
  101.8 0.6 join_columns.2.refs_1_.x0_ref
  102.5 5.5 %collective-permute-start.23 = (bf16[144,2048]{1,0:T(8,128)(2,1)S(1)}, bf16[144,2048]{1,0:T(8,128)(2,1)S(1)}, u32[]{:S(2)}, u32[]{:S(2)}) collective-permute-start(bf16[144,2048]{1,0:T(8,128)(2,1)S(1)} %join_columns.2.refs_1_.x0_ref), channel_id=1, source_target_pairs={{0,3},{1,0},{2,1},{3,2},{4,7},{5,4},{6,5},{7,6},{8,11},{9,8},{10,9... | collective-permute-start | bytes 1769480 | tf_op jit(solution)/shard_map/ppermute | solution.py:606
  108.0 0.6 join_columns.3.refs_2_.x1_ref
  108.7 1.5 collective-permute-start.24
  110.2 5.0 %fetched.1.refs_4_.w_ref = bf16[2,2048,1664]{2,1,0:T(8,128)(2,1)S(1)} custom-call(bf16[2,2048,1664]{2,1,0:T(8,128)(2,1)} %refs_0_.1, bf16[144,2048]{1,0:T(8,128)(2,1)S(1)} %join_columns.2.refs_1_.x0_ref, bf16[144,2048]{1,0:T(8,128)(2,1)} %copy-done), custom_call_target="tpu_custom_call" | custom-call | bytes 30000000 | tf_op jit(solution)/shard_map/fetched/pallas_call | solution.py:403
  115.2 1.1 copy-done.1
  116.2 3.3 %head_own.1.refs_6_ = f32[16,128]{1,0:T(8,128)S(1)} custom-call(s32[1]{0:T(128)} %bitcast.place_ref, s32[2]{0:T(128)S(1)} %copy-done.5, bf16[144,2048]{1,0:T(8,128)(2,1)S(1)} %join_columns.2.refs_1_.x0_ref, bf16[144,2048]{1,0:T(8,128)(2,1)S(1)} %copy-done.1, bf16[2,2048,1664]{2,1,0:T(8,128)(2,1)S(1)} %fetched.1.refs_4_.w_ref, s32[4,128]{1,0:T(4,128)S(1)} %bitcast.16), custom_call_target="tpu_custom_call" | custom-call | flops 1744830464 | bytes 10000000 | tf_op jit(solution)/shard_map/head_own/pallas_call | solution.py:489
  119.6 2.3 %collective-permute-done.22.refs_0_ = bf16[144,2048]{1,0:T(8,128)(2,1)S(1)} collective-permute-done((bf16[144,2048]{1,0:T(8,128)(2,1)S(1)}, bf16[144,2048]{1,0:T(8,128)(2,1)S(1)}, u32[]{:S(2)}, u32[]{:S(2)}) %collective-permute-start.22) | collective-permute-done | bytes 589856 | tf_op jit(solution)/shard_map/ppermute | solution.py:606
  121.9 0.3 collective-permute-done.24.refs_2_
  122.4 2.9 %collective-permute-start.27 = (bf16[72,2048]{1,0:T(8,128)(2,1)S(1)}, bf16[72,2048]{1,0:T(8,128)(2,1)S(1)}, u32[]{:S(2)}, u32[]{:S(2)}) collective-permute-start(bf16[72,2048]{1,0:T(8,128)(2,1)S(1)} %get-tuple-element.47), channel_id=1, source_target_pairs={{0,3},{1,0},{2,1},{3,2},{4,7},{5,4},{6,5},{7,6},{8,11},{9,8},{10,9... | collective-permute-start | bytes 884744 | tf_op jit(solution)/shard_map/ppermute | solution.py:606
  125.4 2.6 %collective-permute-start.29 = (bf16[72,2048]{1,0:T(8,128)(2,1)S(1)}, bf16[72,2048]{1,0:T(8,128)(2,1)S(1)}, u32[]{:S(2)}, u32[]{:S(2)}) collective-permute-start(bf16[72,2048]{1,0:T(8,128)(2,1)S(1)} %get-tuple-element.49), channel_id=1, source_target_pairs={{0,12},{4,0},{8,4},{12,8},{1,13},{5,1},{9,5},{13,9},{2,14},{6,2},{... | collective-permute-start | bytes 884744 | tf_op jit(solution)/shard_map/ppermute | solution.py:606
  128.0 5.2 %head_near.1.refs_6_ = f32[16,128]{1,0:T(8,128)S(1)} custom-call(s32[1]{0:T(128)} %bitcast.place_ref, s32[2]{0:T(128)S(1)} %copy-done.5, bf16[144,2048]{1,0:T(8,128)(2,1)S(1)} %collective-permute-done.22.refs_0_, bf16[144,2048]{1,0:T(8,128)(2,1)S(1)} %collective-permute-done.23.refs_1_, bf16[144,2048]{1,0:T(8,128)(2,1)S(1)} %collective-permute-done.24.refs_2_, ...), custom_call_target="tpu_custom_call" | custom-call | flops 3489660928 | bytes 10000000 | tf_op jit(solution)/shard_map/head_near/pallas_call | solution.py:498
  133.2 3.3 %head_far.1 = f32[16,16,128]{2,1,0:T(8,128)S(1)} custom-call(s32[1]{0:T(128)} %bitcast.place_ref, s32[2]{0:T(128)S(1)} %copy-done.5, bf16[72,2048]{1,0:T(8,128)(2,1)S(1)} %collective-permute-done.26.refs_0_, bf16[72,2048]{1,0:T(8,128)(2,1)S(1)} %collective-permute-done.27.refs_1_, bf16[72,2048]{1,0:T(8,128)(2,1)S(1)} %collective-permute-done.28.refs_2_, ...), custom_call_target="tpu_custom_call" | custom-call | flops 1744830464 | bytes 10000000 | tf_op jit(solution)/shard_map/head_far/pallas_call | solution.py:507
  136.6 10.7 %all_to_all.15.stat_ref = f32[16,16,128]{2,1,0:T(8,128)} all-to-all(f32[16,16,128]{2,1,0:T(8,128)S(1)} %head_far.1), channel_id=1, replica_groups=mesh['y'=4,'core'=2,'x'=4,'z'=4] {'x','z'}, dimensions={0} | all-to-all | bytes 262144 | tf_op jit(solution)/shard_map/all_to_all | solution.py:649
  147.3 1.7 %token_diffs.1 = (f32[4,128]{1,0:T(4,128)}, f32[8,128]{1,0:T(8,128)}) custom-call(f32[16,16,128]{2,1,0:T(8,128)} %all_to_all.15.stat_ref, s32[2]{0:T(128)} %live_ref.1, s32[4,128]{1,0:T(4,128)} %bitcast.22), custom_call_target="tpu_custom_call" | custom-call | tf_op jit(solution)/shard_map/token_diffs/pallas_call | solution.py:563
  149.0 6.6 %collective-permute-start.30 = (f32[8,128]{1,0:T(8,128)}, f32[8,128]{1,0:T(8,128)S(1)}, u32[]{:S(2)}, u32[]{:S(2)}) collective-permute-start(f32[8,128]{1,0:T(8,128)} %get-tuple-element.51), channel_id=1, source_target_pairs={{0,16},{16,0},{1,17},{17,1},{2,18},{18,2},{3,19},{19,3},{4,20},{20... | collective-permute-start | bytes 12296 | tf_op jit(solution)/shard_map/ppermute | solution.py:651
  155.6 1.0 collective-permute-done.30
  156.6 0.7 add.20
  157.3 2.2 %collective-permute-start.32 = (f32[8,128]{1,0:T(8,128)S(1)}, f32[8,128]{1,0:T(8,128)S(1)}, u32[]{:S(2)}, u32[]{:S(2)}) collective-permute-start(f32[8,128]{1,0:T(8,128)S(1)} %add.20), channel_id=1, source_target_pairs={{0,64},{32,96},{64,0},{96,32},{1,65},{33,97},{65,1},{97,33},{2,66}... | collective-permute-start | bytes 12296 | tf_op jit(solution)/shard_map/ppermute | solution.py:606
  159.8 1.5 collective-permute-done.32
  161.3 1.9 %collective-permute-done.31 = f32[8,128]{1,0:T(8,128)S(1)} collective-permute-done((f32[8,128]{1,0:T(8,128)S(1)}, f32[8,128]{1,0:T(8,128)S(1)}, u32[]{:S(2)}, u32[]{:S(2)}) %collective-permute-start.31) | collective-permute-done | bytes 4128 | tf_op jit(solution)/shard_map/ppermute | solution.py:606
  163.3 0.5 fusion
  (63 shorter events, 1.5 us)
Async XLA Ops:
  1.3 9.8 %copy-start.10 = (bf16[2,2048,2,128]{3,2,1,0:T(2,128)(2,1)S(1)}, bf16[2,2048,2,128]{3,2,1,0:T(2,128)(2,1)}, u32[]{:S(2)}) copy-start(bf16[2,2048,2,128]{3,2,1,0:T(2,128)(2,1)} %param.20) | copy-start | bytes 6291460
  5.2 38.1 %all-to-all-start.1 = ((bf16[4,256,512]{2,1,0:T(8,128)(2,1)}), bf16[4,256,512]{2,1,0:T(8,128)(2,1)S(1)}, u32[]{:S(2)}, u32[]{:S(2)}) async-start(bf16[4,256,512]{2,1,0:T(8,128)(2,1)} %get-tuple-element.40), calls=%async_computation.1 | async-start | bytes 2097152 | tf_op jit(solution)/shard_map/all_to_all | solution.py:632
  11.0 2.9 %copy-start.9 = (bf16[2,2048,2,256]{3,2,1,0:T(2,128)(2,1)S(1)}, bf16[2,2048,2,256]{3,2,1,0:T(2,128)(2,1)}, u32[]{:S(2)}) copy-start(bf16[2,2048,2,256]{3,2,1,0:T(2,128)(2,1)} %param.19) | copy-start | bytes 12582916
  31.7 15.5 %collective-permute-start.3 = (bf16[2,272,128]{2,1,0:T(8,128)(2,1)}, bf16[2,272,128]{2,1,0:T(8,128)(2,1)S(1)}, u32[]{:S(2)}, u32[]{:S(2)}) collective-permute-start(bf16[2,272,128]{2,1,0:T(8,128)(2,1)} %get-tuple-element.31), channel_id=1, source_target_pairs={{0,64},{16,80},{32,96},{48,112},{1,65},{17,81},{33,97},{49,113},{2... | collective-permute-start | bytes 417800 | tf_op jit(solution)/shard_map/ppermute | solution.py:634
  36.6 10.7 %collective-permute-start.2 = (bf16[2,272,128]{2,1,0:T(8,128)(2,1)}, bf16[2,272,128]{2,1,0:T(8,128)(2,1)S(1)}, u32[]{:S(2)}, u32[]{:S(2)}) collective-permute-start(bf16[2,272,128]{2,1,0:T(8,128)(2,1)} %get-tuple-element.31), channel_id=1, source_target_pairs={{0,48},{16,64},{32,80},{48,96},{64,112},{1,49},{17,65},{33,81},{49... | collective-permute-start | bytes 417800 | tf_op jit(solution)/shard_map/ppermute | solution.py:634
  38.7 8.6 %collective-permute-start.1 = (bf16[2,272,128]{2,1,0:T(8,128)(2,1)}, bf16[2,272,128]{2,1,0:T(8,128)(2,1)S(1)}, u32[]{:S(2)}, u32[]{:S(2)}) collective-permute-start(bf16[2,272,128]{2,1,0:T(8,128)(2,1)} %get-tuple-element.31), channel_id=1, source_target_pairs={{0,32},{16,48},{32,64},{48,80},{64,96},{80,112},{1,33},{17,49},{33... | collective-permute-start | bytes 417800 | tf_op jit(solution)/shard_map/ppermute | solution.py:634
  41.0 6.8 %collective-permute-start = (bf16[2,272,128]{2,1,0:T(8,128)(2,1)}, bf16[2,272,128]{2,1,0:T(8,128)(2,1)S(1)}, u32[]{:S(2)}, u32[]{:S(2)}) collective-permute-start(bf16[2,272,128]{2,1,0:T(8,128)(2,1)} %get-tuple-element.31), channel_id=1, source_target_pairs={{0,16},{16,32},{32,48},{48,64},{64,80},{80,96},{96,112},{1,17},{17... | collective-permute-start | bytes 417800 | tf_op jit(solution)/shard_map/ppermute | solution.py:634
  43.2 38.3 %all-to-all-start = ((bf16[4,256,512]{2,1,0:T(8,128)(2,1)}), bf16[4,256,512]{2,1,0:T(8,128)(2,1)S(1)}, u32[]{:S(2)}, u32[]{:S(2)}) async-start(bf16[4,256,512]{2,1,0:T(8,128)(2,1)} %get-tuple-element.33), calls=%async_computation | async-start | bytes 2097152 | tf_op jit(solution)/shard_map/all_to_all | solution.py:632
  47.3 0.7 copy-start.11
  47.3 0.7 copy-start.12
  47.3 0.7 copy-start.13
  47.9 0.7 copy-start.14
  48.5 25.2 %copy-start.5 = (s32[2]{0:T(128)S(1)}, s32[2]{0:T(128)}, u32[]{:S(2)}) copy-start(s32[2]{0:T(128)} %pad_add_fusion.at_ref.refs_0_) | copy-start | bytes 28
  54.8 32.4 %copy-start.3 = (bf16[128,512]{1,0:T(8,128)(2,1)S(1)}, bf16[128,512]{1,0:T(8,128)(2,1)}, u32[]{:S(2)}) copy-start(bf16[128,512]{1,0:T(8,128)(2,1)} %get-tuple-element.45.refs_5_) | copy-start | bytes 393220
  54.8 32.4 %copy-start.4 = (f32[2,2048]{1,0:T(2,128)S(1)}, f32[2,2048]{1,0:T(2,128)}, u32[]{:S(2)}) copy-start(f32[2,2048]{1,0:T(2,128)} %refs_6_.3) | copy-start | bytes 49156
  54.8 15.2 %collective-permute-start.12 = (bf16[528,256]{1,0:T(8,128)(2,1)}, bf16[528,256]{1,0:T(8,128)(2,1)S(1)}, u32[]{:S(2)}, u32[]{:S(2)}) collective-permute-start(bf16[528,256]{1,0:T(8,128)(2,1)} %get-tuple-element.39.refs_1_), channel_id=1, source_target_pairs={{0,3},{1,0},{2,1},{3,2},{4,7},{5,4},{6,5},{7,6},{8,11},{9,8},{10,9... | collective-permute-start | bytes 811016 | tf_op jit(solution)/shard_map/ppermute | solution.py:606
  57.7 13.2 %collective-permute-start.11 = (bf16[528,256]{1,0:T(8,128)(2,1)}, bf16[528,256]{1,0:T(8,128)(2,1)S(1)}, u32[]{:S(2)}, u32[]{:S(2)}) collective-permute-start(bf16[528,256]{1,0:T(8,128)(2,1)} %get-tuple-element.39.refs_1_), channel_id=1, source_target_pairs={{0,2},{1,3},{2,0},{3,1},{4,6},{5,7},{6,4},{7,5},{8,10},{9,11},{10,... | collective-permute-start | bytes 811016 | tf_op jit(solution)/shard_map/ppermute | solution.py:606
  58.3 15.4 %collective-permute-start.10 = (bf16[528,256]{1,0:T(8,128)(2,1)}, bf16[528,256]{1,0:T(8,128)(2,1)S(1)}, u32[]{:S(2)}, u32[]{:S(2)}) collective-permute-start(bf16[528,256]{1,0:T(8,128)(2,1)} %get-tuple-element.39.refs_1_), channel_id=1, source_target_pairs={{0,1},{1,2},{2,3},{3,0},{4,5},{5,6},{6,7},{7,4},{8,9},{9,10},{10,1... | collective-permute-start | bytes 811016 | tf_op jit(solution)/shard_map/ppermute | solution.py:606
  58.9 33.8 %copy-start.2 = (bf16[128,512]{1,0:T(8,128)(2,1)S(1)}, bf16[128,512]{1,0:T(8,128)(2,1)}, u32[]{:S(2)}) copy-start(bf16[128,512]{1,0:T(8,128)(2,1)} %get-tuple-element.38.refs_5_) | copy-start | bytes 393220
  58.9 21.5 %collective-permute-start.6 = (bf16[528,256]{1,0:T(8,128)(2,1)}, bf16[528,256]{1,0:T(8,128)(2,1)S(1)}, u32[]{:S(2)}, u32[]{:S(2)}) collective-permute-start(bf16[528,256]{1,0:T(8,128)(2,1)} %get-tuple-element.32.refs_1_), channel_id=1, source_target_pairs={{0,12},{4,0},{8,4},{12,8},{1,13},{5,1},{9,5},{13,9},{2,14},{6,2},{... | collective-permute-start | bytes 811016 | tf_op jit(solution)/shard_map/ppermute | solution.py:606
  61.4 20.1 %collective-permute-start.5 = (bf16[528,256]{1,0:T(8,128)(2,1)}, bf16[528,256]{1,0:T(8,128)(2,1)S(1)}, u32[]{:S(2)}, u32[]{:S(2)}) collective-permute-start(bf16[528,256]{1,0:T(8,128)(2,1)} %get-tuple-element.32.refs_1_), channel_id=1, source_target_pairs={{0,8},{4,12},{8,0},{12,4},{1,9},{5,13},{9,1},{13,5},{2,10},{6,14},... | collective-permute-start | bytes 811016 | tf_op jit(solution)/shard_map/ppermute | solution.py:606
  70.0 11.5 %collective-permute-start.4 = (bf16[528,256]{1,0:T(8,128)(2,1)}, bf16[528,256]{1,0:T(8,128)(2,1)S(1)}, u32[]{:S(2)}, u32[]{:S(2)}) collective-permute-start(bf16[528,256]{1,0:T(8,128)(2,1)} %get-tuple-element.32.refs_1_), channel_id=1, source_target_pairs={{0,4},{4,8},{8,12},{12,0},{1,5},{5,9},{9,13},{13,1},{2,6},{6,10},{... | collective-permute-start | bytes 811016 | tf_op jit(solution)/shard_map/ppermute | solution.py:606
  73.7 1.0 copy-start.8
  76.8 9.4 %collective-permute-start.16 = (bf16[144,512]{1,0:T(8,128)(2,1)}, bf16[144,512]{1,0:T(8,128)(2,1)S(1)}, u32[]{:S(2)}, u32[]{:S(2)}) collective-permute-start(bf16[144,512]{1,0:T(8,128)(2,1)} %get-tuple-element.42), channel_id=1, source_target_pairs={{0,4},{4,8},{8,12},{12,0},{1,5},{5,9},{9,13},{13,1},{2,6},{6,10},{... | collective-permute-start | bytes 442376 | tf_op jit(solution)/shard_map/ppermute | solution.py:606
  77.9 9.3 %collective-permute-start.17 = (bf16[144,512]{1,0:T(8,128)(2,1)}, bf16[144,512]{1,0:T(8,128)(2,1)S(1)}, u32[]{:S(2)}, u32[]{:S(2)}) collective-permute-start(bf16[144,512]{1,0:T(8,128)(2,1)} %get-tuple-element.43), channel_id=1, source_target_pairs={{0,8},{4,12},{8,0},{12,4},{1,9},{5,13},{9,1},{13,5},{2,10},{6,14},... | collective-permute-start | bytes 442376 | tf_op jit(solution)/shard_map/ppermute | solution.py:606
  80.4 6.8 %collective-permute-start.18 = (bf16[144,512]{1,0:T(8,128)(2,1)S(1)}, bf16[144,512]{1,0:T(8,128)(2,1)S(1)}, u32[]{:S(2)}, u32[]{:S(2)}) collective-permute-start(bf16[144,512]{1,0:T(8,128)(2,1)S(1)} %get-tuple-element.44), channel_id=1, source_target_pairs={{0,12},{4,0},{8,4},{12,8},{1,13},{5,1},{9,5},{13,9},{2,14},{6,2},{... | collective-permute-start | bytes 442376 | tf_op jit(solution)/shard_map/ppermute | solution.py:606
  81.5 1.0 copy-start.7
  83.8 7.2 %collective-permute-start.7 = (bf16[144,512]{1,0:T(8,128)(2,1)S(1)}, bf16[144,512]{1,0:T(8,128)(2,1)S(1)}, u32[]{:S(2)}, u32[]{:S(2)}) collective-permute-start(bf16[144,512]{1,0:T(8,128)(2,1)S(1)} %get-tuple-element.35), channel_id=1, source_target_pairs={{0,1},{1,2},{2,3},{3,0},{4,5},{5,6},{6,7},{7,4},{8,9},{9,10},{10,1... | collective-permute-start | bytes 442376 | tf_op jit(solution)/shard_map/ppermute | solution.py:606
  83.9 7.3 %collective-permute-start.8 = (bf16[144,512]{1,0:T(8,128)(2,1)S(1)}, bf16[144,512]{1,0:T(8,128)(2,1)S(1)}, u32[]{:S(2)}, u32[]{:S(2)}) collective-permute-start(bf16[144,512]{1,0:T(8,128)(2,1)S(1)} %get-tuple-element.36), channel_id=1, source_target_pairs={{0,2},{1,3},{2,0},{3,1},{4,6},{5,7},{6,4},{7,5},{8,10},{9,11},{10,... | collective-permute-start | bytes 442376 | tf_op jit(solution)/shard_map/ppermute | solution.py:606
  86.1 6.6 %collective-permute-start.9 = (bf16[144,512]{1,0:T(8,128)(2,1)S(1)}, bf16[144,512]{1,0:T(8,128)(2,1)S(1)}, u32[]{:S(2)}, u32[]{:S(2)}) collective-permute-start(bf16[144,512]{1,0:T(8,128)(2,1)S(1)} %get-tuple-element.37), channel_id=1, source_target_pairs={{0,3},{1,0},{2,1},{3,2},{4,7},{5,4},{6,5},{7,6},{8,11},{9,8},{10,9... | collective-permute-start | bytes 442376 | tf_op jit(solution)/shard_map/ppermute | solution.py:606
  88.1 8.5 %collective-permute-start.21 = (bf16[144,512]{1,0:T(8,128)(2,1)S(1)}, bf16[144,512]{1,0:T(8,128)(2,1)S(1)}, u32[]{:S(2)}, u32[]{:S(2)}) collective-permute-start(bf16[144,512]{1,0:T(8,128)(2,1)S(1)} %residual_block.3.refs_1_), channel_id=1, source_target_pairs={{0,3},{1,0},{2,1},{3,2},{4,7},{5,4},{6,5},{7,6},{8,11},{9,8},{10,9... | collective-permute-start | bytes 442376 | tf_op jit(solution)/shard_map/ppermute | solution.py:606
  90.1 6.5 %collective-permute-start.20 = (bf16[144,512]{1,0:T(8,128)(2,1)S(1)}, bf16[144,512]{1,0:T(8,128)(2,1)S(1)}, u32[]{:S(2)}, u32[]{:S(2)}) collective-permute-start(bf16[144,512]{1,0:T(8,128)(2,1)S(1)} %residual_block.3.refs_1_), channel_id=1, source_target_pairs={{0,2},{1,3},{2,0},{3,1},{4,6},{5,7},{6,4},{7,5},{8,10},{9,11},{10,... | collective-permute-start | bytes 442376 | tf_op jit(solution)/shard_map/ppermute | solution.py:606
  91.0 7.2 %collective-permute-start.19 = (bf16[144,512]{1,0:T(8,128)(2,1)S(1)}, bf16[144,512]{1,0:T(8,128)(2,1)S(1)}, u32[]{:S(2)}, u32[]{:S(2)}) collective-permute-start(bf16[144,512]{1,0:T(8,128)(2,1)S(1)} %residual_block.3.refs_1_), channel_id=1, source_target_pairs={{0,1},{1,2},{2,3},{3,0},{4,5},{5,6},{6,7},{7,4},{8,9},{9,10},{10,1... | collective-permute-start | bytes 442376 | tf_op jit(solution)/shard_map/ppermute | solution.py:606
  93.5 4.7 %collective-permute-start.15 = (bf16[144,512]{1,0:T(8,128)(2,1)S(1)}, bf16[144,512]{1,0:T(8,128)(2,1)S(1)}, u32[]{:S(2)}, u32[]{:S(2)}) collective-permute-start(bf16[144,512]{1,0:T(8,128)(2,1)S(1)} %residual_block.2.refs_1_), channel_id=1, source_target_pairs={{0,12},{4,0},{8,4},{12,8},{1,13},{5,1},{9,5},{13,9},{2,14},{6,2},{... | collective-permute-start | bytes 442376 | tf_op jit(solution)/shard_map/ppermute | solution.py:606
  93.6 5.6 %collective-permute-start.14 = (bf16[144,512]{1,0:T(8,128)(2,1)S(1)}, bf16[144,512]{1,0:T(8,128)(2,1)S(1)}, u32[]{:S(2)}, u32[]{:S(2)}) collective-permute-start(bf16[144,512]{1,0:T(8,128)(2,1)S(1)} %residual_block.2.refs_1_), channel_id=1, source_target_pairs={{0,8},{4,12},{8,0},{12,4},{1,9},{5,13},{9,1},{13,5},{2,10},{6,14},... | collective-permute-start | bytes 442376 | tf_op jit(solution)/shard_map/ppermute | solution.py:606
  96.6 5.2 %collective-permute-start.13 = (bf16[144,512]{1,0:T(8,128)(2,1)S(1)}, bf16[144,512]{1,0:T(8,128)(2,1)S(1)}, u32[]{:S(2)}, u32[]{:S(2)}) collective-permute-start(bf16[144,512]{1,0:T(8,128)(2,1)S(1)} %residual_block.2.refs_1_), channel_id=1, source_target_pairs={{0,4},{4,8},{8,12},{12,0},{1,5},{5,9},{9,13},{13,1},{2,6},{6,10},{... | collective-permute-start | bytes 442376 | tf_op jit(solution)/shard_map/ppermute | solution.py:606
  102.5 17.1 %collective-permute-start.23 = (bf16[144,2048]{1,0:T(8,128)(2,1)S(1)}, bf16[144,2048]{1,0:T(8,128)(2,1)S(1)}, u32[]{:S(2)}, u32[]{:S(2)}) collective-permute-start(bf16[144,2048]{1,0:T(8,128)(2,1)S(1)} %join_columns.2.refs_1_.x0_ref), channel_id=1, source_target_pairs={{0,3},{1,0},{2,1},{3,2},{4,7},{5,4},{6,5},{7,6},{8,11},{9,8},{10,9... | collective-permute-start | bytes 1769480 | tf_op jit(solution)/shard_map/ppermute | solution.py:606
  108.0 13.9 %collective-permute-start.22 = (bf16[144,2048]{1,0:T(8,128)(2,1)S(1)}, bf16[144,2048]{1,0:T(8,128)(2,1)S(1)}, u32[]{:S(2)}, u32[]{:S(2)}) collective-permute-start(bf16[144,2048]{1,0:T(8,128)(2,1)S(1)} %join_columns.2.refs_1_.x0_ref), channel_id=1, source_target_pairs={{0,1},{1,2},{2,3},{3,0},{4,5},{5,6},{6,7},{7,4},{8,9},{9,10},{10,1... | collective-permute-start | bytes 1769480 | tf_op jit(solution)/shard_map/ppermute | solution.py:606
  108.6 1.5 copy-start
  108.7 13.2 %collective-permute-start.25 = (bf16[144,2048]{1,0:T(8,128)(2,1)S(1)}, bf16[144,2048]{1,0:T(8,128)(2,1)S(1)}, u32[]{:S(2)}, u32[]{:S(2)}) collective-permute-start(bf16[144,2048]{1,0:T(8,128)(2,1)S(1)} %join_columns.3.refs_2_.x1_ref), channel_id=1, source_target_pairs={{0,12},{4,0},{8,4},{12,8},{1,13},{5,1},{9,5},{13,9},{2,14},{6,2},{... | collective-permute-start | bytes 1769480 | tf_op jit(solution)/shard_map/ppermute | solution.py:606
  108.7 13.5 %collective-permute-start.24 = (bf16[144,2048]{1,0:T(8,128)(2,1)S(1)}, bf16[144,2048]{1,0:T(8,128)(2,1)S(1)}, u32[]{:S(2)}, u32[]{:S(2)}) collective-permute-start(bf16[144,2048]{1,0:T(8,128)(2,1)S(1)} %join_columns.3.refs_2_.x1_ref), channel_id=1, source_target_pairs={{0,4},{4,8},{8,12},{12,0},{1,5},{5,9},{9,13},{13,1},{2,6},{6,10},{... | collective-permute-start | bytes 1769480 | tf_op jit(solution)/shard_map/ppermute | solution.py:606
  110.2 5.0 %copy-start.6 = (s32[512]{0:T(512)S(1)}, s32[512]{0:T(512)}, u32[]{:S(2)}) copy-start(s32[512]{0:T(512)} %param.30) | copy-start | bytes 6148
  115.2 1.1 copy-start.1
  122.3 10.9 %collective-permute-start.26 = (bf16[72,2048]{1,0:T(8,128)(2,1)S(1)}, bf16[72,2048]{1,0:T(8,128)(2,1)S(1)}, u32[]{:S(2)}, u32[]{:S(2)}) collective-permute-start(bf16[72,2048]{1,0:T(8,128)(2,1)S(1)} %get-tuple-element.46), channel_id=1, source_target_pairs={{0,1},{1,2},{2,3},{3,0},{4,5},{5,6},{6,7},{7,4},{8,9},{9,10},{10,1... | collective-permute-start | bytes 884744 | tf_op jit(solution)/shard_map/ppermute | solution.py:606
  122.4 10.8 %collective-permute-start.27 = (bf16[72,2048]{1,0:T(8,128)(2,1)S(1)}, bf16[72,2048]{1,0:T(8,128)(2,1)S(1)}, u32[]{:S(2)}, u32[]{:S(2)}) collective-permute-start(bf16[72,2048]{1,0:T(8,128)(2,1)S(1)} %get-tuple-element.47), channel_id=1, source_target_pairs={{0,3},{1,0},{2,1},{3,2},{4,7},{5,4},{6,5},{7,6},{8,11},{9,8},{10,9... | collective-permute-start | bytes 884744 | tf_op jit(solution)/shard_map/ppermute | solution.py:606
  125.3 7.9 %collective-permute-start.28 = (bf16[72,2048]{1,0:T(8,128)(2,1)S(1)}, bf16[72,2048]{1,0:T(8,128)(2,1)S(1)}, u32[]{:S(2)}, u32[]{:S(2)}) collective-permute-start(bf16[72,2048]{1,0:T(8,128)(2,1)S(1)} %get-tuple-element.48), channel_id=1, source_target_pairs={{0,4},{4,8},{8,12},{12,0},{1,5},{5,9},{9,13},{13,1},{2,6},{6,10},{... | collective-permute-start | bytes 884744 | tf_op jit(solution)/shard_map/ppermute | solution.py:606
  125.4 7.8 %collective-permute-start.29 = (bf16[72,2048]{1,0:T(8,128)(2,1)S(1)}, bf16[72,2048]{1,0:T(8,128)(2,1)S(1)}, u32[]{:S(2)}, u32[]{:S(2)}) collective-permute-start(bf16[72,2048]{1,0:T(8,128)(2,1)S(1)} %get-tuple-element.49), channel_id=1, source_target_pairs={{0,12},{4,0},{8,4},{12,8},{1,13},{5,1},{9,5},{13,9},{2,14},{6,2},{... | collective-permute-start | bytes 884744 | tf_op jit(solution)/shard_map/ppermute | solution.py:606
  133.2 30.1 %copy-start.15 = (s32[4]{0:T(128)S(1)}, s32[4]{0:T(128)}, u32[]{:S(2)}) copy-start(s32[4]{0:T(128)} %param.35) | copy-start | bytes 52
  149.0 7.6 %collective-permute-start.30 = (f32[8,128]{1,0:T(8,128)}, f32[8,128]{1,0:T(8,128)S(1)}, u32[]{:S(2)}, u32[]{:S(2)}) collective-permute-start(f32[8,128]{1,0:T(8,128)} %get-tuple-element.51), channel_id=1, source_target_pairs={{0,16},{16,0},{1,17},{17,1},{2,18},{18,2},{3,19},{19,3},{4,20},{20... | collective-permute-start | bytes 12296 | tf_op jit(solution)/shard_map/ppermute | solution.py:651
  157.3 2.5 %collective-permute-start.33 = (f32[8,128]{1,0:T(8,128)S(1)}, f32[8,128]{1,0:T(8,128)S(1)}, u32[]{:S(2)}, u32[]{:S(2)}) collective-permute-start(f32[8,128]{1,0:T(8,128)S(1)} %add.20), channel_id=1, source_target_pairs={{0,96},{32,0},{64,32},{96,64},{1,97},{33,1},{65,33},{97,65},{2,98}... | collective-permute-start | bytes 12296 | tf_op jit(solution)/shard_map/ppermute | solution.py:606
  157.3 4.0 %collective-permute-start.32 = (f32[8,128]{1,0:T(8,128)S(1)}, f32[8,128]{1,0:T(8,128)S(1)}, u32[]{:S(2)}, u32[]{:S(2)}) collective-permute-start(f32[8,128]{1,0:T(8,128)S(1)} %add.20), channel_id=1, source_target_pairs={{0,64},{32,96},{64,0},{96,32},{1,65},{33,97},{65,1},{97,33},{2,66}... | collective-permute-start | bytes 12296 | tf_op jit(solution)/shard_map/ppermute | solution.py:606
  159.5 3.7 %collective-permute-start.31 = (f32[8,128]{1,0:T(8,128)S(1)}, f32[8,128]{1,0:T(8,128)S(1)}, u32[]{:S(2)}, u32[]{:S(2)}) collective-permute-start(f32[8,128]{1,0:T(8,128)S(1)} %add.20), channel_id=1, source_target_pairs={{0,32},{32,64},{64,96},{96,0},{1,33},{33,65},{65,97},{97,1},{2,34}... | collective-permute-start | bytes 12296 | tf_op jit(solution)/shard_map/ppermute | solution.py:606
